TPU v7x, 32 devices: a whole 2x2x4 slice. The times are simulated.
32 devices in a mesh: tm: 8 (over z, y), slab: 4 (over x, core).
Axes of the slice: x: 2, y: 2, z: 4, core: 2. Of those that a mesh axis runs over, the one named last changes fastest.
Arguments:
- features: bfloat16 [8, 6144, 256], P('tm', 'slab'), may hold values from -6 to 6
- ref_lists: int32 [8, 4, 16], P('tm'), may hold values from 0 to 11
- tile_rows: int32 [8, 128], P('tm', 'slab'), may hold values from 0 to 11
- tile_sources: int32 [8, 128], P('tm', 'slab'), may hold values from 0 to 15
- tile_counts: int32 [8, 4], P('tm', 'slab'), may hold values from 9 to 32
- tile_values: bfloat16 [8, 128, 128, 128], P('tm', 'slab'), may hold values from -0.3125 to 0.3125
- w_input: bfloat16 [2, 256, 1024], replicated, may hold values from -0.375 to 0.375
- w_hidden: bfloat16 [2, 256, 1024], replicated, may hold values from -0.375 to 0.375
- bias: float32 [2, 1024], replicated, may hold values from -4 to 4
Outputs:
- hidden_out: bfloat16 [8, 6144, 256], P('tm', 'slab')
Inputs may be any that keep to these rules, and one draw needn't show every extreme that they name: `ref_lists`: row tile indices within a slab. `tile_counts`: slots at or after the count are ignored.
All inputs are finite; a program needn't handle non-finite values.
Results may differ from a plain program's by a relative error of at most 0.0055.
Values may be sent and summed in bfloat16 or wider, within the bound.
No kernel may reach another device: no remote copies, remote signals or barrier semaphores. Data moves between devices by JAX's collectives and lax.ppermute only.
A program may use at most 64 MiB of HBM per device.

v0:
```python
import jax
import jax.numpy as jnp
from jax import lax
from jax.experimental import pallas as pl
from jax.experimental.pallas import tpu as pltpu
from jax.sharding import PartitionSpec as P


HBM = pl.BlockSpec(memory_space=pltpu.HBM)
VMEM = pl.BlockSpec(memory_space=pltpu.VMEM)
PARAMS = pltpu.CompilerParams(vmem_limit_bytes=16 * 2**20)
UNROLL = 4
LANES = 128
CHUNKS = 2
AXES = ("tm", "slab")
LOWER, UPPER, BOTH = 0, 1, None


def seat(group):
    index = lax.axis_index("tm")
    half = index // group
    place = index % group
    return half, place, place ^ (half * mirror(group))


def mirror(group):
    return group - 2 if group > 2 else 0


def only(mode, half):
    def run(body):
        if mode is BOTH:
            body()
        else:
            pl.when(half == mode)(body)

    return run


def pick_tiles(parts, ref_table, slab_count, row_count, tile, group, column):
    part_count = len(parts)
    part_rows = parts[0].shape[0]
    listed = ref_table.shape[2] // slab_count
    whole = part_count == 1

    def kernel(table_hbm, *refs):
        sources = refs[:part_count]
        outs = refs[part_count : part_count + slab_count]
        table, table_sem, rows, sems = refs[part_count + slab_count :]
        slab = lax.axis_index("slab")
        _, _, lead = seat(group)
        fetch = pltpu.make_async_copy(table_hbm, table, table_sem)
        fetch.start()
        if not whole:
            for k in range(part_count):
                start = pl.multiple_of((lead ^ k) * part_rows, part_rows)
                rows[pl.ds(start, part_rows), :] = sources[k][...]
        fetch.wait()
        copies = []
        for k in reversed(range(slab_count)):
            for j in range(listed):
                index = table[0, slab ^ k, slab * listed + j]
                start = pl.multiple_of(index * tile, tile)
                if whole:
                    source = sources[0].at[pl.ds(start, tile), pl.ds(column * LANES, LANES)]
                    target = outs[k].at[pl.ds(j * tile, tile)]
                    copies.append(pltpu.make_async_copy(source, target, sems.at[k, j]))
                else:
                    outs[k][j * tile : (j + 1) * tile, :] = rows[pl.ds(start, tile), :]
        for copy in copies:
            copy.start()
        for copy in copies:
            copy.wait()

    dtype = parts[0].dtype
    return pl.pallas_call(
        kernel,
        in_specs=[HBM] + [HBM if whole else VMEM] * part_count,
        out_specs=[VMEM] * slab_count,
        out_shape=[jax.ShapeDtypeStruct((listed * tile, LANES), dtype)] * slab_count,
        scratch_shapes=[
            pltpu.SMEM(ref_table.shape, ref_table.dtype),
            pltpu.SemaphoreType.DMA(()),
            pltpu.VMEM((tile if whole else row_count, LANES), dtype),
            pltpu.SemaphoreType.DMA((slab_count, listed)),
        ],
        compiler_params=PARAMS,
        name="pick_tiles",
    )(ref_table, *parts)


def convolve(arrived, tile_rows, tile_sources, tile_counts, tile_values, row_count, group):
    slab_count = len(arrived)
    piece, width = arrived[0].shape
    tile = tile_values.shape[2]
    group_rows = row_count // group

    tables = (tile_rows, tile_sources, tile_counts)

    def kernel(*refs):
        values = refs[3]
        pieces = refs[4 : 4 + slab_count]
        outs = refs[4 + slab_count : 4 + slab_count + group]
        rows, sources, counts, sems, inputs, total = refs[4 + slab_count + group :]
        slab = lax.axis_index("slab")
        _, _, lead = seat(group)
        fetches = [
            pltpu.make_async_copy(refs[n], local_ref, sems.at[n])
            for n, local_ref in enumerate((rows, sources, counts))
        ]
        for fetch in fetches:
            fetch.start()
        for k in range(slab_count):
            start = pl.multiple_of((slab ^ k) * piece, piece)
            inputs[pl.ds(start, piece), :] = pieces[k][...]
        total[...] = jnp.zeros_like(total)
        for fetch in fetches:
            fetch.wait()
        count = counts[0, 0]

        def step(index, carry):
            products = []
            for lane in range(UNROLL):
                slot = index * UNROLL + lane
                start = pl.multiple_of(sources[0, slot] * tile, tile)
                product = jnp.dot(
                    values[0, slot],
                    inputs[pl.ds(start, tile), :],
                    preferred_element_type=jnp.float32,
                )
                products.append(jnp.where(slot < count, product, 0.0))
            for lane in range(UNROLL):
                target = pl.multiple_of(rows[0, index * UNROLL + lane] * tile, tile)
                total[pl.ds(target, tile), :] += products[lane]
            return carry

        lax.fori_loop(0, (count + UNROLL - 1) // UNROLL, step, 0)
        for k in range(group):
            start = pl.multiple_of((lead ^ k) * group_rows, group_rows)
            outs[k][...] = total[pl.ds(start, group_rows), :].astype(outs[k].dtype)

    dtype = arrived[0].dtype
    return pl.pallas_call(
        kernel,
        in_specs=[HBM, HBM, HBM, VMEM] + [VMEM] * slab_count,
        out_specs=[VMEM] * group,
        out_shape=[jax.ShapeDtypeStruct((group_rows, width), dtype)] * group,
        scratch_shapes=[pltpu.SMEM(table.shape, table.dtype) for table in tables]
        + [
            pltpu.SemaphoreType.DMA((3,)),
            pltpu.VMEM((slab_count * piece, width), dtype),
            pltpu.VMEM((row_count, width), jnp.float32),
        ],
        compiler_params=PARAMS,
        name="convolve",
    )(*tables, tile_values, *arrived)


def sigmoid(value):
    return 0.5 * jnp.tanh(0.5 * value) + 0.5


def pack(mixed):
    columns, group = len(mixed), len(mixed[0])
    rows, lanes = mixed[0][0].shape
    blocks = [part for column in mixed for part in column]
    size = rows // CHUNKS

    def kernel(*refs):
        _, place, _ = seat(group)
        for n in range(len(blocks)):
            first = n // group * lanes
            for chunk, out in enumerate(refs[len(blocks) :]):
                source = refs[n][chunk * size : (chunk + 1) * size, :]
                out[place ^ (n % group), :, first : first + lanes] = source

    out_shape = jax.ShapeDtypeStruct((group, size, columns * lanes), blocks[0].dtype)
    return list(pl.pallas_call(
        kernel,
        in_specs=[VMEM] * len(blocks),
        out_specs=[VMEM] * CHUNKS,
        out_shape=[out_shape] * CHUNKS,
        compiler_params=PARAMS,
        name="pack",
    )(*blocks))


def spread_into(outs, chunks, place, group):
    lanes = outs[0].shape[1]
    for n, out in enumerate(outs):
        first = n // group * lanes
        base = 0
        for chunk in chunks:
            size = chunk.shape[1]
            out[base : base + size, :] = chunk[place ^ (n % group), :, first : first + lanes]
            base += size


def spread(chunks, lanes):
    group, size, units = chunks[0].shape
    count = units // lanes * group

    def kernel(*refs):
        _, place, _ = seat(group)
        spread_into(refs[len(chunks) :], refs[: len(chunks)], place, group)

    results = pl.pallas_call(
        kernel,
        in_specs=[VMEM] * len(chunks),
        out_specs=[VMEM] * count,
        out_shape=[jax.ShapeDtypeStruct((size * len(chunks), lanes), chunks[0].dtype)] * count,
        compiler_params=PARAMS,
        name="spread",
    )(*chunks)
    return [results[n : n + group] for n in range(0, count, group)]


def recur(mixed, layer, w_input, w_hidden, bias, mode, state=None, done=(), keep=(), lanes=0):
    group, size, _ = mixed.shape
    units = w_hidden.shape[1]
    first = state is None
    operands = [mixed] + list(done) + list(keep) + ([] if first else [state])
    outputs = units // lanes * group if lanes else 1

    def kernel(w_in, w_rec, gate_bias, *refs):
        inputs = refs[0]
        earlier = refs[1 : 1 + len(done)]
        kept = refs[1 + len(done) : 1 + len(done) + len(keep)]
        start = refs[len(operands) - 1]
        outs = refs[len(operands) : len(operands) + outputs]
        memory = refs[-1]
        states = refs[-2] if lanes else outs[0]
        half, place, _ = seat(group)

        if keep:

            @pl.when(half != mode)
            def _():
                spread_into(outs, kept, place, group)

        @only(mode, half)
        def _():
            line = gate_bias[layer : layer + 1, :]

            def advance(gates, old, time):
                i, f, g, o = (gates[:, n * units : (n + 1) * units] for n in range(4))
                new = sigmoid(i) * jnp.tanh(g)
                if old is not None:
                    new = sigmoid(f) * old + new
                memory[...] = new
                states[time] = (sigmoid(o) * jnp.tanh(new)).astype(states.dtype)

            def project(time):
                return jnp.dot(inputs[time], w_in[layer], preferred_element_type=jnp.float32) + line

            def step(time, hidden):
                gates = project(time) + jnp.dot(
                    hidden, w_rec[layer], preferred_element_type=jnp.float32
                )
                advance(gates, memory[...], time)

            if first:
                advance(project(0), None, 0)
            else:
                memory[...] = start[1].astype(jnp.float32)
                step(0, start[0])

            def loop(time, carry):
                step(time, states[time - 1])
                return carry

            lax.fori_loop(1, group, loop, 0)
            if lanes:
                spread_into(outs, [*earlier, states], place, group)
            if first:
                last = refs[len(operands) + outputs]
                last[0] = states[group - 1]
                last[1] = memory[...].astype(last.dtype)

    dtype = mixed.dtype
    if lanes:
        out_shape = [jax.ShapeDtypeStruct((size * CHUNKS, lanes), dtype)] * outputs
    else:
        out_shape = [jax.ShapeDtypeStruct((group, size, units), dtype)]
    if first:
        out_shape.append(jax.ShapeDtypeStruct((2, size, units), dtype))
    scratch = [pltpu.VMEM((group, size, units), dtype)] if lanes else []
    results = pl.pallas_call(
        kernel,
        in_specs=[VMEM] * (3 + len(operands)),
        out_specs=[VMEM] * len(out_shape),
        out_shape=out_shape,
        scratch_shapes=scratch + [pltpu.VMEM((size, units), jnp.float32)],
        compiler_params=PARAMS,
        name="recur",
    )(w_input, w_hidden, bias, *operands)
    if lanes:
        return [results[n : n + group] for n in range(0, outputs, group)]
    return results if first else results[0]


def assemble(parts):
    columns, group = len(parts), len(parts[0])
    part_rows, part_lanes = parts[0][0].shape
    count = columns * group

    def kernel(*refs):
        out, sems = refs[-2:]
        _, _, lead = seat(group)
        copies = []
        for n in range(count):
            start = pl.multiple_of((lead ^ (n % group)) * part_rows, part_rows)
            lanes = pl.ds(n // group * part_lanes, part_lanes)
            target = out.at[0, pl.ds(start, part_rows), lanes]
            copies.append(pltpu.make_async_copy(refs[n], target, sems.at[n]))
        for copy in copies:
            copy.start()
        for copy in copies:
            copy.wait()

    return pl.pallas_call(
        kernel,
        in_specs=[VMEM] * count,
        out_specs=HBM,
        out_shape=jax.ShapeDtypeStruct(
            (1, group * part_rows, columns * part_lanes), parts[0][0].dtype
        ),
        scratch_shapes=[pltpu.SemaphoreType.DMA((count,))],
        compiler_params=PARAMS,
        name="assemble",
    )(*(part for column in parts for part in column))


def send(array, target, lower_only=False):
    slab_count = lax.axis_size("slab")
    times = lax.axis_size("tm")
    pairs = []
    for time in range(times // 2 if lower_only else times):
        for slab in range(slab_count):
            to_time, to_slab = target(time, slab)
            pairs.append((time * slab_count + slab, to_time * slab_count + to_slab))
    return lax.ppermute(array, AXES, pairs)


def swap_slabs(arrays):
    got = list(arrays)
    for k in range(len(arrays) - 1, 0, -1):
        got[k] = send(arrays[k], lambda time, slab: (time, slab ^ k))
    return got


def swap_times(arrays):
    got = list(arrays)
    for k in range(len(arrays) - 1, 0, -1):
        got[k] = send(arrays[k], lambda time, slab: (time ^ k, slab))
    return got


def hand_over(last, group):
    flip = mirror(group)
    return send(last, lambda time, slab: (group + (time ^ flip), slab), lower_only=True)


def local(
    features, ref_lists, tile_rows, tile_sources, tile_counts, tile_values, w_input, w_hidden, bias
):
    row_count = features.shape[1]
    tile = tile_values.shape[2]
    slab_count = lax.axis_size("slab")
    layers = w_input.shape[0]
    group = lax.axis_size("tm") // 2
    half = lax.axis_index("tm") // group

    def mix(parts, column=0):
        listed = pick_tiles(parts, ref_lists, slab_count, row_count, tile, group, column)
        arrived = swap_slabs(listed)
        return swap_times(
            convolve(
                arrived, tile_rows, tile_sources, tile_counts, tile_values, row_count, group
            )
        )

    def back_and_mix(hidden):
        return pack([mix(swap_times(column)) for column in hidden])

    def run(mixed, layer, mode, *rest):
        return recur(mixed, layer, w_input, w_hidden, bias, mode, *rest)

    def run_lower(mixed, layer):
        chunks, handed = [], []
        for part in mixed:
            states, last = run(part, layer, LOWER)
            handed.append(hand_over(last, group))
            chunks.append(states)
        return chunks, handed

    def run_upper(mixed, layer, states):
        return [run(part, layer, UPPER, state) for part, state in zip(mixed[:-1], states)]

    features = features[0]
    width = features.shape[1]
    upper_mixed = pack([mix([features], column) for column in range(width // LANES)])
    hidden, handed = run_lower(upper_mixed, 0)
    for layer in range(1, layers):

        def lower_layer(hidden):
            return back_and_mix(spread(hidden, LANES)), half + 1

        def upper_layer(mixed, done, state):
            return back_and_mix(run(mixed[-1], layer - 1, BOTH, state, done, (), LANES))

        lower_mixed, turn = lax.cond(
            half == LOWER, lower_layer, lambda hidden: (hidden, half), hidden
        )
        hidden, following = run_lower(lower_mixed, layer)
        done = run_upper(upper_mixed, layer - 1, handed)
        upper_mixed = lax.cond(
            half == turn,
            upper_layer,
            lambda mixed, done, state: mixed,
            upper_mixed,
            done,
            handed[-1],
        )
        handed = following
    done = run_upper(upper_mixed, layers - 1, handed)
    units = w_hidden.shape[1]
    hidden = run(upper_mixed[-1], layers - 1, UPPER, handed[-1], done, hidden, units)
    return assemble([swap_times(column) for column in hidden])


def solution(mesh):
    in_specs = (
        P("tm", "slab", None),
        P("tm", None, None),
        P("tm", "slab"),
        P("tm", "slab"),
        P("tm", "slab"),
        P("tm", "slab", None, None),
        P(),
        P(),
        P(),
    )
    out_specs = P("tm", "slab", None)
    return jax.shard_map(local, mesh=mesh, in_specs=in_specs, out_specs=out_specs, check_vma=False)
```

profile of v0, /device:TPU:0, one launch (start us, length us, event | category | flops | bytes accessed | tf_op | source)
XLA Modules:
  0.0 168.7 jit_solution(11725038998677622463)
XLA Ops:
  0.0 1.1 copy-done
  1.1 1.1 pick_tiles.10
  2.9 2.6 %collective-permute-start.37 = (bf16[512,128]{1,0:T(8,128)(2,1)S(1)}, bf16[512,128]{1,0:T(8,128)(2,1)S(1)}, u32[]{:S(2)}, u32[]{:S(2)}) collective-permute-start(bf16[512,128]{1,0:T(8,128)(2,1)S(1)} %get-tuple-element.159), channel_id=1, source_target_pairs={{0,2},{1,3},{2,0},{3,1},{4,6},{5,7},{6,4},{7,5},{8,10},{9,11},{10,... | collective-permute-start | bytes 393224 | tf_op jit(solution)/shard_map/ppermute | solution.py:342
  5.4 1.0 pick_tiles.11
  6.7 1.9 %collective-permute-start.43 = (bf16[512,128]{1,0:T(8,128)(2,1)S(1)}, bf16[512,128]{1,0:T(8,128)(2,1)S(1)}, u32[]{:S(2)}, u32[]{:S(2)}) collective-permute-start(bf16[512,128]{1,0:T(8,128)(2,1)S(1)} %get-tuple-element.167), channel_id=1, source_target_pairs={{0,2},{1,3},{2,0},{3,1},{4,6},{5,7},{6,4},{7,5},{8,10},{9,11},{10,... | collective-permute-start | bytes 393224 | tf_op jit(solution)/shard_map/ppermute | solution.py:342
  9.8 2.4 %collective-permute-done.38.refs_7_ = bf16[512,128]{1,0:T(8,128)(2,1)S(1)} collective-permute-done((bf16[512,128]{1,0:T(8,128)(2,1)S(1)}, bf16[512,128]{1,0:T(8,128)(2,1)S(1)}, u32[]{:S(2)}, u32[]{:S(2)}) %collective-permute-start.38) | collective-permute-done | bytes 131104 | tf_op jit(solution)/shard_map/ppermute | solution.py:342
  12.1 1.8 %convolve.10 = (bf16[384,128]{1,0:T(8,128)(2,1)S(1)}, bf16[384,128]{1,0:T(8,128)(2,1)S(1)}, bf16[384,128]{1,0:T(8,128)(2,1)S(1)}, bf16[384,128]{1,0:T(8,128)(2,1)S(1)}) custom-call(s32[1,32]{1,0:T(1,128)S(1)} %copy-done.13, s32[1,32]{1,0:T(1,128)S(1)} %copy-done.14, s32[1,1]{1,0:T(1,128)S(6)} %copy.20.refs_2_, bf16[1,32,128,128]{3,2,1,0:T(8,128)(2,1)S(1)} %copy-done.4, ...), custom_call_target="tpu_custom_call" | custom-call | tf_op jit(solution)/shard_map/convolve/pallas_call | solution.py:143
  13.9 1.6 collective-permute-start.39
  15.5 1.9 %collective-permute-start.40 = (bf16[384,128]{1,0:T(8,128)(2,1)S(1)}, bf16[384,128]{1,0:T(8,128)(2,1)S(1)}, u32[]{:S(2)}, u32[]{:S(2)}) collective-permute-start(bf16[384,128]{1,0:T(8,128)(2,1)S(1)} %get-tuple-element.163), channel_id=1, source_target_pairs={{0,8},{1,9},{2,10},{3,11},{4,12},{5,13},{6,14},{7,15},{8,0},{9,1},... | collective-permute-start | bytes 294920 | tf_op jit(solution)/shard_map/ppermute | solution.py:342
  17.7 1.8 %convolve.11 = (bf16[384,128]{1,0:T(8,128)(2,1)S(1)}, bf16[384,128]{1,0:T(8,128)(2,1)S(1)}, bf16[384,128]{1,0:T(8,128)(2,1)S(1)}, bf16[384,128]{1,0:T(8,128)(2,1)S(1)}) custom-call(s32[1,32]{1,0:T(1,128)S(1)} %copy-done.13, s32[1,32]{1,0:T(1,128)S(1)} %copy-done.14, s32[1,1]{1,0:T(1,128)S(6)} %copy.20.refs_2_, bf16[1,32,128,128]{3,2,1,0:T(8,128)(2,1)S(1)} %copy-done.4, ...), custom_call_target="tpu_custom_call" | custom-call | tf_op jit(solution)/shard_map/convolve/pallas_call | solution.py:143
  19.5 1.6 collective-permute-start.45
  21.0 2.2 %collective-permute-start.46 = (bf16[384,128]{1,0:T(8,128)(2,1)S(1)}, bf16[384,128]{1,0:T(8,128)(2,1)S(1)}, u32[]{:S(2)}, u32[]{:S(2)}) collective-permute-start(bf16[384,128]{1,0:T(8,128)(2,1)S(1)} %get-tuple-element.171), channel_id=1, source_target_pairs={{0,8},{1,9},{2,10},{3,11},{4,12},{5,13},{6,14},{7,15},{8,0},{9,1},... | collective-permute-start | bytes 294920 | tf_op jit(solution)/shard_map/ppermute | solution.py:342
  23.3 1.8 %collective-permute-done.45.refs_5_ = bf16[384,128]{1,0:T(8,128)(2,1)S(1)} collective-permute-done((bf16[384,128]{1,0:T(8,128)(2,1)S(1)}, bf16[384,128]{1,0:T(8,128)(2,1)S(1)}, u32[]{:S(2)}, u32[]{:S(2)}) %collective-permute-start.45) | collective-permute-done | bytes 98336 | tf_op jit(solution)/shard_map/ppermute | solution.py:342
  25.1 1.1 collective-permute-done.46.refs_6_
  26.2 2.5 %collective-permute-done.47.refs_7_ = bf16[384,128]{1,0:T(8,128)(2,1)S(1)} collective-permute-done((bf16[384,128]{1,0:T(8,128)(2,1)S(1)}, bf16[384,128]{1,0:T(8,128)(2,1)S(1)}, u32[]{:S(2)}, u32[]{:S(2)}) %collective-permute-start.47) | collective-permute-done | bytes 98336 | tf_op jit(solution)/shard_map/ppermute | solution.py:342
  28.8 0.9 pack.5
  29.7 3.5 %recur.9 = (bf16[4,192,256]{2,1,0:T(8,128)(2,1)}, bf16[2,192,256]{2,1,0:T(8,128)(2,1)S(1)}) custom-call(bf16[2,256,1024]{2,1,0:T(8,128)(2,1)S(1)} %copy-done.1, bf16[2,256,1024]{2,1,0:T(8,128)(2,1)S(1)} %copy-done.2, f32[2,1024]{1,0:T(2,128)S(1)} %copy-done.11, bf16[4,192,256]{2,1,0:T(8,128)(2,1)} %get-tuple-element.173.refs_0_), custom_call_target="tpu_custom_call" | custom-call | tf_op jit(solution)/shard_map/recur/pallas_call | solution.py:288
  33.2 2.4 %recur.10 = (bf16[4,192,256]{2,1,0:T(8,128)(2,1)}, bf16[2,192,256]{2,1,0:T(8,128)(2,1)S(1)}) custom-call(bf16[2,256,1024]{2,1,0:T(8,128)(2,1)S(1)} %copy-done.1, bf16[2,256,1024]{2,1,0:T(8,128)(2,1)S(1)} %copy-done.2, f32[2,1024]{1,0:T(2,128)S(1)} %copy-done.11, bf16[4,192,256]{2,1,0:T(8,128)(2,1)S(1)} %get-tuple-element.175.refs_0_), custom_call_target="tpu_custom_call" | custom-call | tf_op jit(solution)/shard_map/recur/pallas_call | solution.py:288
  35.6 0.7 copy-done.12
  36.3 40.8 %conditional.2 = (bf16[4,192,256]{2,1,0:T(8,128)(2,1)}, bf16[4,192,256]{2,1,0:T(8,128)(2,1)}, s32[]{:T(128)}) conditional(s32[]{:T(128)} %convert_element_type.6, (bf16[4,192,256]{2,1,0:T(8,128)(2,1)}, bf16[4,192,256]{2,1,0:T(8,128)(2,1)}, s32[]{:T(128)}) %tuple.17, (bf16[4,192,256]{2,1,0:T(8,128)(2,1)}, bf16[4,192,256]{2,1,0:T(8,128)(2,1)}, ...), branch_computations={%region_0.1_spmd, %region_1.2_spmd} | conditional | flops 1 | bytes 12059408 | solution.py:412
  36.3 1.6 spread.1
  37.9 0.7 collective-permute-start
  38.6 1.5 collective-permute-start.1
  40.1 1.4 collective-permute-start.2
  41.4 0.6 collective-permute-start.9
  42.1 2.1 %collective-permute-done.refs_1_ = bf16[384,128]{1,0:T(8,128)(2,1)S(1)} collective-permute-done((bf16[384,128]{1,0:T(8,128)(2,1)S(1)}, bf16[384,128]{1,0:T(8,128)(2,1)S(1)}, u32[]{:S(2)}, u32[]{:S(2)}) %collective-permute-start) | collective-permute-done | bytes 98336 | tf_op jit(solution)/shard_map/cond/branch_1_fun/ppermute | solution.py:342
  44.2 1.5 collective-permute-done.2.refs_3_
  45.7 0.8 pick_tiles.6
  46.5 1.0 collective-permute-start.10
  47.6 1.5 collective-permute-start.11
  49.1 1.7 %collective-permute-start.4 = (bf16[512,128]{1,0:T(8,128)(2,1)S(1)}, bf16[512,128]{1,0:T(8,128)(2,1)S(1)}, u32[]{:S(2)}, u32[]{:S(2)}) collective-permute-start(bf16[512,128]{1,0:T(8,128)(2,1)S(1)} %get-tuple-element.66), channel_id=1, source_target_pairs={{0,2},{1,3},{2,0},{3,1},{4,6},{5,7},{6,4},{7,5},{8,10},{9,11},{10,... | collective-permute-start | bytes 393224 | tf_op jit(solution)/shard_map/cond/branch_1_fun/ppermute | solution.py:342
  50.8 1.5 collective-permute-done.10.refs_2_
  52.3 2.0 %collective-permute-done.11.refs_3_ = bf16[384,128]{1,0:T(8,128)(2,1)S(1)} collective-permute-done((bf16[384,128]{1,0:T(8,128)(2,1)S(1)}, bf16[384,128]{1,0:T(8,128)(2,1)S(1)}, u32[]{:S(2)}, u32[]{:S(2)}) %collective-permute-start.11) | collective-permute-done | bytes 98336 | tf_op jit(solution)/shard_map/cond/branch_1_fun/ppermute | solution.py:342
  54.3 0.8 pick_tiles.7
  55.1 1.8 %collective-permute-start.13 = (bf16[512,128]{1,0:T(8,128)(2,1)S(1)}, bf16[512,128]{1,0:T(8,128)(2,1)S(1)}, u32[]{:S(2)}, u32[]{:S(2)}) collective-permute-start(bf16[512,128]{1,0:T(8,128)(2,1)S(1)} %get-tuple-element.78), channel_id=1, source_target_pairs={{0,2},{1,3},{2,0},{3,1},{4,6},{5,7},{6,4},{7,5},{8,10},{9,11},{10,... | collective-permute-start | bytes 393224 | tf_op jit(solution)/shard_map/cond/branch_1_fun/ppermute | solution.py:342
  57.0 2.5 %convolve.6 = (bf16[384,128]{1,0:T(8,128)(2,1)S(1)}, bf16[384,128]{1,0:T(8,128)(2,1)S(1)}, bf16[384,128]{1,0:T(8,128)(2,1)S(1)}, bf16[384,128]{1,0:T(8,128)(2,1)S(1)}) custom-call(s32[1,32]{1,0:T(1,128)S(1)} %get-tuple-element.53.refs_0_, s32[1,32]{1,0:T(1,128)S(1)} %get-tuple-element.54.refs_1_, s32[1,1]{1,0:T(1,128)} %get-tuple-element.55.refs_2_, ...), custom_call_target="tpu_custom_call" | custom-call | tf_op jit(solution)/shard_map/cond/branch_1_fun/convolve/pallas_call | solution.py:143
  59.5 1.3 collective-permute-start.6
  60.8 1.2 collective-permute-start.7
  61.9 1.1 collective-permute-start.8
  63.3 3.6 %convolve.7 = (bf16[384,128]{1,0:T(8,128)(2,1)S(1)}, bf16[384,128]{1,0:T(8,128)(2,1)S(1)}, bf16[384,128]{1,0:T(8,128)(2,1)S(1)}, bf16[384,128]{1,0:T(8,128)(2,1)S(1)}) custom-call(s32[1,32]{1,0:T(1,128)S(1)} %get-tuple-element.53.refs_0_, s32[1,32]{1,0:T(1,128)S(1)} %get-tuple-element.54.refs_1_, s32[1,1]{1,0:T(1,128)} %get-tuple-element.55.refs_2_, ...), custom_call_target="tpu_custom_call" | custom-call | tf_op jit(solution)/shard_map/cond/branch_1_fun/convolve/pallas_call | solution.py:143
  66.9 1.5 collective-permute-start.15
  68.5 1.0 collective-permute-start.16
  69.5 1.0 collective-permute-start.17
  70.5 2.1 %collective-permute-done.15.refs_5_ = bf16[384,128]{1,0:T(8,128)(2,1)S(1)} collective-permute-done((bf16[384,128]{1,0:T(8,128)(2,1)S(1)}, bf16[384,128]{1,0:T(8,128)(2,1)S(1)}, u32[]{:S(2)}, u32[]{:S(2)}) %collective-permute-start.15) | collective-permute-done | bytes 98336 | tf_op jit(solution)/shard_map/cond/branch_1_fun/ppermute | solution.py:342
  72.6 0.9 collective-permute-done.16.refs_6_
  73.5 2.6 %collective-permute-done.17.refs_7_ = bf16[384,128]{1,0:T(8,128)(2,1)S(1)} collective-permute-done((bf16[384,128]{1,0:T(8,128)(2,1)S(1)}, bf16[384,128]{1,0:T(8,128)(2,1)S(1)}, u32[]{:S(2)}, u32[]{:S(2)}) %collective-permute-start.17) | collective-permute-done | bytes 98336 | tf_op jit(solution)/shard_map/cond/branch_1_fun/ppermute | solution.py:342
  76.0 1.0 pack.3
  77.1 1.3 collective-permute-start.48
  78.4 2.0 %collective-permute-start.49 = (bf16[2,192,256]{2,1,0:T(8,128)(2,1)S(1)}, bf16[2,192,256]{2,1,0:T(8,128)(2,1)}, u32[]{:S(2)}, u32[]{:S(2)}) collective-permute-start(bf16[2,192,256]{2,1,0:T(8,128)(2,1)S(1)} %get-tuple-element.179), channel_id=1, source_target_pairs={{0,24},{1,25},{2,26},{3,27},{4,28},{5,29},{6,30},{7,31},{8,16},{9,... | collective-permute-start | bytes 589832 | tf_op jit(solution)/shard_map/ppermute | solution.py:342
  80.4 3.0 %recur.12 = (bf16[4,192,256]{2,1,0:T(8,128)(2,1)S(1)}, bf16[2,192,256]{2,1,0:T(8,128)(2,1)S(1)}) custom-call(bf16[2,256,1024]{2,1,0:T(8,128)(2,1)S(1)} %copy-done.1, bf16[2,256,1024]{2,1,0:T(8,128)(2,1)} %w_rec.13, f32[2,1024]{1,0:T(2,128)S(1)} %copy-done.11, bf16[4,192,256]{2,1,0:T(8,128)(2,1)} %get-tuple-element.182.refs_0_), custom_call_target="tpu_custom_call" | custom-call | tf_op jit(solution)/shard_map/recur/pallas_call | solution.py:288
  83.7 1.8 %recur.11 = bf16[4,192,256]{2,1,0:T(8,128)(2,1)} custom-call(bf16[2,256,1024]{2,1,0:T(8,128)(2,1)S(1)} %copy-done.1, bf16[2,256,1024]{2,1,0:T(8,128)(2,1)S(1)} %copy-done.3, f32[2,1024]{1,0:T(2,128)S(1)} %copy-done.11, bf16[4,192,256]{2,1,0:T(8,128)(2,1)} %get-tuple-element.173.refs_0_, bf16[2,192,256]{2,1,0:T(8,128)(2,1)S(1)} %collective-permute-done.48.refs_1_), custom_call_target="tpu_custom_call" | custom-call | tf_op jit(solution)/shard_map/recur/pallas_call | solution.py:288
  85.4 1.6 collective-permute-done.49
  87.1 53.9 %collective-permute-start.50 = (bf16[2,192,256]{2,1,0:T(8,128)(2,1)S(1)}, bf16[2,192,256]{2,1,0:T(8,128)(2,1)S(1)}, u32[]{:S(2)}, u32[]{:S(2)}) collective-permute-start(bf16[2,192,256]{2,1,0:T(8,128)(2,1)S(1)} %get-tuple-element.183), channel_id=1, source_target_pairs={{0,24},{1,25},{2,26},{3,27},{4,28},{5,29},{6,30},{7,31},{8,16},{9,... | collective-permute-start | bytes 589832 | tf_op jit(solution)/shard_map/ppermute | solution.py:342
  141.0 1.6 recur.14
  142.6 1.3 collective-permute-start.51
  143.9 1.9 %collective-permute-done.50.refs_1_ = bf16[2,192,256]{2,1,0:T(8,128)(2,1)S(1)} collective-permute-done((bf16[2,192,256]{2,1,0:T(8,128)(2,1)S(1)}, bf16[2,192,256]{2,1,0:T(8,128)(2,1)S(1)}, u32[]{:S(2)}, u32[]{:S(2)}) %collective-permute-start.50) | collective-permute-done | bytes 196640 | tf_op jit(solution)/shard_map/ppermute | solution.py:342
  145.8 1.0 recur.13.refs_1_
  146.8 1.9 %collective-permute-done.51.refs_4_ = bf16[2,192,256]{2,1,0:T(8,128)(2,1)S(1)} collective-permute-done((bf16[2,192,256]{2,1,0:T(8,128)(2,1)S(1)}, bf16[2,192,256]{2,1,0:T(8,128)(2,1)S(1)}, u32[]{:S(2)}, u32[]{:S(2)}) %collective-permute-start.51) | collective-permute-done | bytes 196640 | tf_op jit(solution)/shard_map/ppermute | solution.py:342
  148.8 2.5 %collective-permute-start.52 = (bf16[384,256]{1,0:T(8,128)(2,1)S(1)}, bf16[384,256]{1,0:T(8,128)(2,1)S(1)}, u32[]{:S(2)}, u32[]{:S(2)}) collective-permute-start(bf16[384,256]{1,0:T(8,128)(2,1)S(1)} %get-tuple-element.189), channel_id=1, source_target_pairs={{0,4},{1,5},{2,6},{3,7},{4,0},{5,1},{6,2},{7,3},{8,12},{9,13},{10,... | collective-permute-start | bytes 589832 | tf_op jit(solution)/shard_map/ppermute | solution.py:342
  151.3 7.1 %collective-permute-start.53 = (bf16[384,256]{1,0:T(8,128)(2,1)S(1)}, bf16[384,256]{1,0:T(8,128)(2,1)S(1)}, u32[]{:S(2)}, u32[]{:S(2)}) collective-permute-start(bf16[384,256]{1,0:T(8,128)(2,1)S(1)} %get-tuple-element.190), channel_id=1, source_target_pairs={{0,8},{1,9},{2,10},{3,11},{4,12},{5,13},{6,14},{7,15},{8,0},{9,1},... | collective-permute-start | bytes 589832 | tf_op jit(solution)/shard_map/ppermute | solution.py:342
  158.3 1.1 collective-permute-start.54
  159.4 4.6 %collective-permute-done.53.refs_2_ = bf16[384,256]{1,0:T(8,128)(2,1)S(1)} collective-permute-done((bf16[384,256]{1,0:T(8,128)(2,1)S(1)}, bf16[384,256]{1,0:T(8,128)(2,1)S(1)}, u32[]{:S(2)}, u32[]{:S(2)}) %collective-permute-start.53) | collective-permute-done | bytes 196640 | tf_op jit(solution)/shard_map/ppermute | solution.py:342
  164.1 3.7 %collective-permute-done.54.refs_3_ = bf16[384,256]{1,0:T(8,128)(2,1)S(1)} collective-permute-done((bf16[384,256]{1,0:T(8,128)(2,1)S(1)}, bf16[384,256]{1,0:T(8,128)(2,1)S(1)}, u32[]{:S(2)}, u32[]{:S(2)}) %collective-permute-start.54) | collective-permute-done | bytes 196640 | tf_op jit(solution)/shard_map/ppermute | solution.py:342
  167.8 0.9 assemble.1
  (59 shorter events, 2.4 us)
Async XLA Ops:
  0.0 1.1 copy-start
  1.1 11.0 %copy-start.4 = (bf16[1,32,128,128]{3,2,1,0:T(8,128)(2,1)S(1)}, bf16[1,32,128,128]{3,2,1,0:T(8,128)(2,1)}, u32[]{:S(2)}) copy-start(bf16[1,32,128,128]{3,2,1,0:T(8,128)(2,1)} %refs_3_.3) | copy-start | bytes 3145732
  2.3 6.3 %collective-permute-start.36 = (bf16[512,128]{1,0:T(8,128)(2,1)S(1)}, bf16[512,128]{1,0:T(8,128)(2,1)S(1)}, u32[]{:S(2)}, u32[]{:S(2)}) collective-permute-start(bf16[512,128]{1,0:T(8,128)(2,1)S(1)} %get-tuple-element.158), channel_id=1, source_target_pairs={{0,1},{1,0},{2,3},{3,2},{4,5},{5,4},{6,7},{7,6},{8,9},{9,8},{10,11... | collective-permute-start | bytes 393224 | tf_op jit(solution)/shard_map/ppermute | solution.py:342
  2.9 6.9 %collective-permute-start.37 = (bf16[512,128]{1,0:T(8,128)(2,1)S(1)}, bf16[512,128]{1,0:T(8,128)(2,1)S(1)}, u32[]{:S(2)}, u32[]{:S(2)}) collective-permute-start(bf16[512,128]{1,0:T(8,128)(2,1)S(1)} %get-tuple-element.159), channel_id=1, source_target_pairs={{0,2},{1,3},{2,0},{3,1},{4,6},{5,7},{6,4},{7,5},{8,10},{9,11},{10,... | collective-permute-start | bytes 393224 | tf_op jit(solution)/shard_map/ppermute | solution.py:342
  5.4 6.7 %collective-permute-start.38 = (bf16[512,128]{1,0:T(8,128)(2,1)S(1)}, bf16[512,128]{1,0:T(8,128)(2,1)S(1)}, u32[]{:S(2)}, u32[]{:S(2)}) collective-permute-start(bf16[512,128]{1,0:T(8,128)(2,1)S(1)} %get-tuple-element.160), channel_id=1, source_target_pairs={{0,3},{1,2},{2,1},{3,0},{4,7},{5,6},{6,5},{7,4},{8,11},{9,10},{10,... | collective-permute-start | bytes 393224 | tf_op jit(solution)/shard_map/ppermute | solution.py:342
  6.5 11.0 %collective-permute-start.42 = (bf16[512,128]{1,0:T(8,128)(2,1)S(1)}, bf16[512,128]{1,0:T(8,128)(2,1)S(1)}, u32[]{:S(2)}, u32[]{:S(2)}) collective-permute-start(bf16[512,128]{1,0:T(8,128)(2,1)S(1)} %get-tuple-element.166), channel_id=1, source_target_pairs={{0,1},{1,0},{2,3},{3,2},{4,5},{5,4},{6,7},{7,6},{8,9},{9,8},{10,11... | collective-permute-start | bytes 393224 | tf_op jit(solution)/shard_map/ppermute | solution.py:342
  6.7 10.8 %collective-permute-start.43 = (bf16[512,128]{1,0:T(8,128)(2,1)S(1)}, bf16[512,128]{1,0:T(8,128)(2,1)S(1)}, u32[]{:S(2)}, u32[]{:S(2)}) collective-permute-start(bf16[512,128]{1,0:T(8,128)(2,1)S(1)} %get-tuple-element.167), channel_id=1, source_target_pairs={{0,2},{1,3},{2,0},{3,1},{4,6},{5,7},{6,4},{7,5},{8,10},{9,11},{10,... | collective-permute-start | bytes 393224 | tf_op jit(solution)/shard_map/ppermute | solution.py:342
  8.6 9.0 %collective-permute-start.44 = (bf16[512,128]{1,0:T(8,128)(2,1)S(1)}, bf16[512,128]{1,0:T(8,128)(2,1)S(1)}, u32[]{:S(2)}, u32[]{:S(2)}) collective-permute-start(bf16[512,128]{1,0:T(8,128)(2,1)S(1)} %get-tuple-element.168), channel_id=1, source_target_pairs={{0,3},{1,2},{2,1},{3,0},{4,7},{5,6},{6,5},{7,4},{8,11},{9,10},{10,... | collective-permute-start | bytes 393224 | tf_op jit(solution)/shard_map/ppermute | solution.py:342
  9.3 2.8 %copy-start.13 = (s32[1,32]{1,0:T(1,128)S(1)}, s32[1,32]{1,0:T(1,128)}, u32[]{:S(2)}) copy-start(s32[1,32]{1,0:T(1,128)} %refs_0_.3) | copy-start | bytes 388
  9.3 2.8 %copy-start.14 = (s32[1,32]{1,0:T(1,128)S(1)}, s32[1,32]{1,0:T(1,128)}, u32[]{:S(2)}) copy-start(s32[1,32]{1,0:T(1,128)} %refs_1_.3) | copy-start | bytes 388
  13.9 9.3 %collective-permute-start.39 = (bf16[384,128]{1,0:T(8,128)(2,1)S(1)}, bf16[384,128]{1,0:T(8,128)(2,1)S(1)}, u32[]{:S(2)}, u32[]{:S(2)}) collective-permute-start(bf16[384,128]{1,0:T(8,128)(2,1)S(1)} %get-tuple-element.162), channel_id=1, source_target_pairs={{0,4},{1,5},{2,6},{3,7},{4,0},{5,1},{6,2},{7,3},{8,12},{9,13},{10,... | collective-permute-start | bytes 294920 | tf_op jit(solution)/shard_map/ppermute | solution.py:342
  15.5 7.7 %collective-permute-start.40 = (bf16[384,128]{1,0:T(8,128)(2,1)S(1)}, bf16[384,128]{1,0:T(8,128)(2,1)S(1)}, u32[]{:S(2)}, u32[]{:S(2)}) collective-permute-start(bf16[384,128]{1,0:T(8,128)(2,1)S(1)} %get-tuple-element.163), channel_id=1, source_target_pairs={{0,8},{1,9},{2,10},{3,11},{4,12},{5,13},{6,14},{7,15},{8,0},{9,1},... | collective-permute-start | bytes 294920 | tf_op jit(solution)/shard_map/ppermute | solution.py:342
  17.5 5.8 %collective-permute-start.41 = (bf16[384,128]{1,0:T(8,128)(2,1)S(1)}, bf16[384,128]{1,0:T(8,128)(2,1)S(1)}, u32[]{:S(2)}, u32[]{:S(2)}) collective-permute-start(bf16[384,128]{1,0:T(8,128)(2,1)S(1)} %get-tuple-element.164), channel_id=1, source_target_pairs={{0,12},{1,13},{2,14},{3,15},{4,8},{5,9},{6,10},{7,11},{8,4},{9,5},... | collective-permute-start | bytes 294920 | tf_op jit(solution)/shard_map/ppermute | solution.py:342
  17.7 12.0 %copy-start.1 = (bf16[2,256,1024]{2,1,0:T(8,128)(2,1)S(1)}, bf16[2,256,1024]{2,1,0:T(8,128)(2,1)}, u32[]{:S(2)}) copy-start(bf16[2,256,1024]{2,1,0:T(8,128)(2,1)} %w_in.13) | copy-start | bytes 3145732
  17.7 12.0 %copy-start.2 = (bf16[2,256,1024]{2,1,0:T(8,128)(2,1)S(1)}, bf16[2,256,1024]{2,1,0:T(8,128)(2,1)}, u32[]{:S(2)}) copy-start(bf16[2,256,1024]{2,1,0:T(8,128)(2,1)} %w_rec.13) | copy-start | bytes 3145732
  19.5 5.6 %collective-permute-start.45 = (bf16[384,128]{1,0:T(8,128)(2,1)S(1)}, bf16[384,128]{1,0:T(8,128)(2,1)S(1)}, u32[]{:S(2)}, u32[]{:S(2)}) collective-permute-start(bf16[384,128]{1,0:T(8,128)(2,1)S(1)} %get-tuple-element.170), channel_id=1, source_target_pairs={{0,4},{1,5},{2,6},{3,7},{4,0},{5,1},{6,2},{7,3},{8,12},{9,13},{10,... | collective-permute-start | bytes 294920 | tf_op jit(solution)/shard_map/ppermute | solution.py:342
  21.0 5.2 %collective-permute-start.46 = (bf16[384,128]{1,0:T(8,128)(2,1)S(1)}, bf16[384,128]{1,0:T(8,128)(2,1)S(1)}, u32[]{:S(2)}, u32[]{:S(2)}) collective-permute-start(bf16[384,128]{1,0:T(8,128)(2,1)S(1)} %get-tuple-element.171), channel_id=1, source_target_pairs={{0,8},{1,9},{2,10},{3,11},{4,12},{5,13},{6,14},{7,15},{8,0},{9,1},... | collective-permute-start | bytes 294920 | tf_op jit(solution)/shard_map/ppermute | solution.py:342
  23.2 5.5 %collective-permute-start.47 = (bf16[384,128]{1,0:T(8,128)(2,1)S(1)}, bf16[384,128]{1,0:T(8,128)(2,1)S(1)}, u32[]{:S(2)}, u32[]{:S(2)}) collective-permute-start(bf16[384,128]{1,0:T(8,128)(2,1)S(1)} %get-tuple-element.172), channel_id=1, source_target_pairs={{0,12},{1,13},{2,14},{3,15},{4,8},{5,9},{6,10},{7,11},{8,4},{9,5},... | collective-permute-start | bytes 294920 | tf_op jit(solution)/shard_map/ppermute | solution.py:342
  28.8 0.9 copy-start.11
  29.6 3.5 %copy-start.8 = (bf16[4,192,256]{2,1,0:T(8,128)(2,1)}, bf16[4,192,256]{2,1,0:T(8,128)(2,1)S(1)}, u32[]{:S(2)}) copy-start(bf16[4,192,256]{2,1,0:T(8,128)(2,1)S(1)} %get-tuple-element.175.refs_0_) | copy-start | bytes 1179652
  33.2 2.4 %copy-start.5 = (bf16[1,32,128,128]{3,2,1,0:T(8,128)(2,1)S(1)}, bf16[1,32,128,128]{3,2,1,0:T(8,128)(2,1)}, u32[]{:S(2)}) copy-start(bf16[1,32,128,128]{3,2,1,0:T(8,128)(2,1)} %refs_3_.3) | copy-start | bytes 3145732
  35.6 0.7 copy-start.12
  36.3 23.2 %copy-start.6 = (bf16[1,32,128,128]{3,2,1,0:T(8,128)(2,1)}, bf16[1,32,128,128]{3,2,1,0:T(8,128)(2,1)S(1)}, u32[]{:S(2)}) copy-start(bf16[1,32,128,128]{3,2,1,0:T(8,128)(2,1)S(1)} %get-tuple-element.56.refs_3_) | copy-start | bytes 3145732 | tf_op jit(solution)/shard_map/cond
  37.9 6.3 %collective-permute-start = (bf16[384,128]{1,0:T(8,128)(2,1)S(1)}, bf16[384,128]{1,0:T(8,128)(2,1)S(1)}, u32[]{:S(2)}, u32[]{:S(2)}) collective-permute-start(bf16[384,128]{1,0:T(8,128)(2,1)S(1)} %get-tuple-element.61), channel_id=1, source_target_pairs={{0,4},{1,5},{2,6},{3,7},{4,0},{5,1},{6,2},{7,3},{8,12},{9,13},{10,... | collective-permute-start | bytes 294920 | tf_op jit(solution)/shard_map/cond/branch_1_fun/ppermute | solution.py:342
  38.6 5.6 %collective-permute-start.1 = (bf16[384,128]{1,0:T(8,128)(2,1)S(1)}, bf16[384,128]{1,0:T(8,128)(2,1)S(1)}, u32[]{:S(2)}, u32[]{:S(2)}) collective-permute-start(bf16[384,128]{1,0:T(8,128)(2,1)S(1)} %get-tuple-element.62), channel_id=1, source_target_pairs={{0,8},{1,9},{2,10},{3,11},{4,12},{5,13},{6,14},{7,15},{8,0},{9,1},... | collective-permute-start | bytes 294920 | tf_op jit(solution)/shard_map/cond/branch_1_fun/ppermute | solution.py:342
  40.1 5.6 %collective-permute-start.2 = (bf16[384,128]{1,0:T(8,128)(2,1)S(1)}, bf16[384,128]{1,0:T(8,128)(2,1)S(1)}, u32[]{:S(2)}, u32[]{:S(2)}) collective-permute-start(bf16[384,128]{1,0:T(8,128)(2,1)S(1)} %get-tuple-element.63), channel_id=1, source_target_pairs={{0,12},{1,13},{2,14},{3,15},{4,8},{5,9},{6,10},{7,11},{8,4},{9,5},... | collective-permute-start | bytes 294920 | tf_op jit(solution)/shard_map/cond/branch_1_fun/ppermute | solution.py:342
  41.4 9.3 %collective-permute-start.9 = (bf16[384,128]{1,0:T(8,128)(2,1)S(1)}, bf16[384,128]{1,0:T(8,128)(2,1)S(1)}, u32[]{:S(2)}, u32[]{:S(2)}) collective-permute-start(bf16[384,128]{1,0:T(8,128)(2,1)S(1)} %get-tuple-element.73), channel_id=1, source_target_pairs={{0,4},{1,5},{2,6},{3,7},{4,0},{5,1},{6,2},{7,3},{8,12},{9,13},{10,... | collective-permute-start | bytes 294920 | tf_op jit(solution)/shard_map/cond/branch_1_fun/ppermute | solution.py:342
  46.5 10.4 %collective-permute-start.3 = (bf16[512,128]{1,0:T(8,128)(2,1)S(1)}, bf16[512,128]{1,0:T(8,128)(2,1)S(1)}, u32[]{:S(2)}, u32[]{:S(2)}) collective-permute-start(bf16[512,128]{1,0:T(8,128)(2,1)S(1)} %get-tuple-element.65), channel_id=1, source_target_pairs={{0,1},{1,0},{2,3},{3,2},{4,5},{5,4},{6,7},{7,6},{8,9},{9,8},{10,11... | collective-permute-start | bytes 393224 | tf_op jit(solution)/shard_map/cond/branch_1_fun/ppermute | solution.py:342
  46.5 5.7 %collective-permute-start.10 = (bf16[384,128]{1,0:T(8,128)(2,1)S(1)}, bf16[384,128]{1,0:T(8,128)(2,1)S(1)}, u32[]{:S(2)}, u32[]{:S(2)}) collective-permute-start(bf16[384,128]{1,0:T(8,128)(2,1)S(1)} %get-tuple-element.74), channel_id=1, source_target_pairs={{0,8},{1,9},{2,10},{3,11},{4,12},{5,13},{6,14},{7,15},{8,0},{9,1},... | collective-permute-start | bytes 294920 | tf_op jit(solution)/shard_map/cond/branch_1_fun/ppermute | solution.py:342
  47.6 6.7 %collective-permute-start.11 = (bf16[384,128]{1,0:T(8,128)(2,1)S(1)}, bf16[384,128]{1,0:T(8,128)(2,1)S(1)}, u32[]{:S(2)}, u32[]{:S(2)}) collective-permute-start(bf16[384,128]{1,0:T(8,128)(2,1)S(1)} %get-tuple-element.75), channel_id=1, source_target_pairs={{0,12},{1,13},{2,14},{3,15},{4,8},{5,9},{6,10},{7,11},{8,4},{9,5},... | collective-permute-start | bytes 294920 | tf_op jit(solution)/shard_map/cond/branch_1_fun/ppermute | solution.py:342
  49.1 7.9 %collective-permute-start.4 = (bf16[512,128]{1,0:T(8,128)(2,1)S(1)}, bf16[512,128]{1,0:T(8,128)(2,1)S(1)}, u32[]{:S(2)}, u32[]{:S(2)}) collective-permute-start(bf16[512,128]{1,0:T(8,128)(2,1)S(1)} %get-tuple-element.66), channel_id=1, source_target_pairs={{0,2},{1,3},{2,0},{3,1},{4,6},{5,7},{6,4},{7,5},{8,10},{9,11},{10,... | collective-permute-start | bytes 393224 | tf_op jit(solution)/shard_map/cond/branch_1_fun/ppermute | solution.py:342
  50.8 6.2 %collective-permute-start.5 = (bf16[512,128]{1,0:T(8,128)(2,1)S(1)}, bf16[512,128]{1,0:T(8,128)(2,1)S(1)}, u32[]{:S(2)}, u32[]{:S(2)}) collective-permute-start(bf16[512,128]{1,0:T(8,128)(2,1)S(1)} %get-tuple-element.67), channel_id=1, source_target_pairs={{0,3},{1,2},{2,1},{3,0},{4,7},{5,6},{6,5},{7,4},{8,11},{9,10},{10,... | collective-permute-start | bytes 393224 | tf_op jit(solution)/shard_map/cond/branch_1_fun/ppermute | solution.py:342
  55.1 6.9 %collective-permute-start.12 = (bf16[512,128]{1,0:T(8,128)(2,1)S(1)}, bf16[512,128]{1,0:T(8,128)(2,1)S(1)}, u32[]{:S(2)}, u32[]{:S(2)}) collective-permute-start(bf16[512,128]{1,0:T(8,128)(2,1)S(1)} %get-tuple-element.77), channel_id=1, source_target_pairs={{0,1},{1,0},{2,3},{3,2},{4,5},{5,4},{6,7},{7,6},{8,9},{9,8},{10,11... | collective-permute-start | bytes 393224 | tf_op jit(solution)/shard_map/cond/branch_1_fun/ppermute | solution.py:342
  55.1 7.9 %collective-permute-start.13 = (bf16[512,128]{1,0:T(8,128)(2,1)S(1)}, bf16[512,128]{1,0:T(8,128)(2,1)S(1)}, u32[]{:S(2)}, u32[]{:S(2)}) collective-permute-start(bf16[512,128]{1,0:T(8,128)(2,1)S(1)} %get-tuple-element.78), channel_id=1, source_target_pairs={{0,2},{1,3},{2,0},{3,1},{4,6},{5,7},{6,4},{7,5},{8,10},{9,11},{10,... | collective-permute-start | bytes 393224 | tf_op jit(solution)/shard_map/cond/branch_1_fun/ppermute | solution.py:342
  56.9 6.4 %collective-permute-start.14 = (bf16[512,128]{1,0:T(8,128)(2,1)S(1)}, bf16[512,128]{1,0:T(8,128)(2,1)S(1)}, u32[]{:S(2)}, u32[]{:S(2)}) collective-permute-start(bf16[512,128]{1,0:T(8,128)(2,1)S(1)} %get-tuple-element.79), channel_id=1, source_target_pairs={{0,3},{1,2},{2,1},{3,0},{4,7},{5,6},{6,5},{7,4},{8,11},{9,10},{10,... | collective-permute-start | bytes 393224 | tf_op jit(solution)/shard_map/cond/branch_1_fun/ppermute | solution.py:342
  59.5 10.0 %collective-permute-start.6 = (bf16[384,128]{1,0:T(8,128)(2,1)S(1)}, bf16[384,128]{1,0:T(8,128)(2,1)S(1)}, u32[]{:S(2)}, u32[]{:S(2)}) collective-permute-start(bf16[384,128]{1,0:T(8,128)(2,1)S(1)} %get-tuple-element.69), channel_id=1, source_target_pairs={{0,4},{1,5},{2,6},{3,7},{4,0},{5,1},{6,2},{7,3},{8,12},{9,13},{10,... | collective-permute-start | bytes 294920 | tf_op jit(solution)/shard_map/cond/branch_1_fun/ppermute | solution.py:342
  60.8 9.7 %collective-permute-start.7 = (bf16[384,128]{1,0:T(8,128)(2,1)S(1)}, bf16[384,128]{1,0:T(8,128)(2,1)S(1)}, u32[]{:S(2)}, u32[]{:S(2)}) collective-permute-start(bf16[384,128]{1,0:T(8,128)(2,1)S(1)} %get-tuple-element.70), channel_id=1, source_target_pairs={{0,8},{1,9},{2,10},{3,11},{4,12},{5,13},{6,14},{7,15},{8,0},{9,1},... | collective-permute-start | bytes 294920 | tf_op jit(solution)/shard_map/cond/branch_1_fun/ppermute | solution.py:342
  61.9 8.6 %collective-permute-start.8 = (bf16[384,128]{1,0:T(8,128)(2,1)S(1)}, bf16[384,128]{1,0:T(8,128)(2,1)S(1)}, u32[]{:S(2)}, u32[]{:S(2)}) collective-permute-start(bf16[384,128]{1,0:T(8,128)(2,1)S(1)} %get-tuple-element.71), channel_id=1, source_target_pairs={{0,12},{1,13},{2,14},{3,15},{4,8},{5,9},{6,10},{7,11},{8,4},{9,5},... | collective-permute-start | bytes 294920 | tf_op jit(solution)/shard_map/cond/branch_1_fun/ppermute | solution.py:342
  66.9 5.7 %collective-permute-start.15 = (bf16[384,128]{1,0:T(8,128)(2,1)S(1)}, bf16[384,128]{1,0:T(8,128)(2,1)S(1)}, u32[]{:S(2)}, u32[]{:S(2)}) collective-permute-start(bf16[384,128]{1,0:T(8,128)(2,1)S(1)} %get-tuple-element.81), channel_id=1, source_target_pairs={{0,4},{1,5},{2,6},{3,7},{4,0},{5,1},{6,2},{7,3},{8,12},{9,13},{10,... | collective-permute-start | bytes 294920 | tf_op jit(solution)/shard_map/cond/branch_1_fun/ppermute | solution.py:342
  68.5 5.0 %collective-permute-start.16 = (bf16[384,128]{1,0:T(8,128)(2,1)S(1)}, bf16[384,128]{1,0:T(8,128)(2,1)S(1)}, u32[]{:S(2)}, u32[]{:S(2)}) collective-permute-start(bf16[384,128]{1,0:T(8,128)(2,1)S(1)} %get-tuple-element.82), channel_id=1, source_target_pairs={{0,8},{1,9},{2,10},{3,11},{4,12},{5,13},{6,14},{7,15},{8,0},{9,1},... | collective-permute-start | bytes 294920 | tf_op jit(solution)/shard_map/cond/branch_1_fun/ppermute | solution.py:342
  69.5 6.5 %collective-permute-start.17 = (bf16[384,128]{1,0:T(8,128)(2,1)S(1)}, bf16[384,128]{1,0:T(8,128)(2,1)S(1)}, u32[]{:S(2)}, u32[]{:S(2)}) collective-permute-start(bf16[384,128]{1,0:T(8,128)(2,1)S(1)} %get-tuple-element.83), channel_id=1, source_target_pairs={{0,12},{1,13},{2,14},{3,15},{4,8},{5,9},{6,10},{7,11},{8,4},{9,5},... | collective-permute-start | bytes 294920 | tf_op jit(solution)/shard_map/cond/branch_1_fun/ppermute | solution.py:342
  77.1 6.6 %collective-permute-start.48 = (bf16[2,192,256]{2,1,0:T(8,128)(2,1)S(1)}, bf16[2,192,256]{2,1,0:T(8,128)(2,1)S(1)}, u32[]{:S(2)}, u32[]{:S(2)}) collective-permute-start(bf16[2,192,256]{2,1,0:T(8,128)(2,1)S(1)} %get-tuple-element.178), channel_id=1, source_target_pairs={{0,24},{1,25},{2,26},{3,27},{4,28},{5,29},{6,30},{7,31},{8,16},{9,... | collective-permute-start | bytes 589832 | tf_op jit(solution)/shard_map/ppermute | solution.py:342
  78.4 8.7 %collective-permute-start.49 = (bf16[2,192,256]{2,1,0:T(8,128)(2,1)S(1)}, bf16[2,192,256]{2,1,0:T(8,128)(2,1)}, u32[]{:S(2)}, u32[]{:S(2)}) collective-permute-start(bf16[2,192,256]{2,1,0:T(8,128)(2,1)S(1)} %get-tuple-element.179), channel_id=1, source_target_pairs={{0,24},{1,25},{2,26},{3,27},{4,28},{5,29},{6,30},{7,31},{8,16},{9,... | collective-permute-start | bytes 589832 | tf_op jit(solution)/shard_map/ppermute | solution.py:342
  80.4 3.3 %copy-start.3 = (bf16[2,256,1024]{2,1,0:T(8,128)(2,1)S(1)}, bf16[2,256,1024]{2,1,0:T(8,128)(2,1)}, u32[]{:S(2)}) copy-start(bf16[2,256,1024]{2,1,0:T(8,128)(2,1)} %w_rec.13) | copy-start | bytes 3145732
  87.1 53.9 %copy-start.10 = (bf16[4,192,256]{2,1,0:T(8,128)(2,1)S(1)}, bf16[4,192,256]{2,1,0:T(8,128)(2,1)}, u32[]{:S(2)}) copy-start(bf16[4,192,256]{2,1,0:T(8,128)(2,1)} %get-tuple-element.185.refs_0_) | copy-start | bytes 1179652
  87.1 58.7 %collective-permute-start.50 = (bf16[2,192,256]{2,1,0:T(8,128)(2,1)S(1)}, bf16[2,192,256]{2,1,0:T(8,128)(2,1)S(1)}, u32[]{:S(2)}, u32[]{:S(2)}) collective-permute-start(bf16[2,192,256]{2,1,0:T(8,128)(2,1)S(1)} %get-tuple-element.183), channel_id=1, source_target_pairs={{0,24},{1,25},{2,26},{3,27},{4,28},{5,29},{6,30},{7,31},{8,16},{9,... | collective-permute-start | bytes 589832 | tf_op jit(solution)/shard_map/ppermute | solution.py:342
  142.6 6.1 %collective-permute-start.51 = (bf16[2,192,256]{2,1,0:T(8,128)(2,1)S(1)}, bf16[2,192,256]{2,1,0:T(8,128)(2,1)S(1)}, u32[]{:S(2)}, u32[]{:S(2)}) collective-permute-start(bf16[2,192,256]{2,1,0:T(8,128)(2,1)S(1)} %get-tuple-element.187), channel_id=1, source_target_pairs={{0,24},{1,25},{2,26},{3,27},{4,28},{5,29},{6,30},{7,31},{8,16},{9,... | collective-permute-start | bytes 589832 | tf_op jit(solution)/shard_map/ppermute | solution.py:342
  145.8 2.9 %copy-start.9 = (bf16[4,192,256]{2,1,0:T(8,128)(2,1)S(1)}, bf16[4,192,256]{2,1,0:T(8,128)(2,1)}, u32[]{:S(2)}) copy-start(bf16[4,192,256]{2,1,0:T(8,128)(2,1)} %get-tuple-element.180.refs_0_) | copy-start | bytes 1179652
  148.8 10.7 %collective-permute-start.52 = (bf16[384,256]{1,0:T(8,128)(2,1)S(1)}, bf16[384,256]{1,0:T(8,128)(2,1)S(1)}, u32[]{:S(2)}, u32[]{:S(2)}) collective-permute-start(bf16[384,256]{1,0:T(8,128)(2,1)S(1)} %get-tuple-element.189), channel_id=1, source_target_pairs={{0,4},{1,5},{2,6},{3,7},{4,0},{5,1},{6,2},{7,3},{8,12},{9,13},{10,... | collective-permute-start | bytes 589832 | tf_op jit(solution)/shard_map/ppermute | solution.py:342
  151.3 12.8 %collective-permute-start.53 = (bf16[384,256]{1,0:T(8,128)(2,1)S(1)}, bf16[384,256]{1,0:T(8,128)(2,1)S(1)}, u32[]{:S(2)}, u32[]{:S(2)}) collective-permute-start(bf16[384,256]{1,0:T(8,128)(2,1)S(1)} %get-tuple-element.190), channel_id=1, source_target_pairs={{0,8},{1,9},{2,10},{3,11},{4,12},{5,13},{6,14},{7,15},{8,0},{9,1},... | collective-permute-start | bytes 589832 | tf_op jit(solution)/shard_map/ppermute | solution.py:342
  158.3 9.4 %collective-permute-start.54 = (bf16[384,256]{1,0:T(8,128)(2,1)S(1)}, bf16[384,256]{1,0:T(8,128)(2,1)S(1)}, u32[]{:S(2)}, u32[]{:S(2)}) collective-permute-start(bf16[384,256]{1,0:T(8,128)(2,1)S(1)} %get-tuple-element.191), channel_id=1, source_target_pairs={{0,12},{1,13},{2,14},{3,15},{4,8},{5,9},{6,10},{7,11},{8,4},{9,5},... | collective-permute-start | bytes 589832 | tf_op jit(solution)/shard_map/ppermute | solution.py:342
where the time goes:
time: 171 us; the launch traced here: 169 us
  starting transfers between devices  99.3 us (58%)
  waiting for transfers between devices  35.4 us (21%)
  Pallas kernels  31.3 us (18%)
  local copies, waits for them, and re-layouts  1.86 us (1%)
    ppermute x37, starting transfers between devices, send(): return lax.ppermute(array, AXES, pairs)  99.3 us
    ppermute x37, waiting for transfers between devices, send(): return lax.ppermute(array, AXES, pairs)  35.4 us
    pallas_call x7, Pallas kernels, recur(): pl.pallas_call(kernel, in_specs=[VMEM] * (3 + len(operands)), out_specs=[...  13.4 us
    pallas_call x4, Pallas kernels, convolve(): pl.pallas_call(kernel, in_specs=[HBM, HBM, HBM, VMEM] + [VMEM] * slab_cou...  9.71 us
    pallas_call x4, Pallas kernels, pick_tiles(): pl.pallas_call(kernel, in_specs=[HBM] + [HBM if whole else VMEM] * part_c...  3.69 us
  transfers between devices with their start and end apart: 37, of which 20 were waited for; matrix products, arithmetic and copies ran while one was open for 0% of the time, Pallas kernels for 12%

commit v1 on v0

--- a/solution.py
+++ b/solution.py
@@ -9,7 +9,7 @@
 HBM = pl.BlockSpec(memory_space=pltpu.HBM)
 VMEM = pl.BlockSpec(memory_space=pltpu.VMEM)
 PARAMS = pltpu.CompilerParams(vmem_limit_bytes=16 * 2**20)
-UNROLL = 4
+UNROLL = 32
 LANES = 128
 CHUNKS = 2
 AXES = ("tm", "slab")
@@ -37,7 +37,7 @@
     return run
 
 
-def pick_tiles(parts, ref_table, slab_count, row_count, tile, group, column):
+def pick_tiles(parts, ref_table, slab_count, row_count, tile, group, column, carried=()):
     part_count = len(parts)
     part_rows = parts[0].shape[0]
     listed = ref_table.shape[2] // slab_count
@@ -45,8 +45,9 @@
 
     def kernel(table_hbm, *refs):
         sources = refs[:part_count]
-        outs = refs[part_count : part_count + slab_count]
-        table, table_sem, rows, sems = refs[part_count + slab_count :]
+        first_out = part_count + len(carried)
+        outs = refs[first_out : first_out + slab_count]
+        table, table_sem, rows, sems = refs[-4:]
         slab = lax.axis_index("slab")
         _, _, lead = seat(group)
         fetch = pltpu.make_async_copy(table_hbm, table, table_sem)
@@ -69,15 +70,18 @@
                     outs[k][j * tile : (j + 1) * tile, :] = rows[pl.ds(start, tile), :]
         for copy in copies:
             copy.start()
+        for n in range(len(carried)):
+            refs[first_out + slab_count + n][...] = refs[part_count + n][...]
         for copy in copies:
             copy.wait()
 
     dtype = parts[0].dtype
-    return pl.pallas_call(
-        kernel,
-        in_specs=[HBM] + [HBM if whole else VMEM] * part_count,
-        out_specs=[VMEM] * slab_count,
-        out_shape=[jax.ShapeDtypeStruct((listed * tile, LANES), dtype)] * slab_count,
+    results = pl.pallas_call(
+        kernel,
+        in_specs=[HBM] + [HBM if whole else VMEM] * part_count + [VMEM] * len(carried),
+        out_specs=[VMEM] * (slab_count + len(carried)),
+        out_shape=[jax.ShapeDtypeStruct((listed * tile, LANES), dtype)] * slab_count
+        + [jax.ShapeDtypeStruct(array.shape, array.dtype) for array in carried],
         scratch_shapes=[
             pltpu.SMEM(ref_table.shape, ref_table.dtype),
             pltpu.SemaphoreType.DMA(()),
@@ -86,7 +90,8 @@
         ],
         compiler_params=PARAMS,
         name="pick_tiles",
-    )(ref_table, *parts)
+    )(ref_table, *parts, *carried)
+    return results[:slab_count], results[slab_count:]
 
 
 def convolve(arrived, tile_rows, tile_sources, tile_counts, tile_values, row_count, group):
@@ -96,6 +101,7 @@
     group_rows = row_count // group
 
     tables = (tile_rows, tile_sources, tile_counts)
+    unroll = min(UNROLL, tile_values.shape[1])
 
     def kernel(*refs):
         values = refs[3]
@@ -120,8 +126,8 @@
 
         def step(index, carry):
             products = []
-            for lane in range(UNROLL):
-                slot = index * UNROLL + lane
+            for lane in range(unroll):
+                slot = index * unroll + lane
                 start = pl.multiple_of(sources[0, slot] * tile, tile)
                 product = jnp.dot(
                     values[0, slot],
@@ -129,12 +135,12 @@
                     preferred_element_type=jnp.float32,
                 )
                 products.append(jnp.where(slot < count, product, 0.0))
-            for lane in range(UNROLL):
-                target = pl.multiple_of(rows[0, index * UNROLL + lane] * tile, tile)
+            for lane in range(unroll):
+                target = pl.multiple_of(rows[0, index * unroll + lane] * tile, tile)
                 total[pl.ds(target, tile), :] += products[lane]
             return carry
 
-        lax.fori_loop(0, (count + UNROLL - 1) // UNROLL, step, 0)
+        lax.fori_loop(0, (count + unroll - 1) // unroll, step, 0)
         for k in range(group):
             start = pl.multiple_of((lead ^ k) * group_rows, group_rows)
             outs[k][...] = total[pl.ds(start, group_rows), :].astype(outs[k].dtype)
@@ -269,7 +275,7 @@
                 step(time, states[time - 1])
                 return carry
 
-            lax.fori_loop(1, group, loop, 0)
+            lax.fori_loop(1, group, loop, 0, unroll=True)
             if lanes:
                 spread_into(outs, [*earlier, states], place, group)
             if first:
@@ -279,7 +285,7 @@
 
     dtype = mixed.dtype
     if lanes:
-        out_shape = [jax.ShapeDtypeStruct((size * CHUNKS, lanes), dtype)] * outputs
+        out_shape = [jax.ShapeDtypeStruct((size * (1 + len(done)), lanes), dtype)] * outputs
     else:
         out_shape = [jax.ShapeDtypeStruct((group, size, units), dtype)]
     if first:
@@ -300,18 +306,18 @@
 
 
 def assemble(parts):
-    columns, group = len(parts), len(parts[0])
-    part_rows, part_lanes = parts[0][0].shape
-    count = columns * group
+    group = len(parts[0])
+    size, width = parts[0][0].shape
+    part_rows = size * len(parts)
+    count = len(parts) * group
 
     def kernel(*refs):
         out, sems = refs[-2:]
         _, _, lead = seat(group)
         copies = []
         for n in range(count):
-            start = pl.multiple_of((lead ^ (n % group)) * part_rows, part_rows)
-            lanes = pl.ds(n // group * part_lanes, part_lanes)
-            target = out.at[0, pl.ds(start, part_rows), lanes]
+            start = (lead ^ (n % group)) * part_rows + n // group * size
+            target = out.at[0, pl.ds(pl.multiple_of(start, size), size)]
             copies.append(pltpu.make_async_copy(refs[n], target, sems.at[n]))
         for copy in copies:
             copy.start()
@@ -322,13 +328,11 @@
         kernel,
         in_specs=[VMEM] * count,
         out_specs=HBM,
-        out_shape=jax.ShapeDtypeStruct(
-            (1, group * part_rows, columns * part_lanes), parts[0][0].dtype
-        ),
+        out_shape=jax.ShapeDtypeStruct((1, group * part_rows, width), parts[0][0].dtype),
         scratch_shapes=[pltpu.SemaphoreType.DMA((count,))],
         compiler_params=PARAMS,
         name="assemble",
-    )(*(part for column in parts for part in column))
+    )(*(part for chunk in parts for part in chunk))
 
 
 def send(array, target, lower_only=False):
@@ -371,8 +375,10 @@
     group = lax.axis_size("tm") // 2
     half = lax.axis_index("tm") // group
 
-    def mix(parts, column=0):
-        listed = pick_tiles(parts, ref_lists, slab_count, row_count, tile, group, column)
+    def pick(parts, table, column=0, carried=()):
+        return pick_tiles(parts, table, slab_count, row_count, tile, group, column, carried)
+
+    def mix(listed):
         arrived = swap_slabs(listed)
         return swap_times(
             convolve(
@@ -381,10 +387,10 @@
         )
 
     def back_and_mix(hidden):
-        return pack([mix(swap_times(column)) for column in hidden])
+        return pack([mix(pick(swap_times(column), table)[0]) for column in hidden])
 
     def run(mixed, layer, mode, *rest):
-        return recur(mixed, layer, w_input, w_hidden, bias, mode, *rest)
+        return recur(mixed, layer, w_input, w_hidden, gate_bias, mode, *rest)
 
     def run_lower(mixed, layer):
         chunks, handed = [], []
@@ -398,8 +404,10 @@
         return [run(part, layer, UPPER, state) for part, state in zip(mixed[:-1], states)]
 
     features = features[0]
-    width = features.shape[1]
-    upper_mixed = pack([mix([features], column) for column in range(width // LANES)])
+    columns = features.shape[1] // LANES
+    listed = [pick([features], ref_lists, column)[0] for column in range(columns - 1)]
+    last, (table, gate_bias) = pick([features], ref_lists, columns - 1, (ref_lists, bias))
+    upper_mixed = pack([mix(column) for column in [*listed, last]])
     hidden, handed = run_lower(upper_mixed, 0)
     for layer in range(1, layers):
 
@@ -423,10 +431,12 @@
             handed[-1],
         )
         handed = following
-    done = run_upper(upper_mixed, layers - 1, handed)
     units = w_hidden.shape[1]
-    hidden = run(upper_mixed[-1], layers - 1, UPPER, handed[-1], done, hidden, units)
-    return assemble([swap_times(column) for column in hidden])
+    parts = []
+    for number, (part, state) in enumerate(zip(upper_mixed, handed)):
+        (states,) = run(part, layers - 1, UPPER, state, (), hidden[number : number + 1], units)
+        parts.append(swap_times(states))
+    return assemble(parts)
 
 
 def solution(mesh):

time: 171 us -> 164 us (0.959)
  Pallas kernels: 31.3 us -> 25.6 us
  waiting for transfers between devices: 35.4 us -> 29.8 us
  starting transfers between devices: 99.3 us -> 103 us
    ppermute x37 -> x40, waiting for transfers between devices: 35.4 us -> 29.8 us  [send(): return lax.ppermute(array, AXES, pairs)]
    ppermute x37 -> x40, starting transfers between devices: 99.3 us -> 103 us  [send(): return lax.ppermute(array, AXES, pairs)]
    pallas_call x4, Pallas kernels: 9.71 us -> 5.85 us  [convolve(): pl.pallas_call(kernel, in_specs=[HBM, HBM, HBM, VMEM] + [VMEM] * slab_cou...]
  transfers between devices with their start and end apart: 37 -> 40, of which waited for: 20 -> 20; matrix products, arithmetic and copies ran while one was open for 0% -> 0% of each run, Pallas kernels for 12% -> 10%
where the time goes in v1:
time: 164 us; the launch traced here: 162 us
  starting transfers between devices  103 us (63%)
  waiting for transfers between devices  29.8 us (18%)
  Pallas kernels  25.6 us (16%)
  local copies, waits for them, and re-layouts  2.51 us (2%)
    ppermute x40, starting transfers between devices, send(): return lax.ppermute(array, AXES, pairs)  103 us
    ppermute x40, waiting for transfers between devices, send(): return lax.ppermute(array, AXES, pairs)  29.8 us
    pallas_call x7, Pallas kernels, recur(): pl.pallas_call(kernel, in_specs=[VMEM] * (3 + len(operands)), out_specs=[...  12.2 us
    pallas_call x4, Pallas kernels, convolve(): pl.pallas_call(kernel, in_specs=[HBM, HBM, HBM, VMEM] + [VMEM] * slab_cou...  5.85 us
    pallas_call x4, Pallas kernels, pick_tiles(): pl.pallas_call(kernel, in_specs=[HBM] + [HBM if whole else VMEM] * part_c...  3.31 us
  transfers between devices with their start and end apart: 40, of which 20 were waited for; matrix products, arithmetic and copies ran while one was open for 0% of the time, Pallas kernels for 10%

profile of v1, /device:TPU:0, one launch (start us, length us, event | category | flops | bytes accessed | tf_op | source)
XLA Modules:
  0.0 162.1 jit_solution(9429771563155030802)
XLA Ops:
  0.0 1.1 copy-done
  1.1 0.7 copy-done.1
  1.8 0.9 pick_tiles.11
  3.3 2.6 %collective-permute-start.37 = (bf16[512,128]{1,0:T(8,128)(2,1)S(1)}, bf16[512,128]{1,0:T(8,128)(2,1)S(1)}, u32[]{:S(2)}, u32[]{:S(2)}) collective-permute-start(bf16[512,128]{1,0:T(8,128)(2,1)S(1)} %get-tuple-element.166), channel_id=1, source_target_pairs={{0,2},{1,3},{2,0},{3,1},{4,6},{5,7},{6,4},{7,5},{8,10},{9,11},{10,... | collective-permute-start | bytes 393224 | tf_op jit(solution)/shard_map/ppermute | solution.py:346
  5.9 0.9 pick_tiles.10
  7.0 1.9 %collective-permute-start.43 = (bf16[512,128]{1,0:T(8,128)(2,1)S(1)}, bf16[512,128]{1,0:T(8,128)(2,1)S(1)}, u32[]{:S(2)}, u32[]{:S(2)}) collective-permute-start(bf16[512,128]{1,0:T(8,128)(2,1)S(1)} %get-tuple-element.174), channel_id=1, source_target_pairs={{0,2},{1,3},{2,0},{3,1},{4,6},{5,7},{6,4},{7,5},{8,10},{9,11},{10,... | collective-permute-start | bytes 393224 | tf_op jit(solution)/shard_map/ppermute | solution.py:346
  10.2 2.4 %collective-permute-done.38.refs_7_ = bf16[512,128]{1,0:T(8,128)(2,1)S(1)} collective-permute-done((bf16[512,128]{1,0:T(8,128)(2,1)S(1)}, bf16[512,128]{1,0:T(8,128)(2,1)S(1)}, u32[]{:S(2)}, u32[]{:S(2)}) %collective-permute-start.38) | collective-permute-done | bytes 131104 | tf_op jit(solution)/shard_map/ppermute | solution.py:346
  12.5 1.1 convolve.10
  13.7 1.6 collective-permute-start.39
  15.3 1.6 collective-permute-start.40
  17.2 0.8 collective-permute-done.44.refs_7_
  18.1 1.1 convolve.11
  19.2 1.6 collective-permute-start.45
  20.8 1.6 collective-permute-start.46
  22.8 2.0 %collective-permute-done.45.refs_5_ = bf16[384,128]{1,0:T(8,128)(2,1)S(1)} collective-permute-done((bf16[384,128]{1,0:T(8,128)(2,1)S(1)}, bf16[384,128]{1,0:T(8,128)(2,1)S(1)}, u32[]{:S(2)}, u32[]{:S(2)}) %collective-permute-start.45) | collective-permute-done | bytes 98336 | tf_op jit(solution)/shard_map/ppermute | solution.py:346
  24.8 1.7 %collective-permute-done.46.refs_6_ = bf16[384,128]{1,0:T(8,128)(2,1)S(1)} collective-permute-done((bf16[384,128]{1,0:T(8,128)(2,1)S(1)}, bf16[384,128]{1,0:T(8,128)(2,1)S(1)}, u32[]{:S(2)}, u32[]{:S(2)}) %collective-permute-start.46) | collective-permute-done | bytes 98336 | tf_op jit(solution)/shard_map/ppermute | solution.py:346
  26.5 1.6 collective-permute-done.47.refs_7_
  28.1 0.9 pack.5
  29.0 3.0 %recur.9 = (bf16[4,192,256]{2,1,0:T(8,128)(2,1)}, bf16[2,192,256]{2,1,0:T(8,128)(2,1)S(1)}) custom-call(bf16[2,256,1024]{2,1,0:T(8,128)(2,1)S(1)} %copy-done.3, bf16[2,256,1024]{2,1,0:T(8,128)(2,1)S(1)} %copy-done.4, f32[2,1024]{1,0:T(2,128)S(1)} %get-tuple-element.163.gate_bias, bf16[4,192,256]{2,1,0:T(8,128)(2,1)} %get-tuple-element.180.refs_0_), custom_call_target="tpu_custom_call" | custom-call | tf_op jit(solution)/shard_map/recur/pallas_call | solution.py:294
  32.0 1.8 %recur.10 = (bf16[4,192,256]{2,1,0:T(8,128)(2,1)}, bf16[2,192,256]{2,1,0:T(8,128)(2,1)S(1)}) custom-call(bf16[2,256,1024]{2,1,0:T(8,128)(2,1)S(1)} %copy-done.3, bf16[2,256,1024]{2,1,0:T(8,128)(2,1)S(1)} %copy-done.4, f32[2,1024]{1,0:T(2,128)S(1)} %get-tuple-element.163.gate_bias, bf16[4,192,256]{2,1,0:T(8,128)(2,1)S(1)} %get-tuple-element.182.refs_0_), custom_call_target="tpu_custom_call" | custom-call | tf_op jit(solution)/shard_map/recur/pallas_call | solution.py:294
  34.4 38.7 %conditional.2 = (bf16[4,192,256]{2,1,0:T(8,128)(2,1)}, bf16[4,192,256]{2,1,0:T(8,128)(2,1)}, s32[]{:T(128)}) conditional(s32[]{:T(128)} %convert_element_type.6, (bf16[4,192,256]{2,1,0:T(8,128)(2,1)}, bf16[4,192,256]{2,1,0:T(8,128)(2,1)}, s32[]{:T(128)}) %tuple.17, (bf16[4,192,256]{2,1,0:T(8,128)(2,1)}, bf16[4,192,256]{2,1,0:T(8,128)(2,1)}, ...), branch_computations={%region_0.1_spmd, %region_1.2_spmd} | conditional | flops 1 | bytes 12059408 | solution.py:420
  34.4 1.3 spread.1
  35.8 1.5 collective-permute-start
  37.2 1.6 collective-permute-start.1
  39.3 1.4 collective-permute-start.9
  40.7 1.7 %collective-permute-done.1.refs_2_ = bf16[384,128]{1,0:T(8,128)(2,1)S(1)} collective-permute-done((bf16[384,128]{1,0:T(8,128)(2,1)S(1)}, bf16[384,128]{1,0:T(8,128)(2,1)S(1)}, u32[]{:S(2)}, u32[]{:S(2)}) %collective-permute-start.1) | collective-permute-done | bytes 98336 | tf_op jit(solution)/shard_map/cond/branch_1_fun/ppermute | solution.py:346
  42.4 1.9 %collective-permute-done.2.refs_3_ = bf16[384,128]{1,0:T(8,128)(2,1)S(1)} collective-permute-done((bf16[384,128]{1,0:T(8,128)(2,1)S(1)}, bf16[384,128]{1,0:T(8,128)(2,1)S(1)}, u32[]{:S(2)}, u32[]{:S(2)}) %collective-permute-start.2) | collective-permute-done | bytes 98336 | tf_op jit(solution)/shard_map/cond/branch_1_fun/ppermute | solution.py:346
  44.3 0.8 pick_tiles.6
  45.2 0.7 collective-permute-start.10
  45.9 1.5 collective-permute-start.11
  47.4 1.5 collective-permute-start.4
  48.9 2.0 %collective-permute-done.10.refs_2_ = bf16[384,128]{1,0:T(8,128)(2,1)S(1)} collective-permute-done((bf16[384,128]{1,0:T(8,128)(2,1)S(1)}, bf16[384,128]{1,0:T(8,128)(2,1)S(1)}, u32[]{:S(2)}, u32[]{:S(2)}) %collective-permute-start.10) | collective-permute-done | bytes 98336 | tf_op jit(solution)/shard_map/cond/branch_1_fun/ppermute | solution.py:346
  50.9 1.7 %collective-permute-done.11.refs_3_ = bf16[384,128]{1,0:T(8,128)(2,1)S(1)} collective-permute-done((bf16[384,128]{1,0:T(8,128)(2,1)S(1)}, bf16[384,128]{1,0:T(8,128)(2,1)S(1)}, u32[]{:S(2)}, u32[]{:S(2)}) %collective-permute-start.11) | collective-permute-done | bytes 98336 | tf_op jit(solution)/shard_map/cond/branch_1_fun/ppermute | solution.py:346
  52.6 0.8 pick_tiles.7
  53.4 1.6 collective-permute-start.13
  55.3 1.8 %convolve.6 = (bf16[384,128]{1,0:T(8,128)(2,1)S(1)}, bf16[384,128]{1,0:T(8,128)(2,1)S(1)}, bf16[384,128]{1,0:T(8,128)(2,1)S(1)}, bf16[384,128]{1,0:T(8,128)(2,1)S(1)}) custom-call(s32[1,32]{1,0:T(1,128)S(1)} %get-tuple-element.53.refs_0_, s32[1,32]{1,0:T(1,128)S(1)} %get-tuple-element.54.refs_1_, s32[1,1]{1,0:T(1,128)} %get-tuple-element.55.refs_2_, ...), custom_call_target="tpu_custom_call" | custom-call | tf_op jit(solution)/shard_map/cond/branch_1_fun/convolve/pallas_call | solution.py:149
  57.1 1.4 collective-permute-start.6
  59.1 1.5 collective-permute-start.8
  60.7 0.9 collective-permute-done.14.refs_7_
  61.6 1.8 %convolve.7 = (bf16[384,128]{1,0:T(8,128)(2,1)S(1)}, bf16[384,128]{1,0:T(8,128)(2,1)S(1)}, bf16[384,128]{1,0:T(8,128)(2,1)S(1)}, bf16[384,128]{1,0:T(8,128)(2,1)S(1)}) custom-call(s32[1,32]{1,0:T(1,128)S(1)} %get-tuple-element.53.refs_0_, s32[1,32]{1,0:T(1,128)S(1)} %get-tuple-element.54.refs_1_, s32[1,1]{1,0:T(1,128)} %get-tuple-element.55.refs_2_, ...), custom_call_target="tpu_custom_call" | custom-call | tf_op jit(solution)/shard_map/cond/branch_1_fun/convolve/pallas_call | solution.py:149
  63.4 1.4 collective-permute-start.15
  65.4 1.5 collective-permute-start.17
  67.0 1.8 %collective-permute-done.15.refs_5_ = bf16[384,128]{1,0:T(8,128)(2,1)S(1)} collective-permute-done((bf16[384,128]{1,0:T(8,128)(2,1)S(1)}, bf16[384,128]{1,0:T(8,128)(2,1)S(1)}, u32[]{:S(2)}, u32[]{:S(2)}) %collective-permute-start.15) | collective-permute-done | bytes 98336 | tf_op jit(solution)/shard_map/cond/branch_1_fun/ppermute | solution.py:346
  68.8 1.6 %collective-permute-done.16.refs_6_ = bf16[384,128]{1,0:T(8,128)(2,1)S(1)} collective-permute-done((bf16[384,128]{1,0:T(8,128)(2,1)S(1)}, bf16[384,128]{1,0:T(8,128)(2,1)S(1)}, u32[]{:S(2)}, u32[]{:S(2)}) %collective-permute-start.16) | collective-permute-done | bytes 98336 | tf_op jit(solution)/shard_map/cond/branch_1_fun/ppermute | solution.py:346
  70.5 1.6 %collective-permute-done.17.refs_7_ = bf16[384,128]{1,0:T(8,128)(2,1)S(1)} collective-permute-done((bf16[384,128]{1,0:T(8,128)(2,1)S(1)}, bf16[384,128]{1,0:T(8,128)(2,1)S(1)}, u32[]{:S(2)}, u32[]{:S(2)}) %collective-permute-start.17) | collective-permute-done | bytes 98336 | tf_op jit(solution)/shard_map/cond/branch_1_fun/ppermute | solution.py:346
  72.1 1.0 pack.3
  73.1 1.3 collective-permute-start.48
  74.4 1.3 collective-permute-start.49
  75.8 2.5 %recur.12 = (bf16[4,192,256]{2,1,0:T(8,128)(2,1)S(1)}, bf16[2,192,256]{2,1,0:T(8,128)(2,1)S(1)}) custom-call(bf16[2,256,1024]{2,1,0:T(8,128)(2,1)S(1)} %copy-done.3, bf16[2,256,1024]{2,1,0:T(8,128)(2,1)} %w_rec.13, f32[2,1024]{1,0:T(2,128)S(1)} %get-tuple-element.163.gate_bias, bf16[4,192,256]{2,1,0:T(8,128)(2,1)} %get-tuple-element.189.refs_0_), custom_call_target="tpu_custom_call" | custom-call | tf_op jit(solution)/shard_map/recur/pallas_call | solution.py:294
  78.2 1.5 collective-permute-done.48.refs_1_
  79.7 1.8 %recur.11 = bf16[4,192,256]{2,1,0:T(8,128)(2,1)} custom-call(bf16[2,256,1024]{2,1,0:T(8,128)(2,1)S(1)} %copy-done.3, bf16[2,256,1024]{2,1,0:T(8,128)(2,1)S(1)} %copy-done.5, f32[2,1024]{1,0:T(2,128)S(1)} %get-tuple-element.163.gate_bias, bf16[4,192,256]{2,1,0:T(8,128)(2,1)} %get-tuple-element.180.refs_0_, ...), custom_call_target="tpu_custom_call" | custom-call | tf_op jit(solution)/shard_map/recur/pallas_call | solution.py:294
  81.5 1.3 collective-permute-done.49
  82.8 53.4 %collective-permute-start.50 = (bf16[2,192,256]{2,1,0:T(8,128)(2,1)S(1)}, bf16[2,192,256]{2,1,0:T(8,128)(2,1)S(1)}, u32[]{:S(2)}, u32[]{:S(2)}) collective-permute-start(bf16[2,192,256]{2,1,0:T(8,128)(2,1)S(1)} %get-tuple-element.191), channel_id=1, source_target_pairs={{0,24},{1,25},{2,26},{3,27},{4,28},{5,29},{6,30},{7,31},{8,16},{9,... | collective-permute-start | bytes 589832 | tf_op jit(solution)/shard_map/ppermute | solution.py:346
  136.2 2.1 %recur.14 = (bf16[4,192,256]{2,1,0:T(8,128)(2,1)S(1)}, bf16[2,192,256]{2,1,0:T(8,128)(2,1)S(1)}) custom-call(bf16[2,256,1024]{2,1,0:T(8,128)(2,1)S(1)} %copy-done.3, bf16[2,256,1024]{2,1,0:T(8,128)(2,1)S(1)} %copy-done.5, f32[2,1024]{1,0:T(2,128)S(1)} %get-tuple-element.163.gate_bias, bf16[4,192,256]{2,1,0:T(8,128)(2,1)} %get-tuple-element.197.refs_0_), custom_call_target="tpu_custom_call" | custom-call | tf_op jit(solution)/shard_map/recur/pallas_call | solution.py:294
  138.3 1.3 collective-permute-start.54
  139.6 1.5 collective-permute-done.50.refs_2_
  141.1 1.1 recur.13
  142.2 0.7 collective-permute-start.51
  142.9 9.1 %collective-permute-start.52 = (bf16[192,256]{1,0:T(8,128)(2,1)S(1)}, bf16[192,256]{1,0:T(8,128)(2,1)S(1)}, u32[]{:S(2)}, u32[]{:S(2)}) collective-permute-start(bf16[192,256]{1,0:T(8,128)(2,1)S(1)} %get-tuple-element.194), channel_id=1, source_target_pairs={{0,8},{1,9},{2,10},{3,11},{4,12},{5,13},{6,14},{7,15},{8,0},{9,1},... | collective-permute-start | bytes 294920 | tf_op jit(solution)/shard_map/ppermute | solution.py:346
  152.5 1.0 collective-permute-start.55
  153.5 2.0 %collective-permute-start.56 = (bf16[192,256]{1,0:T(8,128)(2,1)S(1)}, bf16[192,256]{1,0:T(8,128)(2,1)S(1)}, u32[]{:S(2)}, u32[]{:S(2)}) collective-permute-start(bf16[192,256]{1,0:T(8,128)(2,1)S(1)} %get-tuple-element.202), channel_id=1, source_target_pairs={{0,8},{1,9},{2,10},{3,11},{4,12},{5,13},{6,14},{7,15},{8,0},{9,1},... | collective-permute-start | bytes 294920 | tf_op jit(solution)/shard_map/ppermute | solution.py:346
  155.5 2.4 %collective-permute-start.57 = (bf16[192,256]{1,0:T(8,128)(2,1)S(1)}, bf16[192,256]{1,0:T(8,128)(2,1)S(1)}, u32[]{:S(2)}, u32[]{:S(2)}) collective-permute-start(bf16[192,256]{1,0:T(8,128)(2,1)S(1)} %get-tuple-element.203), channel_id=1, source_target_pairs={{0,12},{1,13},{2,14},{3,15},{4,8},{5,9},{6,10},{7,11},{8,4},{9,5},... | collective-permute-start | bytes 294920 | tf_op jit(solution)/shard_map/ppermute | solution.py:346
  159.3 1.8 %collective-permute-done.57.refs_7_ = bf16[192,256]{1,0:T(8,128)(2,1)S(1)} collective-permute-done((bf16[192,256]{1,0:T(8,128)(2,1)S(1)}, bf16[192,256]{1,0:T(8,128)(2,1)S(1)}, u32[]{:S(2)}, u32[]{:S(2)}) %collective-permute-start.57) | collective-permute-done | bytes 98336 | tf_op jit(solution)/shard_map/ppermute | solution.py:346
  161.0 0.9 assemble.1
  (63 shorter events, 7.1 us)
Async XLA Ops:
  0.0 1.1 copy-start
  1.1 0.7 copy-start.1
  1.8 4.1 %copy-start.2 = (f32[2,1024]{1,0:T(2,128)S(1)}, f32[2,1024]{1,0:T(2,128)}, u32[]{:S(2)}) copy-start(f32[2,1024]{1,0:T(2,128)} %refs_2_.3) | copy-start | bytes 24580
  1.8 10.7 %copy-start.6 = (bf16[1,32,128,128]{3,2,1,0:T(8,128)(2,1)S(1)}, bf16[1,32,128,128]{3,2,1,0:T(8,128)(2,1)}, u32[]{:S(2)}) copy-start(bf16[1,32,128,128]{3,2,1,0:T(8,128)(2,1)} %refs_3_.3) | copy-start | bytes 3145732
  2.7 6.2 %collective-permute-start.36 = (bf16[512,128]{1,0:T(8,128)(2,1)S(1)}, bf16[512,128]{1,0:T(8,128)(2,1)S(1)}, u32[]{:S(2)}, u32[]{:S(2)}) collective-permute-start(bf16[512,128]{1,0:T(8,128)(2,1)S(1)} %get-tuple-element.165), channel_id=1, source_target_pairs={{0,1},{1,0},{2,3},{3,2},{4,5},{5,4},{6,7},{7,6},{8,9},{9,8},{10,11... | collective-permute-start | bytes 393224 | tf_op jit(solution)/shard_map/ppermute | solution.py:346
  3.3 6.9 %collective-permute-start.37 = (bf16[512,128]{1,0:T(8,128)(2,1)S(1)}, bf16[512,128]{1,0:T(8,128)(2,1)S(1)}, u32[]{:S(2)}, u32[]{:S(2)}) collective-permute-start(bf16[512,128]{1,0:T(8,128)(2,1)S(1)} %get-tuple-element.166), channel_id=1, source_target_pairs={{0,2},{1,3},{2,0},{3,1},{4,6},{5,7},{6,4},{7,5},{8,10},{9,11},{10,... | collective-permute-start | bytes 393224 | tf_op jit(solution)/shard_map/ppermute | solution.py:346
  5.8 6.7 %collective-permute-start.38 = (bf16[512,128]{1,0:T(8,128)(2,1)S(1)}, bf16[512,128]{1,0:T(8,128)(2,1)S(1)}, u32[]{:S(2)}, u32[]{:S(2)}) collective-permute-start(bf16[512,128]{1,0:T(8,128)(2,1)S(1)} %get-tuple-element.167), channel_id=1, source_target_pairs={{0,3},{1,2},{2,1},{3,0},{4,7},{5,6},{6,5},{7,4},{8,11},{9,10},{10,... | collective-permute-start | bytes 393224 | tf_op jit(solution)/shard_map/ppermute | solution.py:346
  6.8 10.1 %collective-permute-start.42 = (bf16[512,128]{1,0:T(8,128)(2,1)S(1)}, bf16[512,128]{1,0:T(8,128)(2,1)S(1)}, u32[]{:S(2)}, u32[]{:S(2)}) collective-permute-start(bf16[512,128]{1,0:T(8,128)(2,1)S(1)} %get-tuple-element.173), channel_id=1, source_target_pairs={{0,1},{1,0},{2,3},{3,2},{4,5},{5,4},{6,7},{7,6},{8,9},{9,8},{10,11... | collective-permute-start | bytes 393224 | tf_op jit(solution)/shard_map/ppermute | solution.py:346
  7.0 10.2 %collective-permute-start.43 = (bf16[512,128]{1,0:T(8,128)(2,1)S(1)}, bf16[512,128]{1,0:T(8,128)(2,1)S(1)}, u32[]{:S(2)}, u32[]{:S(2)}) collective-permute-start(bf16[512,128]{1,0:T(8,128)(2,1)S(1)} %get-tuple-element.174), channel_id=1, source_target_pairs={{0,2},{1,3},{2,0},{3,1},{4,6},{5,7},{6,4},{7,5},{8,10},{9,11},{10,... | collective-permute-start | bytes 393224 | tf_op jit(solution)/shard_map/ppermute | solution.py:346
  9.0 9.1 %collective-permute-start.44 = (bf16[512,128]{1,0:T(8,128)(2,1)S(1)}, bf16[512,128]{1,0:T(8,128)(2,1)S(1)}, u32[]{:S(2)}, u32[]{:S(2)}) collective-permute-start(bf16[512,128]{1,0:T(8,128)(2,1)S(1)} %get-tuple-element.175), channel_id=1, source_target_pairs={{0,3},{1,2},{2,1},{3,0},{4,7},{5,6},{6,5},{7,4},{8,11},{9,10},{10,... | collective-permute-start | bytes 393224 | tf_op jit(solution)/shard_map/ppermute | solution.py:346
  9.6 2.9 %copy-start.11 = (s32[1,32]{1,0:T(1,128)S(1)}, s32[1,32]{1,0:T(1,128)}, u32[]{:S(2)}) copy-start(s32[1,32]{1,0:T(1,128)} %refs_0_.3) | copy-start | bytes 388
  9.6 2.9 %copy-start.12 = (s32[1,32]{1,0:T(1,128)S(1)}, s32[1,32]{1,0:T(1,128)}, u32[]{:S(2)}) copy-start(s32[1,32]{1,0:T(1,128)} %refs_1_.5) | copy-start | bytes 388
  13.7 8.7 %collective-permute-start.39 = (bf16[384,128]{1,0:T(8,128)(2,1)S(1)}, bf16[384,128]{1,0:T(8,128)(2,1)S(1)}, u32[]{:S(2)}, u32[]{:S(2)}) collective-permute-start(bf16[384,128]{1,0:T(8,128)(2,1)S(1)} %get-tuple-element.169), channel_id=1, source_target_pairs={{0,4},{1,5},{2,6},{3,7},{4,0},{5,1},{6,2},{7,3},{8,12},{9,13},{10,... | collective-permute-start | bytes 294920 | tf_op jit(solution)/shard_map/ppermute | solution.py:346
  15.3 7.5 %collective-permute-start.40 = (bf16[384,128]{1,0:T(8,128)(2,1)S(1)}, bf16[384,128]{1,0:T(8,128)(2,1)S(1)}, u32[]{:S(2)}, u32[]{:S(2)}) collective-permute-start(bf16[384,128]{1,0:T(8,128)(2,1)S(1)} %get-tuple-element.170), channel_id=1, source_target_pairs={{0,8},{1,9},{2,10},{3,11},{4,12},{5,13},{6,14},{7,15},{8,0},{9,1},... | collective-permute-start | bytes 294920 | tf_op jit(solution)/shard_map/ppermute | solution.py:346
  16.9 5.9 %collective-permute-start.41 = (bf16[384,128]{1,0:T(8,128)(2,1)S(1)}, bf16[384,128]{1,0:T(8,128)(2,1)S(1)}, u32[]{:S(2)}, u32[]{:S(2)}) collective-permute-start(bf16[384,128]{1,0:T(8,128)(2,1)S(1)} %get-tuple-element.171), channel_id=1, source_target_pairs={{0,12},{1,13},{2,14},{3,15},{4,8},{5,9},{6,10},{7,11},{8,4},{9,5},... | collective-permute-start | bytes 294920 | tf_op jit(solution)/shard_map/ppermute | solution.py:346
  18.1 10.9 %copy-start.3 = (bf16[2,256,1024]{2,1,0:T(8,128)(2,1)S(1)}, bf16[2,256,1024]{2,1,0:T(8,128)(2,1)}, u32[]{:S(2)}) copy-start(bf16[2,256,1024]{2,1,0:T(8,128)(2,1)} %w_in.13) | copy-start | bytes 3145732
  18.1 10.9 %copy-start.4 = (bf16[2,256,1024]{2,1,0:T(8,128)(2,1)S(1)}, bf16[2,256,1024]{2,1,0:T(8,128)(2,1)}, u32[]{:S(2)}) copy-start(bf16[2,256,1024]{2,1,0:T(8,128)(2,1)} %w_rec.13) | copy-start | bytes 3145732
  19.2 5.6 %collective-permute-start.45 = (bf16[384,128]{1,0:T(8,128)(2,1)S(1)}, bf16[384,128]{1,0:T(8,128)(2,1)S(1)}, u32[]{:S(2)}, u32[]{:S(2)}) collective-permute-start(bf16[384,128]{1,0:T(8,128)(2,1)S(1)} %get-tuple-element.177), channel_id=1, source_target_pairs={{0,4},{1,5},{2,6},{3,7},{4,0},{5,1},{6,2},{7,3},{8,12},{9,13},{10,... | collective-permute-start | bytes 294920 | tf_op jit(solution)/shard_map/ppermute | solution.py:346
  20.8 5.7 %collective-permute-start.46 = (bf16[384,128]{1,0:T(8,128)(2,1)S(1)}, bf16[384,128]{1,0:T(8,128)(2,1)S(1)}, u32[]{:S(2)}, u32[]{:S(2)}) collective-permute-start(bf16[384,128]{1,0:T(8,128)(2,1)S(1)} %get-tuple-element.178), channel_id=1, source_target_pairs={{0,8},{1,9},{2,10},{3,11},{4,12},{5,13},{6,14},{7,15},{8,0},{9,1},... | collective-permute-start | bytes 294920 | tf_op jit(solution)/shard_map/ppermute | solution.py:346
  22.4 5.7 %collective-permute-start.47 = (bf16[384,128]{1,0:T(8,128)(2,1)S(1)}, bf16[384,128]{1,0:T(8,128)(2,1)S(1)}, u32[]{:S(2)}, u32[]{:S(2)}) collective-permute-start(bf16[384,128]{1,0:T(8,128)(2,1)S(1)} %get-tuple-element.179), channel_id=1, source_target_pairs={{0,12},{1,13},{2,14},{3,15},{4,8},{5,9},{6,10},{7,11},{8,4},{9,5},... | collective-permute-start | bytes 294920 | tf_op jit(solution)/shard_map/ppermute | solution.py:346
  29.0 3.0 %copy-start.9 = (bf16[4,192,256]{2,1,0:T(8,128)(2,1)}, bf16[4,192,256]{2,1,0:T(8,128)(2,1)S(1)}, u32[]{:S(2)}) copy-start(bf16[4,192,256]{2,1,0:T(8,128)(2,1)S(1)} %get-tuple-element.182.refs_0_) | copy-start | bytes 1179652
  33.8 0.7 copy-start.13
  34.4 20.9 %copy-start.7 = (bf16[1,32,128,128]{3,2,1,0:T(8,128)(2,1)S(1)}, bf16[1,32,128,128]{3,2,1,0:T(8,128)(2,1)}, u32[]{:S(2)}) copy-start(bf16[1,32,128,128]{3,2,1,0:T(8,128)(2,1)} %get-tuple-element.56.refs_3_) | copy-start | bytes 3145732 | tf_op jit(solution)/shard_map/cond
  35.8 4.9 %collective-permute-start = (bf16[384,128]{1,0:T(8,128)(2,1)S(1)}, bf16[384,128]{1,0:T(8,128)(2,1)S(1)}, u32[]{:S(2)}, u32[]{:S(2)}) collective-permute-start(bf16[384,128]{1,0:T(8,128)(2,1)S(1)} %get-tuple-element.61), channel_id=1, source_target_pairs={{0,4},{1,5},{2,6},{3,7},{4,0},{5,1},{6,2},{7,3},{8,12},{9,13},{10,... | collective-permute-start | bytes 294920 | tf_op jit(solution)/shard_map/cond/branch_1_fun/ppermute | solution.py:346
  37.2 5.2 %collective-permute-start.1 = (bf16[384,128]{1,0:T(8,128)(2,1)S(1)}, bf16[384,128]{1,0:T(8,128)(2,1)S(1)}, u32[]{:S(2)}, u32[]{:S(2)}) collective-permute-start(bf16[384,128]{1,0:T(8,128)(2,1)S(1)} %get-tuple-element.62), channel_id=1, source_target_pairs={{0,8},{1,9},{2,10},{3,11},{4,12},{5,13},{6,14},{7,15},{8,0},{9,1},... | collective-permute-start | bytes 294920 | tf_op jit(solution)/shard_map/cond/branch_1_fun/ppermute | solution.py:346
  38.8 5.5 %collective-permute-start.2 = (bf16[384,128]{1,0:T(8,128)(2,1)S(1)}, bf16[384,128]{1,0:T(8,128)(2,1)S(1)}, u32[]{:S(2)}, u32[]{:S(2)}) collective-permute-start(bf16[384,128]{1,0:T(8,128)(2,1)S(1)} %get-tuple-element.63), channel_id=1, source_target_pairs={{0,12},{1,13},{2,14},{3,15},{4,8},{5,9},{6,10},{7,11},{8,4},{9,5},... | collective-permute-start | bytes 294920 | tf_op jit(solution)/shard_map/cond/branch_1_fun/ppermute | solution.py:346
  39.3 9.6 %collective-permute-start.9 = (bf16[384,128]{1,0:T(8,128)(2,1)S(1)}, bf16[384,128]{1,0:T(8,128)(2,1)S(1)}, u32[]{:S(2)}, u32[]{:S(2)}) collective-permute-start(bf16[384,128]{1,0:T(8,128)(2,1)S(1)} %get-tuple-element.73), channel_id=1, source_target_pairs={{0,4},{1,5},{2,6},{3,7},{4,0},{5,1},{6,2},{7,3},{8,12},{9,13},{10,... | collective-permute-start | bytes 294920 | tf_op jit(solution)/shard_map/cond/branch_1_fun/ppermute | solution.py:346
  45.1 9.9 %collective-permute-start.3 = (bf16[512,128]{1,0:T(8,128)(2,1)S(1)}, bf16[512,128]{1,0:T(8,128)(2,1)S(1)}, u32[]{:S(2)}, u32[]{:S(2)}) collective-permute-start(bf16[512,128]{1,0:T(8,128)(2,1)S(1)} %get-tuple-element.65), channel_id=1, source_target_pairs={{0,1},{1,0},{2,3},{3,2},{4,5},{5,4},{6,7},{7,6},{8,9},{9,8},{10,11... | collective-permute-start | bytes 393224 | tf_op jit(solution)/shard_map/cond/branch_1_fun/ppermute | solution.py:346
  45.2 5.7 %collective-permute-start.10 = (bf16[384,128]{1,0:T(8,128)(2,1)S(1)}, bf16[384,128]{1,0:T(8,128)(2,1)S(1)}, u32[]{:S(2)}, u32[]{:S(2)}) collective-permute-start(bf16[384,128]{1,0:T(8,128)(2,1)S(1)} %get-tuple-element.74), channel_id=1, source_target_pairs={{0,8},{1,9},{2,10},{3,11},{4,12},{5,13},{6,14},{7,15},{8,0},{9,1},... | collective-permute-start | bytes 294920 | tf_op jit(solution)/shard_map/cond/branch_1_fun/ppermute | solution.py:346
  45.9 6.7 %collective-permute-start.11 = (bf16[384,128]{1,0:T(8,128)(2,1)S(1)}, bf16[384,128]{1,0:T(8,128)(2,1)S(1)}, u32[]{:S(2)}, u32[]{:S(2)}) collective-permute-start(bf16[384,128]{1,0:T(8,128)(2,1)S(1)} %get-tuple-element.75), channel_id=1, source_target_pairs={{0,12},{1,13},{2,14},{3,15},{4,8},{5,9},{6,10},{7,11},{8,4},{9,5},... | collective-permute-start | bytes 294920 | tf_op jit(solution)/shard_map/cond/branch_1_fun/ppermute | solution.py:346
  47.4 7.9 %collective-permute-start.4 = (bf16[512,128]{1,0:T(8,128)(2,1)S(1)}, bf16[512,128]{1,0:T(8,128)(2,1)S(1)}, u32[]{:S(2)}, u32[]{:S(2)}) collective-permute-start(bf16[512,128]{1,0:T(8,128)(2,1)S(1)} %get-tuple-element.66), channel_id=1, source_target_pairs={{0,2},{1,3},{2,0},{3,1},{4,6},{5,7},{6,4},{7,5},{8,10},{9,11},{10,... | collective-permute-start | bytes 393224 | tf_op jit(solution)/shard_map/cond/branch_1_fun/ppermute | solution.py:346
  48.9 6.4 %collective-permute-start.5 = (bf16[512,128]{1,0:T(8,128)(2,1)S(1)}, bf16[512,128]{1,0:T(8,128)(2,1)S(1)}, u32[]{:S(2)}, u32[]{:S(2)}) collective-permute-start(bf16[512,128]{1,0:T(8,128)(2,1)S(1)} %get-tuple-element.67), channel_id=1, source_target_pairs={{0,3},{1,2},{2,1},{3,0},{4,7},{5,6},{6,5},{7,4},{8,11},{9,10},{10,... | collective-permute-start | bytes 393224 | tf_op jit(solution)/shard_map/cond/branch_1_fun/ppermute | solution.py:346
  53.4 5.8 %collective-permute-start.12 = (bf16[512,128]{1,0:T(8,128)(2,1)S(1)}, bf16[512,128]{1,0:T(8,128)(2,1)S(1)}, u32[]{:S(2)}, u32[]{:S(2)}) collective-permute-start(bf16[512,128]{1,0:T(8,128)(2,1)S(1)} %get-tuple-element.77), channel_id=1, source_target_pairs={{0,1},{1,0},{2,3},{3,2},{4,5},{5,4},{6,7},{7,6},{8,9},{9,8},{10,11... | collective-permute-start | bytes 393224 | tf_op jit(solution)/shard_map/cond/branch_1_fun/ppermute | solution.py:346
  53.4 7.2 %collective-permute-start.13 = (bf16[512,128]{1,0:T(8,128)(2,1)S(1)}, bf16[512,128]{1,0:T(8,128)(2,1)S(1)}, u32[]{:S(2)}, u32[]{:S(2)}) collective-permute-start(bf16[512,128]{1,0:T(8,128)(2,1)S(1)} %get-tuple-element.78), channel_id=1, source_target_pairs={{0,2},{1,3},{2,0},{3,1},{4,6},{5,7},{6,4},{7,5},{8,10},{9,11},{10,... | collective-permute-start | bytes 393224 | tf_op jit(solution)/shard_map/cond/branch_1_fun/ppermute | solution.py:346
  55.0 6.6 %collective-permute-start.14 = (bf16[512,128]{1,0:T(8,128)(2,1)S(1)}, bf16[512,128]{1,0:T(8,128)(2,1)S(1)}, u32[]{:S(2)}, u32[]{:S(2)}) collective-permute-start(bf16[512,128]{1,0:T(8,128)(2,1)S(1)} %get-tuple-element.79), channel_id=1, source_target_pairs={{0,3},{1,2},{2,1},{3,0},{4,7},{5,6},{6,5},{7,4},{8,11},{9,10},{10,... | collective-permute-start | bytes 393224 | tf_op jit(solution)/shard_map/cond/branch_1_fun/ppermute | solution.py:346
  57.1 8.3 %collective-permute-start.6 = (bf16[384,128]{1,0:T(8,128)(2,1)S(1)}, bf16[384,128]{1,0:T(8,128)(2,1)S(1)}, u32[]{:S(2)}, u32[]{:S(2)}) collective-permute-start(bf16[384,128]{1,0:T(8,128)(2,1)S(1)} %get-tuple-element.69), channel_id=1, source_target_pairs={{0,4},{1,5},{2,6},{3,7},{4,0},{5,1},{6,2},{7,3},{8,12},{9,13},{10,... | collective-permute-start | bytes 294920 | tf_op jit(solution)/shard_map/cond/branch_1_fun/ppermute | solution.py:346
  58.5 8.5 %collective-permute-start.7 = (bf16[384,128]{1,0:T(8,128)(2,1)S(1)}, bf16[384,128]{1,0:T(8,128)(2,1)S(1)}, u32[]{:S(2)}, u32[]{:S(2)}) collective-permute-start(bf16[384,128]{1,0:T(8,128)(2,1)S(1)} %get-tuple-element.70), channel_id=1, source_target_pairs={{0,8},{1,9},{2,10},{3,11},{4,12},{5,13},{6,14},{7,15},{8,0},{9,1},... | collective-permute-start | bytes 294920 | tf_op jit(solution)/shard_map/cond/branch_1_fun/ppermute | solution.py:346
  59.1 7.8 %collective-permute-start.8 = (bf16[384,128]{1,0:T(8,128)(2,1)S(1)}, bf16[384,128]{1,0:T(8,128)(2,1)S(1)}, u32[]{:S(2)}, u32[]{:S(2)}) collective-permute-start(bf16[384,128]{1,0:T(8,128)(2,1)S(1)} %get-tuple-element.71), channel_id=1, source_target_pairs={{0,12},{1,13},{2,14},{3,15},{4,8},{5,9},{6,10},{7,11},{8,4},{9,5},... | collective-permute-start | bytes 294920 | tf_op jit(solution)/shard_map/cond/branch_1_fun/ppermute | solution.py:346
  63.4 5.4 %collective-permute-start.15 = (bf16[384,128]{1,0:T(8,128)(2,1)S(1)}, bf16[384,128]{1,0:T(8,128)(2,1)S(1)}, u32[]{:S(2)}, u32[]{:S(2)}) collective-permute-start(bf16[384,128]{1,0:T(8,128)(2,1)S(1)} %get-tuple-element.81), channel_id=1, source_target_pairs={{0,4},{1,5},{2,6},{3,7},{4,0},{5,1},{6,2},{7,3},{8,12},{9,13},{10,... | collective-permute-start | bytes 294920 | tf_op jit(solution)/shard_map/cond/branch_1_fun/ppermute | solution.py:346
  64.8 5.7 %collective-permute-start.16 = (bf16[384,128]{1,0:T(8,128)(2,1)S(1)}, bf16[384,128]{1,0:T(8,128)(2,1)S(1)}, u32[]{:S(2)}, u32[]{:S(2)}) collective-permute-start(bf16[384,128]{1,0:T(8,128)(2,1)S(1)} %get-tuple-element.82), channel_id=1, source_target_pairs={{0,8},{1,9},{2,10},{3,11},{4,12},{5,13},{6,14},{7,15},{8,0},{9,1},... | collective-permute-start | bytes 294920 | tf_op jit(solution)/shard_map/cond/branch_1_fun/ppermute | solution.py:346
  65.4 6.7 %collective-permute-start.17 = (bf16[384,128]{1,0:T(8,128)(2,1)S(1)}, bf16[384,128]{1,0:T(8,128)(2,1)S(1)}, u32[]{:S(2)}, u32[]{:S(2)}) collective-permute-start(bf16[384,128]{1,0:T(8,128)(2,1)S(1)} %get-tuple-element.83), channel_id=1, source_target_pairs={{0,12},{1,13},{2,14},{3,15},{4,8},{5,9},{6,10},{7,11},{8,4},{9,5},... | collective-permute-start | bytes 294920 | tf_op jit(solution)/shard_map/cond/branch_1_fun/ppermute | solution.py:346
  73.1 6.6 %collective-permute-start.48 = (bf16[2,192,256]{2,1,0:T(8,128)(2,1)S(1)}, bf16[2,192,256]{2,1,0:T(8,128)(2,1)S(1)}, u32[]{:S(2)}, u32[]{:S(2)}) collective-permute-start(bf16[2,192,256]{2,1,0:T(8,128)(2,1)S(1)} %get-tuple-element.186), channel_id=1, source_target_pairs={{0,24},{1,25},{2,26},{3,27},{4,28},{5,29},{6,30},{7,31},{8,16},{9,... | collective-permute-start | bytes 589832 | tf_op jit(solution)/shard_map/ppermute | solution.py:346
  74.4 8.3 %collective-permute-start.49 = (bf16[2,192,256]{2,1,0:T(8,128)(2,1)S(1)}, bf16[2,192,256]{2,1,0:T(8,128)(2,1)S(1)}, u32[]{:S(2)}, u32[]{:S(2)}) collective-permute-start(bf16[2,192,256]{2,1,0:T(8,128)(2,1)S(1)} %get-tuple-element.187), channel_id=1, source_target_pairs={{0,24},{1,25},{2,26},{3,27},{4,28},{5,29},{6,30},{7,31},{8,16},{9,... | collective-permute-start | bytes 589832 | tf_op jit(solution)/shard_map/ppermute | solution.py:346
  75.7 3.9 %copy-start.5 = (bf16[2,256,1024]{2,1,0:T(8,128)(2,1)S(1)}, bf16[2,256,1024]{2,1,0:T(8,128)(2,1)}, u32[]{:S(2)}) copy-start(bf16[2,256,1024]{2,1,0:T(8,128)(2,1)} %w_rec.13) | copy-start | bytes 3145732
  82.8 58.3 %collective-permute-start.50 = (bf16[2,192,256]{2,1,0:T(8,128)(2,1)S(1)}, bf16[2,192,256]{2,1,0:T(8,128)(2,1)S(1)}, u32[]{:S(2)}, u32[]{:S(2)}) collective-permute-start(bf16[2,192,256]{2,1,0:T(8,128)(2,1)S(1)} %get-tuple-element.191), channel_id=1, source_target_pairs={{0,24},{1,25},{2,26},{3,27},{4,28},{5,29},{6,30},{7,31},{8,16},{9,... | collective-permute-start | bytes 589832 | tf_op jit(solution)/shard_map/ppermute | solution.py:346
  138.3 14.2 %collective-permute-start.54 = (bf16[2,192,256]{2,1,0:T(8,128)(2,1)S(1)}, bf16[2,192,256]{2,1,0:T(8,128)(2,1)S(1)}, u32[]{:S(2)}, u32[]{:S(2)}) collective-permute-start(bf16[2,192,256]{2,1,0:T(8,128)(2,1)S(1)} %get-tuple-element.199), channel_id=1, source_target_pairs={{0,24},{1,25},{2,26},{3,27},{4,28},{5,29},{6,30},{7,31},{8,16},{9,... | collective-permute-start | bytes 589832 | tf_op jit(solution)/shard_map/ppermute | solution.py:346
  141.1 11.4 %copy-start.10 = (bf16[4,192,256]{2,1,0:T(8,128)(2,1)S(1)}, bf16[4,192,256]{2,1,0:T(8,128)(2,1)}, u32[]{:S(2)}) copy-start(bf16[4,192,256]{2,1,0:T(8,128)(2,1)} %get-tuple-element.196.refs_0_) | copy-start | bytes 1179652
  142.2 13.4 %collective-permute-start.51 = (bf16[192,256]{1,0:T(8,128)(2,1)S(1)}, bf16[192,256]{1,0:T(8,128)(2,1)S(1)}, u32[]{:S(2)}, u32[]{:S(2)}) collective-permute-start(bf16[192,256]{1,0:T(8,128)(2,1)S(1)} %get-tuple-element.193), channel_id=1, source_target_pairs={{0,4},{1,5},{2,6},{3,7},{4,0},{5,1},{6,2},{7,3},{8,12},{9,13},{10,... | collective-permute-start | bytes 294920 | tf_op jit(solution)/shard_map/ppermute | solution.py:346
  142.9 15.0 %collective-permute-start.52 = (bf16[192,256]{1,0:T(8,128)(2,1)S(1)}, bf16[192,256]{1,0:T(8,128)(2,1)S(1)}, u32[]{:S(2)}, u32[]{:S(2)}) collective-permute-start(bf16[192,256]{1,0:T(8,128)(2,1)S(1)} %get-tuple-element.194), channel_id=1, source_target_pairs={{0,8},{1,9},{2,10},{3,11},{4,12},{5,13},{6,14},{7,15},{8,0},{9,1},... | collective-permute-start | bytes 294920 | tf_op jit(solution)/shard_map/ppermute | solution.py:346
  151.9 6.7 %collective-permute-start.53 = (bf16[192,256]{1,0:T(8,128)(2,1)S(1)}, bf16[192,256]{1,0:T(8,128)(2,1)S(1)}, u32[]{:S(2)}, u32[]{:S(2)}) collective-permute-start(bf16[192,256]{1,0:T(8,128)(2,1)S(1)} %get-tuple-element.195), channel_id=1, source_target_pairs={{0,12},{1,13},{2,14},{3,15},{4,8},{5,9},{6,10},{7,11},{8,4},{9,5},... | collective-permute-start | bytes 294920 | tf_op jit(solution)/shard_map/ppermute | solution.py:346
  152.5 6.8 %collective-permute-start.55 = (bf16[192,256]{1,0:T(8,128)(2,1)S(1)}, bf16[192,256]{1,0:T(8,128)(2,1)S(1)}, u32[]{:S(2)}, u32[]{:S(2)}) collective-permute-start(bf16[192,256]{1,0:T(8,128)(2,1)S(1)} %get-tuple-element.201), channel_id=1, source_target_pairs={{0,4},{1,5},{2,6},{3,7},{4,0},{5,1},{6,2},{7,3},{8,12},{9,13},{10,... | collective-permute-start | bytes 294920 | tf_op jit(solution)/shard_map/ppermute | solution.py:346
  153.5 5.8 %collective-permute-start.56 = (bf16[192,256]{1,0:T(8,128)(2,1)S(1)}, bf16[192,256]{1,0:T(8,128)(2,1)S(1)}, u32[]{:S(2)}, u32[]{:S(2)}) collective-permute-start(bf16[192,256]{1,0:T(8,128)(2,1)S(1)} %get-tuple-element.202), channel_id=1, source_target_pairs={{0,8},{1,9},{2,10},{3,11},{4,12},{5,13},{6,14},{7,15},{8,0},{9,1},... | collective-permute-start | bytes 294920 | tf_op jit(solution)/shard_map/ppermute | solution.py:346
  155.5 5.5 %collective-permute-start.57 = (bf16[192,256]{1,0:T(8,128)(2,1)S(1)}, bf16[192,256]{1,0:T(8,128)(2,1)S(1)}, u32[]{:S(2)}, u32[]{:S(2)}) collective-permute-start(bf16[192,256]{1,0:T(8,128)(2,1)S(1)} %get-tuple-element.203), channel_id=1, source_target_pairs={{0,12},{1,13},{2,14},{3,15},{4,8},{5,9},{6,10},{7,11},{8,4},{9,5},... | collective-permute-start | bytes 294920 | tf_op jit(solution)/shard_map/ppermute | solution.py:346

commit v2 on v1

--- a/solution.py
+++ b/solution.py
@@ -9,7 +9,7 @@
 HBM = pl.BlockSpec(memory_space=pltpu.HBM)
 VMEM = pl.BlockSpec(memory_space=pltpu.VMEM)
 PARAMS = pltpu.CompilerParams(vmem_limit_bytes=16 * 2**20)
-UNROLL = 32
+BATCH = 8
 LANES = 128
 CHUNKS = 2
 AXES = ("tm", "slab")
@@ -101,21 +101,29 @@
     group_rows = row_count // group
 
     tables = (tile_rows, tile_sources, tile_counts)
-    unroll = min(UNROLL, tile_values.shape[1])
+
+    slots = tile_values.shape[1]
 
     def kernel(*refs):
-        values = refs[3]
         pieces = refs[4 : 4 + slab_count]
         outs = refs[4 + slab_count : 4 + slab_count + group]
-        rows, sources, counts, sems, inputs, total = refs[4 + slab_count + group :]
+        rows, sources, counts, values, sems, inputs, total = refs[4 + slab_count + group :]
         slab = lax.axis_index("slab")
         _, _, lead = seat(group)
         fetches = [
             pltpu.make_async_copy(refs[n], local_ref, sems.at[n])
             for n, local_ref in enumerate((rows, sources, counts))
         ]
-        for fetch in fetches:
-            fetch.start()
+        batches = [
+            pltpu.make_async_copy(
+                refs[3].at[0, pl.ds(slot, BATCH)],
+                values.at[pl.ds(slot, BATCH)],
+                sems.at[3 + slot // BATCH],
+            )
+            for slot in range(0, slots, BATCH)
+        ]
+        for copy in fetches + batches:
+            copy.start()
         for k in range(slab_count):
             start = pl.multiple_of((slab ^ k) * piece, piece)
             inputs[pl.ds(start, piece), :] = pieces[k][...]
@@ -123,24 +131,20 @@
         for fetch in fetches:
             fetch.wait()
         count = counts[0, 0]
-
-        def step(index, carry):
-            products = []
-            for lane in range(unroll):
-                slot = index * unroll + lane
-                start = pl.multiple_of(sources[0, slot] * tile, tile)
-                product = jnp.dot(
-                    values[0, slot],
-                    inputs[pl.ds(start, tile), :],
-                    preferred_element_type=jnp.float32,
-                )
-                products.append(jnp.where(slot < count, product, 0.0))
-            for lane in range(unroll):
-                target = pl.multiple_of(rows[0, index * unroll + lane] * tile, tile)
-                total[pl.ds(target, tile), :] += products[lane]
-            return carry
-
-        lax.fori_loop(0, (count + unroll - 1) // unroll, step, 0)
+        products = []
+        for slot in range(slots):
+            if slot % BATCH == 0:
+                batches[slot // BATCH].wait()
+            start = pl.multiple_of(sources[0, slot] * tile, tile)
+            product = jnp.dot(
+                values[slot],
+                inputs[pl.ds(start, tile), :],
+                preferred_element_type=jnp.float32,
+            )
+            products.append(jnp.where(slot < count, product, 0.0))
+        for slot in range(slots):
+            target = pl.multiple_of(rows[0, slot] * tile, tile)
+            total[pl.ds(target, tile), :] += products[slot]
         for k in range(group):
             start = pl.multiple_of((lead ^ k) * group_rows, group_rows)
             outs[k][...] = total[pl.ds(start, group_rows), :].astype(outs[k].dtype)
@@ -148,12 +152,13 @@
     dtype = arrived[0].dtype
     return pl.pallas_call(
         kernel,
-        in_specs=[HBM, HBM, HBM, VMEM] + [VMEM] * slab_count,
+        in_specs=[HBM] * 4 + [VMEM] * slab_count,
         out_specs=[VMEM] * group,
         out_shape=[jax.ShapeDtypeStruct((group_rows, width), dtype)] * group,
         scratch_shapes=[pltpu.SMEM(table.shape, table.dtype) for table in tables]
         + [
-            pltpu.SemaphoreType.DMA((3,)),
+            pltpu.VMEM(tile_values.shape[1:], tile_values.dtype),
+            pltpu.SemaphoreType.DMA((3 + slots // BATCH,)),
             pltpu.VMEM((slab_count * piece, width), dtype),
             pltpu.VMEM((row_count, width), jnp.float32),
         ],
@@ -221,31 +226,94 @@
     return [results[n : n + group] for n in range(0, count, group)]
 
 
-def recur(mixed, layer, w_input, w_hidden, bias, mode, state=None, done=(), keep=(), lanes=0):
+def project(mixed, layer, w_input, w_hidden, bias, mode, after):
+    group, size, _ = mixed[0].shape
+    gates = w_input.shape[2]
+    count = len(mixed)
+
+    def kernel(w_in, w_rec, gate_bias, *refs):
+        outs = refs[count + 1 :]
+        half, _, _ = seat(group)
+
+        @only(mode, half)
+        def _():
+            outs[count][...] = w_rec[layer]
+            for n in range(count):
+                for time in range(group):
+                    part = jnp.dot(
+                        refs[n][time], w_in[layer], preferred_element_type=jnp.float32
+                    )
+                    outs[n][time] = part + gate_bias[layer : layer + 1, :]
+
+    results = pl.pallas_call(
+        kernel,
+        in_specs=[VMEM] * (4 + count),
+        out_specs=[VMEM] * (count + 1),
+        out_shape=[jax.ShapeDtypeStruct((group, size, gates), jnp.float32)] * count
+        + [jax.ShapeDtypeStruct(w_hidden.shape[1:], w_hidden.dtype)],
+        compiler_params=PARAMS,
+        name="project",
+    )(w_input, w_hidden, bias, *mixed, after)
+    return results[:count], results[count]
+
+
+def recur_projected(projected, weights, state, mode):
+    group, size, gates = projected.shape
+    units = gates // 4
+
+    def kernel(inputs, w_rec, start, states, memory):
+        half, _, _ = seat(group)
+
+        @only(mode, half)
+        def _():
+            memory[...] = start[1].astype(jnp.float32)
+            hidden = start[0]
+            for time in range(group):
+                gate = inputs[time] + jnp.dot(
+                    hidden, w_rec[...], preferred_element_type=jnp.float32
+                )
+                i, f, g, o = (gate[:, n * units : (n + 1) * units] for n in range(4))
+                new = sigmoid(f) * memory[...] + sigmoid(i) * jnp.tanh(g)
+                memory[...] = new
+                states[time] = (sigmoid(o) * jnp.tanh(new)).astype(states.dtype)
+                hidden = states[time]
+
+    return pl.pallas_call(
+        kernel,
+        in_specs=[VMEM] * 3,
+        out_specs=VMEM,
+        out_shape=jax.ShapeDtypeStruct((group, size, units), state.dtype),
+        scratch_shapes=[pltpu.VMEM((size, units), jnp.float32)],
+        compiler_params=PARAMS,
+        name="recur",
+    )(projected, weights, state)
+
+
+def recur(mixed, layer, w_input, w_hidden, bias, mode, state=None, keep=None, lanes=0):
     group, size, _ = mixed.shape
     units = w_hidden.shape[1]
     first = state is None
-    operands = [mixed] + list(done) + list(keep) + ([] if first else [state])
+    operands = [mixed] + ([] if keep is None else [keep]) + ([] if first else [state])
     outputs = units // lanes * group if lanes else 1
 
-    def kernel(w_in, w_rec, gate_bias, *refs):
+    def kernel(w_in, w_rec_hbm, gate_bias, *refs):
         inputs = refs[0]
-        earlier = refs[1 : 1 + len(done)]
-        kept = refs[1 + len(done) : 1 + len(done) + len(keep)]
         start = refs[len(operands) - 1]
         outs = refs[len(operands) : len(operands) + outputs]
-        memory = refs[-1]
-        states = refs[-2] if lanes else outs[0]
+        w_rec, sem, memory = refs[-3:]
+        states = refs[-4] if lanes else outs[0]
         half, place, _ = seat(group)
 
-        if keep:
+        if keep is not None:
 
             @pl.when(half != mode)
             def _():
-                spread_into(outs, kept, place, group)
+                spread_into(outs, refs[1:2], place, group)
 
         @only(mode, half)
         def _():
+            fetch = pltpu.make_async_copy(w_rec_hbm.at[layer], w_rec, sem)
+            fetch.start()
             line = gate_bias[layer : layer + 1, :]
 
             def advance(gates, old, time):
@@ -256,47 +324,52 @@
                 memory[...] = new
                 states[time] = (sigmoid(o) * jnp.tanh(new)).astype(states.dtype)
 
-            def project(time):
-                return jnp.dot(inputs[time], w_in[layer], preferred_element_type=jnp.float32) + line
-
-            def step(time, hidden):
-                gates = project(time) + jnp.dot(
-                    hidden, w_rec[layer], preferred_element_type=jnp.float32
-                )
-                advance(gates, memory[...], time)
-
-            if first:
-                advance(project(0), None, 0)
-            else:
+            hidden = None if first else start[0]
+            if not first:
                 memory[...] = start[1].astype(jnp.float32)
-                step(0, start[0])
-
-            def loop(time, carry):
-                step(time, states[time - 1])
-                return carry
-
-            lax.fori_loop(1, group, loop, 0, unroll=True)
+            for time in range(group):
+                gates = jnp.dot(inputs[time], w_in[layer], preferred_element_type=jnp.float32)
+                gates = gates + line
+                if time == (1 if first else 0):
+                    fetch.wait()
+                if hidden is not None:
+                    gates = gates + jnp.dot(
+                        hidden, w_rec[...], preferred_element_type=jnp.float32
+                    )
+                advance(gates, None if hidden is None else memory[...], time)
+                hidden = states[time]
+            if group == 1 and first:
+                fetch.wait()
             if lanes:
-                spread_into(outs, [*earlier, states], place, group)
+                spread_into(outs, [states], place, group)
             if first:
                 last = refs[len(operands) + outputs]
                 last[0] = states[group - 1]
                 last[1] = memory[...].astype(last.dtype)
 
+        if first:
+            side = refs[len(operands) + outputs + 1]
+            side[...] = jnp.full(side.shape, half, side.dtype)
+
     dtype = mixed.dtype
     if lanes:
-        out_shape = [jax.ShapeDtypeStruct((size * (1 + len(done)), lanes), dtype)] * outputs
+        out_shape = [jax.ShapeDtypeStruct((size, lanes), dtype)] * outputs
     else:
         out_shape = [jax.ShapeDtypeStruct((group, size, units), dtype)]
     if first:
         out_shape.append(jax.ShapeDtypeStruct((2, size, units), dtype))
-    scratch = [pltpu.VMEM((group, size, units), dtype)] if lanes else []
+        out_shape.append(jax.ShapeDtypeStruct((8, LANES), jnp.int32))
     results = pl.pallas_call(
         kernel,
-        in_specs=[VMEM] * (3 + len(operands)),
+        in_specs=[VMEM, HBM, VMEM] + [VMEM] * len(operands),
         out_specs=[VMEM] * len(out_shape),
         out_shape=out_shape,
-        scratch_shapes=scratch + [pltpu.VMEM((size, units), jnp.float32)],
+        scratch_shapes=([pltpu.VMEM((group, size, units), dtype)] if lanes else [])
+        + [
+            pltpu.VMEM(w_hidden.shape[1:], w_hidden.dtype),
+            pltpu.SemaphoreType.DMA(()),
+            pltpu.VMEM((size, units), jnp.float32),
+        ],
         compiler_params=PARAMS,
         name="recur",
     )(w_input, w_hidden, bias, *operands)
@@ -373,7 +446,6 @@
     slab_count = lax.axis_size("slab")
     layers = w_input.shape[0]
     group = lax.axis_size("tm") // 2
-    half = lax.axis_index("tm") // group
 
     def pick(parts, table, column=0, carried=()):
         return pick_tiles(parts, table, slab_count, row_count, tile, group, column, carried)
@@ -395,46 +467,40 @@
     def run_lower(mixed, layer):
         chunks, handed = [], []
         for part in mixed:
-            states, last = run(part, layer, LOWER)
+            states, last, side = run(part, layer, LOWER)
             handed.append(hand_over(last, group))
             chunks.append(states)
-        return chunks, handed
-
-    def run_upper(mixed, layer, states):
-        return [run(part, layer, UPPER, state) for part, state in zip(mixed[:-1], states)]
+        return chunks, handed, side[0, 0]
 
     features = features[0]
     columns = features.shape[1] // LANES
     listed = [pick([features], ref_lists, column)[0] for column in range(columns - 1)]
     last, (table, gate_bias) = pick([features], ref_lists, columns - 1, (ref_lists, bias))
     upper_mixed = pack([mix(column) for column in [*listed, last]])
-    hidden, handed = run_lower(upper_mixed, 0)
+    hidden, handed, half = run_lower(upper_mixed, 0)
     for layer in range(1, layers):
 
         def lower_layer(hidden):
-            return back_and_mix(spread(hidden, LANES)), half + 1
-
-        def upper_layer(mixed, done, state):
-            return back_and_mix(run(mixed[-1], layer - 1, BOTH, state, done, (), LANES))
-
-        lower_mixed, turn = lax.cond(
-            half == LOWER, lower_layer, lambda hidden: (hidden, half), hidden
+            return back_and_mix(spread(hidden, LANES))
+
+        def upper_layer(states):
+            return back_and_mix(spread(states, LANES))
+
+        lower_mixed = lax.cond(half == LOWER, lower_layer, lambda hidden: hidden, hidden)
+        hidden, following, half = run_lower(lower_mixed, layer)
+        projected, recurrent = project(
+            upper_mixed, layer - 1, w_input, w_hidden, gate_bias, UPPER, hidden[-1]
         )
-        hidden, following = run_lower(lower_mixed, layer)
-        done = run_upper(upper_mixed, layer - 1, handed)
-        upper_mixed = lax.cond(
-            half == turn,
-            upper_layer,
-            lambda mixed, done, state: mixed,
-            upper_mixed,
-            done,
-            handed[-1],
-        )
+        states = [
+            recur_projected(part, recurrent, state, UPPER)
+            for part, state in zip(projected, handed)
+        ]
+        upper_mixed = lax.cond(half == UPPER, upper_layer, lambda states: states, states)
         handed = following
     units = w_hidden.shape[1]
     parts = []
     for number, (part, state) in enumerate(zip(upper_mixed, handed)):
-        (states,) = run(part, layers - 1, UPPER, state, (), hidden[number : number + 1], units)
+        (states,) = run(part, layers - 1, UPPER, state, hidden[number], units)
         parts.append(swap_times(states))
     return assemble(parts)
 

time: 164 us -> 166 us (1.012)
  waiting for transfers between devices: 29.8 us -> 28 us
    pallas_call x11 -> x13, Pallas kernels: 18.1 us -> 20.1 us  [the longest x6 9.45 us: recur(): pl.pallas_call(kernel, in_specs=[VMEM, HBM, VMEM] + [VMEM] * len(operands...]
    ppermute x40, waiting for transfers between devices: 29.8 us -> 28 us  [send(): return lax.ppermute(array, AXES, pairs)]
  transfers between devices with their start and end apart: 40 -> 40, of which waited for: 20 -> 16; matrix products, arithmetic and copies ran while one was open for 0% -> 0% of each run, Pallas kernels for 10% -> 11%
where the time goes in v2:
time: 166 us; the launch traced here: 164 us
  starting transfers between devices  103 us (62%)
  waiting for transfers between devices  28 us (17%)
  Pallas kernels  26.9 us (16%)
  local copies, waits for them, and re-layouts  3.79 us (2%)
  between operations  2.34 us (1%)
    ppermute x40, starting transfers between devices, send(): return lax.ppermute(array, AXES, pairs)  103 us
    ppermute x40, waiting for transfers between devices, send(): return lax.ppermute(array, AXES, pairs)  28 us
    pallas_call x6, Pallas kernels, recur(): pl.pallas_call(kernel, in_specs=[VMEM, HBM, VMEM] + [VMEM] * len(operands...  9.45 us
    pallas_call x4, Pallas kernels, convolve(): pl.pallas_call(kernel, in_specs=[HBM] * 4 + [VMEM] * slab_count, out_spec...  9.14 us
  transfers between devices with their start and end apart: 40, of which 16 were waited for; matrix products, arithmetic and copies ran while one was open for 0% of the time, Pallas kernels for 11%

profile of v2, /device:TPU:0, one launch (start us, length us, event | category | flops | bytes accessed | tf_op | source)
XLA Modules:
  0.0 164.3 jit_solution(11839341290870510551)
XLA Ops:
  0.0 1.3 copy-done.2
  1.3 0.7 copy-done.3
  2.0 0.9 pick_tiles.11
  3.4 2.6 %collective-permute-start.37 = (bf16[512,128]{1,0:T(8,128)(2,1)S(1)}, bf16[512,128]{1,0:T(8,128)(2,1)S(1)}, u32[]{:S(2)}, u32[]{:S(2)}) collective-permute-start(bf16[512,128]{1,0:T(8,128)(2,1)S(1)} %get-tuple-element.151), channel_id=1, source_target_pairs={{0,2},{1,3},{2,0},{3,1},{4,6},{5,7},{6,4},{7,5},{8,10},{9,11},{10,... | collective-permute-start | bytes 393224 | tf_op jit(solution)/shard_map/ppermute | solution.py:419
  6.0 0.7 copy-done.4
  6.7 0.9 pick_tiles.10
  7.8 1.9 %collective-permute-start.43 = (bf16[512,128]{1,0:T(8,128)(2,1)S(1)}, bf16[512,128]{1,0:T(8,128)(2,1)S(1)}, u32[]{:S(2)}, u32[]{:S(2)}) collective-permute-start(bf16[512,128]{1,0:T(8,128)(2,1)S(1)} %get-tuple-element.159), channel_id=1, source_target_pairs={{0,2},{1,3},{2,0},{3,1},{4,6},{5,7},{6,4},{7,5},{8,10},{9,11},{10,... | collective-permute-start | bytes 393224 | tf_op jit(solution)/shard_map/ppermute | solution.py:419
  10.5 2.2 %collective-permute-done.38.refs_7_ = bf16[512,128]{1,0:T(8,128)(2,1)S(1)} collective-permute-done((bf16[512,128]{1,0:T(8,128)(2,1)S(1)}, bf16[512,128]{1,0:T(8,128)(2,1)S(1)}, u32[]{:S(2)}, u32[]{:S(2)}) %collective-permute-start.38) | collective-permute-done | bytes 131104 | tf_op jit(solution)/shard_map/ppermute | solution.py:419
  12.7 2.1 %convolve.10 = (bf16[384,128]{1,0:T(8,128)(2,1)S(1)}, bf16[384,128]{1,0:T(8,128)(2,1)S(1)}, bf16[384,128]{1,0:T(8,128)(2,1)S(1)}, bf16[384,128]{1,0:T(8,128)(2,1)S(1)}) custom-call(s32[1,32]{1,0:T(1,128)} %refs_0_.3, s32[1,32]{1,0:T(1,128)} %refs_1_.5, s32[1,1]{1,0:T(1,128)S(6)} %copy.18.refs_2_, bf16[1,32,128,128]{3,2,1,0:T(8,128)(2,1)} %refs_3_.3, ...), custom_call_target="tpu_custom_call" | custom-call | tf_op jit(solution)/shard_map/convolve/pallas_call | solution.py:153
  14.8 1.6 collective-permute-start.39
  16.3 1.6 collective-permute-start.40
  18.3 2.1 %convolve.11 = (bf16[384,128]{1,0:T(8,128)(2,1)S(1)}, bf16[384,128]{1,0:T(8,128)(2,1)S(1)}, bf16[384,128]{1,0:T(8,128)(2,1)S(1)}, bf16[384,128]{1,0:T(8,128)(2,1)S(1)}) custom-call(s32[1,32]{1,0:T(1,128)} %refs_0_.3, s32[1,32]{1,0:T(1,128)} %refs_1_.5, s32[1,1]{1,0:T(1,128)S(6)} %copy.18.refs_2_, bf16[1,32,128,128]{3,2,1,0:T(8,128)(2,1)} %refs_3_.3, ...), custom_call_target="tpu_custom_call" | custom-call | tf_op jit(solution)/shard_map/convolve/pallas_call | solution.py:153
  20.4 1.6 collective-permute-start.45
  22.0 1.6 collective-permute-start.46
  24.0 1.9 %collective-permute-done.45.refs_5_ = bf16[384,128]{1,0:T(8,128)(2,1)S(1)} collective-permute-done((bf16[384,128]{1,0:T(8,128)(2,1)S(1)}, bf16[384,128]{1,0:T(8,128)(2,1)S(1)}, u32[]{:S(2)}, u32[]{:S(2)}) %collective-permute-start.45) | collective-permute-done | bytes 98336 | tf_op jit(solution)/shard_map/ppermute | solution.py:419
  25.9 1.8 %collective-permute-done.46.refs_6_ = bf16[384,128]{1,0:T(8,128)(2,1)S(1)} collective-permute-done((bf16[384,128]{1,0:T(8,128)(2,1)S(1)}, bf16[384,128]{1,0:T(8,128)(2,1)S(1)}, u32[]{:S(2)}, u32[]{:S(2)}) %collective-permute-start.46) | collective-permute-done | bytes 98336 | tf_op jit(solution)/shard_map/ppermute | solution.py:419
  27.7 1.5 collective-permute-done.47.refs_7_
  29.3 2.1 %recur.8 = (bf16[4,192,256]{2,1,0:T(8,128)(2,1)}, bf16[2,192,256]{2,1,0:T(8,128)(2,1)}, s32[8,128]{1,0:T(8,128)S(1)}) custom-call(bf16[2,256,1024]{2,1,0:T(8,128)(2,1)S(1)} %copy-done, bf16[2,256,1024]{2,1,0:T(8,128)(2,1)S(1)} %copy-done.1, f32[2,1024]{1,0:T(2,128)S(1)} %get-tuple-element.148.gate_bias, ...), custom_call_target="tpu_custom_call" | custom-call | tf_op jit(solution)/shard_map/recur/pallas_call | solution.py:362
  32.6 2.1 %recur.9 = (bf16[4,192,256]{2,1,0:T(8,128)(2,1)}, bf16[2,192,256]{2,1,0:T(8,128)(2,1)}, s32[8,128]{1,0:T(8,128)}) custom-call(bf16[2,256,1024]{2,1,0:T(8,128)(2,1)S(1)} %copy-done, bf16[2,256,1024]{2,1,0:T(8,128)(2,1)S(1)} %copy-done.1, f32[2,1024]{1,0:T(2,128)S(1)} %get-tuple-element.148.gate_bias, bf16[4,192,256]{2,1,0:T(8,128)(2,1)S(1)} %get-tuple-element.167.refs_0_), custom_call_target="tpu_custom_call" | custom-call | tf_op jit(solution)/shard_map/recur/pallas_call | solution.py:362
  34.7 39.1 %conditional.2 = ((bf16[4,192,256]{2,1,0:T(8,128)(2,1)}, bf16[4,192,256]{2,1,0:T(8,128)(2,1)})) conditional(s32[]{:T(128)} %bitcast.1, (bf16[4,192,256]{2,1,0:T(8,128)(2,1)}, bf16[4,192,256]{2,1,0:T(8,128)(2,1)}) %tuple.17, (bf16[4,192,256]{2,1,0:T(8,128)(2,1)}, bf16[4,192,256]{2,1,0:T(8,128)(2,1)}, s32[1,4,16]{2,1,0:T(4,128)S(1)}, ...), branch_computations={%region_0.0_spmd, %region_1.0_spmd} | conditional | bytes 12059380 | solution.py:489
  34.8 1.3 spread.2
  36.1 1.4 collective-permute-start
  37.5 1.6 collective-permute-start.1
  39.7 1.4 collective-permute-start.9
  41.0 1.6 collective-permute-done.1.refs_2_
  42.6 2.0 %collective-permute-done.2.refs_3_ = bf16[384,128]{1,0:T(8,128)(2,1)S(1)} collective-permute-done((bf16[384,128]{1,0:T(8,128)(2,1)S(1)}, bf16[384,128]{1,0:T(8,128)(2,1)S(1)}, u32[]{:S(2)}, u32[]{:S(2)}) %collective-permute-start.2) | collective-permute-done | bytes 98336 | tf_op jit(solution)/shard_map/cond/branch_1_fun/ppermute | solution.py:419
  44.6 0.8 pick_tiles.6
  45.5 0.6 collective-permute-start.10
  46.1 1.5 collective-permute-start.11
  47.6 1.6 collective-permute-start.4
  49.2 2.0 %collective-permute-done.10.refs_2_ = bf16[384,128]{1,0:T(8,128)(2,1)S(1)} collective-permute-done((bf16[384,128]{1,0:T(8,128)(2,1)S(1)}, bf16[384,128]{1,0:T(8,128)(2,1)S(1)}, u32[]{:S(2)}, u32[]{:S(2)}) %collective-permute-start.10) | collective-permute-done | bytes 98336 | tf_op jit(solution)/shard_map/cond/branch_1_fun/ppermute | solution.py:419
  51.2 1.6 collective-permute-done.11.refs_3_
  52.8 0.8 pick_tiles.7
  53.7 1.6 collective-permute-start.13
  55.5 2.7 %convolve.6 = (bf16[384,128]{1,0:T(8,128)(2,1)S(1)}, bf16[384,128]{1,0:T(8,128)(2,1)S(1)}, bf16[384,128]{1,0:T(8,128)(2,1)S(1)}, bf16[384,128]{1,0:T(8,128)(2,1)S(1)}) custom-call(s32[1,32]{1,0:T(1,128)S(1)} %get-tuple-element.41.refs_0_, s32[1,32]{1,0:T(1,128)S(1)} %get-tuple-element.42.refs_1_, s32[1,1]{1,0:T(1,128)} %get-tuple-element.43.refs_2_, ...), custom_call_target="tpu_custom_call" | custom-call | tf_op jit(solution)/shard_map/cond/branch_1_fun/convolve/pallas_call | solution.py:153
  58.3 1.5 collective-permute-start.6
  60.3 1.5 collective-permute-start.8
  61.9 2.3 %convolve.7 = (bf16[384,128]{1,0:T(8,128)(2,1)S(1)}, bf16[384,128]{1,0:T(8,128)(2,1)S(1)}, bf16[384,128]{1,0:T(8,128)(2,1)S(1)}, bf16[384,128]{1,0:T(8,128)(2,1)S(1)}) custom-call(s32[1,32]{1,0:T(1,128)S(1)} %get-tuple-element.41.refs_0_, s32[1,32]{1,0:T(1,128)S(1)} %get-tuple-element.42.refs_1_, s32[1,1]{1,0:T(1,128)} %get-tuple-element.43.refs_2_, ...), custom_call_target="tpu_custom_call" | custom-call | tf_op jit(solution)/shard_map/cond/branch_1_fun/convolve/pallas_call | solution.py:153
  64.1 1.5 collective-permute-start.15
  66.2 1.5 collective-permute-start.17
  67.7 1.9 %collective-permute-done.15.refs_5_ = bf16[384,128]{1,0:T(8,128)(2,1)S(1)} collective-permute-done((bf16[384,128]{1,0:T(8,128)(2,1)S(1)}, bf16[384,128]{1,0:T(8,128)(2,1)S(1)}, u32[]{:S(2)}, u32[]{:S(2)}) %collective-permute-start.15) | collective-permute-done | bytes 98336 | tf_op jit(solution)/shard_map/cond/branch_1_fun/ppermute | solution.py:419
  69.6 1.7 %collective-permute-done.16.refs_6_ = bf16[384,128]{1,0:T(8,128)(2,1)S(1)} collective-permute-done((bf16[384,128]{1,0:T(8,128)(2,1)S(1)}, bf16[384,128]{1,0:T(8,128)(2,1)S(1)}, u32[]{:S(2)}, u32[]{:S(2)}) %collective-permute-start.16) | collective-permute-done | bytes 98336 | tf_op jit(solution)/shard_map/cond/branch_1_fun/ppermute | solution.py:419
  71.3 1.6 collective-permute-done.17.refs_7_
  72.8 1.0 pack.3
  73.9 1.4 collective-permute-start.48
  75.3 1.3 collective-permute-start.49
  76.6 2.2 %recur.10 = (bf16[4,192,256]{2,1,0:T(8,128)(2,1)S(1)}, bf16[2,192,256]{2,1,0:T(8,128)(2,1)S(1)}, s32[8,128]{1,0:T(8,128)S(1)}) custom-call(bf16[2,256,1024]{2,1,0:T(8,128)(2,1)S(1)} %copy-done, bf16[2,256,1024]{2,1,0:T(8,128)(2,1)S(1)} %copy-done.1, f32[2,1024]{1,0:T(2,128)S(1)} %get-tuple-element.148.gate_bias, bf16[4,192,256]{2,1,0:T(8,128)(2,1)} %get-tuple-element.171.refs_0_), custom_call_target="tpu_custom_call" | custom-call | tf_op jit(solution)/shard_map/recur/pallas_call | solution.py:362
  80.0 2.0 %recur.13 = (bf16[4,192,256]{2,1,0:T(8,128)(2,1)S(1)}, bf16[2,192,256]{2,1,0:T(8,128)(2,1)S(1)}, s32[8,128]{1,0:T(8,128)}) custom-call(bf16[2,256,1024]{2,1,0:T(8,128)(2,1)S(1)} %copy-done, bf16[2,256,1024]{2,1,0:T(8,128)(2,1)S(1)} %copy-done.1, f32[2,1024]{1,0:T(2,128)S(1)} %get-tuple-element.148.gate_bias, bf16[4,192,256]{2,1,0:T(8,128)(2,1)S(1)} %copy-done.8), custom_call_target="tpu_custom_call" | custom-call | tf_op jit(solution)/shard_map/recur/pallas_call | solution.py:362
  82.1 0.8 recur.11
  82.9 1.1 collective-permute-done.49.start
  84.0 0.7 recur.12
  84.7 53.8 %collective-permute-start.50 = (bf16[2,192,256]{2,1,0:T(8,128)(2,1)S(1)}, bf16[2,192,256]{2,1,0:T(8,128)(2,1)S(1)}, u32[]{:S(2)}, u32[]{:S(2)}) collective-permute-start(bf16[2,192,256]{2,1,0:T(8,128)(2,1)S(1)} %get-tuple-element.182), channel_id=1, source_target_pairs={{0,24},{1,25},{2,26},{3,27},{4,28},{5,29},{6,30},{7,31},{8,16},{9,... | collective-permute-start | bytes 589832 | tf_op jit(solution)/shard_map/ppermute | solution.py:419
  138.5 1.3 collective-permute-start.54
  139.8 4.0 %collective-permute-done.50.refs_2_ = bf16[2,192,256]{2,1,0:T(8,128)(2,1)S(1)} collective-permute-done((bf16[2,192,256]{2,1,0:T(8,128)(2,1)S(1)}, bf16[2,192,256]{2,1,0:T(8,128)(2,1)S(1)}, u32[]{:S(2)}, u32[]{:S(2)}) %collective-permute-start.50) | collective-permute-done | bytes 196640 | tf_op jit(solution)/shard_map/ppermute | solution.py:419
  143.8 1.0 recur.14
  144.8 0.7 collective-permute-start.51
  145.5 8.5 %collective-permute-start.52 = (bf16[192,256]{1,0:T(8,128)(2,1)S(1)}, bf16[192,256]{1,0:T(8,128)(2,1)S(1)}, u32[]{:S(2)}, u32[]{:S(2)}) collective-permute-start(bf16[192,256]{1,0:T(8,128)(2,1)S(1)} %get-tuple-element.185), channel_id=1, source_target_pairs={{0,8},{1,9},{2,10},{3,11},{4,12},{5,13},{6,14},{7,15},{8,0},{9,1},... | collective-permute-start | bytes 294920 | tf_op jit(solution)/shard_map/ppermute | solution.py:419
  154.7 1.0 collective-permute-start.55
  155.7 2.0 %collective-permute-start.56 = (bf16[192,256]{1,0:T(8,128)(2,1)S(1)}, bf16[192,256]{1,0:T(8,128)(2,1)S(1)}, u32[]{:S(2)}, u32[]{:S(2)}) collective-permute-start(bf16[192,256]{1,0:T(8,128)(2,1)S(1)} %get-tuple-element.191), channel_id=1, source_target_pairs={{0,8},{1,9},{2,10},{3,11},{4,12},{5,13},{6,14},{7,15},{8,0},{9,1},... | collective-permute-start | bytes 294920 | tf_op jit(solution)/shard_map/ppermute | solution.py:419
  157.7 2.4 %collective-permute-start.57 = (bf16[192,256]{1,0:T(8,128)(2,1)S(1)}, bf16[192,256]{1,0:T(8,128)(2,1)S(1)}, u32[]{:S(2)}, u32[]{:S(2)}) collective-permute-start(bf16[192,256]{1,0:T(8,128)(2,1)S(1)} %get-tuple-element.192), channel_id=1, source_target_pairs={{0,12},{1,13},{2,14},{3,15},{4,8},{5,9},{6,10},{7,11},{8,4},{9,5},... | collective-permute-start | bytes 294920 | tf_op jit(solution)/shard_map/ppermute | solution.py:419
  160.1 0.7 collective-permute-done.53.refs_3_
  160.8 0.7 collective-permute-done.55.refs_5_
  161.5 1.7 %collective-permute-done.57.refs_7_ = bf16[192,256]{1,0:T(8,128)(2,1)S(1)} collective-permute-done((bf16[192,256]{1,0:T(8,128)(2,1)S(1)}, bf16[192,256]{1,0:T(8,128)(2,1)S(1)}, u32[]{:S(2)}, u32[]{:S(2)}) %collective-permute-start.57) | collective-permute-done | bytes 98336 | tf_op jit(solution)/shard_map/ppermute | solution.py:419
  163.2 0.9 assemble.1
  (61 shorter events, 5.6 us)
Async XLA Ops:
  0.0 29.3 %copy-start = (bf16[2,256,1024]{2,1,0:T(8,128)(2,1)S(1)}, bf16[2,256,1024]{2,1,0:T(8,128)(2,1)}, u32[]{:S(2)}) copy-start(bf16[2,256,1024]{2,1,0:T(8,128)(2,1)} %w_in.13) | copy-start | bytes 3145732
  0.0 29.3 %copy-start.1 = (bf16[2,256,1024]{2,1,0:T(8,128)(2,1)S(1)}, bf16[2,256,1024]{2,1,0:T(8,128)(2,1)}, u32[]{:S(2)}) copy-start(bf16[2,256,1024]{2,1,0:T(8,128)(2,1)} %w_rec_hbm.11) | copy-start | bytes 3145732
  0.0 1.3 copy-start.2
  1.3 0.7 copy-start.3
  2.9 6.9 %collective-permute-start.36 = (bf16[512,128]{1,0:T(8,128)(2,1)S(1)}, bf16[512,128]{1,0:T(8,128)(2,1)S(1)}, u32[]{:S(2)}, u32[]{:S(2)}) collective-permute-start(bf16[512,128]{1,0:T(8,128)(2,1)S(1)} %get-tuple-element.150), channel_id=1, source_target_pairs={{0,1},{1,0},{2,3},{3,2},{4,5},{5,4},{6,7},{7,6},{8,9},{9,8},{10,11... | collective-permute-start | bytes 393224 | tf_op jit(solution)/shard_map/ppermute | solution.py:419
  3.4 7.0 %collective-permute-start.37 = (bf16[512,128]{1,0:T(8,128)(2,1)S(1)}, bf16[512,128]{1,0:T(8,128)(2,1)S(1)}, u32[]{:S(2)}, u32[]{:S(2)}) collective-permute-start(bf16[512,128]{1,0:T(8,128)(2,1)S(1)} %get-tuple-element.151), channel_id=1, source_target_pairs={{0,2},{1,3},{2,0},{3,1},{4,6},{5,7},{6,4},{7,5},{8,10},{9,11},{10,... | collective-permute-start | bytes 393224 | tf_op jit(solution)/shard_map/ppermute | solution.py:419
  6.0 6.7 %collective-permute-start.38 = (bf16[512,128]{1,0:T(8,128)(2,1)S(1)}, bf16[512,128]{1,0:T(8,128)(2,1)S(1)}, u32[]{:S(2)}, u32[]{:S(2)}) collective-permute-start(bf16[512,128]{1,0:T(8,128)(2,1)S(1)} %get-tuple-element.152), channel_id=1, source_target_pairs={{0,3},{1,2},{2,1},{3,0},{4,7},{5,6},{6,5},{7,4},{8,11},{9,10},{10,... | collective-permute-start | bytes 393224 | tf_op jit(solution)/shard_map/ppermute | solution.py:419
  6.0 0.7 copy-start.4
  7.6 10.3 %collective-permute-start.42 = (bf16[512,128]{1,0:T(8,128)(2,1)S(1)}, bf16[512,128]{1,0:T(8,128)(2,1)S(1)}, u32[]{:S(2)}, u32[]{:S(2)}) collective-permute-start(bf16[512,128]{1,0:T(8,128)(2,1)S(1)} %get-tuple-element.158), channel_id=1, source_target_pairs={{0,1},{1,0},{2,3},{3,2},{4,5},{5,4},{6,7},{7,6},{8,9},{9,8},{10,11... | collective-permute-start | bytes 393224 | tf_op jit(solution)/shard_map/ppermute | solution.py:419
  7.8 10.5 %collective-permute-start.43 = (bf16[512,128]{1,0:T(8,128)(2,1)S(1)}, bf16[512,128]{1,0:T(8,128)(2,1)S(1)}, u32[]{:S(2)}, u32[]{:S(2)}) collective-permute-start(bf16[512,128]{1,0:T(8,128)(2,1)S(1)} %get-tuple-element.159), channel_id=1, source_target_pairs={{0,2},{1,3},{2,0},{3,1},{4,6},{5,7},{6,4},{7,5},{8,10},{9,11},{10,... | collective-permute-start | bytes 393224 | tf_op jit(solution)/shard_map/ppermute | solution.py:419
  9.8 8.5 %collective-permute-start.44 = (bf16[512,128]{1,0:T(8,128)(2,1)S(1)}, bf16[512,128]{1,0:T(8,128)(2,1)S(1)}, u32[]{:S(2)}, u32[]{:S(2)}) collective-permute-start(bf16[512,128]{1,0:T(8,128)(2,1)S(1)} %get-tuple-element.160), channel_id=1, source_target_pairs={{0,3},{1,2},{2,1},{3,0},{4,7},{5,6},{6,5},{7,4},{8,11},{9,10},{10,... | collective-permute-start | bytes 393224 | tf_op jit(solution)/shard_map/ppermute | solution.py:419
  14.8 8.8 %collective-permute-start.39 = (bf16[384,128]{1,0:T(8,128)(2,1)S(1)}, bf16[384,128]{1,0:T(8,128)(2,1)S(1)}, u32[]{:S(2)}, u32[]{:S(2)}) collective-permute-start(bf16[384,128]{1,0:T(8,128)(2,1)S(1)} %get-tuple-element.154), channel_id=1, source_target_pairs={{0,4},{1,5},{2,6},{3,7},{4,0},{5,1},{6,2},{7,3},{8,12},{9,13},{10,... | collective-permute-start | bytes 294920 | tf_op jit(solution)/shard_map/ppermute | solution.py:419
  16.3 7.6 %collective-permute-start.40 = (bf16[384,128]{1,0:T(8,128)(2,1)S(1)}, bf16[384,128]{1,0:T(8,128)(2,1)S(1)}, u32[]{:S(2)}, u32[]{:S(2)}) collective-permute-start(bf16[384,128]{1,0:T(8,128)(2,1)S(1)} %get-tuple-element.155), channel_id=1, source_target_pairs={{0,8},{1,9},{2,10},{3,11},{4,12},{5,13},{6,14},{7,15},{8,0},{9,1},... | collective-permute-start | bytes 294920 | tf_op jit(solution)/shard_map/ppermute | solution.py:419
  17.9 6.1 %collective-permute-start.41 = (bf16[384,128]{1,0:T(8,128)(2,1)S(1)}, bf16[384,128]{1,0:T(8,128)(2,1)S(1)}, u32[]{:S(2)}, u32[]{:S(2)}) collective-permute-start(bf16[384,128]{1,0:T(8,128)(2,1)S(1)} %get-tuple-element.156), channel_id=1, source_target_pairs={{0,12},{1,13},{2,14},{3,15},{4,8},{5,9},{6,10},{7,11},{8,4},{9,5},... | collective-permute-start | bytes 294920 | tf_op jit(solution)/shard_map/ppermute | solution.py:419
  20.4 14.3 %copy-start.9 = (s32[1,32]{1,0:T(1,128)S(1)}, s32[1,32]{1,0:T(1,128)}, u32[]{:S(2)}) copy-start(s32[1,32]{1,0:T(1,128)} %refs_0_.3) | copy-start | bytes 388
  20.4 14.3 %copy-start.10 = (s32[1,32]{1,0:T(1,128)S(1)}, s32[1,32]{1,0:T(1,128)}, u32[]{:S(2)}) copy-start(s32[1,32]{1,0:T(1,128)} %refs_1_.5) | copy-start | bytes 388
  20.4 5.4 %collective-permute-start.45 = (bf16[384,128]{1,0:T(8,128)(2,1)S(1)}, bf16[384,128]{1,0:T(8,128)(2,1)S(1)}, u32[]{:S(2)}, u32[]{:S(2)}) collective-permute-start(bf16[384,128]{1,0:T(8,128)(2,1)S(1)} %get-tuple-element.162), channel_id=1, source_target_pairs={{0,4},{1,5},{2,6},{3,7},{4,0},{5,1},{6,2},{7,3},{8,12},{9,13},{10,... | collective-permute-start | bytes 294920 | tf_op jit(solution)/shard_map/ppermute | solution.py:419
  22.0 5.7 %collective-permute-start.46 = (bf16[384,128]{1,0:T(8,128)(2,1)S(1)}, bf16[384,128]{1,0:T(8,128)(2,1)S(1)}, u32[]{:S(2)}, u32[]{:S(2)}) collective-permute-start(bf16[384,128]{1,0:T(8,128)(2,1)S(1)} %get-tuple-element.163), channel_id=1, source_target_pairs={{0,8},{1,9},{2,10},{3,11},{4,12},{5,13},{6,14},{7,15},{8,0},{9,1},... | collective-permute-start | bytes 294920 | tf_op jit(solution)/shard_map/ppermute | solution.py:419
  23.6 5.6 %collective-permute-start.47 = (bf16[384,128]{1,0:T(8,128)(2,1)S(1)}, bf16[384,128]{1,0:T(8,128)(2,1)S(1)}, u32[]{:S(2)}, u32[]{:S(2)}) collective-permute-start(bf16[384,128]{1,0:T(8,128)(2,1)S(1)} %get-tuple-element.164), channel_id=1, source_target_pairs={{0,12},{1,13},{2,14},{3,15},{4,8},{5,9},{6,10},{7,11},{8,4},{9,5},... | collective-permute-start | bytes 294920 | tf_op jit(solution)/shard_map/ppermute | solution.py:419
  34.7 27.1 %copy-start.5 = (bf16[1,32,128,128]{3,2,1,0:T(8,128)(2,1)S(1)}, bf16[1,32,128,128]{3,2,1,0:T(8,128)(2,1)}, u32[]{:S(2)}) copy-start(bf16[1,32,128,128]{3,2,1,0:T(8,128)(2,1)} %get-tuple-element.44.refs_3_) | copy-start | bytes 3145732 | tf_op jit(solution)/shard_map/cond
  36.1 4.9 %collective-permute-start = (bf16[384,128]{1,0:T(8,128)(2,1)S(1)}, bf16[384,128]{1,0:T(8,128)(2,1)S(1)}, u32[]{:S(2)}, u32[]{:S(2)}) collective-permute-start(bf16[384,128]{1,0:T(8,128)(2,1)S(1)} %get-tuple-element.49), channel_id=1, source_target_pairs={{0,4},{1,5},{2,6},{3,7},{4,0},{5,1},{6,2},{7,3},{8,12},{9,13},{10,... | collective-permute-start | bytes 294920 | tf_op jit(solution)/shard_map/cond/branch_1_fun/ppermute | solution.py:419
  37.5 5.1 %collective-permute-start.1 = (bf16[384,128]{1,0:T(8,128)(2,1)S(1)}, bf16[384,128]{1,0:T(8,128)(2,1)S(1)}, u32[]{:S(2)}, u32[]{:S(2)}) collective-permute-start(bf16[384,128]{1,0:T(8,128)(2,1)S(1)} %get-tuple-element.50), channel_id=1, source_target_pairs={{0,8},{1,9},{2,10},{3,11},{4,12},{5,13},{6,14},{7,15},{8,0},{9,1},... | collective-permute-start | bytes 294920 | tf_op jit(solution)/shard_map/cond/branch_1_fun/ppermute | solution.py:419
  39.1 5.5 %collective-permute-start.2 = (bf16[384,128]{1,0:T(8,128)(2,1)S(1)}, bf16[384,128]{1,0:T(8,128)(2,1)S(1)}, u32[]{:S(2)}, u32[]{:S(2)}) collective-permute-start(bf16[384,128]{1,0:T(8,128)(2,1)S(1)} %get-tuple-element.51), channel_id=1, source_target_pairs={{0,12},{1,13},{2,14},{3,15},{4,8},{5,9},{6,10},{7,11},{8,4},{9,5},... | collective-permute-start | bytes 294920 | tf_op jit(solution)/shard_map/cond/branch_1_fun/ppermute | solution.py:419
  39.7 9.5 %collective-permute-start.9 = (bf16[384,128]{1,0:T(8,128)(2,1)S(1)}, bf16[384,128]{1,0:T(8,128)(2,1)S(1)}, u32[]{:S(2)}, u32[]{:S(2)}) collective-permute-start(bf16[384,128]{1,0:T(8,128)(2,1)S(1)} %get-tuple-element.61), channel_id=1, source_target_pairs={{0,4},{1,5},{2,6},{3,7},{4,0},{5,1},{6,2},{7,3},{8,12},{9,13},{10,... | collective-permute-start | bytes 294920 | tf_op jit(solution)/shard_map/cond/branch_1_fun/ppermute | solution.py:419
  45.4 9.9 %collective-permute-start.3 = (bf16[512,128]{1,0:T(8,128)(2,1)S(1)}, bf16[512,128]{1,0:T(8,128)(2,1)S(1)}, u32[]{:S(2)}, u32[]{:S(2)}) collective-permute-start(bf16[512,128]{1,0:T(8,128)(2,1)S(1)} %get-tuple-element.53), channel_id=1, source_target_pairs={{0,1},{1,0},{2,3},{3,2},{4,5},{5,4},{6,7},{7,6},{8,9},{9,8},{10,11... | collective-permute-start | bytes 393224 | tf_op jit(solution)/shard_map/cond/branch_1_fun/ppermute | solution.py:419
  45.5 5.7 %collective-permute-start.10 = (bf16[384,128]{1,0:T(8,128)(2,1)S(1)}, bf16[384,128]{1,0:T(8,128)(2,1)S(1)}, u32[]{:S(2)}, u32[]{:S(2)}) collective-permute-start(bf16[384,128]{1,0:T(8,128)(2,1)S(1)} %get-tuple-element.62), channel_id=1, source_target_pairs={{0,8},{1,9},{2,10},{3,11},{4,12},{5,13},{6,14},{7,15},{8,0},{9,1},... | collective-permute-start | bytes 294920 | tf_op jit(solution)/shard_map/cond/branch_1_fun/ppermute | solution.py:419
  46.1 6.7 %collective-permute-start.11 = (bf16[384,128]{1,0:T(8,128)(2,1)S(1)}, bf16[384,128]{1,0:T(8,128)(2,1)S(1)}, u32[]{:S(2)}, u32[]{:S(2)}) collective-permute-start(bf16[384,128]{1,0:T(8,128)(2,1)S(1)} %get-tuple-element.63), channel_id=1, source_target_pairs={{0,12},{1,13},{2,14},{3,15},{4,8},{5,9},{6,10},{7,11},{8,4},{9,5},... | collective-permute-start | bytes 294920 | tf_op jit(solution)/shard_map/cond/branch_1_fun/ppermute | solution.py:419
  47.6 7.9 %collective-permute-start.4 = (bf16[512,128]{1,0:T(8,128)(2,1)S(1)}, bf16[512,128]{1,0:T(8,128)(2,1)S(1)}, u32[]{:S(2)}, u32[]{:S(2)}) collective-permute-start(bf16[512,128]{1,0:T(8,128)(2,1)S(1)} %get-tuple-element.54), channel_id=1, source_target_pairs={{0,2},{1,3},{2,0},{3,1},{4,6},{5,7},{6,4},{7,5},{8,10},{9,11},{10,... | collective-permute-start | bytes 393224 | tf_op jit(solution)/shard_map/cond/branch_1_fun/ppermute | solution.py:419
  49.2 6.3 %collective-permute-start.5 = (bf16[512,128]{1,0:T(8,128)(2,1)S(1)}, bf16[512,128]{1,0:T(8,128)(2,1)S(1)}, u32[]{:S(2)}, u32[]{:S(2)}) collective-permute-start(bf16[512,128]{1,0:T(8,128)(2,1)S(1)} %get-tuple-element.55), channel_id=1, source_target_pairs={{0,3},{1,2},{2,1},{3,0},{4,7},{5,6},{6,5},{7,4},{8,11},{9,10},{10,... | collective-permute-start | bytes 393224 | tf_op jit(solution)/shard_map/cond/branch_1_fun/ppermute | solution.py:419
  53.6 6.7 %collective-permute-start.12 = (bf16[512,128]{1,0:T(8,128)(2,1)S(1)}, bf16[512,128]{1,0:T(8,128)(2,1)S(1)}, u32[]{:S(2)}, u32[]{:S(2)}) collective-permute-start(bf16[512,128]{1,0:T(8,128)(2,1)S(1)} %get-tuple-element.65), channel_id=1, source_target_pairs={{0,1},{1,0},{2,3},{3,2},{4,5},{5,4},{6,7},{7,6},{8,9},{9,8},{10,11... | collective-permute-start | bytes 393224 | tf_op jit(solution)/shard_map/cond/branch_1_fun/ppermute | solution.py:419
  53.7 8.1 %collective-permute-start.13 = (bf16[512,128]{1,0:T(8,128)(2,1)S(1)}, bf16[512,128]{1,0:T(8,128)(2,1)S(1)}, u32[]{:S(2)}, u32[]{:S(2)}) collective-permute-start(bf16[512,128]{1,0:T(8,128)(2,1)S(1)} %get-tuple-element.66), channel_id=1, source_target_pairs={{0,2},{1,3},{2,0},{3,1},{4,6},{5,7},{6,4},{7,5},{8,10},{9,11},{10,... | collective-permute-start | bytes 393224 | tf_op jit(solution)/shard_map/cond/branch_1_fun/ppermute | solution.py:419
  55.3 6.5 %collective-permute-start.14 = (bf16[512,128]{1,0:T(8,128)(2,1)S(1)}, bf16[512,128]{1,0:T(8,128)(2,1)S(1)}, u32[]{:S(2)}, u32[]{:S(2)}) collective-permute-start(bf16[512,128]{1,0:T(8,128)(2,1)S(1)} %get-tuple-element.67), channel_id=1, source_target_pairs={{0,3},{1,2},{2,1},{3,0},{4,7},{5,6},{6,5},{7,4},{8,11},{9,10},{10,... | collective-permute-start | bytes 393224 | tf_op jit(solution)/shard_map/cond/branch_1_fun/ppermute | solution.py:419
  58.3 7.9 %collective-permute-start.6 = (bf16[384,128]{1,0:T(8,128)(2,1)S(1)}, bf16[384,128]{1,0:T(8,128)(2,1)S(1)}, u32[]{:S(2)}, u32[]{:S(2)}) collective-permute-start(bf16[384,128]{1,0:T(8,128)(2,1)S(1)} %get-tuple-element.57), channel_id=1, source_target_pairs={{0,4},{1,5},{2,6},{3,7},{4,0},{5,1},{6,2},{7,3},{8,12},{9,13},{10,... | collective-permute-start | bytes 294920 | tf_op jit(solution)/shard_map/cond/branch_1_fun/ppermute | solution.py:419
  59.7 7.9 %collective-permute-start.7 = (bf16[384,128]{1,0:T(8,128)(2,1)S(1)}, bf16[384,128]{1,0:T(8,128)(2,1)S(1)}, u32[]{:S(2)}, u32[]{:S(2)}) collective-permute-start(bf16[384,128]{1,0:T(8,128)(2,1)S(1)} %get-tuple-element.58), channel_id=1, source_target_pairs={{0,8},{1,9},{2,10},{3,11},{4,12},{5,13},{6,14},{7,15},{8,0},{9,1},... | collective-permute-start | bytes 294920 | tf_op jit(solution)/shard_map/cond/branch_1_fun/ppermute | solution.py:419
  60.3 7.4 %collective-permute-start.8 = (bf16[384,128]{1,0:T(8,128)(2,1)S(1)}, bf16[384,128]{1,0:T(8,128)(2,1)S(1)}, u32[]{:S(2)}, u32[]{:S(2)}) collective-permute-start(bf16[384,128]{1,0:T(8,128)(2,1)S(1)} %get-tuple-element.59), channel_id=1, source_target_pairs={{0,12},{1,13},{2,14},{3,15},{4,8},{5,9},{6,10},{7,11},{8,4},{9,5},... | collective-permute-start | bytes 294920 | tf_op jit(solution)/shard_map/cond/branch_1_fun/ppermute | solution.py:419
  64.1 5.4 %collective-permute-start.15 = (bf16[384,128]{1,0:T(8,128)(2,1)S(1)}, bf16[384,128]{1,0:T(8,128)(2,1)S(1)}, u32[]{:S(2)}, u32[]{:S(2)}) collective-permute-start(bf16[384,128]{1,0:T(8,128)(2,1)S(1)} %get-tuple-element.69), channel_id=1, source_target_pairs={{0,4},{1,5},{2,6},{3,7},{4,0},{5,1},{6,2},{7,3},{8,12},{9,13},{10,... | collective-permute-start | bytes 294920 | tf_op jit(solution)/shard_map/cond/branch_1_fun/ppermute | solution.py:419
  65.6 5.7 %collective-permute-start.16 = (bf16[384,128]{1,0:T(8,128)(2,1)S(1)}, bf16[384,128]{1,0:T(8,128)(2,1)S(1)}, u32[]{:S(2)}, u32[]{:S(2)}) collective-permute-start(bf16[384,128]{1,0:T(8,128)(2,1)S(1)} %get-tuple-element.70), channel_id=1, source_target_pairs={{0,8},{1,9},{2,10},{3,11},{4,12},{5,13},{6,14},{7,15},{8,0},{9,1},... | collective-permute-start | bytes 294920 | tf_op jit(solution)/shard_map/cond/branch_1_fun/ppermute | solution.py:419
  66.2 6.7 %collective-permute-start.17 = (bf16[384,128]{1,0:T(8,128)(2,1)S(1)}, bf16[384,128]{1,0:T(8,128)(2,1)S(1)}, u32[]{:S(2)}, u32[]{:S(2)}) collective-permute-start(bf16[384,128]{1,0:T(8,128)(2,1)S(1)} %get-tuple-element.71), channel_id=1, source_target_pairs={{0,12},{1,13},{2,14},{3,15},{4,8},{5,9},{6,10},{7,11},{8,4},{9,5},... | collective-permute-start | bytes 294920 | tf_op jit(solution)/shard_map/cond/branch_1_fun/ppermute | solution.py:419
  73.9 6.2 %copy-start.8 = (bf16[4,192,256]{2,1,0:T(8,128)(2,1)S(1)}, bf16[4,192,256]{2,1,0:T(8,128)(2,1)}, u32[]{:S(2)}) copy-start(bf16[4,192,256]{2,1,0:T(8,128)(2,1)} %get-tuple-element.180.refs_0_) | copy-start | bytes 1179652
  73.9 8.2 %collective-permute-start.48 = (bf16[2,192,256]{2,1,0:T(8,128)(2,1)}, bf16[2,192,256]{2,1,0:T(8,128)(2,1)S(1)}, u32[]{:S(2)}, u32[]{:S(2)}) collective-permute-start(bf16[2,192,256]{2,1,0:T(8,128)(2,1)} %get-tuple-element.176), channel_id=1, source_target_pairs={{0,24},{1,25},{2,26},{3,27},{4,28},{5,29},{6,30},{7,31},{8,16},{9,... | collective-permute-start | bytes 589832 | tf_op jit(solution)/shard_map/ppermute | solution.py:419
  75.3 8.7 %collective-permute-start.49 = (bf16[2,192,256]{2,1,0:T(8,128)(2,1)}, bf16[2,192,256]{2,1,0:T(8,128)(2,1)S(1)}, u32[]{:S(2)}, u32[]{:S(2)}) collective-permute-start(bf16[2,192,256]{2,1,0:T(8,128)(2,1)} %get-tuple-element.178), channel_id=1, source_target_pairs={{0,24},{1,25},{2,26},{3,27},{4,28},{5,29},{6,30},{7,31},{8,16},{9,... | collective-permute-start | bytes 589832 | tf_op jit(solution)/shard_map/ppermute | solution.py:419
  84.7 70.0 %copy-start.7 = (bf16[4,192,256]{2,1,0:T(8,128)(2,1)S(1)}, bf16[4,192,256]{2,1,0:T(8,128)(2,1)}, u32[]{:S(2)}) copy-start(bf16[4,192,256]{2,1,0:T(8,128)(2,1)} %get-tuple-element.187.refs_0_) | copy-start | bytes 1179652
  84.7 59.1 %collective-permute-start.50 = (bf16[2,192,256]{2,1,0:T(8,128)(2,1)S(1)}, bf16[2,192,256]{2,1,0:T(8,128)(2,1)S(1)}, u32[]{:S(2)}, u32[]{:S(2)}) collective-permute-start(bf16[2,192,256]{2,1,0:T(8,128)(2,1)S(1)} %get-tuple-element.182), channel_id=1, source_target_pairs={{0,24},{1,25},{2,26},{3,27},{4,28},{5,29},{6,30},{7,31},{8,16},{9,... | collective-permute-start | bytes 589832 | tf_op jit(solution)/shard_map/ppermute | solution.py:419
  138.5 16.1 %collective-permute-start.54 = (bf16[2,192,256]{2,1,0:T(8,128)(2,1)S(1)}, bf16[2,192,256]{2,1,0:T(8,128)(2,1)S(1)}, u32[]{:S(2)}, u32[]{:S(2)}) collective-permute-start(bf16[2,192,256]{2,1,0:T(8,128)(2,1)S(1)} %get-tuple-element.188), channel_id=1, source_target_pairs={{0,24},{1,25},{2,26},{3,27},{4,28},{5,29},{6,30},{7,31},{8,16},{9,... | collective-permute-start | bytes 589832 | tf_op jit(solution)/shard_map/ppermute | solution.py:419
  144.8 12.9 %collective-permute-start.51 = (bf16[192,256]{1,0:T(8,128)(2,1)S(1)}, bf16[192,256]{1,0:T(8,128)(2,1)S(1)}, u32[]{:S(2)}, u32[]{:S(2)}) collective-permute-start(bf16[192,256]{1,0:T(8,128)(2,1)S(1)} %get-tuple-element.184), channel_id=1, source_target_pairs={{0,4},{1,5},{2,6},{3,7},{4,0},{5,1},{6,2},{7,3},{8,12},{9,13},{10,... | collective-permute-start | bytes 294920 | tf_op jit(solution)/shard_map/ppermute | solution.py:419
  145.5 14.5 %collective-permute-start.52 = (bf16[192,256]{1,0:T(8,128)(2,1)S(1)}, bf16[192,256]{1,0:T(8,128)(2,1)S(1)}, u32[]{:S(2)}, u32[]{:S(2)}) collective-permute-start(bf16[192,256]{1,0:T(8,128)(2,1)S(1)} %get-tuple-element.185), channel_id=1, source_target_pairs={{0,8},{1,9},{2,10},{3,11},{4,12},{5,13},{6,14},{7,15},{8,0},{9,1},... | collective-permute-start | bytes 294920 | tf_op jit(solution)/shard_map/ppermute | solution.py:419
  154.1 6.7 %collective-permute-start.53 = (bf16[192,256]{1,0:T(8,128)(2,1)S(1)}, bf16[192,256]{1,0:T(8,128)(2,1)S(1)}, u32[]{:S(2)}, u32[]{:S(2)}) collective-permute-start(bf16[192,256]{1,0:T(8,128)(2,1)S(1)} %get-tuple-element.186), channel_id=1, source_target_pairs={{0,12},{1,13},{2,14},{3,15},{4,8},{5,9},{6,10},{7,11},{8,4},{9,5},... | collective-permute-start | bytes 294920 | tf_op jit(solution)/shard_map/ppermute | solution.py:419
  154.7 6.8 %collective-permute-start.55 = (bf16[192,256]{1,0:T(8,128)(2,1)S(1)}, bf16[192,256]{1,0:T(8,128)(2,1)S(1)}, u32[]{:S(2)}, u32[]{:S(2)}) collective-permute-start(bf16[192,256]{1,0:T(8,128)(2,1)S(1)} %get-tuple-element.190), channel_id=1, source_target_pairs={{0,4},{1,5},{2,6},{3,7},{4,0},{5,1},{6,2},{7,3},{8,12},{9,13},{10,... | collective-permute-start | bytes 294920 | tf_op jit(solution)/shard_map/ppermute | solution.py:419
  155.7 5.8 %collective-permute-start.56 = (bf16[192,256]{1,0:T(8,128)(2,1)S(1)}, bf16[192,256]{1,0:T(8,128)(2,1)S(1)}, u32[]{:S(2)}, u32[]{:S(2)}) collective-permute-start(bf16[192,256]{1,0:T(8,128)(2,1)S(1)} %get-tuple-element.191), channel_id=1, source_target_pairs={{0,8},{1,9},{2,10},{3,11},{4,12},{5,13},{6,14},{7,15},{8,0},{9,1},... | collective-permute-start | bytes 294920 | tf_op jit(solution)/shard_map/ppermute | solution.py:419
  157.7 5.5 %collective-permute-start.57 = (bf16[192,256]{1,0:T(8,128)(2,1)S(1)}, bf16[192,256]{1,0:T(8,128)(2,1)S(1)}, u32[]{:S(2)}, u32[]{:S(2)}) collective-permute-start(bf16[192,256]{1,0:T(8,128)(2,1)S(1)} %get-tuple-element.192), channel_id=1, source_target_pairs={{0,12},{1,13},{2,14},{3,15},{4,8},{5,9},{6,10},{7,11},{8,4},{9,5},... | collective-permute-start | bytes 294920 | tf_op jit(solution)/shard_map/ppermute | solution.py:419

commit v3 on v1

--- a/solution.py
+++ b/solution.py
@@ -20,11 +20,7 @@
     index = lax.axis_index("tm")
     half = index // group
     place = index % group
-    return half, place, place ^ (half * mirror(group))
-
-
-def mirror(group):
-    return group - 2 if group > 2 else 0
+    return half, place
 
 
 def only(mode, half):
@@ -49,12 +45,12 @@
         outs = refs[first_out : first_out + slab_count]
         table, table_sem, rows, sems = refs[-4:]
         slab = lax.axis_index("slab")
-        _, _, lead = seat(group)
+        _, place = seat(group)
         fetch = pltpu.make_async_copy(table_hbm, table, table_sem)
         fetch.start()
         if not whole:
             for k in range(part_count):
-                start = pl.multiple_of((lead ^ k) * part_rows, part_rows)
+                start = pl.multiple_of((place ^ k) * part_rows, part_rows)
                 rows[pl.ds(start, part_rows), :] = sources[k][...]
         fetch.wait()
         copies = []
@@ -109,7 +105,7 @@
         outs = refs[4 + slab_count : 4 + slab_count + group]
         rows, sources, counts, sems, inputs, total = refs[4 + slab_count + group :]
         slab = lax.axis_index("slab")
-        _, _, lead = seat(group)
+        _, place = seat(group)
         fetches = [
             pltpu.make_async_copy(refs[n], local_ref, sems.at[n])
             for n, local_ref in enumerate((rows, sources, counts))
@@ -142,7 +138,7 @@
 
         lax.fori_loop(0, (count + unroll - 1) // unroll, step, 0)
         for k in range(group):
-            start = pl.multiple_of((lead ^ k) * group_rows, group_rows)
+            start = pl.multiple_of((place ^ k) * group_rows, group_rows)
             outs[k][...] = total[pl.ds(start, group_rows), :].astype(outs[k].dtype)
 
     dtype = arrived[0].dtype
@@ -173,7 +169,7 @@
     size = rows // CHUNKS
 
     def kernel(*refs):
-        _, place, _ = seat(group)
+        _, place = seat(group)
         for n in range(len(blocks)):
             first = n // group * lanes
             for chunk, out in enumerate(refs[len(blocks) :]):
@@ -207,7 +203,7 @@
     count = units // lanes * group
 
     def kernel(*refs):
-        _, place, _ = seat(group)
+        _, place = seat(group)
         spread_into(refs[len(chunks) :], refs[: len(chunks)], place, group)
 
     results = pl.pallas_call(
@@ -228,15 +224,15 @@
     operands = [mixed] + list(done) + list(keep) + ([] if first else [state])
     outputs = units // lanes * group if lanes else 1
 
-    def kernel(w_in, w_rec, gate_bias, *refs):
+    def kernel(w_in, w_rec_hbm, gate_bias, *refs):
         inputs = refs[0]
         earlier = refs[1 : 1 + len(done)]
         kept = refs[1 + len(done) : 1 + len(done) + len(keep)]
         start = refs[len(operands) - 1]
         outs = refs[len(operands) : len(operands) + outputs]
-        memory = refs[-1]
-        states = refs[-2] if lanes else outs[0]
-        half, place, _ = seat(group)
+        w_rec, sem, memory = refs[-3:]
+        states = refs[-4] if lanes else outs[0]
+        half, place = seat(group)
 
         if keep:
 
@@ -246,6 +242,8 @@
 
         @only(mode, half)
         def _():
+            fetch = pltpu.make_async_copy(w_rec_hbm.at[layer], w_rec, sem)
+            fetch.start()
             line = gate_bias[layer : layer + 1, :]
 
             def advance(gates, old, time):
@@ -256,26 +254,20 @@
                 memory[...] = new
                 states[time] = (sigmoid(o) * jnp.tanh(new)).astype(states.dtype)
 
-            def project(time):
-                return jnp.dot(inputs[time], w_in[layer], preferred_element_type=jnp.float32) + line
-
-            def step(time, hidden):
-                gates = project(time) + jnp.dot(
-                    hidden, w_rec[layer], preferred_element_type=jnp.float32
-                )
-                advance(gates, memory[...], time)
-
-            if first:
-                advance(project(0), None, 0)
-            else:
+            hidden = None if first else start[0]
+            if not first:
                 memory[...] = start[1].astype(jnp.float32)
-                step(0, start[0])
-
-            def loop(time, carry):
-                step(time, states[time - 1])
-                return carry
-
-            lax.fori_loop(1, group, loop, 0, unroll=True)
+            for time in range(group):
+                gates = jnp.dot(inputs[time], w_in[layer], preferred_element_type=jnp.float32)
+                gates = gates + line
+                if time == min(int(first), group - 1):
+                    fetch.wait()
+                if hidden is not None:
+                    gates = gates + jnp.dot(
+                        hidden, w_rec[...], preferred_element_type=jnp.float32
+                    )
+                advance(gates, None if hidden is None else memory[...], time)
+                hidden = states[time]
             if lanes:
                 spread_into(outs, [*earlier, states], place, group)
             if first:
@@ -291,9 +283,10 @@
     if first:
         out_shape.append(jax.ShapeDtypeStruct((2, size, units), dtype))
     scratch = [pltpu.VMEM((group, size, units), dtype)] if lanes else []
+    scratch += [pltpu.VMEM(w_hidden.shape[1:], w_hidden.dtype), pltpu.SemaphoreType.DMA(())]
     results = pl.pallas_call(
         kernel,
-        in_specs=[VMEM] * (3 + len(operands)),
+        in_specs=[VMEM, HBM, VMEM] + [VMEM] * len(operands),
         out_specs=[VMEM] * len(out_shape),
         out_shape=out_shape,
         scratch_shapes=scratch + [pltpu.VMEM((size, units), jnp.float32)],
@@ -313,10 +306,10 @@
 
     def kernel(*refs):
         out, sems = refs[-2:]
-        _, _, lead = seat(group)
+        _, place = seat(group)
         copies = []
         for n in range(count):
-            start = (lead ^ (n % group)) * part_rows + n // group * size
+            start = (place ^ (n % group)) * part_rows + n // group * size
             target = out.at[0, pl.ds(pl.multiple_of(start, size), size)]
             copies.append(pltpu.make_async_copy(refs[n], target, sems.at[n]))
         for copy in copies:
@@ -361,8 +354,7 @@
 
 
 def hand_over(last, group):
-    flip = mirror(group)
-    return send(last, lambda time, slab: (group + (time ^ flip), slab), lower_only=True)
+    return send(last, lambda time, slab: (group + time, slab), lower_only=True)
 
 
 def local(

time: 164 us -> 165 us (level)
  no operation moved by 1% of the time
where the time goes in v3:
time: 165 us; the launch traced here: 163 us
  starting transfers between devices  102 us (62%)
  waiting for transfers between devices  30.7 us (19%)
  Pallas kernels  26.6 us (16%)
  local copies, waits for them, and re-layouts  2.51 us (2%)
    ppermute x40, starting transfers between devices, send(): return lax.ppermute(array, AXES, pairs)  102 us
    ppermute x40, waiting for transfers between devices, send(): return lax.ppermute(array, AXES, pairs)  30.7 us
    pallas_call x7, Pallas kernels, recur(): pl.pallas_call(kernel, in_specs=[VMEM, HBM, VMEM] + [VMEM] * len(operands...  13.3 us
    pallas_call x4, Pallas kernels, convolve(): pl.pallas_call(kernel, in_specs=[HBM, HBM, HBM, VMEM] + [VMEM] * slab_cou...  5.81 us
    pallas_call x4, Pallas kernels, pick_tiles(): pl.pallas_call(kernel, in_specs=[HBM] + [HBM if whole else VMEM] * part_c...  3.31 us
  transfers between devices with their start and end apart: 40, of which 20 were waited for; matrix products, arithmetic and copies ran while one was open for 0% of the time, Pallas kernels for 10%

profile of v3, /device:TPU:0, one launch (start us, length us, event | category | flops | bytes accessed | tf_op | source)
XLA Modules:
  0.0 163.3 jit_solution(13923086060127155924)
XLA Ops:
  0.0 1.1 copy-done
  1.8 0.9 pick_tiles.11
  3.3 2.6 %collective-permute-start.37 = (bf16[512,128]{1,0:T(8,128)(2,1)S(1)}, bf16[512,128]{1,0:T(8,128)(2,1)S(1)}, u32[]{:S(2)}, u32[]{:S(2)}) collective-permute-start(bf16[512,128]{1,0:T(8,128)(2,1)S(1)} %get-tuple-element.166), channel_id=1, source_target_pairs={{0,2},{1,3},{2,0},{3,1},{4,6},{5,7},{6,4},{7,5},{8,10},{9,11},{10,... | collective-permute-start | bytes 393224 | tf_op jit(solution)/shard_map/ppermute | solution.py:339
  5.9 0.9 pick_tiles.10
  7.0 1.9 %collective-permute-start.43 = (bf16[512,128]{1,0:T(8,128)(2,1)S(1)}, bf16[512,128]{1,0:T(8,128)(2,1)S(1)}, u32[]{:S(2)}, u32[]{:S(2)}) collective-permute-start(bf16[512,128]{1,0:T(8,128)(2,1)S(1)} %get-tuple-element.174), channel_id=1, source_target_pairs={{0,2},{1,3},{2,0},{3,1},{4,6},{5,7},{6,4},{7,5},{8,10},{9,11},{10,... | collective-permute-start | bytes 393224 | tf_op jit(solution)/shard_map/ppermute | solution.py:339
  10.2 2.4 %collective-permute-done.38.refs_7_ = bf16[512,128]{1,0:T(8,128)(2,1)S(1)} collective-permute-done((bf16[512,128]{1,0:T(8,128)(2,1)S(1)}, bf16[512,128]{1,0:T(8,128)(2,1)S(1)}, u32[]{:S(2)}, u32[]{:S(2)}) %collective-permute-start.38) | collective-permute-done | bytes 131104 | tf_op jit(solution)/shard_map/ppermute | solution.py:339
  12.5 1.1 convolve.10
  13.7 1.6 collective-permute-start.39
  15.3 1.6 collective-permute-start.40
  17.2 0.8 collective-permute-done.44.refs_7_
  18.1 1.1 convolve.11
  19.2 1.6 collective-permute-start.45
  20.8 1.6 collective-permute-start.46
  22.8 2.0 %collective-permute-done.45.refs_5_ = bf16[384,128]{1,0:T(8,128)(2,1)S(1)} collective-permute-done((bf16[384,128]{1,0:T(8,128)(2,1)S(1)}, bf16[384,128]{1,0:T(8,128)(2,1)S(1)}, u32[]{:S(2)}, u32[]{:S(2)}) %collective-permute-start.45) | collective-permute-done | bytes 98336 | tf_op jit(solution)/shard_map/ppermute | solution.py:339
  24.8 1.6 %collective-permute-done.46.refs_6_ = bf16[384,128]{1,0:T(8,128)(2,1)S(1)} collective-permute-done((bf16[384,128]{1,0:T(8,128)(2,1)S(1)}, bf16[384,128]{1,0:T(8,128)(2,1)S(1)}, u32[]{:S(2)}, u32[]{:S(2)}) %collective-permute-start.46) | collective-permute-done | bytes 98336 | tf_op jit(solution)/shard_map/ppermute | solution.py:339
  26.5 1.6 collective-permute-done.47.refs_7_
  28.1 0.9 pack.5
  29.0 3.1 %recur.9 = (bf16[4,192,256]{2,1,0:T(8,128)(2,1)}, bf16[2,192,256]{2,1,0:T(8,128)(2,1)S(1)}) custom-call(bf16[2,256,1024]{2,1,0:T(8,128)(2,1)S(1)} %copy-done.3, bf16[2,256,1024]{2,1,0:T(8,128)(2,1)S(1)} %copy-done.4, f32[2,1024]{1,0:T(2,128)S(1)} %get-tuple-element.163.gate_bias, bf16[4,192,256]{2,1,0:T(8,128)(2,1)} %get-tuple-element.180.refs_0_), custom_call_target="tpu_custom_call" | custom-call | tf_op jit(solution)/shard_map/recur/pallas_call | solution.py:287
  32.1 2.0 %recur.10 = (bf16[4,192,256]{2,1,0:T(8,128)(2,1)}, bf16[2,192,256]{2,1,0:T(8,128)(2,1)S(1)}) custom-call(bf16[2,256,1024]{2,1,0:T(8,128)(2,1)S(1)} %copy-done.3, bf16[2,256,1024]{2,1,0:T(8,128)(2,1)S(1)} %copy-done.4, f32[2,1024]{1,0:T(2,128)S(1)} %get-tuple-element.163.gate_bias, bf16[4,192,256]{2,1,0:T(8,128)(2,1)S(1)} %get-tuple-element.182.refs_0_), custom_call_target="tpu_custom_call" | custom-call | tf_op jit(solution)/shard_map/recur/pallas_call | solution.py:287
  34.8 38.7 %conditional.2 = (bf16[4,192,256]{2,1,0:T(8,128)(2,1)}, bf16[4,192,256]{2,1,0:T(8,128)(2,1)}, s32[]{:T(128)}) conditional(s32[]{:T(128)} %convert_element_type.6, (bf16[4,192,256]{2,1,0:T(8,128)(2,1)}, bf16[4,192,256]{2,1,0:T(8,128)(2,1)}, s32[]{:T(128)}) %tuple.17, (bf16[4,192,256]{2,1,0:T(8,128)(2,1)}, bf16[4,192,256]{2,1,0:T(8,128)(2,1)}, ...), branch_computations={%region_0.1_spmd, %region_1.2_spmd} | conditional | flops 1 | bytes 12059408 | solution.py:412
  34.8 1.3 spread.1
  36.1 1.4 collective-permute-start
  37.6 1.6 collective-permute-start.1
  39.7 1.4 collective-permute-start.9
  41.1 1.7 %collective-permute-done.1.refs_2_ = bf16[384,128]{1,0:T(8,128)(2,1)S(1)} collective-permute-done((bf16[384,128]{1,0:T(8,128)(2,1)S(1)}, bf16[384,128]{1,0:T(8,128)(2,1)S(1)}, u32[]{:S(2)}, u32[]{:S(2)}) %collective-permute-start.1) | collective-permute-done | bytes 98336 | tf_op jit(solution)/shard_map/cond/branch_1_fun/ppermute | solution.py:339
  42.7 1.9 %collective-permute-done.2.refs_3_ = bf16[384,128]{1,0:T(8,128)(2,1)S(1)} collective-permute-done((bf16[384,128]{1,0:T(8,128)(2,1)S(1)}, bf16[384,128]{1,0:T(8,128)(2,1)S(1)}, u32[]{:S(2)}, u32[]{:S(2)}) %collective-permute-start.2) | collective-permute-done | bytes 98336 | tf_op jit(solution)/shard_map/cond/branch_1_fun/ppermute | solution.py:339
  44.7 0.8 pick_tiles.6
  45.5 0.7 collective-permute-start.10
  46.2 1.5 collective-permute-start.11
  47.7 1.5 collective-permute-start.4
  49.2 2.0 %collective-permute-done.10.refs_2_ = bf16[384,128]{1,0:T(8,128)(2,1)S(1)} collective-permute-done((bf16[384,128]{1,0:T(8,128)(2,1)S(1)}, bf16[384,128]{1,0:T(8,128)(2,1)S(1)}, u32[]{:S(2)}, u32[]{:S(2)}) %collective-permute-start.10) | collective-permute-done | bytes 98336 | tf_op jit(solution)/shard_map/cond/branch_1_fun/ppermute | solution.py:339
  51.2 1.7 %collective-permute-done.11.refs_3_ = bf16[384,128]{1,0:T(8,128)(2,1)S(1)} collective-permute-done((bf16[384,128]{1,0:T(8,128)(2,1)S(1)}, bf16[384,128]{1,0:T(8,128)(2,1)S(1)}, u32[]{:S(2)}, u32[]{:S(2)}) %collective-permute-start.11) | collective-permute-done | bytes 98336 | tf_op jit(solution)/shard_map/cond/branch_1_fun/ppermute | solution.py:339
  52.9 0.8 pick_tiles.7
  53.8 1.6 collective-permute-start.13
  55.7 1.8 %convolve.6 = (bf16[384,128]{1,0:T(8,128)(2,1)S(1)}, bf16[384,128]{1,0:T(8,128)(2,1)S(1)}, bf16[384,128]{1,0:T(8,128)(2,1)S(1)}, bf16[384,128]{1,0:T(8,128)(2,1)S(1)}) custom-call(s32[1,32]{1,0:T(1,128)S(1)} %get-tuple-element.53.refs_0_, s32[1,32]{1,0:T(1,128)S(1)} %get-tuple-element.54.refs_1_, s32[1,1]{1,0:T(1,128)} %get-tuple-element.55.refs_2_, ...), custom_call_target="tpu_custom_call" | custom-call | tf_op jit(solution)/shard_map/cond/branch_1_fun/convolve/pallas_call | solution.py:145
  57.4 1.4 collective-permute-start.6
  59.5 1.5 collective-permute-start.8
  61.0 1.0 collective-permute-done.14.refs_7_
  62.0 1.8 %convolve.7 = (bf16[384,128]{1,0:T(8,128)(2,1)S(1)}, bf16[384,128]{1,0:T(8,128)(2,1)S(1)}, bf16[384,128]{1,0:T(8,128)(2,1)S(1)}, bf16[384,128]{1,0:T(8,128)(2,1)S(1)}) custom-call(s32[1,32]{1,0:T(1,128)S(1)} %get-tuple-element.53.refs_0_, s32[1,32]{1,0:T(1,128)S(1)} %get-tuple-element.54.refs_1_, s32[1,1]{1,0:T(1,128)} %get-tuple-element.55.refs_2_, ...), custom_call_target="tpu_custom_call" | custom-call | tf_op jit(solution)/shard_map/cond/branch_1_fun/convolve/pallas_call | solution.py:145
  63.7 1.4 collective-permute-start.15
  65.8 1.5 collective-permute-start.17
  67.3 1.9 %collective-permute-done.15.refs_5_ = bf16[384,128]{1,0:T(8,128)(2,1)S(1)} collective-permute-done((bf16[384,128]{1,0:T(8,128)(2,1)S(1)}, bf16[384,128]{1,0:T(8,128)(2,1)S(1)}, u32[]{:S(2)}, u32[]{:S(2)}) %collective-permute-start.15) | collective-permute-done | bytes 98336 | tf_op jit(solution)/shard_map/cond/branch_1_fun/ppermute | solution.py:339
  69.2 1.6 collective-permute-done.16.refs_6_
  70.8 1.7 %collective-permute-done.17.refs_7_ = bf16[384,128]{1,0:T(8,128)(2,1)S(1)} collective-permute-done((bf16[384,128]{1,0:T(8,128)(2,1)S(1)}, bf16[384,128]{1,0:T(8,128)(2,1)S(1)}, u32[]{:S(2)}, u32[]{:S(2)}) %collective-permute-start.17) | collective-permute-done | bytes 98336 | tf_op jit(solution)/shard_map/cond/branch_1_fun/ppermute | solution.py:339
  72.5 1.0 pack.3
  73.5 1.3 collective-permute-start.48
  74.8 1.3 collective-permute-start.49
  76.1 3.0 %recur.12 = (bf16[4,192,256]{2,1,0:T(8,128)(2,1)S(1)}, bf16[2,192,256]{2,1,0:T(8,128)(2,1)S(1)}) custom-call(bf16[2,256,1024]{2,1,0:T(8,128)(2,1)S(1)} %copy-done.3, bf16[2,256,1024]{2,1,0:T(8,128)(2,1)} %w_rec_hbm.13, f32[2,1024]{1,0:T(2,128)S(1)} %get-tuple-element.163.gate_bias, bf16[4,192,256]{2,1,0:T(8,128)(2,1)} %get-tuple-element.189.refs_0_), custom_call_target="tpu_custom_call" | custom-call | tf_op jit(solution)/shard_map/recur/pallas_call | solution.py:287
  79.1 0.9 collective-permute-done.48.refs_1_
  80.1 1.8 %recur.11 = bf16[4,192,256]{2,1,0:T(8,128)(2,1)} custom-call(bf16[2,256,1024]{2,1,0:T(8,128)(2,1)S(1)} %copy-done.3, bf16[2,256,1024]{2,1,0:T(8,128)(2,1)S(1)} %copy-done.5, f32[2,1024]{1,0:T(2,128)S(1)} %get-tuple-element.163.gate_bias, bf16[4,192,256]{2,1,0:T(8,128)(2,1)} %get-tuple-element.180.refs_0_, ...), custom_call_target="tpu_custom_call" | custom-call | tf_op jit(solution)/shard_map/recur/pallas_call | solution.py:287
  81.9 1.3 collective-permute-done.49
  83.2 53.5 %collective-permute-start.50 = (bf16[2,192,256]{2,1,0:T(8,128)(2,1)S(1)}, bf16[2,192,256]{2,1,0:T(8,128)(2,1)S(1)}, u32[]{:S(2)}, u32[]{:S(2)}) collective-permute-start(bf16[2,192,256]{2,1,0:T(8,128)(2,1)S(1)} %get-tuple-element.191), channel_id=1, source_target_pairs={{0,16},{1,17},{2,18},{3,19},{4,20},{5,21},{6,22},{7,23},{8,24},{9,... | collective-permute-start | bytes 589832 | tf_op jit(solution)/shard_map/ppermute | solution.py:339
  136.7 2.2 %recur.14 = (bf16[4,192,256]{2,1,0:T(8,128)(2,1)S(1)}, bf16[2,192,256]{2,1,0:T(8,128)(2,1)S(1)}) custom-call(bf16[2,256,1024]{2,1,0:T(8,128)(2,1)S(1)} %copy-done.3, bf16[2,256,1024]{2,1,0:T(8,128)(2,1)S(1)} %copy-done.5, f32[2,1024]{1,0:T(2,128)S(1)} %get-tuple-element.163.gate_bias, bf16[4,192,256]{2,1,0:T(8,128)(2,1)} %get-tuple-element.197.refs_0_), custom_call_target="tpu_custom_call" | custom-call | tf_op jit(solution)/shard_map/recur/pallas_call | solution.py:287
  138.9 1.3 collective-permute-start.54
  140.2 1.2 collective-permute-done.50.refs_2_
  141.4 1.1 recur.13
  143.2 9.2 %collective-permute-start.52 = (bf16[192,256]{1,0:T(8,128)(2,1)S(1)}, bf16[192,256]{1,0:T(8,128)(2,1)S(1)}, u32[]{:S(2)}, u32[]{:S(2)}) collective-permute-start(bf16[192,256]{1,0:T(8,128)(2,1)S(1)} %get-tuple-element.194), channel_id=1, source_target_pairs={{0,8},{1,9},{2,10},{3,11},{4,12},{5,13},{6,14},{7,15},{8,0},{9,1},... | collective-permute-start | bytes 294920 | tf_op jit(solution)/shard_map/ppermute | solution.py:339
  152.4 0.9 collective-permute-start.53
  154.0 2.0 %collective-permute-start.56 = (bf16[192,256]{1,0:T(8,128)(2,1)S(1)}, bf16[192,256]{1,0:T(8,128)(2,1)S(1)}, u32[]{:S(2)}, u32[]{:S(2)}) collective-permute-start(bf16[192,256]{1,0:T(8,128)(2,1)S(1)} %get-tuple-element.202), channel_id=1, source_target_pairs={{0,8},{1,9},{2,10},{3,11},{4,12},{5,13},{6,14},{7,15},{8,0},{9,1},... | collective-permute-start | bytes 294920 | tf_op jit(solution)/shard_map/ppermute | solution.py:339
  156.0 1.3 collective-permute-start.57
  157.4 1.6 collective-permute-done.53.refs_3_
  159.0 1.3 collective-permute-done.56.refs_6_
  160.3 1.8 %collective-permute-done.57.refs_7_ = bf16[192,256]{1,0:T(8,128)(2,1)S(1)} collective-permute-done((bf16[192,256]{1,0:T(8,128)(2,1)S(1)}, bf16[192,256]{1,0:T(8,128)(2,1)S(1)}, u32[]{:S(2)}, u32[]{:S(2)}) %collective-permute-start.57) | collective-permute-done | bytes 98336 | tf_op jit(solution)/shard_map/ppermute | solution.py:339
  162.2 0.9 assemble.1
  (63 shorter events, 7.3 us)
Async XLA Ops:
  0.0 1.1 copy-start
  1.1 0.7 copy-start.1
  1.8 4.1 %copy-start.2 = (f32[2,1024]{1,0:T(2,128)S(1)}, f32[2,1024]{1,0:T(2,128)}, u32[]{:S(2)}) copy-start(f32[2,1024]{1,0:T(2,128)} %refs_2_.3) | copy-start | bytes 24580
  1.8 10.7 %copy-start.6 = (bf16[1,32,128,128]{3,2,1,0:T(8,128)(2,1)S(1)}, bf16[1,32,128,128]{3,2,1,0:T(8,128)(2,1)}, u32[]{:S(2)}) copy-start(bf16[1,32,128,128]{3,2,1,0:T(8,128)(2,1)} %refs_3_.3) | copy-start | bytes 3145732
  2.7 6.2 %collective-permute-start.36 = (bf16[512,128]{1,0:T(8,128)(2,1)S(1)}, bf16[512,128]{1,0:T(8,128)(2,1)S(1)}, u32[]{:S(2)}, u32[]{:S(2)}) collective-permute-start(bf16[512,128]{1,0:T(8,128)(2,1)S(1)} %get-tuple-element.165), channel_id=1, source_target_pairs={{0,1},{1,0},{2,3},{3,2},{4,5},{5,4},{6,7},{7,6},{8,9},{9,8},{10,11... | collective-permute-start | bytes 393224 | tf_op jit(solution)/shard_map/ppermute | solution.py:339
  3.3 6.9 %collective-permute-start.37 = (bf16[512,128]{1,0:T(8,128)(2,1)S(1)}, bf16[512,128]{1,0:T(8,128)(2,1)S(1)}, u32[]{:S(2)}, u32[]{:S(2)}) collective-permute-start(bf16[512,128]{1,0:T(8,128)(2,1)S(1)} %get-tuple-element.166), channel_id=1, source_target_pairs={{0,2},{1,3},{2,0},{3,1},{4,6},{5,7},{6,4},{7,5},{8,10},{9,11},{10,... | collective-permute-start | bytes 393224 | tf_op jit(solution)/shard_map/ppermute | solution.py:339
  5.8 6.7 %collective-permute-start.38 = (bf16[512,128]{1,0:T(8,128)(2,1)S(1)}, bf16[512,128]{1,0:T(8,128)(2,1)S(1)}, u32[]{:S(2)}, u32[]{:S(2)}) collective-permute-start(bf16[512,128]{1,0:T(8,128)(2,1)S(1)} %get-tuple-element.167), channel_id=1, source_target_pairs={{0,3},{1,2},{2,1},{3,0},{4,7},{5,6},{6,5},{7,4},{8,11},{9,10},{10,... | collective-permute-start | bytes 393224 | tf_op jit(solution)/shard_map/ppermute | solution.py:339
  6.8 10.1 %collective-permute-start.42 = (bf16[512,128]{1,0:T(8,128)(2,1)S(1)}, bf16[512,128]{1,0:T(8,128)(2,1)S(1)}, u32[]{:S(2)}, u32[]{:S(2)}) collective-permute-start(bf16[512,128]{1,0:T(8,128)(2,1)S(1)} %get-tuple-element.173), channel_id=1, source_target_pairs={{0,1},{1,0},{2,3},{3,2},{4,5},{5,4},{6,7},{7,6},{8,9},{9,8},{10,11... | collective-permute-start | bytes 393224 | tf_op jit(solution)/shard_map/ppermute | solution.py:339
  7.0 10.2 %collective-permute-start.43 = (bf16[512,128]{1,0:T(8,128)(2,1)S(1)}, bf16[512,128]{1,0:T(8,128)(2,1)S(1)}, u32[]{:S(2)}, u32[]{:S(2)}) collective-permute-start(bf16[512,128]{1,0:T(8,128)(2,1)S(1)} %get-tuple-element.174), channel_id=1, source_target_pairs={{0,2},{1,3},{2,0},{3,1},{4,6},{5,7},{6,4},{7,5},{8,10},{9,11},{10,... | collective-permute-start | bytes 393224 | tf_op jit(solution)/shard_map/ppermute | solution.py:339
  9.0 9.1 %collective-permute-start.44 = (bf16[512,128]{1,0:T(8,128)(2,1)S(1)}, bf16[512,128]{1,0:T(8,128)(2,1)S(1)}, u32[]{:S(2)}, u32[]{:S(2)}) collective-permute-start(bf16[512,128]{1,0:T(8,128)(2,1)S(1)} %get-tuple-element.175), channel_id=1, source_target_pairs={{0,3},{1,2},{2,1},{3,0},{4,7},{5,6},{6,5},{7,4},{8,11},{9,10},{10,... | collective-permute-start | bytes 393224 | tf_op jit(solution)/shard_map/ppermute | solution.py:339
  9.6 2.9 %copy-start.11 = (s32[1,32]{1,0:T(1,128)S(1)}, s32[1,32]{1,0:T(1,128)}, u32[]{:S(2)}) copy-start(s32[1,32]{1,0:T(1,128)} %refs_0_.3) | copy-start | bytes 388
  9.6 2.9 %copy-start.12 = (s32[1,32]{1,0:T(1,128)S(1)}, s32[1,32]{1,0:T(1,128)}, u32[]{:S(2)}) copy-start(s32[1,32]{1,0:T(1,128)} %refs_1_.5) | copy-start | bytes 388
  13.7 8.7 %collective-permute-start.39 = (bf16[384,128]{1,0:T(8,128)(2,1)S(1)}, bf16[384,128]{1,0:T(8,128)(2,1)S(1)}, u32[]{:S(2)}, u32[]{:S(2)}) collective-permute-start(bf16[384,128]{1,0:T(8,128)(2,1)S(1)} %get-tuple-element.169), channel_id=1, source_target_pairs={{0,4},{1,5},{2,6},{3,7},{4,0},{5,1},{6,2},{7,3},{8,12},{9,13},{10,... | collective-permute-start | bytes 294920 | tf_op jit(solution)/shard_map/ppermute | solution.py:339
  15.3 7.5 %collective-permute-start.40 = (bf16[384,128]{1,0:T(8,128)(2,1)S(1)}, bf16[384,128]{1,0:T(8,128)(2,1)S(1)}, u32[]{:S(2)}, u32[]{:S(2)}) collective-permute-start(bf16[384,128]{1,0:T(8,128)(2,1)S(1)} %get-tuple-element.170), channel_id=1, source_target_pairs={{0,8},{1,9},{2,10},{3,11},{4,12},{5,13},{6,14},{7,15},{8,0},{9,1},... | collective-permute-start | bytes 294920 | tf_op jit(solution)/shard_map/ppermute | solution.py:339
  16.8 5.9 %collective-permute-start.41 = (bf16[384,128]{1,0:T(8,128)(2,1)S(1)}, bf16[384,128]{1,0:T(8,128)(2,1)S(1)}, u32[]{:S(2)}, u32[]{:S(2)}) collective-permute-start(bf16[384,128]{1,0:T(8,128)(2,1)S(1)} %get-tuple-element.171), channel_id=1, source_target_pairs={{0,12},{1,13},{2,14},{3,15},{4,8},{5,9},{6,10},{7,11},{8,4},{9,5},... | collective-permute-start | bytes 294920 | tf_op jit(solution)/shard_map/ppermute | solution.py:339
  18.1 10.9 %copy-start.3 = (bf16[2,256,1024]{2,1,0:T(8,128)(2,1)S(1)}, bf16[2,256,1024]{2,1,0:T(8,128)(2,1)}, u32[]{:S(2)}) copy-start(bf16[2,256,1024]{2,1,0:T(8,128)(2,1)} %w_in.13) | copy-start | bytes 3145732
  18.1 10.9 %copy-start.4 = (bf16[2,256,1024]{2,1,0:T(8,128)(2,1)S(1)}, bf16[2,256,1024]{2,1,0:T(8,128)(2,1)}, u32[]{:S(2)}) copy-start(bf16[2,256,1024]{2,1,0:T(8,128)(2,1)} %w_rec_hbm.13) | copy-start | bytes 3145732
  19.2 5.6 %collective-permute-start.45 = (bf16[384,128]{1,0:T(8,128)(2,1)S(1)}, bf16[384,128]{1,0:T(8,128)(2,1)S(1)}, u32[]{:S(2)}, u32[]{:S(2)}) collective-permute-start(bf16[384,128]{1,0:T(8,128)(2,1)S(1)} %get-tuple-element.177), channel_id=1, source_target_pairs={{0,4},{1,5},{2,6},{3,7},{4,0},{5,1},{6,2},{7,3},{8,12},{9,13},{10,... | collective-permute-start | bytes 294920 | tf_op jit(solution)/shard_map/ppermute | solution.py:339
  20.8 5.7 %collective-permute-start.46 = (bf16[384,128]{1,0:T(8,128)(2,1)S(1)}, bf16[384,128]{1,0:T(8,128)(2,1)S(1)}, u32[]{:S(2)}, u32[]{:S(2)}) collective-permute-start(bf16[384,128]{1,0:T(8,128)(2,1)S(1)} %get-tuple-element.178), channel_id=1, source_target_pairs={{0,8},{1,9},{2,10},{3,11},{4,12},{5,13},{6,14},{7,15},{8,0},{9,1},... | collective-permute-start | bytes 294920 | tf_op jit(solution)/shard_map/ppermute | solution.py:339
  22.4 5.7 %collective-permute-start.47 = (bf16[384,128]{1,0:T(8,128)(2,1)S(1)}, bf16[384,128]{1,0:T(8,128)(2,1)S(1)}, u32[]{:S(2)}, u32[]{:S(2)}) collective-permute-start(bf16[384,128]{1,0:T(8,128)(2,1)S(1)} %get-tuple-element.179), channel_id=1, source_target_pairs={{0,12},{1,13},{2,14},{3,15},{4,8},{5,9},{6,10},{7,11},{8,4},{9,5},... | collective-permute-start | bytes 294920 | tf_op jit(solution)/shard_map/ppermute | solution.py:339
  29.0 3.2 %copy-start.9 = (bf16[4,192,256]{2,1,0:T(8,128)(2,1)}, bf16[4,192,256]{2,1,0:T(8,128)(2,1)S(1)}, u32[]{:S(2)}) copy-start(bf16[4,192,256]{2,1,0:T(8,128)(2,1)S(1)} %get-tuple-element.182.refs_0_) | copy-start | bytes 1179652
  34.1 0.7 copy-start.13
  34.8 20.9 %copy-start.7 = (bf16[1,32,128,128]{3,2,1,0:T(8,128)(2,1)S(1)}, bf16[1,32,128,128]{3,2,1,0:T(8,128)(2,1)}, u32[]{:S(2)}) copy-start(bf16[1,32,128,128]{3,2,1,0:T(8,128)(2,1)} %get-tuple-element.56.refs_3_) | copy-start | bytes 3145732 | tf_op jit(solution)/shard_map/cond
  36.1 4.9 %collective-permute-start = (bf16[384,128]{1,0:T(8,128)(2,1)S(1)}, bf16[384,128]{1,0:T(8,128)(2,1)S(1)}, u32[]{:S(2)}, u32[]{:S(2)}) collective-permute-start(bf16[384,128]{1,0:T(8,128)(2,1)S(1)} %get-tuple-element.61), channel_id=1, source_target_pairs={{0,4},{1,5},{2,6},{3,7},{4,0},{5,1},{6,2},{7,3},{8,12},{9,13},{10,... | collective-permute-start | bytes 294920 | tf_op jit(solution)/shard_map/cond/branch_1_fun/ppermute | solution.py:339
  37.6 5.2 %collective-permute-start.1 = (bf16[384,128]{1,0:T(8,128)(2,1)S(1)}, bf16[384,128]{1,0:T(8,128)(2,1)S(1)}, u32[]{:S(2)}, u32[]{:S(2)}) collective-permute-start(bf16[384,128]{1,0:T(8,128)(2,1)S(1)} %get-tuple-element.62), channel_id=1, source_target_pairs={{0,8},{1,9},{2,10},{3,11},{4,12},{5,13},{6,14},{7,15},{8,0},{9,1},... | collective-permute-start | bytes 294920 | tf_op jit(solution)/shard_map/cond/branch_1_fun/ppermute | solution.py:339
  39.1 5.5 %collective-permute-start.2 = (bf16[384,128]{1,0:T(8,128)(2,1)S(1)}, bf16[384,128]{1,0:T(8,128)(2,1)S(1)}, u32[]{:S(2)}, u32[]{:S(2)}) collective-permute-start(bf16[384,128]{1,0:T(8,128)(2,1)S(1)} %get-tuple-element.63), channel_id=1, source_target_pairs={{0,12},{1,13},{2,14},{3,15},{4,8},{5,9},{6,10},{7,11},{8,4},{9,5},... | collective-permute-start | bytes 294920 | tf_op jit(solution)/shard_map/cond/branch_1_fun/ppermute | solution.py:339
  39.7 9.6 %collective-permute-start.9 = (bf16[384,128]{1,0:T(8,128)(2,1)S(1)}, bf16[384,128]{1,0:T(8,128)(2,1)S(1)}, u32[]{:S(2)}, u32[]{:S(2)}) collective-permute-start(bf16[384,128]{1,0:T(8,128)(2,1)S(1)} %get-tuple-element.73), channel_id=1, source_target_pairs={{0,4},{1,5},{2,6},{3,7},{4,0},{5,1},{6,2},{7,3},{8,12},{9,13},{10,... | collective-permute-start | bytes 294920 | tf_op jit(solution)/shard_map/cond/branch_1_fun/ppermute | solution.py:339
  45.4 9.9 %collective-permute-start.3 = (bf16[512,128]{1,0:T(8,128)(2,1)S(1)}, bf16[512,128]{1,0:T(8,128)(2,1)S(1)}, u32[]{:S(2)}, u32[]{:S(2)}) collective-permute-start(bf16[512,128]{1,0:T(8,128)(2,1)S(1)} %get-tuple-element.65), channel_id=1, source_target_pairs={{0,1},{1,0},{2,3},{3,2},{4,5},{5,4},{6,7},{7,6},{8,9},{9,8},{10,11... | collective-permute-start | bytes 393224 | tf_op jit(solution)/shard_map/cond/branch_1_fun/ppermute | solution.py:339
  45.5 5.7 %collective-permute-start.10 = (bf16[384,128]{1,0:T(8,128)(2,1)S(1)}, bf16[384,128]{1,0:T(8,128)(2,1)S(1)}, u32[]{:S(2)}, u32[]{:S(2)}) collective-permute-start(bf16[384,128]{1,0:T(8,128)(2,1)S(1)} %get-tuple-element.74), channel_id=1, source_target_pairs={{0,8},{1,9},{2,10},{3,11},{4,12},{5,13},{6,14},{7,15},{8,0},{9,1},... | collective-permute-start | bytes 294920 | tf_op jit(solution)/shard_map/cond/branch_1_fun/ppermute | solution.py:339
  46.2 6.7 %collective-permute-start.11 = (bf16[384,128]{1,0:T(8,128)(2,1)S(1)}, bf16[384,128]{1,0:T(8,128)(2,1)S(1)}, u32[]{:S(2)}, u32[]{:S(2)}) collective-permute-start(bf16[384,128]{1,0:T(8,128)(2,1)S(1)} %get-tuple-element.75), channel_id=1, source_target_pairs={{0,12},{1,13},{2,14},{3,15},{4,8},{5,9},{6,10},{7,11},{8,4},{9,5},... | collective-permute-start | bytes 294920 | tf_op jit(solution)/shard_map/cond/branch_1_fun/ppermute | solution.py:339
  47.7 7.9 %collective-permute-start.4 = (bf16[512,128]{1,0:T(8,128)(2,1)S(1)}, bf16[512,128]{1,0:T(8,128)(2,1)S(1)}, u32[]{:S(2)}, u32[]{:S(2)}) collective-permute-start(bf16[512,128]{1,0:T(8,128)(2,1)S(1)} %get-tuple-element.66), channel_id=1, source_target_pairs={{0,2},{1,3},{2,0},{3,1},{4,6},{5,7},{6,4},{7,5},{8,10},{9,11},{10,... | collective-permute-start | bytes 393224 | tf_op jit(solution)/shard_map/cond/branch_1_fun/ppermute | solution.py:339
  49.2 6.4 %collective-permute-start.5 = (bf16[512,128]{1,0:T(8,128)(2,1)S(1)}, bf16[512,128]{1,0:T(8,128)(2,1)S(1)}, u32[]{:S(2)}, u32[]{:S(2)}) collective-permute-start(bf16[512,128]{1,0:T(8,128)(2,1)S(1)} %get-tuple-element.67), channel_id=1, source_target_pairs={{0,3},{1,2},{2,1},{3,0},{4,7},{5,6},{6,5},{7,4},{8,11},{9,10},{10,... | collective-permute-start | bytes 393224 | tf_op jit(solution)/shard_map/cond/branch_1_fun/ppermute | solution.py:339
  53.7 5.8 %collective-permute-start.12 = (bf16[512,128]{1,0:T(8,128)(2,1)S(1)}, bf16[512,128]{1,0:T(8,128)(2,1)S(1)}, u32[]{:S(2)}, u32[]{:S(2)}) collective-permute-start(bf16[512,128]{1,0:T(8,128)(2,1)S(1)} %get-tuple-element.77), channel_id=1, source_target_pairs={{0,1},{1,0},{2,3},{3,2},{4,5},{5,4},{6,7},{7,6},{8,9},{9,8},{10,11... | collective-permute-start | bytes 393224 | tf_op jit(solution)/shard_map/cond/branch_1_fun/ppermute | solution.py:339
  53.8 7.2 %collective-permute-start.13 = (bf16[512,128]{1,0:T(8,128)(2,1)S(1)}, bf16[512,128]{1,0:T(8,128)(2,1)S(1)}, u32[]{:S(2)}, u32[]{:S(2)}) collective-permute-start(bf16[512,128]{1,0:T(8,128)(2,1)S(1)} %get-tuple-element.78), channel_id=1, source_target_pairs={{0,2},{1,3},{2,0},{3,1},{4,6},{5,7},{6,4},{7,5},{8,10},{9,11},{10,... | collective-permute-start | bytes 393224 | tf_op jit(solution)/shard_map/cond/branch_1_fun/ppermute | solution.py:339
  55.4 6.6 %collective-permute-start.14 = (bf16[512,128]{1,0:T(8,128)(2,1)S(1)}, bf16[512,128]{1,0:T(8,128)(2,1)S(1)}, u32[]{:S(2)}, u32[]{:S(2)}) collective-permute-start(bf16[512,128]{1,0:T(8,128)(2,1)S(1)} %get-tuple-element.79), channel_id=1, source_target_pairs={{0,3},{1,2},{2,1},{3,0},{4,7},{5,6},{6,5},{7,4},{8,11},{9,10},{10,... | collective-permute-start | bytes 393224 | tf_op jit(solution)/shard_map/cond/branch_1_fun/ppermute | solution.py:339
  57.4 8.3 %collective-permute-start.6 = (bf16[384,128]{1,0:T(8,128)(2,1)S(1)}, bf16[384,128]{1,0:T(8,128)(2,1)S(1)}, u32[]{:S(2)}, u32[]{:S(2)}) collective-permute-start(bf16[384,128]{1,0:T(8,128)(2,1)S(1)} %get-tuple-element.69), channel_id=1, source_target_pairs={{0,4},{1,5},{2,6},{3,7},{4,0},{5,1},{6,2},{7,3},{8,12},{9,13},{10,... | collective-permute-start | bytes 294920 | tf_op jit(solution)/shard_map/cond/branch_1_fun/ppermute | solution.py:339
  58.8 8.5 %collective-permute-start.7 = (bf16[384,128]{1,0:T(8,128)(2,1)S(1)}, bf16[384,128]{1,0:T(8,128)(2,1)S(1)}, u32[]{:S(2)}, u32[]{:S(2)}) collective-permute-start(bf16[384,128]{1,0:T(8,128)(2,1)S(1)} %get-tuple-element.70), channel_id=1, source_target_pairs={{0,8},{1,9},{2,10},{3,11},{4,12},{5,13},{6,14},{7,15},{8,0},{9,1},... | collective-permute-start | bytes 294920 | tf_op jit(solution)/shard_map/cond/branch_1_fun/ppermute | solution.py:339
  59.5 7.8 %collective-permute-start.8 = (bf16[384,128]{1,0:T(8,128)(2,1)S(1)}, bf16[384,128]{1,0:T(8,128)(2,1)S(1)}, u32[]{:S(2)}, u32[]{:S(2)}) collective-permute-start(bf16[384,128]{1,0:T(8,128)(2,1)S(1)} %get-tuple-element.71), channel_id=1, source_target_pairs={{0,12},{1,13},{2,14},{3,15},{4,8},{5,9},{6,10},{7,11},{8,4},{9,5},... | collective-permute-start | bytes 294920 | tf_op jit(solution)/shard_map/cond/branch_1_fun/ppermute | solution.py:339
  63.7 5.4 %collective-permute-start.15 = (bf16[384,128]{1,0:T(8,128)(2,1)S(1)}, bf16[384,128]{1,0:T(8,128)(2,1)S(1)}, u32[]{:S(2)}, u32[]{:S(2)}) collective-permute-start(bf16[384,128]{1,0:T(8,128)(2,1)S(1)} %get-tuple-element.81), channel_id=1, source_target_pairs={{0,4},{1,5},{2,6},{3,7},{4,0},{5,1},{6,2},{7,3},{8,12},{9,13},{10,... | collective-permute-start | bytes 294920 | tf_op jit(solution)/shard_map/cond/branch_1_fun/ppermute | solution.py:339
  65.1 5.7 %collective-permute-start.16 = (bf16[384,128]{1,0:T(8,128)(2,1)S(1)}, bf16[384,128]{1,0:T(8,128)(2,1)S(1)}, u32[]{:S(2)}, u32[]{:S(2)}) collective-permute-start(bf16[384,128]{1,0:T(8,128)(2,1)S(1)} %get-tuple-element.82), channel_id=1, source_target_pairs={{0,8},{1,9},{2,10},{3,11},{4,12},{5,13},{6,14},{7,15},{8,0},{9,1},... | collective-permute-start | bytes 294920 | tf_op jit(solution)/shard_map/cond/branch_1_fun/ppermute | solution.py:339
  65.8 6.7 %collective-permute-start.17 = (bf16[384,128]{1,0:T(8,128)(2,1)S(1)}, bf16[384,128]{1,0:T(8,128)(2,1)S(1)}, u32[]{:S(2)}, u32[]{:S(2)}) collective-permute-start(bf16[384,128]{1,0:T(8,128)(2,1)S(1)} %get-tuple-element.83), channel_id=1, source_target_pairs={{0,12},{1,13},{2,14},{3,15},{4,8},{5,9},{6,10},{7,11},{8,4},{9,5},... | collective-permute-start | bytes 294920 | tf_op jit(solution)/shard_map/cond/branch_1_fun/ppermute | solution.py:339
  73.5 6.6 %collective-permute-start.48 = (bf16[2,192,256]{2,1,0:T(8,128)(2,1)S(1)}, bf16[2,192,256]{2,1,0:T(8,128)(2,1)S(1)}, u32[]{:S(2)}, u32[]{:S(2)}) collective-permute-start(bf16[2,192,256]{2,1,0:T(8,128)(2,1)S(1)} %get-tuple-element.186), channel_id=1, source_target_pairs={{0,16},{1,17},{2,18},{3,19},{4,20},{5,21},{6,22},{7,23},{8,24},{9,... | collective-permute-start | bytes 589832 | tf_op jit(solution)/shard_map/ppermute | solution.py:339
  74.8 8.4 %collective-permute-start.49 = (bf16[2,192,256]{2,1,0:T(8,128)(2,1)S(1)}, bf16[2,192,256]{2,1,0:T(8,128)(2,1)S(1)}, u32[]{:S(2)}, u32[]{:S(2)}) collective-permute-start(bf16[2,192,256]{2,1,0:T(8,128)(2,1)S(1)} %get-tuple-element.187), channel_id=1, source_target_pairs={{0,16},{1,17},{2,18},{3,19},{4,20},{5,21},{6,22},{7,23},{8,24},{9,... | collective-permute-start | bytes 589832 | tf_op jit(solution)/shard_map/ppermute | solution.py:339
  76.1 4.0 %copy-start.5 = (bf16[2,256,1024]{2,1,0:T(8,128)(2,1)S(1)}, bf16[2,256,1024]{2,1,0:T(8,128)(2,1)}, u32[]{:S(2)}) copy-start(bf16[2,256,1024]{2,1,0:T(8,128)(2,1)} %w_rec_hbm.13) | copy-start | bytes 3145732
  83.2 58.3 %collective-permute-start.50 = (bf16[2,192,256]{2,1,0:T(8,128)(2,1)S(1)}, bf16[2,192,256]{2,1,0:T(8,128)(2,1)S(1)}, u32[]{:S(2)}, u32[]{:S(2)}) collective-permute-start(bf16[2,192,256]{2,1,0:T(8,128)(2,1)S(1)} %get-tuple-element.191), channel_id=1, source_target_pairs={{0,16},{1,17},{2,18},{3,19},{4,20},{5,21},{6,22},{7,23},{8,24},{9,... | collective-permute-start | bytes 589832 | tf_op jit(solution)/shard_map/ppermute | solution.py:339
  138.9 14.4 %collective-permute-start.54 = (bf16[2,192,256]{2,1,0:T(8,128)(2,1)S(1)}, bf16[2,192,256]{2,1,0:T(8,128)(2,1)S(1)}, u32[]{:S(2)}, u32[]{:S(2)}) collective-permute-start(bf16[2,192,256]{2,1,0:T(8,128)(2,1)S(1)} %get-tuple-element.199), channel_id=1, source_target_pairs={{0,16},{1,17},{2,18},{3,19},{4,20},{5,21},{6,22},{7,23},{8,24},{9,... | collective-permute-start | bytes 589832 | tf_op jit(solution)/shard_map/ppermute | solution.py:339
  141.4 11.8 %copy-start.10 = (bf16[4,192,256]{2,1,0:T(8,128)(2,1)S(1)}, bf16[4,192,256]{2,1,0:T(8,128)(2,1)}, u32[]{:S(2)}) copy-start(bf16[4,192,256]{2,1,0:T(8,128)(2,1)} %get-tuple-element.196.refs_0_) | copy-start | bytes 1179652
  142.5 13.5 %collective-permute-start.51 = (bf16[192,256]{1,0:T(8,128)(2,1)S(1)}, bf16[192,256]{1,0:T(8,128)(2,1)S(1)}, u32[]{:S(2)}, u32[]{:S(2)}) collective-permute-start(bf16[192,256]{1,0:T(8,128)(2,1)S(1)} %get-tuple-element.193), channel_id=1, source_target_pairs={{0,4},{1,5},{2,6},{3,7},{4,0},{5,1},{6,2},{7,3},{8,12},{9,13},{10,... | collective-permute-start | bytes 294920 | tf_op jit(solution)/shard_map/ppermute | solution.py:339
  143.2 14.2 %collective-permute-start.52 = (bf16[192,256]{1,0:T(8,128)(2,1)S(1)}, bf16[192,256]{1,0:T(8,128)(2,1)S(1)}, u32[]{:S(2)}, u32[]{:S(2)}) collective-permute-start(bf16[192,256]{1,0:T(8,128)(2,1)S(1)} %get-tuple-element.194), channel_id=1, source_target_pairs={{0,8},{1,9},{2,10},{3,11},{4,12},{5,13},{6,14},{7,15},{8,0},{9,1},... | collective-permute-start | bytes 294920 | tf_op jit(solution)/shard_map/ppermute | solution.py:339
  152.4 6.6 %collective-permute-start.53 = (bf16[192,256]{1,0:T(8,128)(2,1)S(1)}, bf16[192,256]{1,0:T(8,128)(2,1)S(1)}, u32[]{:S(2)}, u32[]{:S(2)}) collective-permute-start(bf16[192,256]{1,0:T(8,128)(2,1)S(1)} %get-tuple-element.195), channel_id=1, source_target_pairs={{0,12},{1,13},{2,14},{3,15},{4,8},{5,9},{6,10},{7,11},{8,4},{9,5},... | collective-permute-start | bytes 294920 | tf_op jit(solution)/shard_map/ppermute | solution.py:339
  153.3 5.7 %collective-permute-start.55 = (bf16[192,256]{1,0:T(8,128)(2,1)S(1)}, bf16[192,256]{1,0:T(8,128)(2,1)S(1)}, u32[]{:S(2)}, u32[]{:S(2)}) collective-permute-start(bf16[192,256]{1,0:T(8,128)(2,1)S(1)} %get-tuple-element.201), channel_id=1, source_target_pairs={{0,4},{1,5},{2,6},{3,7},{4,0},{5,1},{6,2},{7,3},{8,12},{9,13},{10,... | collective-permute-start | bytes 294920 | tf_op jit(solution)/shard_map/ppermute | solution.py:339
  154.0 6.3 %collective-permute-start.56 = (bf16[192,256]{1,0:T(8,128)(2,1)S(1)}, bf16[192,256]{1,0:T(8,128)(2,1)S(1)}, u32[]{:S(2)}, u32[]{:S(2)}) collective-permute-start(bf16[192,256]{1,0:T(8,128)(2,1)S(1)} %get-tuple-element.202), channel_id=1, source_target_pairs={{0,8},{1,9},{2,10},{3,11},{4,12},{5,13},{6,14},{7,15},{8,0},{9,1},... | collective-permute-start | bytes 294920 | tf_op jit(solution)/shard_map/ppermute | solution.py:339
  156.0 6.2 %collective-permute-start.57 = (bf16[192,256]{1,0:T(8,128)(2,1)S(1)}, bf16[192,256]{1,0:T(8,128)(2,1)S(1)}, u32[]{:S(2)}, u32[]{:S(2)}) collective-permute-start(bf16[192,256]{1,0:T(8,128)(2,1)S(1)} %get-tuple-element.203), channel_id=1, source_target_pairs={{0,12},{1,13},{2,14},{3,15},{4,8},{5,9},{6,10},{7,11},{8,4},{9,5},... | collective-permute-start | bytes 294920 | tf_op jit(solution)/shard_map/ppermute | solution.py:339

commit v4 on v1

--- a/solution.py
+++ b/solution.py
@@ -47,7 +47,13 @@
         sources = refs[:part_count]
         first_out = part_count + len(carried)
         outs = refs[first_out : first_out + slab_count]
-        table, table_sem, rows, sems = refs[-4:]
+        table, table_sem, rows, sems, carry_sems = refs[-5:]
+        moves = [
+            pltpu.make_async_copy(
+                refs[part_count + n], refs[first_out + slab_count + n], carry_sems.at[n]
+            )
+            for n in range(len(carried))
+        ]
         slab = lax.axis_index("slab")
         _, _, lead = seat(group)
         fetch = pltpu.make_async_copy(table_hbm, table, table_sem)
@@ -68,17 +74,16 @@
                     copies.append(pltpu.make_async_copy(source, target, sems.at[k, j]))
                 else:
                     outs[k][j * tile : (j + 1) * tile, :] = rows[pl.ds(start, tile), :]
+        copies += moves
         for copy in copies:
             copy.start()
-        for n in range(len(carried)):
-            refs[first_out + slab_count + n][...] = refs[part_count + n][...]
         for copy in copies:
             copy.wait()
 
     dtype = parts[0].dtype
     results = pl.pallas_call(
         kernel,
-        in_specs=[HBM] + [HBM if whole else VMEM] * part_count + [VMEM] * len(carried),
+        in_specs=[HBM] + [HBM if whole else VMEM] * part_count + [HBM] * len(carried),
         out_specs=[VMEM] * (slab_count + len(carried)),
         out_shape=[jax.ShapeDtypeStruct((listed * tile, LANES), dtype)] * slab_count
         + [jax.ShapeDtypeStruct(array.shape, array.dtype) for array in carried],
@@ -87,6 +92,7 @@
             pltpu.SemaphoreType.DMA(()),
             pltpu.VMEM((tile if whole else row_count, LANES), dtype),
             pltpu.SemaphoreType.DMA((slab_count, listed)),
+            pltpu.SemaphoreType.DMA((max(len(carried), 1),)),
         ],
         compiler_params=PARAMS,
         name="pick_tiles",
@@ -94,11 +100,12 @@
     return results[:slab_count], results[slab_count:]
 
 
-def convolve(arrived, tile_rows, tile_sources, tile_counts, tile_values, row_count, group):
+def convolve(arrived, tile_rows, tile_sources, tile_counts, tile_values, row_count, group, chunks):
     slab_count = len(arrived)
     piece, width = arrived[0].shape
     tile = tile_values.shape[2]
-    group_rows = row_count // group
+    size = row_count // group // chunks
+    count_out = group * chunks
 
     tables = (tile_rows, tile_sources, tile_counts)
     unroll = min(UNROLL, tile_values.shape[1])
@@ -106,8 +113,8 @@
     def kernel(*refs):
         values = refs[3]
         pieces = refs[4 : 4 + slab_count]
-        outs = refs[4 + slab_count : 4 + slab_count + group]
-        rows, sources, counts, sems, inputs, total = refs[4 + slab_count + group :]
+        outs = refs[4 + slab_count : 4 + slab_count + count_out]
+        rows, sources, counts, sems, inputs, total = refs[4 + slab_count + count_out :]
         slab = lax.axis_index("slab")
         _, _, lead = seat(group)
         fetches = [
@@ -141,16 +148,17 @@
             return carry
 
         lax.fori_loop(0, (count + unroll - 1) // unroll, step, 0)
-        for k in range(group):
-            start = pl.multiple_of((lead ^ k) * group_rows, group_rows)
-            outs[k][...] = total[pl.ds(start, group_rows), :].astype(outs[k].dtype)
+        for n in range(count_out):
+            start = (lead ^ (n % group)) * (size * chunks) + n // group * size
+            rounded = total[pl.ds(pl.multiple_of(start, size), size), :]
+            outs[n][...] = rounded.astype(outs[n].dtype)
 
     dtype = arrived[0].dtype
-    return pl.pallas_call(
+    results = pl.pallas_call(
         kernel,
         in_specs=[HBM, HBM, HBM, VMEM] + [VMEM] * slab_count,
-        out_specs=[VMEM] * group,
-        out_shape=[jax.ShapeDtypeStruct((group_rows, width), dtype)] * group,
+        out_specs=[VMEM] * count_out,
+        out_shape=[jax.ShapeDtypeStruct((size, width), dtype)] * count_out,
         scratch_shapes=[pltpu.SMEM(table.shape, table.dtype) for table in tables]
         + [
             pltpu.SemaphoreType.DMA((3,)),
@@ -160,6 +168,7 @@
         compiler_params=PARAMS,
         name="convolve",
     )(*tables, tile_values, *arrived)
+    return [results[n : n + group] for n in range(0, count_out, group)]
 
 
 def sigmoid(value):
@@ -189,6 +198,30 @@
         compiler_params=PARAMS,
         name="pack",
     )(*blocks))
+
+
+def pack_chunk(mixed, chunk):
+    columns, group = len(mixed), len(mixed[0])
+    size = min(column[0].shape[0] for column in mixed)
+    lanes = mixed[0][0].shape[1]
+    blocks = [part for column in mixed for part in column]
+
+    def kernel(*refs):
+        _, place, _ = seat(group)
+        for n in range(len(blocks)):
+            first = n // group * lanes
+            base = chunk * size if blocks[n].shape[0] > size else 0
+            source = refs[n][base : base + size, :]
+            refs[-1][place ^ (n % group), :, first : first + lanes] = source
+
+    return pl.pallas_call(
+        kernel,
+        in_specs=[VMEM] * len(blocks),
+        out_specs=VMEM,
+        out_shape=jax.ShapeDtypeStruct((group, size, columns * lanes), blocks[0].dtype),
+        compiler_params=PARAMS,
+        name="pack_chunk",
+    )(*blocks)
 
 
 def spread_into(outs, chunks, place, group):
@@ -378,13 +411,15 @@
     def pick(parts, table, column=0, carried=()):
         return pick_tiles(parts, table, slab_count, row_count, tile, group, column, carried)
 
-    def mix(listed):
+    def mix(listed, chunks=1):
         arrived = swap_slabs(listed)
-        return swap_times(
-            convolve(
-                arrived, tile_rows, tile_sources, tile_counts, tile_values, row_count, group
-            )
+        mixed = convolve(
+            arrived, tile_rows, tile_sources, tile_counts, tile_values, row_count, group, chunks
         )
+        got = []
+        for part in mixed:
+            got.append(swap_times(part))
+        return got if chunks > 1 else got[0]
 
     def back_and_mix(hidden):
         return pack([mix(pick(swap_times(column), table)[0]) for column in hidden])
@@ -407,7 +442,10 @@
     columns = features.shape[1] // LANES
     listed = [pick([features], ref_lists, column)[0] for column in range(columns - 1)]
     last, (table, gate_bias) = pick([features], ref_lists, columns - 1, (ref_lists, bias))
-    upper_mixed = pack([mix(column) for column in [*listed, last]])
+    early = [mix(column) for column in listed]
+    upper_mixed = [
+        pack_chunk([*early, part], chunk) for chunk, part in enumerate(mix(last, CHUNKS))
+    ]
     hidden, handed = run_lower(upper_mixed, 0)
     for layer in range(1, layers):
 

time: 164 us -> 169 us (1.030)
  starting transfers between devices: 103 us -> 108 us
    ppermute x40 -> x43, starting transfers between devices: 103 us -> 108 us  [send(): return lax.ppermute(array, AXES, pairs)]
    ppermute x40 -> x43, waiting for transfers between devices: 29.8 us -> 29.7 us  [send(): return lax.ppermute(array, AXES, pairs)]
  transfers between devices with their start and end apart: 40 -> 43, of which waited for: 20 -> 20; matrix products, arithmetic and copies ran while one was open for 0% -> 0% of each run, Pallas kernels for 10% -> 12%
where the time goes in v4:
time: 169 us; the launch traced here: 167 us
  starting transfers between devices  108 us (64%)
  waiting for transfers between devices  29.7 us (18%)
  Pallas kernels  25.5 us (15%)
  local copies, waits for them, and re-layouts  3.21 us (2%)
    ppermute x43, starting transfers between devices, send(): return lax.ppermute(array, AXES, pairs)  108 us
    ppermute x43, waiting for transfers between devices, send(): return lax.ppermute(array, AXES, pairs)  29.7 us
    pallas_call x7, Pallas kernels, recur(): pl.pallas_call(kernel, in_specs=[VMEM] * (3 + len(operands)), out_specs=[...  12.1 us
    pallas_call x4, Pallas kernels, convolve(): pl.pallas_call(kernel, in_specs=[HBM, HBM, HBM, VMEM] + [VMEM] * slab_cou...  5.84 us
  transfers between devices with their start and end apart: 43, of which 20 were waited for; matrix products, arithmetic and copies ran while one was open for 0% of the time, Pallas kernels for 12%

profile of v4, /device:TPU:0, one launch (start us, length us, event | category | flops | bytes accessed | tf_op | source)
XLA Modules:
  0.0 167.1 jit_solution(1942542456035381423)
XLA Ops:
  0.0 1.1 copy-done
  2.5 0.9 pick_tiles.10
  4.0 2.6 %collective-permute-start.43 = (bf16[512,128]{1,0:T(8,128)(2,1)S(1)}, bf16[512,128]{1,0:T(8,128)(2,1)S(1)}, u32[]{:S(2)}, u32[]{:S(2)}) collective-permute-start(bf16[512,128]{1,0:T(8,128)(2,1)S(1)} %get-tuple-element.176), channel_id=1, source_target_pairs={{0,2},{1,3},{2,0},{3,1},{4,6},{5,7},{6,4},{7,5},{8,10},{9,11},{10,... | collective-permute-start | bytes 393224 | tf_op jit(solution)/shard_map/ppermute | solution.py:379
  6.6 0.9 pick_tiles.11
  7.7 1.9 %collective-permute-start.37 = (bf16[512,128]{1,0:T(8,128)(2,1)S(1)}, bf16[512,128]{1,0:T(8,128)(2,1)S(1)}, u32[]{:S(2)}, u32[]{:S(2)}) collective-permute-start(bf16[512,128]{1,0:T(8,128)(2,1)S(1)} %get-tuple-element.168), channel_id=1, source_target_pairs={{0,2},{1,3},{2,0},{3,1},{4,6},{5,7},{6,4},{7,5},{8,10},{9,11},{10,... | collective-permute-start | bytes 393224 | tf_op jit(solution)/shard_map/ppermute | solution.py:379
  10.9 2.4 %collective-permute-done.44.refs_7_ = bf16[512,128]{1,0:T(8,128)(2,1)S(1)} collective-permute-done((bf16[512,128]{1,0:T(8,128)(2,1)S(1)}, bf16[512,128]{1,0:T(8,128)(2,1)S(1)}, u32[]{:S(2)}, u32[]{:S(2)}) %collective-permute-start.44) | collective-permute-done | bytes 131104 | tf_op jit(solution)/shard_map/ppermute | solution.py:379
  13.3 1.1 convolve.11
  14.4 1.6 collective-permute-start.45
  16.5 2.3 %collective-permute-done.38.refs_7_ = bf16[512,128]{1,0:T(8,128)(2,1)S(1)} collective-permute-done((bf16[512,128]{1,0:T(8,128)(2,1)S(1)}, bf16[512,128]{1,0:T(8,128)(2,1)S(1)}, u32[]{:S(2)}, u32[]{:S(2)}) %collective-permute-start.38) | collective-permute-done | bytes 131104 | tf_op jit(solution)/shard_map/ppermute | solution.py:379
  18.8 1.1 convolve.10
  20.0 1.6 collective-permute-start.39
  21.5 1.6 collective-permute-start.40
  23.5 1.6 collective-permute-start.46
  25.1 1.4 collective-permute-start.47
  26.5 3.5 %collective-permute-done.46.refs_6_ = bf16[192,128]{1,0:T(8,128)(2,1)S(1)} collective-permute-done((bf16[192,128]{1,0:T(8,128)(2,1)S(1)}, bf16[192,128]{1,0:T(8,128)(2,1)S(1)}, u32[]{:S(2)}, u32[]{:S(2)}) %collective-permute-start.46) | collective-permute-done | bytes 49184 | tf_op jit(solution)/shard_map/ppermute | solution.py:379
  30.6 1.4 collective-permute-start.49
  32.1 1.4 collective-permute-start.50
  33.5 0.8 pack_chunk.2.refs_0_
  34.3 2.8 %recur.9 = (bf16[4,192,256]{2,1,0:T(8,128)(2,1)}, bf16[2,192,256]{2,1,0:T(8,128)(2,1)S(1)}) custom-call(bf16[2,256,1024]{2,1,0:T(8,128)(2,1)S(1)} %copy-done.3, bf16[2,256,1024]{2,1,0:T(8,128)(2,1)S(1)} %copy-done.4, f32[2,1024]{1,0:T(2,128)S(1)} %get-tuple-element.165.gate_bias, bf16[4,192,256]{2,1,0:T(8,128)(2,1)} %pack_chunk.2.refs_0_), custom_call_target="tpu_custom_call" | custom-call | tf_op jit(solution)/shard_map/recur/pallas_call | solution.py:327
  37.3 1.8 %recur.10 = (bf16[4,192,256]{2,1,0:T(8,128)(2,1)}, bf16[2,192,256]{2,1,0:T(8,128)(2,1)S(1)}) custom-call(bf16[2,256,1024]{2,1,0:T(8,128)(2,1)S(1)} %copy-done.3, bf16[2,256,1024]{2,1,0:T(8,128)(2,1)S(1)} %copy-done.4, f32[2,1024]{1,0:T(2,128)S(1)} %get-tuple-element.165.gate_bias, bf16[4,192,256]{2,1,0:T(8,128)(2,1)S(1)} %pack_chunk.3.refs_0_), custom_call_target="tpu_custom_call" | custom-call | tf_op jit(solution)/shard_map/recur/pallas_call | solution.py:327
  39.8 38.7 %conditional.2 = (bf16[4,192,256]{2,1,0:T(8,128)(2,1)}, bf16[4,192,256]{2,1,0:T(8,128)(2,1)}, s32[]{:T(128)}) conditional(s32[]{:T(128)} %convert_element_type.6, (bf16[4,192,256]{2,1,0:T(8,128)(2,1)}, bf16[4,192,256]{2,1,0:T(8,128)(2,1)}, s32[]{:T(128)}) %tuple.18, (bf16[4,192,256]{2,1,0:T(8,128)(2,1)}, bf16[4,192,256]{2,1,0:T(8,128)(2,1)}, ...), branch_computations={%region_0.1_spmd, %region_1.2_spmd} | conditional | flops 1 | bytes 12059408 | solution.py:458
  39.8 1.3 spread.1
  41.1 1.5 collective-permute-start
  43.3 1.4 collective-permute-start.2
  44.7 1.4 collective-permute-start.9
  46.1 1.6 collective-permute-done.refs_1_
  47.7 1.1 collective-permute-done.2.refs_3_
  49.7 1.4 collective-permute-start.10
  51.1 1.7 collective-permute-start.11
  52.8 1.5 collective-permute-start.4
  54.3 1.2 collective-permute-done.10.refs_2_
  55.4 2.5 %collective-permute-done.11.refs_3_ = bf16[384,128]{1,0:T(8,128)(2,1)S(1)} collective-permute-done((bf16[384,128]{1,0:T(8,128)(2,1)S(1)}, bf16[384,128]{1,0:T(8,128)(2,1)S(1)}, u32[]{:S(2)}, u32[]{:S(2)}) %collective-permute-start.11) | collective-permute-done | bytes 98336 | tf_op jit(solution)/shard_map/cond/branch_1_fun/ppermute | solution.py:379
  58.8 1.6 collective-permute-start.13
  60.7 1.8 %convolve.6 = (bf16[384,128]{1,0:T(8,128)(2,1)S(1)}, bf16[384,128]{1,0:T(8,128)(2,1)S(1)}, bf16[384,128]{1,0:T(8,128)(2,1)S(1)}, bf16[384,128]{1,0:T(8,128)(2,1)S(1)}) custom-call(s32[1,32]{1,0:T(1,128)S(1)} %get-tuple-element.53.refs_0_, s32[1,32]{1,0:T(1,128)S(1)} %get-tuple-element.54.refs_1_, s32[1,1]{1,0:T(1,128)} %get-tuple-element.55.refs_2_, ...), custom_call_target="tpu_custom_call" | custom-call | tf_op jit(solution)/shard_map/cond/branch_1_fun/convolve/pallas_call | solution.py:157
  63.0 1.3 collective-permute-start.7
  64.4 1.7 %collective-permute-start.8 = (bf16[384,128]{1,0:T(8,128)(2,1)S(1)}, bf16[384,128]{1,0:T(8,128)(2,1)S(1)}, u32[]{:S(2)}, u32[]{:S(2)}) collective-permute-start(bf16[384,128]{1,0:T(8,128)(2,1)S(1)} %get-tuple-element.71), channel_id=1, source_target_pairs={{0,12},{1,13},{2,14},{3,15},{4,8},{5,9},{6,10},{7,11},{8,4},{9,5},... | collective-permute-start | bytes 294920 | tf_op jit(solution)/shard_map/cond/branch_1_fun/ppermute | solution.py:379
  66.0 0.9 collective-permute-done.14.refs_7_
  67.0 1.8 %convolve.7 = (bf16[384,128]{1,0:T(8,128)(2,1)S(1)}, bf16[384,128]{1,0:T(8,128)(2,1)S(1)}, bf16[384,128]{1,0:T(8,128)(2,1)S(1)}, bf16[384,128]{1,0:T(8,128)(2,1)S(1)}) custom-call(s32[1,32]{1,0:T(1,128)S(1)} %get-tuple-element.53.refs_0_, s32[1,32]{1,0:T(1,128)S(1)} %get-tuple-element.54.refs_1_, s32[1,1]{1,0:T(1,128)} %get-tuple-element.55.refs_2_, ...), custom_call_target="tpu_custom_call" | custom-call | tf_op jit(solution)/shard_map/cond/branch_1_fun/convolve/pallas_call | solution.py:157
  69.3 1.3 collective-permute-start.16
  70.7 1.7 %collective-permute-start.17 = (bf16[384,128]{1,0:T(8,128)(2,1)S(1)}, bf16[384,128]{1,0:T(8,128)(2,1)S(1)}, u32[]{:S(2)}, u32[]{:S(2)}) collective-permute-start(bf16[384,128]{1,0:T(8,128)(2,1)S(1)} %get-tuple-element.83), channel_id=1, source_target_pairs={{0,12},{1,13},{2,14},{3,15},{4,8},{5,9},{6,10},{7,11},{8,4},{9,5},... | collective-permute-start | bytes 294920 | tf_op jit(solution)/shard_map/cond/branch_1_fun/ppermute | solution.py:379
  72.3 1.8 %collective-permute-done.15.refs_5_ = bf16[384,128]{1,0:T(8,128)(2,1)S(1)} collective-permute-done((bf16[384,128]{1,0:T(8,128)(2,1)S(1)}, bf16[384,128]{1,0:T(8,128)(2,1)S(1)}, u32[]{:S(2)}, u32[]{:S(2)}) %collective-permute-start.15) | collective-permute-done | bytes 98336 | tf_op jit(solution)/shard_map/cond/branch_1_fun/ppermute | solution.py:379
  74.2 0.8 collective-permute-done.16.refs_6_
  75.0 2.5 %collective-permute-done.17.refs_7_ = bf16[384,128]{1,0:T(8,128)(2,1)S(1)} collective-permute-done((bf16[384,128]{1,0:T(8,128)(2,1)S(1)}, bf16[384,128]{1,0:T(8,128)(2,1)S(1)}, u32[]{:S(2)}, u32[]{:S(2)}) %collective-permute-start.17) | collective-permute-done | bytes 98336 | tf_op jit(solution)/shard_map/cond/branch_1_fun/ppermute | solution.py:379
  77.5 1.0 pack.2
  78.5 1.3 collective-permute-start.51
  79.8 1.3 collective-permute-start.52
  81.2 2.5 %recur.12 = (bf16[4,192,256]{2,1,0:T(8,128)(2,1)S(1)}, bf16[2,192,256]{2,1,0:T(8,128)(2,1)S(1)}) custom-call(bf16[2,256,1024]{2,1,0:T(8,128)(2,1)S(1)} %copy-done.3, bf16[2,256,1024]{2,1,0:T(8,128)(2,1)} %w_rec.13, f32[2,1024]{1,0:T(2,128)S(1)} %get-tuple-element.165.gate_bias, bf16[4,192,256]{2,1,0:T(8,128)(2,1)} %get-tuple-element.193.refs_0_), custom_call_target="tpu_custom_call" | custom-call | tf_op jit(solution)/shard_map/recur/pallas_call | solution.py:327
  83.6 1.5 collective-permute-done.51.refs_1_
  85.1 1.8 %recur.11 = bf16[4,192,256]{2,1,0:T(8,128)(2,1)} custom-call(bf16[2,256,1024]{2,1,0:T(8,128)(2,1)S(1)} %copy-done.3, bf16[2,256,1024]{2,1,0:T(8,128)(2,1)S(1)} %copy-done.5, f32[2,1024]{1,0:T(2,128)S(1)} %get-tuple-element.165.gate_bias, bf16[4,192,256]{2,1,0:T(8,128)(2,1)} %pack_chunk.2.refs_0_, bf16[2,192,256]{2,1,0:T(8,128)(2,1)S(1)} %collective-permute-done.51.refs_1_), custom_call_target="tpu_custom_call" | custom-call | tf_op jit(solution)/shard_map/recur/pallas_call | solution.py:327
  86.9 1.3 collective-permute-done.52
  88.2 52.6 %collective-permute-start.53 = (bf16[2,192,256]{2,1,0:T(8,128)(2,1)S(1)}, bf16[2,192,256]{2,1,0:T(8,128)(2,1)S(1)}, u32[]{:S(2)}, u32[]{:S(2)}) collective-permute-start(bf16[2,192,256]{2,1,0:T(8,128)(2,1)S(1)} %get-tuple-element.195), channel_id=1, source_target_pairs={{0,24},{1,25},{2,26},{3,27},{4,28},{5,29},{6,30},{7,31},{8,16},{9,... | collective-permute-start | bytes 589832 | tf_op jit(solution)/shard_map/ppermute | solution.py:379
  140.8 2.1 %recur.14 = (bf16[4,192,256]{2,1,0:T(8,128)(2,1)S(1)}, bf16[2,192,256]{2,1,0:T(8,128)(2,1)S(1)}) custom-call(bf16[2,256,1024]{2,1,0:T(8,128)(2,1)S(1)} %copy-done.3, bf16[2,256,1024]{2,1,0:T(8,128)(2,1)S(1)} %copy-done.5, f32[2,1024]{1,0:T(2,128)S(1)} %get-tuple-element.165.gate_bias, bf16[4,192,256]{2,1,0:T(8,128)(2,1)} %get-tuple-element.201.refs_0_), custom_call_target="tpu_custom_call" | custom-call | tf_op jit(solution)/shard_map/recur/pallas_call | solution.py:327
  142.8 1.3 collective-permute-start.57
  144.2 1.4 collective-permute-done.53.refs_2_
  145.5 1.1 recur.13
  146.6 1.5 collective-permute-start.54
  148.0 8.8 %collective-permute-start.55 = (bf16[192,256]{1,0:T(8,128)(2,1)S(1)}, bf16[192,256]{1,0:T(8,128)(2,1)S(1)}, u32[]{:S(2)}, u32[]{:S(2)}) collective-permute-start(bf16[192,256]{1,0:T(8,128)(2,1)S(1)} %get-tuple-element.198), channel_id=1, source_target_pairs={{0,8},{1,9},{2,10},{3,11},{4,12},{5,13},{6,14},{7,15},{8,0},{9,1},... | collective-permute-start | bytes 294920 | tf_op jit(solution)/shard_map/ppermute | solution.py:379
  157.2 1.2 collective-permute-start.58
  158.4 2.0 %collective-permute-start.59 = (bf16[192,256]{1,0:T(8,128)(2,1)S(1)}, bf16[192,256]{1,0:T(8,128)(2,1)S(1)}, u32[]{:S(2)}, u32[]{:S(2)}) collective-permute-start(bf16[192,256]{1,0:T(8,128)(2,1)S(1)} %get-tuple-element.206), channel_id=1, source_target_pairs={{0,8},{1,9},{2,10},{3,11},{4,12},{5,13},{6,14},{7,15},{8,0},{9,1},... | collective-permute-start | bytes 294920 | tf_op jit(solution)/shard_map/ppermute | solution.py:379
  160.4 1.7 %collective-permute-start.60 = (bf16[192,256]{1,0:T(8,128)(2,1)S(1)}, bf16[192,256]{1,0:T(8,128)(2,1)S(1)}, u32[]{:S(2)}, u32[]{:S(2)}) collective-permute-start(bf16[192,256]{1,0:T(8,128)(2,1)S(1)} %get-tuple-element.207), channel_id=1, source_target_pairs={{0,12},{1,13},{2,14},{3,15},{4,8},{5,9},{6,10},{7,11},{8,4},{9,5},... | collective-permute-start | bytes 294920 | tf_op jit(solution)/shard_map/ppermute | solution.py:379
  162.2 0.9 collective-permute-done.56.refs_3_
  163.0 1.0 collective-permute-done.58.refs_5_
  164.2 1.8 %collective-permute-done.60.refs_7_ = bf16[192,256]{1,0:T(8,128)(2,1)S(1)} collective-permute-done((bf16[192,256]{1,0:T(8,128)(2,1)S(1)}, bf16[192,256]{1,0:T(8,128)(2,1)S(1)}, u32[]{:S(2)}, u32[]{:S(2)}) %collective-permute-start.60) | collective-permute-done | bytes 98336 | tf_op jit(solution)/shard_map/ppermute | solution.py:379
  165.9 0.9 assemble.1
  (70 shorter events, 9.5 us)
Async XLA Ops:
  0.0 1.1 copy-start
  1.1 0.7 copy-start.1
  1.8 0.7 copy-start.2
  2.5 10.8 %copy-start.6 = (bf16[1,32,128,128]{3,2,1,0:T(8,128)(2,1)S(1)}, bf16[1,32,128,128]{3,2,1,0:T(8,128)(2,1)}, u32[]{:S(2)}) copy-start(bf16[1,32,128,128]{3,2,1,0:T(8,128)(2,1)} %refs_3_.3) | copy-start | bytes 3145732
  3.5 6.2 %collective-permute-start.42 = (bf16[512,128]{1,0:T(8,128)(2,1)S(1)}, bf16[512,128]{1,0:T(8,128)(2,1)S(1)}, u32[]{:S(2)}, u32[]{:S(2)}) collective-permute-start(bf16[512,128]{1,0:T(8,128)(2,1)S(1)} %get-tuple-element.175), channel_id=1, source_target_pairs={{0,1},{1,0},{2,3},{3,2},{4,5},{5,4},{6,7},{7,6},{8,9},{9,8},{10,11... | collective-permute-start | bytes 393224 | tf_op jit(solution)/shard_map/ppermute | solution.py:379
  4.0 6.9 %collective-permute-start.43 = (bf16[512,128]{1,0:T(8,128)(2,1)S(1)}, bf16[512,128]{1,0:T(8,128)(2,1)S(1)}, u32[]{:S(2)}, u32[]{:S(2)}) collective-permute-start(bf16[512,128]{1,0:T(8,128)(2,1)S(1)} %get-tuple-element.176), channel_id=1, source_target_pairs={{0,2},{1,3},{2,0},{3,1},{4,6},{5,7},{6,4},{7,5},{8,10},{9,11},{10,... | collective-permute-start | bytes 393224 | tf_op jit(solution)/shard_map/ppermute | solution.py:379
  6.6 6.7 %collective-permute-start.44 = (bf16[512,128]{1,0:T(8,128)(2,1)S(1)}, bf16[512,128]{1,0:T(8,128)(2,1)S(1)}, u32[]{:S(2)}, u32[]{:S(2)}) collective-permute-start(bf16[512,128]{1,0:T(8,128)(2,1)S(1)} %get-tuple-element.177), channel_id=1, source_target_pairs={{0,3},{1,2},{2,1},{3,0},{4,7},{5,6},{6,5},{7,4},{8,11},{9,10},{10,... | collective-permute-start | bytes 393224 | tf_op jit(solution)/shard_map/ppermute | solution.py:379
  7.5 8.5 %collective-permute-start.36 = (bf16[512,128]{1,0:T(8,128)(2,1)S(1)}, bf16[512,128]{1,0:T(8,128)(2,1)S(1)}, u32[]{:S(2)}, u32[]{:S(2)}) collective-permute-start(bf16[512,128]{1,0:T(8,128)(2,1)S(1)} %get-tuple-element.167), channel_id=1, source_target_pairs={{0,1},{1,0},{2,3},{3,2},{4,5},{5,4},{6,7},{7,6},{8,9},{9,8},{10,11... | collective-permute-start | bytes 393224 | tf_op jit(solution)/shard_map/ppermute | solution.py:379
  7.7 8.8 %collective-permute-start.37 = (bf16[512,128]{1,0:T(8,128)(2,1)S(1)}, bf16[512,128]{1,0:T(8,128)(2,1)S(1)}, u32[]{:S(2)}, u32[]{:S(2)}) collective-permute-start(bf16[512,128]{1,0:T(8,128)(2,1)S(1)} %get-tuple-element.168), channel_id=1, source_target_pairs={{0,2},{1,3},{2,0},{3,1},{4,6},{5,7},{6,4},{7,5},{8,10},{9,11},{10,... | collective-permute-start | bytes 393224 | tf_op jit(solution)/shard_map/ppermute | solution.py:379
  9.7 9.1 %collective-permute-start.38 = (bf16[512,128]{1,0:T(8,128)(2,1)S(1)}, bf16[512,128]{1,0:T(8,128)(2,1)S(1)}, u32[]{:S(2)}, u32[]{:S(2)}) collective-permute-start(bf16[512,128]{1,0:T(8,128)(2,1)S(1)} %get-tuple-element.169), channel_id=1, source_target_pairs={{0,3},{1,2},{2,1},{3,0},{4,7},{5,6},{6,5},{7,4},{8,11},{9,10},{10,... | collective-permute-start | bytes 393224 | tf_op jit(solution)/shard_map/ppermute | solution.py:379
  10.3 2.9 %copy-start.11 = (s32[1,32]{1,0:T(1,128)S(1)}, s32[1,32]{1,0:T(1,128)}, u32[]{:S(2)}) copy-start(s32[1,32]{1,0:T(1,128)} %refs_0_.3) | copy-start | bytes 388
  10.4 2.9 %copy-start.12 = (s32[1,32]{1,0:T(1,128)S(1)}, s32[1,32]{1,0:T(1,128)}, u32[]{:S(2)}) copy-start(s32[1,32]{1,0:T(1,128)} %refs_1_.5) | copy-start | bytes 388
  14.4 10.7 %collective-permute-start.45 = (bf16[192,128]{1,0:T(8,128)(2,1)S(1)}, bf16[192,128]{1,0:T(8,128)(2,1)S(1)}, u32[]{:S(2)}, u32[]{:S(2)}) collective-permute-start(bf16[192,128]{1,0:T(8,128)(2,1)S(1)} %get-tuple-element.179), channel_id=1, source_target_pairs={{0,4},{1,5},{2,6},{3,7},{4,0},{5,1},{6,2},{7,3},{8,12},{9,13},{10,... | collective-permute-start | bytes 147464 | tf_op jit(solution)/shard_map/ppermute | solution.py:379
  18.8 15.5 %copy-start.3 = (bf16[2,256,1024]{2,1,0:T(8,128)(2,1)S(1)}, bf16[2,256,1024]{2,1,0:T(8,128)(2,1)}, u32[]{:S(2)}) copy-start(bf16[2,256,1024]{2,1,0:T(8,128)(2,1)} %w_in.13) | copy-start | bytes 3145732
  18.8 15.5 %copy-start.4 = (bf16[2,256,1024]{2,1,0:T(8,128)(2,1)S(1)}, bf16[2,256,1024]{2,1,0:T(8,128)(2,1)}, u32[]{:S(2)}) copy-start(bf16[2,256,1024]{2,1,0:T(8,128)(2,1)} %w_rec.13) | copy-start | bytes 3145732
  20.0 12.1 %collective-permute-start.39 = (bf16[384,128]{1,0:T(8,128)(2,1)S(1)}, bf16[384,128]{1,0:T(8,128)(2,1)S(1)}, u32[]{:S(2)}, u32[]{:S(2)}) collective-permute-start(bf16[384,128]{1,0:T(8,128)(2,1)S(1)} %get-tuple-element.171), channel_id=1, source_target_pairs={{0,4},{1,5},{2,6},{3,7},{4,0},{5,1},{6,2},{7,3},{8,12},{9,13},{10,... | collective-permute-start | bytes 294920 | tf_op jit(solution)/shard_map/ppermute | solution.py:379
  21.5 12.0 %collective-permute-start.40 = (bf16[384,128]{1,0:T(8,128)(2,1)S(1)}, bf16[384,128]{1,0:T(8,128)(2,1)S(1)}, u32[]{:S(2)}, u32[]{:S(2)}) collective-permute-start(bf16[384,128]{1,0:T(8,128)(2,1)S(1)} %get-tuple-element.172), channel_id=1, source_target_pairs={{0,8},{1,9},{2,10},{3,11},{4,12},{5,13},{6,14},{7,15},{8,0},{9,1},... | collective-permute-start | bytes 294920 | tf_op jit(solution)/shard_map/ppermute | solution.py:379
  23.1 10.4 %collective-permute-start.41 = (bf16[384,128]{1,0:T(8,128)(2,1)S(1)}, bf16[384,128]{1,0:T(8,128)(2,1)S(1)}, u32[]{:S(2)}, u32[]{:S(2)}) collective-permute-start(bf16[384,128]{1,0:T(8,128)(2,1)S(1)} %get-tuple-element.173), channel_id=1, source_target_pairs={{0,12},{1,13},{2,14},{3,15},{4,8},{5,9},{6,10},{7,11},{8,4},{9,5},... | collective-permute-start | bytes 294920 | tf_op jit(solution)/shard_map/ppermute | solution.py:379
  23.5 6.5 %collective-permute-start.46 = (bf16[192,128]{1,0:T(8,128)(2,1)S(1)}, bf16[192,128]{1,0:T(8,128)(2,1)S(1)}, u32[]{:S(2)}, u32[]{:S(2)}) collective-permute-start(bf16[192,128]{1,0:T(8,128)(2,1)S(1)} %get-tuple-element.180), channel_id=1, source_target_pairs={{0,8},{1,9},{2,10},{3,11},{4,12},{5,13},{6,14},{7,15},{8,0},{9,1},... | collective-permute-start | bytes 147464 | tf_op jit(solution)/shard_map/ppermute | solution.py:379
  25.1 5.6 %collective-permute-start.47 = (bf16[192,128]{1,0:T(8,128)(2,1)S(1)}, bf16[192,128]{1,0:T(8,128)(2,1)S(1)}, u32[]{:S(2)}, u32[]{:S(2)}) collective-permute-start(bf16[192,128]{1,0:T(8,128)(2,1)S(1)} %get-tuple-element.181), channel_id=1, source_target_pairs={{0,12},{1,13},{2,14},{3,15},{4,8},{5,9},{6,10},{7,11},{8,4},{9,5},... | collective-permute-start | bytes 147464 | tf_op jit(solution)/shard_map/ppermute | solution.py:379
  30.0 7.2 %collective-permute-start.48 = (bf16[192,128]{1,0:T(8,128)(2,1)S(1)}, bf16[192,128]{1,0:T(8,128)(2,1)S(1)}, u32[]{:S(2)}, u32[]{:S(2)}) collective-permute-start(bf16[192,128]{1,0:T(8,128)(2,1)S(1)} %get-tuple-element.184), channel_id=1, source_target_pairs={{0,4},{1,5},{2,6},{3,7},{4,0},{5,1},{6,2},{7,3},{8,12},{9,13},{10,... | collective-permute-start | bytes 147464 | tf_op jit(solution)/shard_map/ppermute | solution.py:379
  30.6 6.5 %collective-permute-start.49 = (bf16[192,128]{1,0:T(8,128)(2,1)S(1)}, bf16[192,128]{1,0:T(8,128)(2,1)S(1)}, u32[]{:S(2)}, u32[]{:S(2)}) collective-permute-start(bf16[192,128]{1,0:T(8,128)(2,1)S(1)} %get-tuple-element.185), channel_id=1, source_target_pairs={{0,8},{1,9},{2,10},{3,11},{4,12},{5,13},{6,14},{7,15},{8,0},{9,1},... | collective-permute-start | bytes 147464 | tf_op jit(solution)/shard_map/ppermute | solution.py:379
  32.1 5.1 %collective-permute-start.50 = (bf16[192,128]{1,0:T(8,128)(2,1)S(1)}, bf16[192,128]{1,0:T(8,128)(2,1)S(1)}, u32[]{:S(2)}, u32[]{:S(2)}) collective-permute-start(bf16[192,128]{1,0:T(8,128)(2,1)S(1)} %get-tuple-element.186), channel_id=1, source_target_pairs={{0,12},{1,13},{2,14},{3,15},{4,8},{5,9},{6,10},{7,11},{8,4},{9,5},... | collective-permute-start | bytes 147464 | tf_op jit(solution)/shard_map/ppermute | solution.py:379
  37.3 1.9 %copy-start.9 = (bf16[4,192,256]{2,1,0:T(8,128)(2,1)}, bf16[4,192,256]{2,1,0:T(8,128)(2,1)S(1)}, u32[]{:S(2)}) copy-start(bf16[4,192,256]{2,1,0:T(8,128)(2,1)S(1)} %pack_chunk.3.refs_0_) | copy-start | bytes 1179652
  39.1 0.7 copy-start.13
  39.8 20.9 %copy-start.7 = (bf16[1,32,128,128]{3,2,1,0:T(8,128)(2,1)S(1)}, bf16[1,32,128,128]{3,2,1,0:T(8,128)(2,1)}, u32[]{:S(2)}) copy-start(bf16[1,32,128,128]{3,2,1,0:T(8,128)(2,1)} %get-tuple-element.56.refs_3_) | copy-start | bytes 3145732 | tf_op jit(solution)/shard_map/cond
  41.1 6.6 %collective-permute-start = (bf16[384,128]{1,0:T(8,128)(2,1)S(1)}, bf16[384,128]{1,0:T(8,128)(2,1)S(1)}, u32[]{:S(2)}, u32[]{:S(2)}) collective-permute-start(bf16[384,128]{1,0:T(8,128)(2,1)S(1)} %get-tuple-element.61), channel_id=1, source_target_pairs={{0,4},{1,5},{2,6},{3,7},{4,0},{5,1},{6,2},{7,3},{8,12},{9,13},{10,... | collective-permute-start | bytes 294920 | tf_op jit(solution)/shard_map/cond/branch_1_fun/ppermute | solution.py:379
  42.6 5.1 %collective-permute-start.1 = (bf16[384,128]{1,0:T(8,128)(2,1)S(1)}, bf16[384,128]{1,0:T(8,128)(2,1)S(1)}, u32[]{:S(2)}, u32[]{:S(2)}) collective-permute-start(bf16[384,128]{1,0:T(8,128)(2,1)S(1)} %get-tuple-element.62), channel_id=1, source_target_pairs={{0,8},{1,9},{2,10},{3,11},{4,12},{5,13},{6,14},{7,15},{8,0},{9,1},... | collective-permute-start | bytes 294920 | tf_op jit(solution)/shard_map/cond/branch_1_fun/ppermute | solution.py:379
  43.3 5.6 %collective-permute-start.2 = (bf16[384,128]{1,0:T(8,128)(2,1)S(1)}, bf16[384,128]{1,0:T(8,128)(2,1)S(1)}, u32[]{:S(2)}, u32[]{:S(2)}) collective-permute-start(bf16[384,128]{1,0:T(8,128)(2,1)S(1)} %get-tuple-element.63), channel_id=1, source_target_pairs={{0,12},{1,13},{2,14},{3,15},{4,8},{5,9},{6,10},{7,11},{8,4},{9,5},... | collective-permute-start | bytes 294920 | tf_op jit(solution)/shard_map/cond/branch_1_fun/ppermute | solution.py:379
  44.7 9.6 %collective-permute-start.9 = (bf16[384,128]{1,0:T(8,128)(2,1)S(1)}, bf16[384,128]{1,0:T(8,128)(2,1)S(1)}, u32[]{:S(2)}, u32[]{:S(2)}) collective-permute-start(bf16[384,128]{1,0:T(8,128)(2,1)S(1)} %get-tuple-element.73), channel_id=1, source_target_pairs={{0,4},{1,5},{2,6},{3,7},{4,0},{5,1},{6,2},{7,3},{8,12},{9,13},{10,... | collective-permute-start | bytes 294920 | tf_op jit(solution)/shard_map/cond/branch_1_fun/ppermute | solution.py:379
  49.6 10.8 %collective-permute-start.3 = (bf16[512,128]{1,0:T(8,128)(2,1)S(1)}, bf16[512,128]{1,0:T(8,128)(2,1)S(1)}, u32[]{:S(2)}, u32[]{:S(2)}) collective-permute-start(bf16[512,128]{1,0:T(8,128)(2,1)S(1)} %get-tuple-element.65), channel_id=1, source_target_pairs={{0,1},{1,0},{2,3},{3,2},{4,5},{5,4},{6,7},{7,6},{8,9},{9,8},{10,11... | collective-permute-start | bytes 393224 | tf_op jit(solution)/shard_map/cond/branch_1_fun/ppermute | solution.py:379
  49.7 5.7 %collective-permute-start.10 = (bf16[384,128]{1,0:T(8,128)(2,1)S(1)}, bf16[384,128]{1,0:T(8,128)(2,1)S(1)}, u32[]{:S(2)}, u32[]{:S(2)}) collective-permute-start(bf16[384,128]{1,0:T(8,128)(2,1)S(1)} %get-tuple-element.74), channel_id=1, source_target_pairs={{0,8},{1,9},{2,10},{3,11},{4,12},{5,13},{6,14},{7,15},{8,0},{9,1},... | collective-permute-start | bytes 294920 | tf_op jit(solution)/shard_map/cond/branch_1_fun/ppermute | solution.py:379
  51.1 6.9 %collective-permute-start.11 = (bf16[384,128]{1,0:T(8,128)(2,1)S(1)}, bf16[384,128]{1,0:T(8,128)(2,1)S(1)}, u32[]{:S(2)}, u32[]{:S(2)}) collective-permute-start(bf16[384,128]{1,0:T(8,128)(2,1)S(1)} %get-tuple-element.75), channel_id=1, source_target_pairs={{0,12},{1,13},{2,14},{3,15},{4,8},{5,9},{6,10},{7,11},{8,4},{9,5},... | collective-permute-start | bytes 294920 | tf_op jit(solution)/shard_map/cond/branch_1_fun/ppermute | solution.py:379
  52.8 7.9 %collective-permute-start.4 = (bf16[512,128]{1,0:T(8,128)(2,1)S(1)}, bf16[512,128]{1,0:T(8,128)(2,1)S(1)}, u32[]{:S(2)}, u32[]{:S(2)}) collective-permute-start(bf16[512,128]{1,0:T(8,128)(2,1)S(1)} %get-tuple-element.66), channel_id=1, source_target_pairs={{0,2},{1,3},{2,0},{3,1},{4,6},{5,7},{6,4},{7,5},{8,10},{9,11},{10,... | collective-permute-start | bytes 393224 | tf_op jit(solution)/shard_map/cond/branch_1_fun/ppermute | solution.py:379
  54.3 6.4 %collective-permute-start.5 = (bf16[512,128]{1,0:T(8,128)(2,1)S(1)}, bf16[512,128]{1,0:T(8,128)(2,1)S(1)}, u32[]{:S(2)}, u32[]{:S(2)}) collective-permute-start(bf16[512,128]{1,0:T(8,128)(2,1)S(1)} %get-tuple-element.67), channel_id=1, source_target_pairs={{0,3},{1,2},{2,1},{3,0},{4,7},{5,6},{6,5},{7,4},{8,11},{9,10},{10,... | collective-permute-start | bytes 393224 | tf_op jit(solution)/shard_map/cond/branch_1_fun/ppermute | solution.py:379
  58.7 5.6 %collective-permute-start.12 = (bf16[512,128]{1,0:T(8,128)(2,1)S(1)}, bf16[512,128]{1,0:T(8,128)(2,1)S(1)}, u32[]{:S(2)}, u32[]{:S(2)}) collective-permute-start(bf16[512,128]{1,0:T(8,128)(2,1)S(1)} %get-tuple-element.77), channel_id=1, source_target_pairs={{0,1},{1,0},{2,3},{3,2},{4,5},{5,4},{6,7},{7,6},{8,9},{9,8},{10,11... | collective-permute-start | bytes 393224 | tf_op jit(solution)/shard_map/cond/branch_1_fun/ppermute | solution.py:379
  58.8 7.2 %collective-permute-start.13 = (bf16[512,128]{1,0:T(8,128)(2,1)S(1)}, bf16[512,128]{1,0:T(8,128)(2,1)S(1)}, u32[]{:S(2)}, u32[]{:S(2)}) collective-permute-start(bf16[512,128]{1,0:T(8,128)(2,1)S(1)} %get-tuple-element.78), channel_id=1, source_target_pairs={{0,2},{1,3},{2,0},{3,1},{4,6},{5,7},{6,4},{7,5},{8,10},{9,11},{10,... | collective-permute-start | bytes 393224 | tf_op jit(solution)/shard_map/cond/branch_1_fun/ppermute | solution.py:379
  60.4 6.6 %collective-permute-start.14 = (bf16[512,128]{1,0:T(8,128)(2,1)S(1)}, bf16[512,128]{1,0:T(8,128)(2,1)S(1)}, u32[]{:S(2)}, u32[]{:S(2)}) collective-permute-start(bf16[512,128]{1,0:T(8,128)(2,1)S(1)} %get-tuple-element.79), channel_id=1, source_target_pairs={{0,3},{1,2},{2,1},{3,0},{4,7},{5,6},{6,5},{7,4},{8,11},{9,10},{10,... | collective-permute-start | bytes 393224 | tf_op jit(solution)/shard_map/cond/branch_1_fun/ppermute | solution.py:379
  62.5 8.2 %collective-permute-start.6 = (bf16[384,128]{1,0:T(8,128)(2,1)S(1)}, bf16[384,128]{1,0:T(8,128)(2,1)S(1)}, u32[]{:S(2)}, u32[]{:S(2)}) collective-permute-start(bf16[384,128]{1,0:T(8,128)(2,1)S(1)} %get-tuple-element.69), channel_id=1, source_target_pairs={{0,4},{1,5},{2,6},{3,7},{4,0},{5,1},{6,2},{7,3},{8,12},{9,13},{10,... | collective-permute-start | bytes 294920 | tf_op jit(solution)/shard_map/cond/branch_1_fun/ppermute | solution.py:379
  63.0 9.3 %collective-permute-start.7 = (bf16[384,128]{1,0:T(8,128)(2,1)S(1)}, bf16[384,128]{1,0:T(8,128)(2,1)S(1)}, u32[]{:S(2)}, u32[]{:S(2)}) collective-permute-start(bf16[384,128]{1,0:T(8,128)(2,1)S(1)} %get-tuple-element.70), channel_id=1, source_target_pairs={{0,8},{1,9},{2,10},{3,11},{4,12},{5,13},{6,14},{7,15},{8,0},{9,1},... | collective-permute-start | bytes 294920 | tf_op jit(solution)/shard_map/cond/branch_1_fun/ppermute | solution.py:379
  64.4 8.0 %collective-permute-start.8 = (bf16[384,128]{1,0:T(8,128)(2,1)S(1)}, bf16[384,128]{1,0:T(8,128)(2,1)S(1)}, u32[]{:S(2)}, u32[]{:S(2)}) collective-permute-start(bf16[384,128]{1,0:T(8,128)(2,1)S(1)} %get-tuple-element.71), channel_id=1, source_target_pairs={{0,12},{1,13},{2,14},{3,15},{4,8},{5,9},{6,10},{7,11},{8,4},{9,5},... | collective-permute-start | bytes 294920 | tf_op jit(solution)/shard_map/cond/branch_1_fun/ppermute | solution.py:379
  68.8 5.4 %collective-permute-start.15 = (bf16[384,128]{1,0:T(8,128)(2,1)S(1)}, bf16[384,128]{1,0:T(8,128)(2,1)S(1)}, u32[]{:S(2)}, u32[]{:S(2)}) collective-permute-start(bf16[384,128]{1,0:T(8,128)(2,1)S(1)} %get-tuple-element.81), channel_id=1, source_target_pairs={{0,4},{1,5},{2,6},{3,7},{4,0},{5,1},{6,2},{7,3},{8,12},{9,13},{10,... | collective-permute-start | bytes 294920 | tf_op jit(solution)/shard_map/cond/branch_1_fun/ppermute | solution.py:379
  69.3 5.7 %collective-permute-start.16 = (bf16[384,128]{1,0:T(8,128)(2,1)S(1)}, bf16[384,128]{1,0:T(8,128)(2,1)S(1)}, u32[]{:S(2)}, u32[]{:S(2)}) collective-permute-start(bf16[384,128]{1,0:T(8,128)(2,1)S(1)} %get-tuple-element.82), channel_id=1, source_target_pairs={{0,8},{1,9},{2,10},{3,11},{4,12},{5,13},{6,14},{7,15},{8,0},{9,1},... | collective-permute-start | bytes 294920 | tf_op jit(solution)/shard_map/cond/branch_1_fun/ppermute | solution.py:379
  70.7 6.8 %collective-permute-start.17 = (bf16[384,128]{1,0:T(8,128)(2,1)S(1)}, bf16[384,128]{1,0:T(8,128)(2,1)S(1)}, u32[]{:S(2)}, u32[]{:S(2)}) collective-permute-start(bf16[384,128]{1,0:T(8,128)(2,1)S(1)} %get-tuple-element.83), channel_id=1, source_target_pairs={{0,12},{1,13},{2,14},{3,15},{4,8},{5,9},{6,10},{7,11},{8,4},{9,5},... | collective-permute-start | bytes 294920 | tf_op jit(solution)/shard_map/cond/branch_1_fun/ppermute | solution.py:379
  78.5 6.6 %collective-permute-start.51 = (bf16[2,192,256]{2,1,0:T(8,128)(2,1)S(1)}, bf16[2,192,256]{2,1,0:T(8,128)(2,1)S(1)}, u32[]{:S(2)}, u32[]{:S(2)}) collective-permute-start(bf16[2,192,256]{2,1,0:T(8,128)(2,1)S(1)} %get-tuple-element.190), channel_id=1, source_target_pairs={{0,24},{1,25},{2,26},{3,27},{4,28},{5,29},{6,30},{7,31},{8,16},{9,... | collective-permute-start | bytes 589832 | tf_op jit(solution)/shard_map/ppermute | solution.py:379
  79.8 8.3 %collective-permute-start.52 = (bf16[2,192,256]{2,1,0:T(8,128)(2,1)S(1)}, bf16[2,192,256]{2,1,0:T(8,128)(2,1)S(1)}, u32[]{:S(2)}, u32[]{:S(2)}) collective-permute-start(bf16[2,192,256]{2,1,0:T(8,128)(2,1)S(1)} %get-tuple-element.191), channel_id=1, source_target_pairs={{0,24},{1,25},{2,26},{3,27},{4,28},{5,29},{6,30},{7,31},{8,16},{9,... | collective-permute-start | bytes 589832 | tf_op jit(solution)/shard_map/ppermute | solution.py:379
  81.1 4.0 %copy-start.5 = (bf16[2,256,1024]{2,1,0:T(8,128)(2,1)S(1)}, bf16[2,256,1024]{2,1,0:T(8,128)(2,1)}, u32[]{:S(2)}) copy-start(bf16[2,256,1024]{2,1,0:T(8,128)(2,1)} %w_rec.13) | copy-start | bytes 3145732
  88.2 57.3 %collective-permute-start.53 = (bf16[2,192,256]{2,1,0:T(8,128)(2,1)S(1)}, bf16[2,192,256]{2,1,0:T(8,128)(2,1)S(1)}, u32[]{:S(2)}, u32[]{:S(2)}) collective-permute-start(bf16[2,192,256]{2,1,0:T(8,128)(2,1)S(1)} %get-tuple-element.195), channel_id=1, source_target_pairs={{0,24},{1,25},{2,26},{3,27},{4,28},{5,29},{6,30},{7,31},{8,16},{9,... | collective-permute-start | bytes 589832 | tf_op jit(solution)/shard_map/ppermute | solution.py:379
  142.8 14.4 %collective-permute-start.57 = (bf16[2,192,256]{2,1,0:T(8,128)(2,1)S(1)}, bf16[2,192,256]{2,1,0:T(8,128)(2,1)S(1)}, u32[]{:S(2)}, u32[]{:S(2)}) collective-permute-start(bf16[2,192,256]{2,1,0:T(8,128)(2,1)S(1)} %get-tuple-element.203), channel_id=1, source_target_pairs={{0,24},{1,25},{2,26},{3,27},{4,28},{5,29},{6,30},{7,31},{8,16},{9,... | collective-permute-start | bytes 589832 | tf_op jit(solution)/shard_map/ppermute | solution.py:379
  145.5 11.7 %copy-start.10 = (bf16[4,192,256]{2,1,0:T(8,128)(2,1)S(1)}, bf16[4,192,256]{2,1,0:T(8,128)(2,1)}, u32[]{:S(2)}) copy-start(bf16[4,192,256]{2,1,0:T(8,128)(2,1)} %get-tuple-element.200.refs_0_) | copy-start | bytes 1179652
  146.6 13.8 %collective-permute-start.54 = (bf16[192,256]{1,0:T(8,128)(2,1)S(1)}, bf16[192,256]{1,0:T(8,128)(2,1)S(1)}, u32[]{:S(2)}, u32[]{:S(2)}) collective-permute-start(bf16[192,256]{1,0:T(8,128)(2,1)S(1)} %get-tuple-element.197), channel_id=1, source_target_pairs={{0,4},{1,5},{2,6},{3,7},{4,0},{5,1},{6,2},{7,3},{8,12},{9,13},{10,... | collective-permute-start | bytes 294920 | tf_op jit(solution)/shard_map/ppermute | solution.py:379
  148.0 14.1 %collective-permute-start.55 = (bf16[192,256]{1,0:T(8,128)(2,1)S(1)}, bf16[192,256]{1,0:T(8,128)(2,1)S(1)}, u32[]{:S(2)}, u32[]{:S(2)}) collective-permute-start(bf16[192,256]{1,0:T(8,128)(2,1)S(1)} %get-tuple-element.198), channel_id=1, source_target_pairs={{0,8},{1,9},{2,10},{3,11},{4,12},{5,13},{6,14},{7,15},{8,0},{9,1},... | collective-permute-start | bytes 294920 | tf_op jit(solution)/shard_map/ppermute | solution.py:379
  156.8 6.2 %collective-permute-start.56 = (bf16[192,256]{1,0:T(8,128)(2,1)S(1)}, bf16[192,256]{1,0:T(8,128)(2,1)S(1)}, u32[]{:S(2)}, u32[]{:S(2)}) collective-permute-start(bf16[192,256]{1,0:T(8,128)(2,1)S(1)} %get-tuple-element.199), channel_id=1, source_target_pairs={{0,12},{1,13},{2,14},{3,15},{4,8},{5,9},{6,10},{7,11},{8,4},{9,5},... | collective-permute-start | bytes 294920 | tf_op jit(solution)/shard_map/ppermute | solution.py:379
  157.2 6.8 %collective-permute-start.58 = (bf16[192,256]{1,0:T(8,128)(2,1)S(1)}, bf16[192,256]{1,0:T(8,128)(2,1)S(1)}, u32[]{:S(2)}, u32[]{:S(2)}) collective-permute-start(bf16[192,256]{1,0:T(8,128)(2,1)S(1)} %get-tuple-element.205), channel_id=1, source_target_pairs={{0,4},{1,5},{2,6},{3,7},{4,0},{5,1},{6,2},{7,3},{8,12},{9,13},{10,... | collective-permute-start | bytes 294920 | tf_op jit(solution)/shard_map/ppermute | solution.py:379
  158.4 5.8 %collective-permute-start.59 = (bf16[192,256]{1,0:T(8,128)(2,1)S(1)}, bf16[192,256]{1,0:T(8,128)(2,1)S(1)}, u32[]{:S(2)}, u32[]{:S(2)}) collective-permute-start(bf16[192,256]{1,0:T(8,128)(2,1)S(1)} %get-tuple-element.206), channel_id=1, source_target_pairs={{0,8},{1,9},{2,10},{3,11},{4,12},{5,13},{6,14},{7,15},{8,0},{9,1},... | collective-permute-start | bytes 294920 | tf_op jit(solution)/shard_map/ppermute | solution.py:379
  160.4 5.5 %collective-permute-start.60 = (bf16[192,256]{1,0:T(8,128)(2,1)S(1)}, bf16[192,256]{1,0:T(8,128)(2,1)S(1)}, u32[]{:S(2)}, u32[]{:S(2)}) collective-permute-start(bf16[192,256]{1,0:T(8,128)(2,1)S(1)} %get-tuple-element.207), channel_id=1, source_target_pairs={{0,12},{1,13},{2,14},{3,15},{4,8},{5,9},{6,10},{7,11},{8,4},{9,5},... | collective-permute-start | bytes 294920 | tf_op jit(solution)/shard_map/ppermute | solution.py:379

commit v5 on v4

--- a/solution.py
+++ b/solution.py
@@ -37,7 +37,9 @@
     return run
 
 
-def pick_tiles(parts, ref_table, slab_count, row_count, tile, group, column, carried=()):
+def pick_tiles(
+    parts, ref_table, slab_count, row_count, tile, group, column, carried=(), scalars=()
+):
     part_count = len(parts)
     part_rows = parts[0].shape[0]
     listed = ref_table.shape[2] // slab_count
@@ -45,9 +47,18 @@
 
     def kernel(table_hbm, *refs):
         sources = refs[:part_count]
-        first_out = part_count + len(carried)
+        first_out = part_count + len(carried) + len(scalars)
         outs = refs[first_out : first_out + slab_count]
-        table, table_sem, rows, sems, carry_sems = refs[-5:]
+        table, table_sem, rows, sems, carry_sems, numbers, number_sems = refs[-7:]
+        last_out = first_out + slab_count + len(carried)
+        loads = [
+            pltpu.make_async_copy(
+                refs[part_count + len(carried) + n], numbers.at[pl.ds(n, 1)], number_sems.at[n]
+            )
+            for n in range(len(scalars))
+        ]
+        for load in loads:
+            load.start()
         moves = [
             pltpu.make_async_copy(
                 refs[part_count + n], refs[first_out + slab_count + n], carry_sems.at[n]
@@ -77,26 +88,33 @@
         copies += moves
         for copy in copies:
             copy.start()
+        for n, load in enumerate(loads):
+            load.wait()
+            spot = refs[last_out + n]
+            spot[...] = jnp.full(spot.shape, numbers[n, 0], spot.dtype)
         for copy in copies:
             copy.wait()
 
     dtype = parts[0].dtype
     results = pl.pallas_call(
         kernel,
-        in_specs=[HBM] + [HBM if whole else VMEM] * part_count + [HBM] * len(carried),
-        out_specs=[VMEM] * (slab_count + len(carried)),
+        in_specs=[HBM] + [HBM if whole else VMEM] * part_count + [HBM] * (len(carried) + len(scalars)),
+        out_specs=[VMEM] * (slab_count + len(carried) + len(scalars)),
         out_shape=[jax.ShapeDtypeStruct((listed * tile, LANES), dtype)] * slab_count
-        + [jax.ShapeDtypeStruct(array.shape, array.dtype) for array in carried],
+        + [jax.ShapeDtypeStruct(array.shape, array.dtype) for array in carried]
+        + [jax.ShapeDtypeStruct((8, LANES), array.dtype) for array in scalars],
         scratch_shapes=[
             pltpu.SMEM(ref_table.shape, ref_table.dtype),
             pltpu.SemaphoreType.DMA(()),
             pltpu.VMEM((tile if whole else row_count, LANES), dtype),
             pltpu.SemaphoreType.DMA((slab_count, listed)),
             pltpu.SemaphoreType.DMA((max(len(carried), 1),)),
+            pltpu.SMEM((max(len(scalars), 1), 1), jnp.int32),
+            pltpu.SemaphoreType.DMA((max(len(scalars), 1),)),
         ],
         compiler_params=PARAMS,
         name="pick_tiles",
-    )(ref_table, *parts, *carried)
+    )(ref_table, *parts, *carried, *scalars)
     return results[:slab_count], results[slab_count:]
 
 
@@ -408,13 +426,13 @@
     group = lax.axis_size("tm") // 2
     half = lax.axis_index("tm") // group
 
-    def pick(parts, table, column=0, carried=()):
-        return pick_tiles(parts, table, slab_count, row_count, tile, group, column, carried)
-
-    def mix(listed, chunks=1):
+    def pick(parts, table, column=0, *carried):
+        return pick_tiles(parts, table, slab_count, row_count, tile, group, column, *carried)
+
+    def mix(listed, live, chunks=1):
         arrived = swap_slabs(listed)
         mixed = convolve(
-            arrived, tile_rows, tile_sources, tile_counts, tile_values, row_count, group, chunks
+            arrived, tile_rows, tile_sources, live, tile_values, row_count, group, chunks
         )
         got = []
         for part in mixed:
@@ -422,7 +440,7 @@
         return got if chunks > 1 else got[0]
 
     def back_and_mix(hidden):
-        return pack([mix(pick(swap_times(column), table)[0]) for column in hidden])
+        return pack([mix(pick(swap_times(column), table)[0], counts) for column in hidden])
 
     def run(mixed, layer, mode, *rest):
         return recur(mixed, layer, w_input, w_hidden, gate_bias, mode, *rest)
@@ -441,10 +459,12 @@
     features = features[0]
     columns = features.shape[1] // LANES
     listed = [pick([features], ref_lists, column)[0] for column in range(columns - 1)]
-    last, (table, gate_bias) = pick([features], ref_lists, columns - 1, (ref_lists, bias))
-    early = [mix(column) for column in listed]
+    last, (table, gate_bias, counts) = pick(
+        [features], ref_lists, columns - 1, (ref_lists, bias), (tile_counts,)
+    )
+    early = [mix(column, tile_counts) for column in listed]
     upper_mixed = [
-        pack_chunk([*early, part], chunk) for chunk, part in enumerate(mix(last, CHUNKS))
+        pack_chunk([*early, part], chunk) for chunk, part in enumerate(mix(last, tile_counts, CHUNKS))
     ]
     hidden, handed = run_lower(upper_mixed, 0)
     for layer in range(1, layers):

time: 169 us -> 167 us (0.988)
  transfers between devices with their start and end apart: 43 -> 43, of which waited for: 20 -> 20; matrix products, arithmetic and copies ran while one was open for 0% -> 0% of each run, Pallas kernels for 12% -> 11%
where the time goes in v5:
time: 167 us; the launch traced here: 166 us
  starting transfers between devices  107 us (64%)
  waiting for transfers between devices  31 us (19%)
  Pallas kernels  24.4 us (15%)
  local copies, waits for them, and re-layouts  2.55 us (2%)
    ppermute x43, starting transfers between devices, send(): return lax.ppermute(array, AXES, pairs)  107 us
    ppermute x43, waiting for transfers between devices, send(): return lax.ppermute(array, AXES, pairs)  31 us
    pallas_call x7, Pallas kernels, recur(): pl.pallas_call(kernel, in_specs=[VMEM] * (3 + len(operands)), out_specs=[...  12.1 us
    pallas_call x4, Pallas kernels, convolve(): pl.pallas_call(kernel, in_specs=[HBM, HBM, HBM, VMEM] + [VMEM] * slab_cou...  4.67 us
    pallas_call x4, Pallas kernels, pick_tiles(): pl.pallas_call(kernel, in_specs=[HBM] + [HBM if whole else VMEM] * part_c...  3.42 us
  transfers between devices with their start and end apart: 43, of which 20 were waited for; matrix products, arithmetic and copies ran while one was open for 0% of the time, Pallas kernels for 11%

profile of v5, /device:TPU:0, one launch (start us, length us, event | category | flops | bytes accessed | tf_op | source)
XLA Modules:
  0.0 166.0 jit_solution(6331172496136704512)
XLA Ops:
  0.7 1.1 copy-done
  2.5 1.0 pick_tiles.10
  4.0 2.6 %collective-permute-start.43 = (bf16[512,128]{1,0:T(8,128)(2,1)S(1)}, bf16[512,128]{1,0:T(8,128)(2,1)S(1)}, u32[]{:S(2)}, u32[]{:S(2)}) collective-permute-start(bf16[512,128]{1,0:T(8,128)(2,1)S(1)} %get-tuple-element.177), channel_id=1, source_target_pairs={{0,2},{1,3},{2,0},{3,1},{4,6},{5,7},{6,4},{7,5},{8,10},{9,11},{10,... | collective-permute-start | bytes 393224 | tf_op jit(solution)/shard_map/ppermute | solution.py:397
  6.6 0.9 pick_tiles.11
  7.8 1.9 %collective-permute-start.37 = (bf16[512,128]{1,0:T(8,128)(2,1)S(1)}, bf16[512,128]{1,0:T(8,128)(2,1)S(1)}, u32[]{:S(2)}, u32[]{:S(2)}) collective-permute-start(bf16[512,128]{1,0:T(8,128)(2,1)S(1)} %get-tuple-element.169), channel_id=1, source_target_pairs={{0,2},{1,3},{2,0},{3,1},{4,6},{5,7},{6,4},{7,5},{8,10},{9,11},{10,... | collective-permute-start | bytes 393224 | tf_op jit(solution)/shard_map/ppermute | solution.py:397
  9.7 1.2 collective-permute-done.43.refs_6_
  10.9 2.4 %collective-permute-done.44.refs_7_ = bf16[512,128]{1,0:T(8,128)(2,1)S(1)} collective-permute-done((bf16[512,128]{1,0:T(8,128)(2,1)S(1)}, bf16[512,128]{1,0:T(8,128)(2,1)S(1)}, u32[]{:S(2)}, u32[]{:S(2)}) %collective-permute-start.44) | collective-permute-done | bytes 131104 | tf_op jit(solution)/shard_map/ppermute | solution.py:397
  13.3 1.1 convolve.11
  14.4 1.6 collective-permute-start.45
  16.6 2.3 %collective-permute-done.38.refs_7_ = bf16[512,128]{1,0:T(8,128)(2,1)S(1)} collective-permute-done((bf16[512,128]{1,0:T(8,128)(2,1)S(1)}, bf16[512,128]{1,0:T(8,128)(2,1)S(1)}, u32[]{:S(2)}, u32[]{:S(2)}) %collective-permute-start.38) | collective-permute-done | bytes 131104 | tf_op jit(solution)/shard_map/ppermute | solution.py:397
  18.8 1.1 convolve.10
  20.0 1.6 collective-permute-start.39
  21.5 1.6 collective-permute-start.40
  23.5 1.5 collective-permute-start.46
  25.1 1.4 collective-permute-start.47
  26.5 3.5 %collective-permute-done.46.refs_6_ = bf16[192,128]{1,0:T(8,128)(2,1)S(1)} collective-permute-done((bf16[192,128]{1,0:T(8,128)(2,1)S(1)}, bf16[192,128]{1,0:T(8,128)(2,1)S(1)}, u32[]{:S(2)}, u32[]{:S(2)}) %collective-permute-start.46) | collective-permute-done | bytes 49184 | tf_op jit(solution)/shard_map/ppermute | solution.py:397
  30.7 1.4 collective-permute-start.49
  32.1 1.4 collective-permute-start.50
  33.5 0.8 pack_chunk.2.refs_0_
  34.3 2.8 %recur.9 = (bf16[4,192,256]{2,1,0:T(8,128)(2,1)}, bf16[2,192,256]{2,1,0:T(8,128)(2,1)S(1)}) custom-call(bf16[2,256,1024]{2,1,0:T(8,128)(2,1)S(1)} %copy-done.3, bf16[2,256,1024]{2,1,0:T(8,128)(2,1)S(1)} %copy-done.4, f32[2,1024]{1,0:T(2,128)S(1)} %get-tuple-element.166.gate_bias, bf16[4,192,256]{2,1,0:T(8,128)(2,1)} %pack_chunk.2.refs_0_), custom_call_target="tpu_custom_call" | custom-call | tf_op jit(solution)/shard_map/recur/pallas_call | solution.py:345
  37.3 1.8 %recur.10 = (bf16[4,192,256]{2,1,0:T(8,128)(2,1)}, bf16[2,192,256]{2,1,0:T(8,128)(2,1)S(1)}) custom-call(bf16[2,256,1024]{2,1,0:T(8,128)(2,1)S(1)} %copy-done.3, bf16[2,256,1024]{2,1,0:T(8,128)(2,1)S(1)} %copy-done.4, f32[2,1024]{1,0:T(2,128)S(1)} %get-tuple-element.166.gate_bias, bf16[4,192,256]{2,1,0:T(8,128)(2,1)S(1)} %pack_chunk.3.refs_0_), custom_call_target="tpu_custom_call" | custom-call | tf_op jit(solution)/shard_map/recur/pallas_call | solution.py:345
  39.8 38.2 %conditional.2 = (bf16[4,192,256]{2,1,0:T(8,128)(2,1)}, bf16[4,192,256]{2,1,0:T(8,128)(2,1)}, s32[]{:T(128)}) conditional(s32[]{:T(128)} %convert_element_type.6, (bf16[4,192,256]{2,1,0:T(8,128)(2,1)}, bf16[4,192,256]{2,1,0:T(8,128)(2,1)}, s32[]{:T(128)}) %tuple.18, (bf16[4,192,256]{2,1,0:T(8,128)(2,1)}, bf16[4,192,256]{2,1,0:T(8,128)(2,1)}, ...), branch_computations={%region_0.1_spmd, %region_1.2_spmd} | conditional | flops 1 | bytes 12059408 | solution.py:478
  39.8 1.3 spread.1
  41.1 1.5 collective-permute-start
  43.3 1.4 collective-permute-start.2
  44.7 1.4 collective-permute-start.9
  46.1 1.6 collective-permute-done.refs_1_
  47.7 1.1 collective-permute-done.2.refs_3_
  49.8 1.4 collective-permute-start.10
  51.1 1.7 %collective-permute-start.11 = (bf16[384,128]{1,0:T(8,128)(2,1)S(1)}, bf16[384,128]{1,0:T(8,128)(2,1)S(1)}, u32[]{:S(2)}, u32[]{:S(2)}) collective-permute-start(bf16[384,128]{1,0:T(8,128)(2,1)S(1)} %get-tuple-element.75), channel_id=1, source_target_pairs={{0,12},{1,13},{2,14},{3,15},{4,8},{5,9},{6,10},{7,11},{8,4},{9,5},... | collective-permute-start | bytes 294920 | tf_op jit(solution)/shard_map/cond/branch_1_fun/ppermute | solution.py:397
  52.8 1.5 collective-permute-start.4
  54.3 1.2 collective-permute-done.10.refs_2_
  55.5 2.5 %collective-permute-done.11.refs_3_ = bf16[384,128]{1,0:T(8,128)(2,1)S(1)} collective-permute-done((bf16[384,128]{1,0:T(8,128)(2,1)S(1)}, bf16[384,128]{1,0:T(8,128)(2,1)S(1)}, u32[]{:S(2)}, u32[]{:S(2)}) %collective-permute-start.11) | collective-permute-done | bytes 98336 | tf_op jit(solution)/shard_map/cond/branch_1_fun/ppermute | solution.py:397
  58.9 1.5 collective-permute-start.13
  60.7 1.2 convolve.6
  62.5 1.3 collective-permute-start.7
  63.9 1.7 %collective-permute-start.8 = (bf16[384,128]{1,0:T(8,128)(2,1)S(1)}, bf16[384,128]{1,0:T(8,128)(2,1)S(1)}, u32[]{:S(2)}, u32[]{:S(2)}) collective-permute-start(bf16[384,128]{1,0:T(8,128)(2,1)S(1)} %get-tuple-element.71), channel_id=1, source_target_pairs={{0,12},{1,13},{2,14},{3,15},{4,8},{5,9},{6,10},{7,11},{8,4},{9,5},... | collective-permute-start | bytes 294920 | tf_op jit(solution)/shard_map/cond/branch_1_fun/ppermute | solution.py:397
  65.5 1.5 collective-permute-done.14.refs_7_
  67.0 1.2 convolve.7
  68.8 1.3 collective-permute-start.16
  70.1 1.7 %collective-permute-start.17 = (bf16[384,128]{1,0:T(8,128)(2,1)S(1)}, bf16[384,128]{1,0:T(8,128)(2,1)S(1)}, u32[]{:S(2)}, u32[]{:S(2)}) collective-permute-start(bf16[384,128]{1,0:T(8,128)(2,1)S(1)} %get-tuple-element.83), channel_id=1, source_target_pairs={{0,12},{1,13},{2,14},{3,15},{4,8},{5,9},{6,10},{7,11},{8,4},{9,5},... | collective-permute-start | bytes 294920 | tf_op jit(solution)/shard_map/cond/branch_1_fun/ppermute | solution.py:397
  71.8 1.9 %collective-permute-done.15.refs_5_ = bf16[384,128]{1,0:T(8,128)(2,1)S(1)} collective-permute-done((bf16[384,128]{1,0:T(8,128)(2,1)S(1)}, bf16[384,128]{1,0:T(8,128)(2,1)S(1)}, u32[]{:S(2)}, u32[]{:S(2)}) %collective-permute-start.15) | collective-permute-done | bytes 98336 | tf_op jit(solution)/shard_map/cond/branch_1_fun/ppermute | solution.py:397
  74.5 2.5 %collective-permute-done.17.refs_7_ = bf16[384,128]{1,0:T(8,128)(2,1)S(1)} collective-permute-done((bf16[384,128]{1,0:T(8,128)(2,1)S(1)}, bf16[384,128]{1,0:T(8,128)(2,1)S(1)}, u32[]{:S(2)}, u32[]{:S(2)}) %collective-permute-start.17) | collective-permute-done | bytes 98336 | tf_op jit(solution)/shard_map/cond/branch_1_fun/ppermute | solution.py:397
  77.0 1.0 pack.2
  78.0 1.3 collective-permute-start.51
  79.3 1.3 collective-permute-start.52
  80.6 2.5 %recur.12 = (bf16[4,192,256]{2,1,0:T(8,128)(2,1)S(1)}, bf16[2,192,256]{2,1,0:T(8,128)(2,1)S(1)}) custom-call(bf16[2,256,1024]{2,1,0:T(8,128)(2,1)S(1)} %copy-done.3, bf16[2,256,1024]{2,1,0:T(8,128)(2,1)} %w_rec.13, f32[2,1024]{1,0:T(2,128)S(1)} %get-tuple-element.166.gate_bias, bf16[4,192,256]{2,1,0:T(8,128)(2,1)} %get-tuple-element.195.refs_0_), custom_call_target="tpu_custom_call" | custom-call | tf_op jit(solution)/shard_map/recur/pallas_call | solution.py:345
  83.1 1.5 collective-permute-done.51.refs_1_
  84.6 1.8 %recur.11 = bf16[4,192,256]{2,1,0:T(8,128)(2,1)} custom-call(bf16[2,256,1024]{2,1,0:T(8,128)(2,1)S(1)} %copy-done.3, bf16[2,256,1024]{2,1,0:T(8,128)(2,1)S(1)} %copy-done.5, f32[2,1024]{1,0:T(2,128)S(1)} %get-tuple-element.166.gate_bias, bf16[4,192,256]{2,1,0:T(8,128)(2,1)} %pack_chunk.2.refs_0_, bf16[2,192,256]{2,1,0:T(8,128)(2,1)S(1)} %collective-permute-done.51.refs_1_), custom_call_target="tpu_custom_call" | custom-call | tf_op jit(solution)/shard_map/recur/pallas_call | solution.py:345
  86.3 1.3 collective-permute-done.52
  87.7 52.0 %collective-permute-start.53 = (bf16[2,192,256]{2,1,0:T(8,128)(2,1)S(1)}, bf16[2,192,256]{2,1,0:T(8,128)(2,1)S(1)}, u32[]{:S(2)}, u32[]{:S(2)}) collective-permute-start(bf16[2,192,256]{2,1,0:T(8,128)(2,1)S(1)} %get-tuple-element.197), channel_id=1, source_target_pairs={{0,24},{1,25},{2,26},{3,27},{4,28},{5,29},{6,30},{7,31},{8,16},{9,... | collective-permute-start | bytes 589832 | tf_op jit(solution)/shard_map/ppermute | solution.py:397
  139.7 2.1 %recur.14 = (bf16[4,192,256]{2,1,0:T(8,128)(2,1)S(1)}, bf16[2,192,256]{2,1,0:T(8,128)(2,1)S(1)}) custom-call(bf16[2,256,1024]{2,1,0:T(8,128)(2,1)S(1)} %copy-done.3, bf16[2,256,1024]{2,1,0:T(8,128)(2,1)S(1)} %copy-done.5, f32[2,1024]{1,0:T(2,128)S(1)} %get-tuple-element.166.gate_bias, bf16[4,192,256]{2,1,0:T(8,128)(2,1)} %get-tuple-element.203.refs_0_), custom_call_target="tpu_custom_call" | custom-call | tf_op jit(solution)/shard_map/recur/pallas_call | solution.py:345
  141.8 1.3 collective-permute-start.57
  143.1 1.4 collective-permute-done.53.refs_2_
  144.4 1.1 recur.13
  145.5 1.4 collective-permute-start.54
  147.0 8.8 %collective-permute-start.55 = (bf16[192,256]{1,0:T(8,128)(2,1)S(1)}, bf16[192,256]{1,0:T(8,128)(2,1)S(1)}, u32[]{:S(2)}, u32[]{:S(2)}) collective-permute-start(bf16[192,256]{1,0:T(8,128)(2,1)S(1)} %get-tuple-element.200), channel_id=1, source_target_pairs={{0,8},{1,9},{2,10},{3,11},{4,12},{5,13},{6,14},{7,15},{8,0},{9,1},... | collective-permute-start | bytes 294920 | tf_op jit(solution)/shard_map/ppermute | solution.py:397
  156.2 1.1 collective-permute-start.58
  157.3 2.0 %collective-permute-start.59 = (bf16[192,256]{1,0:T(8,128)(2,1)S(1)}, bf16[192,256]{1,0:T(8,128)(2,1)S(1)}, u32[]{:S(2)}, u32[]{:S(2)}) collective-permute-start(bf16[192,256]{1,0:T(8,128)(2,1)S(1)} %get-tuple-element.208), channel_id=1, source_target_pairs={{0,8},{1,9},{2,10},{3,11},{4,12},{5,13},{6,14},{7,15},{8,0},{9,1},... | collective-permute-start | bytes 294920 | tf_op jit(solution)/shard_map/ppermute | solution.py:397
  159.3 1.7 %collective-permute-start.60 = (bf16[192,256]{1,0:T(8,128)(2,1)S(1)}, bf16[192,256]{1,0:T(8,128)(2,1)S(1)}, u32[]{:S(2)}, u32[]{:S(2)}) collective-permute-start(bf16[192,256]{1,0:T(8,128)(2,1)S(1)} %get-tuple-element.209), channel_id=1, source_target_pairs={{0,12},{1,13},{2,14},{3,15},{4,8},{5,9},{6,10},{7,11},{8,4},{9,5},... | collective-permute-start | bytes 294920 | tf_op jit(solution)/shard_map/ppermute | solution.py:397
  161.1 0.9 collective-permute-done.56.refs_3_
  162.0 1.0 collective-permute-done.58.refs_5_
  163.1 1.8 %collective-permute-done.60.refs_7_ = bf16[192,256]{1,0:T(8,128)(2,1)S(1)} collective-permute-done((bf16[192,256]{1,0:T(8,128)(2,1)S(1)}, bf16[192,256]{1,0:T(8,128)(2,1)S(1)}, u32[]{:S(2)}, u32[]{:S(2)}) %collective-permute-start.60) | collective-permute-done | bytes 98336 | tf_op jit(solution)/shard_map/ppermute | solution.py:397
  164.8 0.9 assemble.1
  (72 shorter events, 9.2 us)
Async XLA Ops:
  0.0 0.7 copy-start.1
  0.7 1.1 copy-start
  1.8 0.7 copy-start.2
  2.5 10.8 %copy-start.6 = (bf16[1,32,128,128]{3,2,1,0:T(8,128)(2,1)S(1)}, bf16[1,32,128,128]{3,2,1,0:T(8,128)(2,1)}, u32[]{:S(2)}) copy-start(bf16[1,32,128,128]{3,2,1,0:T(8,128)(2,1)} %refs_3_.4) | copy-start | bytes 3145732
  3.5 6.2 %collective-permute-start.42 = (bf16[512,128]{1,0:T(8,128)(2,1)S(1)}, bf16[512,128]{1,0:T(8,128)(2,1)S(1)}, u32[]{:S(2)}, u32[]{:S(2)}) collective-permute-start(bf16[512,128]{1,0:T(8,128)(2,1)S(1)} %get-tuple-element.176), channel_id=1, source_target_pairs={{0,1},{1,0},{2,3},{3,2},{4,5},{5,4},{6,7},{7,6},{8,9},{9,8},{10,11... | collective-permute-start | bytes 393224 | tf_op jit(solution)/shard_map/ppermute | solution.py:397
  4.0 6.9 %collective-permute-start.43 = (bf16[512,128]{1,0:T(8,128)(2,1)S(1)}, bf16[512,128]{1,0:T(8,128)(2,1)S(1)}, u32[]{:S(2)}, u32[]{:S(2)}) collective-permute-start(bf16[512,128]{1,0:T(8,128)(2,1)S(1)} %get-tuple-element.177), channel_id=1, source_target_pairs={{0,2},{1,3},{2,0},{3,1},{4,6},{5,7},{6,4},{7,5},{8,10},{9,11},{10,... | collective-permute-start | bytes 393224 | tf_op jit(solution)/shard_map/ppermute | solution.py:397
  6.6 6.7 %collective-permute-start.44 = (bf16[512,128]{1,0:T(8,128)(2,1)S(1)}, bf16[512,128]{1,0:T(8,128)(2,1)S(1)}, u32[]{:S(2)}, u32[]{:S(2)}) collective-permute-start(bf16[512,128]{1,0:T(8,128)(2,1)S(1)} %get-tuple-element.178), channel_id=1, source_target_pairs={{0,3},{1,2},{2,1},{3,0},{4,7},{5,6},{6,5},{7,4},{8,11},{9,10},{10,... | collective-permute-start | bytes 393224 | tf_op jit(solution)/shard_map/ppermute | solution.py:397
  7.5 8.5 %collective-permute-start.36 = (bf16[512,128]{1,0:T(8,128)(2,1)S(1)}, bf16[512,128]{1,0:T(8,128)(2,1)S(1)}, u32[]{:S(2)}, u32[]{:S(2)}) collective-permute-start(bf16[512,128]{1,0:T(8,128)(2,1)S(1)} %get-tuple-element.168), channel_id=1, source_target_pairs={{0,1},{1,0},{2,3},{3,2},{4,5},{5,4},{6,7},{7,6},{8,9},{9,8},{10,11... | collective-permute-start | bytes 393224 | tf_op jit(solution)/shard_map/ppermute | solution.py:397
  7.8 8.8 %collective-permute-start.37 = (bf16[512,128]{1,0:T(8,128)(2,1)S(1)}, bf16[512,128]{1,0:T(8,128)(2,1)S(1)}, u32[]{:S(2)}, u32[]{:S(2)}) collective-permute-start(bf16[512,128]{1,0:T(8,128)(2,1)S(1)} %get-tuple-element.169), channel_id=1, source_target_pairs={{0,2},{1,3},{2,0},{3,1},{4,6},{5,7},{6,4},{7,5},{8,10},{9,11},{10,... | collective-permute-start | bytes 393224 | tf_op jit(solution)/shard_map/ppermute | solution.py:397
  9.7 3.6 %copy-start.11 = (s32[1,32]{1,0:T(1,128)S(1)}, s32[1,32]{1,0:T(1,128)}, u32[]{:S(2)}) copy-start(s32[1,32]{1,0:T(1,128)} %refs_0_.3) | copy-start | bytes 388
  9.7 3.6 %copy-start.13 = (s32[1,32]{1,0:T(1,128)S(1)}, s32[1,32]{1,0:T(1,128)}, u32[]{:S(2)}) copy-start(s32[1,32]{1,0:T(1,128)} %refs_1_.5) | copy-start | bytes 388
  9.7 9.1 %collective-permute-start.38 = (bf16[512,128]{1,0:T(8,128)(2,1)S(1)}, bf16[512,128]{1,0:T(8,128)(2,1)S(1)}, u32[]{:S(2)}, u32[]{:S(2)}) collective-permute-start(bf16[512,128]{1,0:T(8,128)(2,1)S(1)} %get-tuple-element.170), channel_id=1, source_target_pairs={{0,3},{1,2},{2,1},{3,0},{4,7},{5,6},{6,5},{7,4},{8,11},{9,10},{10,... | collective-permute-start | bytes 393224 | tf_op jit(solution)/shard_map/ppermute | solution.py:397
  14.4 10.7 %collective-permute-start.45 = (bf16[192,128]{1,0:T(8,128)(2,1)S(1)}, bf16[192,128]{1,0:T(8,128)(2,1)S(1)}, u32[]{:S(2)}, u32[]{:S(2)}) collective-permute-start(bf16[192,128]{1,0:T(8,128)(2,1)S(1)} %get-tuple-element.180), channel_id=1, source_target_pairs={{0,4},{1,5},{2,6},{3,7},{4,0},{5,1},{6,2},{7,3},{8,12},{9,13},{10,... | collective-permute-start | bytes 147464 | tf_op jit(solution)/shard_map/ppermute | solution.py:397
  18.8 15.5 %copy-start.3 = (bf16[2,256,1024]{2,1,0:T(8,128)(2,1)S(1)}, bf16[2,256,1024]{2,1,0:T(8,128)(2,1)}, u32[]{:S(2)}) copy-start(bf16[2,256,1024]{2,1,0:T(8,128)(2,1)} %w_in.13) | copy-start | bytes 3145732
  18.8 15.5 %copy-start.4 = (bf16[2,256,1024]{2,1,0:T(8,128)(2,1)S(1)}, bf16[2,256,1024]{2,1,0:T(8,128)(2,1)}, u32[]{:S(2)}) copy-start(bf16[2,256,1024]{2,1,0:T(8,128)(2,1)} %w_rec.13) | copy-start | bytes 3145732
  20.0 12.1 %collective-permute-start.39 = (bf16[384,128]{1,0:T(8,128)(2,1)S(1)}, bf16[384,128]{1,0:T(8,128)(2,1)S(1)}, u32[]{:S(2)}, u32[]{:S(2)}) collective-permute-start(bf16[384,128]{1,0:T(8,128)(2,1)S(1)} %get-tuple-element.172), channel_id=1, source_target_pairs={{0,4},{1,5},{2,6},{3,7},{4,0},{5,1},{6,2},{7,3},{8,12},{9,13},{10,... | collective-permute-start | bytes 294920 | tf_op jit(solution)/shard_map/ppermute | solution.py:397
  21.5 12.0 %collective-permute-start.40 = (bf16[384,128]{1,0:T(8,128)(2,1)S(1)}, bf16[384,128]{1,0:T(8,128)(2,1)S(1)}, u32[]{:S(2)}, u32[]{:S(2)}) collective-permute-start(bf16[384,128]{1,0:T(8,128)(2,1)S(1)} %get-tuple-element.173), channel_id=1, source_target_pairs={{0,8},{1,9},{2,10},{3,11},{4,12},{5,13},{6,14},{7,15},{8,0},{9,1},... | collective-permute-start | bytes 294920 | tf_op jit(solution)/shard_map/ppermute | solution.py:397
  23.1 10.4 %collective-permute-start.41 = (bf16[384,128]{1,0:T(8,128)(2,1)S(1)}, bf16[384,128]{1,0:T(8,128)(2,1)S(1)}, u32[]{:S(2)}, u32[]{:S(2)}) collective-permute-start(bf16[384,128]{1,0:T(8,128)(2,1)S(1)} %get-tuple-element.174), channel_id=1, source_target_pairs={{0,12},{1,13},{2,14},{3,15},{4,8},{5,9},{6,10},{7,11},{8,4},{9,5},... | collective-permute-start | bytes 294920 | tf_op jit(solution)/shard_map/ppermute | solution.py:397
  23.5 6.5 %collective-permute-start.46 = (bf16[192,128]{1,0:T(8,128)(2,1)S(1)}, bf16[192,128]{1,0:T(8,128)(2,1)S(1)}, u32[]{:S(2)}, u32[]{:S(2)}) collective-permute-start(bf16[192,128]{1,0:T(8,128)(2,1)S(1)} %get-tuple-element.181), channel_id=1, source_target_pairs={{0,8},{1,9},{2,10},{3,11},{4,12},{5,13},{6,14},{7,15},{8,0},{9,1},... | collective-permute-start | bytes 147464 | tf_op jit(solution)/shard_map/ppermute | solution.py:397
  25.1 5.6 %collective-permute-start.47 = (bf16[192,128]{1,0:T(8,128)(2,1)S(1)}, bf16[192,128]{1,0:T(8,128)(2,1)S(1)}, u32[]{:S(2)}, u32[]{:S(2)}) collective-permute-start(bf16[192,128]{1,0:T(8,128)(2,1)S(1)} %get-tuple-element.182), channel_id=1, source_target_pairs={{0,12},{1,13},{2,14},{3,15},{4,8},{5,9},{6,10},{7,11},{8,4},{9,5},... | collective-permute-start | bytes 147464 | tf_op jit(solution)/shard_map/ppermute | solution.py:397
  30.0 7.2 %collective-permute-start.48 = (bf16[192,128]{1,0:T(8,128)(2,1)S(1)}, bf16[192,128]{1,0:T(8,128)(2,1)S(1)}, u32[]{:S(2)}, u32[]{:S(2)}) collective-permute-start(bf16[192,128]{1,0:T(8,128)(2,1)S(1)} %get-tuple-element.185), channel_id=1, source_target_pairs={{0,4},{1,5},{2,6},{3,7},{4,0},{5,1},{6,2},{7,3},{8,12},{9,13},{10,... | collective-permute-start | bytes 147464 | tf_op jit(solution)/shard_map/ppermute | solution.py:397
  30.7 6.5 %collective-permute-start.49 = (bf16[192,128]{1,0:T(8,128)(2,1)S(1)}, bf16[192,128]{1,0:T(8,128)(2,1)S(1)}, u32[]{:S(2)}, u32[]{:S(2)}) collective-permute-start(bf16[192,128]{1,0:T(8,128)(2,1)S(1)} %get-tuple-element.186), channel_id=1, source_target_pairs={{0,8},{1,9},{2,10},{3,11},{4,12},{5,13},{6,14},{7,15},{8,0},{9,1},... | collective-permute-start | bytes 147464 | tf_op jit(solution)/shard_map/ppermute | solution.py:397
  32.1 5.1 %collective-permute-start.50 = (bf16[192,128]{1,0:T(8,128)(2,1)S(1)}, bf16[192,128]{1,0:T(8,128)(2,1)S(1)}, u32[]{:S(2)}, u32[]{:S(2)}) collective-permute-start(bf16[192,128]{1,0:T(8,128)(2,1)S(1)} %get-tuple-element.187), channel_id=1, source_target_pairs={{0,12},{1,13},{2,14},{3,15},{4,8},{5,9},{6,10},{7,11},{8,4},{9,5},... | collective-permute-start | bytes 147464 | tf_op jit(solution)/shard_map/ppermute | solution.py:397
  37.3 1.8 %copy-start.9 = (bf16[4,192,256]{2,1,0:T(8,128)(2,1)}, bf16[4,192,256]{2,1,0:T(8,128)(2,1)S(1)}, u32[]{:S(2)}) copy-start(bf16[4,192,256]{2,1,0:T(8,128)(2,1)S(1)} %pack_chunk.3.refs_0_) | copy-start | bytes 1179652
  39.1 0.7 copy-start.12
  39.1 0.7 copy-start.14
  39.8 20.9 %copy-start.7 = (bf16[1,32,128,128]{3,2,1,0:T(8,128)(2,1)S(1)}, bf16[1,32,128,128]{3,2,1,0:T(8,128)(2,1)}, u32[]{:S(2)}) copy-start(bf16[1,32,128,128]{3,2,1,0:T(8,128)(2,1)} %get-tuple-element.56.refs_3_) | copy-start | bytes 3145732 | tf_op jit(solution)/shard_map/cond
  41.1 6.6 %collective-permute-start = (bf16[384,128]{1,0:T(8,128)(2,1)S(1)}, bf16[384,128]{1,0:T(8,128)(2,1)S(1)}, u32[]{:S(2)}, u32[]{:S(2)}) collective-permute-start(bf16[384,128]{1,0:T(8,128)(2,1)S(1)} %get-tuple-element.61), channel_id=1, source_target_pairs={{0,4},{1,5},{2,6},{3,7},{4,0},{5,1},{6,2},{7,3},{8,12},{9,13},{10,... | collective-permute-start | bytes 294920 | tf_op jit(solution)/shard_map/cond/branch_1_fun/ppermute | solution.py:397
  42.6 5.1 %collective-permute-start.1 = (bf16[384,128]{1,0:T(8,128)(2,1)S(1)}, bf16[384,128]{1,0:T(8,128)(2,1)S(1)}, u32[]{:S(2)}, u32[]{:S(2)}) collective-permute-start(bf16[384,128]{1,0:T(8,128)(2,1)S(1)} %get-tuple-element.62), channel_id=1, source_target_pairs={{0,8},{1,9},{2,10},{3,11},{4,12},{5,13},{6,14},{7,15},{8,0},{9,1},... | collective-permute-start | bytes 294920 | tf_op jit(solution)/shard_map/cond/branch_1_fun/ppermute | solution.py:397
  43.3 5.6 %collective-permute-start.2 = (bf16[384,128]{1,0:T(8,128)(2,1)S(1)}, bf16[384,128]{1,0:T(8,128)(2,1)S(1)}, u32[]{:S(2)}, u32[]{:S(2)}) collective-permute-start(bf16[384,128]{1,0:T(8,128)(2,1)S(1)} %get-tuple-element.63), channel_id=1, source_target_pairs={{0,12},{1,13},{2,14},{3,15},{4,8},{5,9},{6,10},{7,11},{8,4},{9,5},... | collective-permute-start | bytes 294920 | tf_op jit(solution)/shard_map/cond/branch_1_fun/ppermute | solution.py:397
  44.7 9.6 %collective-permute-start.9 = (bf16[384,128]{1,0:T(8,128)(2,1)S(1)}, bf16[384,128]{1,0:T(8,128)(2,1)S(1)}, u32[]{:S(2)}, u32[]{:S(2)}) collective-permute-start(bf16[384,128]{1,0:T(8,128)(2,1)S(1)} %get-tuple-element.73), channel_id=1, source_target_pairs={{0,4},{1,5},{2,6},{3,7},{4,0},{5,1},{6,2},{7,3},{8,12},{9,13},{10,... | collective-permute-start | bytes 294920 | tf_op jit(solution)/shard_map/cond/branch_1_fun/ppermute | solution.py:397
  49.7 10.7 %collective-permute-start.3 = (bf16[512,128]{1,0:T(8,128)(2,1)S(1)}, bf16[512,128]{1,0:T(8,128)(2,1)S(1)}, u32[]{:S(2)}, u32[]{:S(2)}) collective-permute-start(bf16[512,128]{1,0:T(8,128)(2,1)S(1)} %get-tuple-element.65), channel_id=1, source_target_pairs={{0,1},{1,0},{2,3},{3,2},{4,5},{5,4},{6,7},{7,6},{8,9},{9,8},{10,11... | collective-permute-start | bytes 393224 | tf_op jit(solution)/shard_map/cond/branch_1_fun/ppermute | solution.py:397
  49.8 5.7 %collective-permute-start.10 = (bf16[384,128]{1,0:T(8,128)(2,1)S(1)}, bf16[384,128]{1,0:T(8,128)(2,1)S(1)}, u32[]{:S(2)}, u32[]{:S(2)}) collective-permute-start(bf16[384,128]{1,0:T(8,128)(2,1)S(1)} %get-tuple-element.74), channel_id=1, source_target_pairs={{0,8},{1,9},{2,10},{3,11},{4,12},{5,13},{6,14},{7,15},{8,0},{9,1},... | collective-permute-start | bytes 294920 | tf_op jit(solution)/shard_map/cond/branch_1_fun/ppermute | solution.py:397
  51.1 6.9 %collective-permute-start.11 = (bf16[384,128]{1,0:T(8,128)(2,1)S(1)}, bf16[384,128]{1,0:T(8,128)(2,1)S(1)}, u32[]{:S(2)}, u32[]{:S(2)}) collective-permute-start(bf16[384,128]{1,0:T(8,128)(2,1)S(1)} %get-tuple-element.75), channel_id=1, source_target_pairs={{0,12},{1,13},{2,14},{3,15},{4,8},{5,9},{6,10},{7,11},{8,4},{9,5},... | collective-permute-start | bytes 294920 | tf_op jit(solution)/shard_map/cond/branch_1_fun/ppermute | solution.py:397
  52.8 7.9 %collective-permute-start.4 = (bf16[512,128]{1,0:T(8,128)(2,1)S(1)}, bf16[512,128]{1,0:T(8,128)(2,1)S(1)}, u32[]{:S(2)}, u32[]{:S(2)}) collective-permute-start(bf16[512,128]{1,0:T(8,128)(2,1)S(1)} %get-tuple-element.66), channel_id=1, source_target_pairs={{0,2},{1,3},{2,0},{3,1},{4,6},{5,7},{6,4},{7,5},{8,10},{9,11},{10,... | collective-permute-start | bytes 393224 | tf_op jit(solution)/shard_map/cond/branch_1_fun/ppermute | solution.py:397
  54.3 6.5 %collective-permute-start.5 = (bf16[512,128]{1,0:T(8,128)(2,1)S(1)}, bf16[512,128]{1,0:T(8,128)(2,1)S(1)}, u32[]{:S(2)}, u32[]{:S(2)}) collective-permute-start(bf16[512,128]{1,0:T(8,128)(2,1)S(1)} %get-tuple-element.67), channel_id=1, source_target_pairs={{0,3},{1,2},{2,1},{3,0},{4,7},{5,6},{6,5},{7,4},{8,11},{9,10},{10,... | collective-permute-start | bytes 393224 | tf_op jit(solution)/shard_map/cond/branch_1_fun/ppermute | solution.py:397
  58.8 5.0 %collective-permute-start.12 = (bf16[512,128]{1,0:T(8,128)(2,1)S(1)}, bf16[512,128]{1,0:T(8,128)(2,1)S(1)}, u32[]{:S(2)}, u32[]{:S(2)}) collective-permute-start(bf16[512,128]{1,0:T(8,128)(2,1)S(1)} %get-tuple-element.77), channel_id=1, source_target_pairs={{0,1},{1,0},{2,3},{3,2},{4,5},{5,4},{6,7},{7,6},{8,9},{9,8},{10,11... | collective-permute-start | bytes 393224 | tf_op jit(solution)/shard_map/cond/branch_1_fun/ppermute | solution.py:397
  58.9 6.6 %collective-permute-start.13 = (bf16[512,128]{1,0:T(8,128)(2,1)S(1)}, bf16[512,128]{1,0:T(8,128)(2,1)S(1)}, u32[]{:S(2)}, u32[]{:S(2)}) collective-permute-start(bf16[512,128]{1,0:T(8,128)(2,1)S(1)} %get-tuple-element.78), channel_id=1, source_target_pairs={{0,2},{1,3},{2,0},{3,1},{4,6},{5,7},{6,4},{7,5},{8,10},{9,11},{10,... | collective-permute-start | bytes 393224 | tf_op jit(solution)/shard_map/cond/branch_1_fun/ppermute | solution.py:397
  60.4 6.6 %collective-permute-start.14 = (bf16[512,128]{1,0:T(8,128)(2,1)S(1)}, bf16[512,128]{1,0:T(8,128)(2,1)S(1)}, u32[]{:S(2)}, u32[]{:S(2)}) collective-permute-start(bf16[512,128]{1,0:T(8,128)(2,1)S(1)} %get-tuple-element.79), channel_id=1, source_target_pairs={{0,3},{1,2},{2,1},{3,0},{4,7},{5,6},{6,5},{7,4},{8,11},{9,10},{10,... | collective-permute-start | bytes 393224 | tf_op jit(solution)/shard_map/cond/branch_1_fun/ppermute | solution.py:397
  62.0 8.2 %collective-permute-start.6 = (bf16[384,128]{1,0:T(8,128)(2,1)S(1)}, bf16[384,128]{1,0:T(8,128)(2,1)S(1)}, u32[]{:S(2)}, u32[]{:S(2)}) collective-permute-start(bf16[384,128]{1,0:T(8,128)(2,1)S(1)} %get-tuple-element.69), channel_id=1, source_target_pairs={{0,4},{1,5},{2,6},{3,7},{4,0},{5,1},{6,2},{7,3},{8,12},{9,13},{10,... | collective-permute-start | bytes 294920 | tf_op jit(solution)/shard_map/cond/branch_1_fun/ppermute | solution.py:397
  62.5 9.3 %collective-permute-start.7 = (bf16[384,128]{1,0:T(8,128)(2,1)S(1)}, bf16[384,128]{1,0:T(8,128)(2,1)S(1)}, u32[]{:S(2)}, u32[]{:S(2)}) collective-permute-start(bf16[384,128]{1,0:T(8,128)(2,1)S(1)} %get-tuple-element.70), channel_id=1, source_target_pairs={{0,8},{1,9},{2,10},{3,11},{4,12},{5,13},{6,14},{7,15},{8,0},{9,1},... | collective-permute-start | bytes 294920 | tf_op jit(solution)/shard_map/cond/branch_1_fun/ppermute | solution.py:397
  63.9 8.0 %collective-permute-start.8 = (bf16[384,128]{1,0:T(8,128)(2,1)S(1)}, bf16[384,128]{1,0:T(8,128)(2,1)S(1)}, u32[]{:S(2)}, u32[]{:S(2)}) collective-permute-start(bf16[384,128]{1,0:T(8,128)(2,1)S(1)} %get-tuple-element.71), channel_id=1, source_target_pairs={{0,12},{1,13},{2,14},{3,15},{4,8},{5,9},{6,10},{7,11},{8,4},{9,5},... | collective-permute-start | bytes 294920 | tf_op jit(solution)/shard_map/cond/branch_1_fun/ppermute | solution.py:397
  68.3 5.4 %collective-permute-start.15 = (bf16[384,128]{1,0:T(8,128)(2,1)S(1)}, bf16[384,128]{1,0:T(8,128)(2,1)S(1)}, u32[]{:S(2)}, u32[]{:S(2)}) collective-permute-start(bf16[384,128]{1,0:T(8,128)(2,1)S(1)} %get-tuple-element.81), channel_id=1, source_target_pairs={{0,4},{1,5},{2,6},{3,7},{4,0},{5,1},{6,2},{7,3},{8,12},{9,13},{10,... | collective-permute-start | bytes 294920 | tf_op jit(solution)/shard_map/cond/branch_1_fun/ppermute | solution.py:397
  68.8 5.7 %collective-permute-start.16 = (bf16[384,128]{1,0:T(8,128)(2,1)S(1)}, bf16[384,128]{1,0:T(8,128)(2,1)S(1)}, u32[]{:S(2)}, u32[]{:S(2)}) collective-permute-start(bf16[384,128]{1,0:T(8,128)(2,1)S(1)} %get-tuple-element.82), channel_id=1, source_target_pairs={{0,8},{1,9},{2,10},{3,11},{4,12},{5,13},{6,14},{7,15},{8,0},{9,1},... | collective-permute-start | bytes 294920 | tf_op jit(solution)/shard_map/cond/branch_1_fun/ppermute | solution.py:397
  70.1 6.8 %collective-permute-start.17 = (bf16[384,128]{1,0:T(8,128)(2,1)S(1)}, bf16[384,128]{1,0:T(8,128)(2,1)S(1)}, u32[]{:S(2)}, u32[]{:S(2)}) collective-permute-start(bf16[384,128]{1,0:T(8,128)(2,1)S(1)} %get-tuple-element.83), channel_id=1, source_target_pairs={{0,12},{1,13},{2,14},{3,15},{4,8},{5,9},{6,10},{7,11},{8,4},{9,5},... | collective-permute-start | bytes 294920 | tf_op jit(solution)/shard_map/cond/branch_1_fun/ppermute | solution.py:397
  78.0 6.6 %collective-permute-start.51 = (bf16[2,192,256]{2,1,0:T(8,128)(2,1)S(1)}, bf16[2,192,256]{2,1,0:T(8,128)(2,1)S(1)}, u32[]{:S(2)}, u32[]{:S(2)}) collective-permute-start(bf16[2,192,256]{2,1,0:T(8,128)(2,1)S(1)} %get-tuple-element.192), channel_id=1, source_target_pairs={{0,24},{1,25},{2,26},{3,27},{4,28},{5,29},{6,30},{7,31},{8,16},{9,... | collective-permute-start | bytes 589832 | tf_op jit(solution)/shard_map/ppermute | solution.py:397
  79.3 8.4 %collective-permute-start.52 = (bf16[2,192,256]{2,1,0:T(8,128)(2,1)S(1)}, bf16[2,192,256]{2,1,0:T(8,128)(2,1)S(1)}, u32[]{:S(2)}, u32[]{:S(2)}) collective-permute-start(bf16[2,192,256]{2,1,0:T(8,128)(2,1)S(1)} %get-tuple-element.193), channel_id=1, source_target_pairs={{0,24},{1,25},{2,26},{3,27},{4,28},{5,29},{6,30},{7,31},{8,16},{9,... | collective-permute-start | bytes 589832 | tf_op jit(solution)/shard_map/ppermute | solution.py:397
  80.6 4.0 %copy-start.5 = (bf16[2,256,1024]{2,1,0:T(8,128)(2,1)S(1)}, bf16[2,256,1024]{2,1,0:T(8,128)(2,1)}, u32[]{:S(2)}) copy-start(bf16[2,256,1024]{2,1,0:T(8,128)(2,1)} %w_rec.13) | copy-start | bytes 3145732
  87.7 56.8 %collective-permute-start.53 = (bf16[2,192,256]{2,1,0:T(8,128)(2,1)S(1)}, bf16[2,192,256]{2,1,0:T(8,128)(2,1)S(1)}, u32[]{:S(2)}, u32[]{:S(2)}) collective-permute-start(bf16[2,192,256]{2,1,0:T(8,128)(2,1)S(1)} %get-tuple-element.197), channel_id=1, source_target_pairs={{0,24},{1,25},{2,26},{3,27},{4,28},{5,29},{6,30},{7,31},{8,16},{9,... | collective-permute-start | bytes 589832 | tf_op jit(solution)/shard_map/ppermute | solution.py:397
  141.8 14.3 %collective-permute-start.57 = (bf16[2,192,256]{2,1,0:T(8,128)(2,1)S(1)}, bf16[2,192,256]{2,1,0:T(8,128)(2,1)S(1)}, u32[]{:S(2)}, u32[]{:S(2)}) collective-permute-start(bf16[2,192,256]{2,1,0:T(8,128)(2,1)S(1)} %get-tuple-element.205), channel_id=1, source_target_pairs={{0,24},{1,25},{2,26},{3,27},{4,28},{5,29},{6,30},{7,31},{8,16},{9,... | collective-permute-start | bytes 589832 | tf_op jit(solution)/shard_map/ppermute | solution.py:397
  144.4 11.7 %copy-start.10 = (bf16[4,192,256]{2,1,0:T(8,128)(2,1)S(1)}, bf16[4,192,256]{2,1,0:T(8,128)(2,1)}, u32[]{:S(2)}) copy-start(bf16[4,192,256]{2,1,0:T(8,128)(2,1)} %get-tuple-element.202.refs_0_) | copy-start | bytes 1179652
  145.5 13.8 %collective-permute-start.54 = (bf16[192,256]{1,0:T(8,128)(2,1)S(1)}, bf16[192,256]{1,0:T(8,128)(2,1)S(1)}, u32[]{:S(2)}, u32[]{:S(2)}) collective-permute-start(bf16[192,256]{1,0:T(8,128)(2,1)S(1)} %get-tuple-element.199), channel_id=1, source_target_pairs={{0,4},{1,5},{2,6},{3,7},{4,0},{5,1},{6,2},{7,3},{8,12},{9,13},{10,... | collective-permute-start | bytes 294920 | tf_op jit(solution)/shard_map/ppermute | solution.py:397
  147.0 14.1 %collective-permute-start.55 = (bf16[192,256]{1,0:T(8,128)(2,1)S(1)}, bf16[192,256]{1,0:T(8,128)(2,1)S(1)}, u32[]{:S(2)}, u32[]{:S(2)}) collective-permute-start(bf16[192,256]{1,0:T(8,128)(2,1)S(1)} %get-tuple-element.200), channel_id=1, source_target_pairs={{0,8},{1,9},{2,10},{3,11},{4,12},{5,13},{6,14},{7,15},{8,0},{9,1},... | collective-permute-start | bytes 294920 | tf_op jit(solution)/shard_map/ppermute | solution.py:397
  155.7 6.2 %collective-permute-start.56 = (bf16[192,256]{1,0:T(8,128)(2,1)S(1)}, bf16[192,256]{1,0:T(8,128)(2,1)S(1)}, u32[]{:S(2)}, u32[]{:S(2)}) collective-permute-start(bf16[192,256]{1,0:T(8,128)(2,1)S(1)} %get-tuple-element.201), channel_id=1, source_target_pairs={{0,12},{1,13},{2,14},{3,15},{4,8},{5,9},{6,10},{7,11},{8,4},{9,5},... | collective-permute-start | bytes 294920 | tf_op jit(solution)/shard_map/ppermute | solution.py:397
  156.2 6.8 %collective-permute-start.58 = (bf16[192,256]{1,0:T(8,128)(2,1)S(1)}, bf16[192,256]{1,0:T(8,128)(2,1)S(1)}, u32[]{:S(2)}, u32[]{:S(2)}) collective-permute-start(bf16[192,256]{1,0:T(8,128)(2,1)S(1)} %get-tuple-element.207), channel_id=1, source_target_pairs={{0,4},{1,5},{2,6},{3,7},{4,0},{5,1},{6,2},{7,3},{8,12},{9,13},{10,... | collective-permute-start | bytes 294920 | tf_op jit(solution)/shard_map/ppermute | solution.py:397
  157.3 5.8 %collective-permute-start.59 = (bf16[192,256]{1,0:T(8,128)(2,1)S(1)}, bf16[192,256]{1,0:T(8,128)(2,1)S(1)}, u32[]{:S(2)}, u32[]{:S(2)}) collective-permute-start(bf16[192,256]{1,0:T(8,128)(2,1)S(1)} %get-tuple-element.208), channel_id=1, source_target_pairs={{0,8},{1,9},{2,10},{3,11},{4,12},{5,13},{6,14},{7,15},{8,0},{9,1},... | collective-permute-start | bytes 294920 | tf_op jit(solution)/shard_map/ppermute | solution.py:397
  159.3 5.5 %collective-permute-start.60 = (bf16[192,256]{1,0:T(8,128)(2,1)S(1)}, bf16[192,256]{1,0:T(8,128)(2,1)S(1)}, u32[]{:S(2)}, u32[]{:S(2)}) collective-permute-start(bf16[192,256]{1,0:T(8,128)(2,1)S(1)} %get-tuple-element.209), channel_id=1, source_target_pairs={{0,12},{1,13},{2,14},{3,15},{4,8},{5,9},{6,10},{7,11},{8,4},{9,5},... | collective-permute-start | bytes 294920 | tf_op jit(solution)/shard_map/ppermute | solution.py:397

commit v6 on v5

--- a/solution.py
+++ b/solution.py
@@ -7,6 +7,7 @@
 
 
 HBM = pl.BlockSpec(memory_space=pltpu.HBM)
+SMEM = pl.BlockSpec(memory_space=pltpu.SMEM)
 VMEM = pl.BlockSpec(memory_space=pltpu.VMEM)
 PARAMS = pltpu.CompilerParams(vmem_limit_bytes=16 * 2**20)
 UNROLL = 32
@@ -38,19 +39,24 @@
 
 
 def pick_tiles(
-    parts, ref_table, slab_count, row_count, tile, group, column, carried=(), scalars=()
+    parts, ref_table, list_length, slab_count, row_count, tile, group, carried=(), scalars=()
 ):
     part_count = len(parts)
     part_rows = parts[0].shape[0]
-    listed = ref_table.shape[2] // slab_count
     whole = part_count == 1
+    entries = ref_table.shape[2] if whole else ref_table.shape[1]
+    listed = list_length
+    emit = whole and len(scalars) > 0
+    columns = parts[0].shape[1] // LANES
+    picked = columns * slab_count
+    matrix_shape = (pl.cdiv(slab_count, 8) * 8, pl.cdiv(entries, LANES) * LANES)
 
     def kernel(table_hbm, *refs):
         sources = refs[:part_count]
         first_out = part_count + len(carried) + len(scalars)
-        outs = refs[first_out : first_out + slab_count]
+        outs = refs[first_out : first_out + picked]
         table, table_sem, rows, sems, carry_sems, numbers, number_sems = refs[-7:]
-        last_out = first_out + slab_count + len(carried)
+        last_out = first_out + picked + len(carried)
         loads = [
             pltpu.make_async_copy(
                 refs[part_count + len(carried) + n], numbers.at[pl.ds(n, 1)], number_sems.at[n]
@@ -61,53 +67,74 @@
             load.start()
         moves = [
             pltpu.make_async_copy(
-                refs[part_count + n], refs[first_out + slab_count + n], carry_sems.at[n]
+                refs[part_count + n], refs[first_out + picked + n], carry_sems.at[n]
             )
             for n in range(len(carried))
         ]
         slab = lax.axis_index("slab")
         _, _, lead = seat(group)
-        fetch = pltpu.make_async_copy(table_hbm, table, table_sem)
-        fetch.start()
-        if not whole:
+        if whole:
+            table = table_hbm
+        else:
+            fetch = pltpu.make_async_copy(table_hbm, table, table_sem)
+            fetch.start()
             for k in range(part_count):
                 start = pl.multiple_of((lead ^ k) * part_rows, part_rows)
                 rows[pl.ds(start, part_rows), :] = sources[k][...]
-        fetch.wait()
+            fetch.wait()
         copies = []
         for k in reversed(range(slab_count)):
             for j in range(listed):
-                index = table[0, slab ^ k, slab * listed + j]
+                spot = (slab ^ k, slab * listed + j)
+                index = table[(0, *spot) if whole else spot]
                 start = pl.multiple_of(index * tile, tile)
-                if whole:
-                    source = sources[0].at[pl.ds(start, tile), pl.ds(column * LANES, LANES)]
-                    target = outs[k].at[pl.ds(j * tile, tile)]
-                    copies.append(pltpu.make_async_copy(source, target, sems.at[k, j]))
-                else:
-                    outs[k][j * tile : (j + 1) * tile, :] = rows[pl.ds(start, tile), :]
+                for column in range(columns):
+                    out = outs[column * slab_count + k]
+                    lanes = pl.ds(column * LANES, LANES)
+                    if whole:
+                        copies.append(
+                            pltpu.make_async_copy(
+                                sources[0].at[pl.ds(start, tile), lanes],
+                                out.at[pl.ds(j * tile, tile)],
+                                sems.at[column * slab_count + k, j],
+                            )
+                        )
+                    else:
+                        out[j * tile : (j + 1) * tile, :] = rows[pl.ds(start, tile), lanes]
         copies += moves
         for copy in copies:
             copy.start()
         for n, load in enumerate(loads):
             load.wait()
-            spot = refs[last_out + n]
-            spot[...] = jnp.full(spot.shape, numbers[n, 0], spot.dtype)
+            spread_out = refs[last_out + n]
+            spread_out[...] = jnp.full(spread_out.shape, numbers[n, 0], jnp.int32)
+        if emit:
+            matrix = refs[last_out + len(scalars)]
+            row = lax.broadcasted_iota(jnp.int32, matrix.shape, 0)
+            lane = lax.broadcasted_iota(jnp.int32, matrix.shape, 1)
+            filled = jnp.zeros(matrix.shape, jnp.int32)
+            for p in range(slab_count):
+                for j in range(entries):
+                    filled = jnp.where((row == p) & (lane == j), table[0, p, j], filled)
+            matrix[...] = filled
         for copy in copies:
             copy.wait()
 
     dtype = parts[0].dtype
     results = pl.pallas_call(
         kernel,
-        in_specs=[HBM] + [HBM if whole else VMEM] * part_count + [HBM] * (len(carried) + len(scalars)),
-        out_specs=[VMEM] * (slab_count + len(carried) + len(scalars)),
-        out_shape=[jax.ShapeDtypeStruct((listed * tile, LANES), dtype)] * slab_count
+        in_specs=[SMEM if whole else HBM]
+        + [HBM if whole else VMEM] * part_count + [HBM] * (len(carried) + len(scalars)),
+        out_specs=[VMEM] * (picked + len(carried) + len(scalars) + emit),
+        out_shape=[jax.ShapeDtypeStruct((listed * tile, LANES), dtype)] * picked
         + [jax.ShapeDtypeStruct(array.shape, array.dtype) for array in carried]
-        + [jax.ShapeDtypeStruct((8, LANES), array.dtype) for array in scalars],
+        + [jax.ShapeDtypeStruct((8, LANES), array.dtype) for array in scalars]
+        + [jax.ShapeDtypeStruct(matrix_shape, ref_table.dtype)] * emit,
         scratch_shapes=[
             pltpu.SMEM(ref_table.shape, ref_table.dtype),
             pltpu.SemaphoreType.DMA(()),
-            pltpu.VMEM((tile if whole else row_count, LANES), dtype),
-            pltpu.SemaphoreType.DMA((slab_count, listed)),
+            pltpu.VMEM((tile if whole else row_count, columns * LANES), dtype),
+            pltpu.SemaphoreType.DMA((picked, listed)),
             pltpu.SemaphoreType.DMA((max(len(carried), 1),)),
             pltpu.SMEM((max(len(scalars), 1), 1), jnp.int32),
             pltpu.SemaphoreType.DMA((max(len(scalars), 1),)),
@@ -115,7 +142,8 @@
         compiler_params=PARAMS,
         name="pick_tiles",
     )(ref_table, *parts, *carried, *scalars)
-    return results[:slab_count], results[slab_count:]
+    lists = [results[n : n + slab_count] for n in range(0, picked, slab_count)]
+    return lists, results[picked:]
 
 
 def convolve(arrived, tile_rows, tile_sources, tile_counts, tile_values, row_count, group, chunks):
@@ -426,8 +454,9 @@
     group = lax.axis_size("tm") // 2
     half = lax.axis_index("tm") // group
 
-    def pick(parts, table, column=0, *carried):
-        return pick_tiles(parts, table, slab_count, row_count, tile, group, column, *carried)
+    def pick(parts, table, *carried):
+        length = ref_lists.shape[2] // slab_count
+        return pick_tiles(parts, table, length, slab_count, row_count, tile, group, *carried)
 
     def mix(listed, live, chunks=1):
         arrived = swap_slabs(listed)
@@ -440,7 +469,7 @@
         return got if chunks > 1 else got[0]
 
     def back_and_mix(hidden):
-        return pack([mix(pick(swap_times(column), table)[0], counts) for column in hidden])
+        return pack([mix(pick(swap_times(column), table)[0][0], counts) for column in hidden])
 
     def run(mixed, layer, mode, *rest):
         return recur(mixed, layer, w_input, w_hidden, gate_bias, mode, *rest)
@@ -456,12 +485,8 @@
     def run_upper(mixed, layer, states):
         return [run(part, layer, UPPER, state) for part, state in zip(mixed[:-1], states)]
 
-    features = features[0]
-    columns = features.shape[1] // LANES
-    listed = [pick([features], ref_lists, column)[0] for column in range(columns - 1)]
-    last, (table, gate_bias, counts) = pick(
-        [features], ref_lists, columns - 1, (ref_lists, bias), (tile_counts,)
-    )
+    listed, (gate_bias, counts, table) = pick([features[0]], ref_lists, (bias,), (tile_counts,))
+    *listed, last = listed
     early = [mix(column, tile_counts) for column in listed]
     upper_mixed = [
         pack_chunk([*early, part], chunk) for chunk, part in enumerate(mix(last, tile_counts, CHUNKS))

time: 167 us -> 169 us (1.012)
    pallas_call x4 -> x3, Pallas kernels: 3.42 us -> 3.17 us  [pick_tiles(): pl.pallas_call(kernel, in_specs=[SMEM if whole else HBM] + [HBM if whole...]
  transfers between devices with their start and end apart: 43 -> 43, of which waited for: 20 -> 19; matrix products, arithmetic and copies ran while one was open for 0% -> 0% of each run, Pallas kernels for 11% -> 11%
where the time goes in v6:
time: 169 us; the launch traced here: 167 us
  starting transfers between devices  108 us (64%)
  waiting for transfers between devices  30.2 us (18%)
  Pallas kernels  25.5 us (15%)
  local copies, waits for them, and re-layouts  2.56 us (2%)
    ppermute x43, starting transfers between devices, send(): return lax.ppermute(array, AXES, pairs)  108 us
    ppermute x43, waiting for transfers between devices, send(): return lax.ppermute(array, AXES, pairs)  30.2 us
    pallas_call x7, Pallas kernels, recur(): pl.pallas_call(kernel, in_specs=[VMEM] * (3 + len(operands)), out_specs=[...  12.1 us
    pallas_call x4, Pallas kernels, convolve(): pl.pallas_call(kernel, in_specs=[HBM, HBM, HBM, VMEM] + [VMEM] * slab_cou...  5.98 us
  transfers between devices with their start and end apart: 43, of which 19 were waited for; matrix products, arithmetic and copies ran while one was open for 0% of the time, Pallas kernels for 11%

profile of v6, /device:TPU:0, one launch (start us, length us, event | category | flops | bytes accessed | tf_op | source)
XLA Modules:
  0.0 166.9 jit_solution(17007670333045226167)
XLA Ops:
  0.7 1.1 copy-done
  2.5 1.5 pick_tiles.9
  4.6 2.6 %collective-permute-start.43 = (bf16[512,128]{1,0:T(8,128)(2,1)S(1)}, bf16[512,128]{1,0:T(8,128)(2,1)S(1)}, u32[]{:S(2)}, u32[]{:S(2)}) collective-permute-start(bf16[512,128]{1,0:T(8,128)(2,1)S(1)} %get-tuple-element.177), channel_id=1, source_target_pairs={{0,2},{1,3},{2,0},{3,1},{4,6},{5,7},{6,4},{7,5},{8,10},{9,11},{10,... | collective-permute-start | bytes 393224 | tf_op jit(solution)/shard_map/ppermute | solution.py:425
  7.4 1.9 %collective-permute-start.37 = (bf16[512,128]{1,0:T(8,128)(2,1)S(1)}, bf16[512,128]{1,0:T(8,128)(2,1)S(1)}, u32[]{:S(2)}, u32[]{:S(2)}) collective-permute-start(bf16[512,128]{1,0:T(8,128)(2,1)S(1)} %get-tuple-element.169), channel_id=1, source_target_pairs={{0,2},{1,3},{2,0},{3,1},{4,6},{5,7},{6,4},{7,5},{8,10},{9,11},{10,... | collective-permute-start | bytes 393224 | tf_op jit(solution)/shard_map/ppermute | solution.py:425
  9.3 2.2 %collective-permute-done.43.refs_6_ = bf16[512,128]{1,0:T(8,128)(2,1)S(1)} collective-permute-done((bf16[512,128]{1,0:T(8,128)(2,1)S(1)}, bf16[512,128]{1,0:T(8,128)(2,1)S(1)}, u32[]{:S(2)}, u32[]{:S(2)}) %collective-permute-start.43) | collective-permute-done | bytes 131104 | tf_op jit(solution)/shard_map/ppermute | solution.py:425
  11.5 2.4 %collective-permute-done.44.refs_7_ = bf16[512,128]{1,0:T(8,128)(2,1)S(1)} collective-permute-done((bf16[512,128]{1,0:T(8,128)(2,1)S(1)}, bf16[512,128]{1,0:T(8,128)(2,1)S(1)}, u32[]{:S(2)}, u32[]{:S(2)}) %collective-permute-start.44) | collective-permute-done | bytes 131104 | tf_op jit(solution)/shard_map/ppermute | solution.py:425
  13.9 2.4 %convolve.11 = (bf16[192,128]{1,0:T(8,128)(2,1)S(1)}, bf16[192,128]{1,0:T(8,128)(2,1)S(1)}, bf16[192,128]{1,0:T(8,128)(2,1)S(1)}, bf16[192,128]{1,0:T(8,128)(2,1...) custom-call(s32[1,32]{1,0:T(1,128)} %refs_0_.3, ...), custom_call_target="tpu_custom_call" | custom-call | tf_op jit(solution)/shard_map/convolve/pallas_call | solution.py:203
  16.4 1.6 collective-permute-start.45
  18.0 1.5 collective-permute-done.38.refs_7_
  19.5 1.1 convolve.10
  20.6 1.6 collective-permute-start.39
  22.2 1.6 collective-permute-start.40
  24.2 1.5 collective-permute-start.46
  25.7 1.4 collective-permute-start.47
  27.1 3.5 %collective-permute-done.46.refs_6_ = bf16[192,128]{1,0:T(8,128)(2,1)S(1)} collective-permute-done((bf16[192,128]{1,0:T(8,128)(2,1)S(1)}, bf16[192,128]{1,0:T(8,128)(2,1)S(1)}, u32[]{:S(2)}, u32[]{:S(2)}) %collective-permute-start.46) | collective-permute-done | bytes 49184 | tf_op jit(solution)/shard_map/ppermute | solution.py:425
  31.3 1.4 collective-permute-start.49
  32.7 1.4 collective-permute-start.50
  34.1 0.8 pack_chunk.2.refs_0_
  35.0 2.8 %recur.9 = (bf16[4,192,256]{2,1,0:T(8,128)(2,1)}, bf16[2,192,256]{2,1,0:T(8,128)(2,1)S(1)}) custom-call(bf16[2,256,1024]{2,1,0:T(8,128)(2,1)S(1)} %copy-done.3, bf16[2,256,1024]{2,1,0:T(8,128)(2,1)S(1)} %copy-done.4, f32[2,1024]{1,0:T(2,128)S(1)} %get-tuple-element.166.gate_bias, bf16[4,192,256]{2,1,0:T(8,128)(2,1)} %pack_chunk.2.refs_0_), custom_call_target="tpu_custom_call" | custom-call | tf_op jit(solution)/shard_map/recur/pallas_call | solution.py:373
  37.9 1.8 %recur.10 = (bf16[4,192,256]{2,1,0:T(8,128)(2,1)}, bf16[2,192,256]{2,1,0:T(8,128)(2,1)S(1)}) custom-call(bf16[2,256,1024]{2,1,0:T(8,128)(2,1)S(1)} %copy-done.3, bf16[2,256,1024]{2,1,0:T(8,128)(2,1)S(1)} %copy-done.4, f32[2,1024]{1,0:T(2,128)S(1)} %get-tuple-element.166.gate_bias, bf16[4,192,256]{2,1,0:T(8,128)(2,1)S(1)} %pack_chunk.3.refs_0_), custom_call_target="tpu_custom_call" | custom-call | tf_op jit(solution)/shard_map/recur/pallas_call | solution.py:373
  40.4 38.3 %conditional.2 = (bf16[4,192,256]{2,1,0:T(8,128)(2,1)}, bf16[4,192,256]{2,1,0:T(8,128)(2,1)}, s32[]{:T(128)}) conditional(s32[]{:T(128)} %convert_element_type.6, (bf16[4,192,256]{2,1,0:T(8,128)(2,1)}, bf16[4,192,256]{2,1,0:T(8,128)(2,1)}, s32[]{:T(128)}) %tuple.18, (bf16[4,192,256]{2,1,0:T(8,128)(2,1)}, bf16[4,192,256]{2,1,0:T(8,128)(2,1)}, ...), branch_computations={%region_0.1_spmd, %region_1.2_spmd} | conditional | flops 1 | bytes 12059408 | solution.py:503
  40.4 1.3 spread.1
  41.8 1.5 collective-permute-start
  43.9 1.4 collective-permute-start.2
  45.3 1.4 collective-permute-start.9
  46.7 1.6 collective-permute-done.refs_1_
  48.4 1.1 collective-permute-done.2.refs_3_
  50.4 1.4 collective-permute-start.10
  51.8 1.7 collective-permute-start.11
  53.5 1.8 %collective-permute-start.4 = (bf16[512,128]{1,0:T(8,128)(2,1)S(1)}, bf16[512,128]{1,0:T(8,128)(2,1)S(1)}, u32[]{:S(2)}, u32[]{:S(2)}) collective-permute-start(bf16[512,128]{1,0:T(8,128)(2,1)S(1)} %get-tuple-element.66), channel_id=1, source_target_pairs={{0,2},{1,3},{2,0},{3,1},{4,6},{5,7},{6,4},{7,5},{8,10},{9,11},{10,... | collective-permute-start | bytes 393224 | tf_op jit(solution)/shard_map/cond/branch_1_fun/ppermute | solution.py:425
  55.2 0.9 collective-permute-done.10.refs_2_
  56.1 2.5 %collective-permute-done.11.refs_3_ = bf16[384,128]{1,0:T(8,128)(2,1)S(1)} collective-permute-done((bf16[384,128]{1,0:T(8,128)(2,1)S(1)}, bf16[384,128]{1,0:T(8,128)(2,1)S(1)}, u32[]{:S(2)}, u32[]{:S(2)}) %collective-permute-start.11) | collective-permute-done | bytes 98336 | tf_op jit(solution)/shard_map/cond/branch_1_fun/ppermute | solution.py:425
  59.6 1.9 %collective-permute-start.13 = (bf16[512,128]{1,0:T(8,128)(2,1)S(1)}, bf16[512,128]{1,0:T(8,128)(2,1)S(1)}, u32[]{:S(2)}, u32[]{:S(2)}) collective-permute-start(bf16[512,128]{1,0:T(8,128)(2,1)S(1)} %get-tuple-element.78), channel_id=1, source_target_pairs={{0,2},{1,3},{2,0},{3,1},{4,6},{5,7},{6,4},{7,5},{8,10},{9,11},{10,... | collective-permute-start | bytes 393224 | tf_op jit(solution)/shard_map/cond/branch_1_fun/ppermute | solution.py:425
  61.5 1.2 convolve.6
  63.3 1.5 collective-permute-start.7
  64.8 1.4 collective-permute-start.8
  66.2 1.6 collective-permute-done.14.refs_7_
  67.8 1.2 convolve.7
  69.7 1.7 %collective-permute-start.16 = (bf16[384,128]{1,0:T(8,128)(2,1)S(1)}, bf16[384,128]{1,0:T(8,128)(2,1)S(1)}, u32[]{:S(2)}, u32[]{:S(2)}) collective-permute-start(bf16[384,128]{1,0:T(8,128)(2,1)S(1)} %get-tuple-element.82), channel_id=1, source_target_pairs={{0,8},{1,9},{2,10},{3,11},{4,12},{5,13},{6,14},{7,15},{8,0},{9,1},... | collective-permute-start | bytes 294920 | tf_op jit(solution)/shard_map/cond/branch_1_fun/ppermute | solution.py:425
  71.4 1.2 collective-permute-start.17
  72.6 1.8 %collective-permute-done.15.refs_5_ = bf16[384,128]{1,0:T(8,128)(2,1)S(1)} collective-permute-done((bf16[384,128]{1,0:T(8,128)(2,1)S(1)}, bf16[384,128]{1,0:T(8,128)(2,1)S(1)}, u32[]{:S(2)}, u32[]{:S(2)}) %collective-permute-start.15) | collective-permute-done | bytes 98336 | tf_op jit(solution)/shard_map/cond/branch_1_fun/ppermute | solution.py:425
  74.4 0.9 collective-permute-done.16.refs_6_
  75.3 2.4 %collective-permute-done.17.refs_7_ = bf16[384,128]{1,0:T(8,128)(2,1)S(1)} collective-permute-done((bf16[384,128]{1,0:T(8,128)(2,1)S(1)}, bf16[384,128]{1,0:T(8,128)(2,1)S(1)}, u32[]{:S(2)}, u32[]{:S(2)}) %collective-permute-start.17) | collective-permute-done | bytes 98336 | tf_op jit(solution)/shard_map/cond/branch_1_fun/ppermute | solution.py:425
  77.7 1.0 pack.2
  78.7 1.3 collective-permute-start.51
  80.0 1.3 collective-permute-start.52
  81.4 2.5 %recur.12 = (bf16[4,192,256]{2,1,0:T(8,128)(2,1)S(1)}, bf16[2,192,256]{2,1,0:T(8,128)(2,1)S(1)}) custom-call(bf16[2,256,1024]{2,1,0:T(8,128)(2,1)S(1)} %copy-done.3, bf16[2,256,1024]{2,1,0:T(8,128)(2,1)} %w_rec.13, f32[2,1024]{1,0:T(2,128)S(1)} %get-tuple-element.166.gate_bias, bf16[4,192,256]{2,1,0:T(8,128)(2,1)} %get-tuple-element.195.refs_0_), custom_call_target="tpu_custom_call" | custom-call | tf_op jit(solution)/shard_map/recur/pallas_call | solution.py:373
  83.8 1.5 collective-permute-done.51.refs_1_
  85.3 1.8 %recur.11 = bf16[4,192,256]{2,1,0:T(8,128)(2,1)} custom-call(bf16[2,256,1024]{2,1,0:T(8,128)(2,1)S(1)} %copy-done.3, bf16[2,256,1024]{2,1,0:T(8,128)(2,1)S(1)} %copy-done.5, f32[2,1024]{1,0:T(2,128)S(1)} %get-tuple-element.166.gate_bias, bf16[4,192,256]{2,1,0:T(8,128)(2,1)} %pack_chunk.2.refs_0_, bf16[2,192,256]{2,1,0:T(8,128)(2,1)S(1)} %collective-permute-done.51.refs_1_), custom_call_target="tpu_custom_call" | custom-call | tf_op jit(solution)/shard_map/recur/pallas_call | solution.py:373
  87.1 1.3 collective-permute-done.52
  88.4 52.4 %collective-permute-start.53 = (bf16[2,192,256]{2,1,0:T(8,128)(2,1)S(1)}, bf16[2,192,256]{2,1,0:T(8,128)(2,1)S(1)}, u32[]{:S(2)}, u32[]{:S(2)}) collective-permute-start(bf16[2,192,256]{2,1,0:T(8,128)(2,1)S(1)} %get-tuple-element.197), channel_id=1, source_target_pairs={{0,24},{1,25},{2,26},{3,27},{4,28},{5,29},{6,30},{7,31},{8,16},{9,... | collective-permute-start | bytes 589832 | tf_op jit(solution)/shard_map/ppermute | solution.py:425
  140.7 2.1 %recur.14 = (bf16[4,192,256]{2,1,0:T(8,128)(2,1)S(1)}, bf16[2,192,256]{2,1,0:T(8,128)(2,1)S(1)}) custom-call(bf16[2,256,1024]{2,1,0:T(8,128)(2,1)S(1)} %copy-done.3, bf16[2,256,1024]{2,1,0:T(8,128)(2,1)S(1)} %copy-done.5, f32[2,1024]{1,0:T(2,128)S(1)} %get-tuple-element.166.gate_bias, bf16[4,192,256]{2,1,0:T(8,128)(2,1)} %get-tuple-element.203.refs_0_), custom_call_target="tpu_custom_call" | custom-call | tf_op jit(solution)/shard_map/recur/pallas_call | solution.py:373
  142.8 1.3 collective-permute-start.57
  144.1 1.1 collective-permute-done.53.refs_2_
  145.2 1.1 recur.13
  146.3 1.3 collective-permute-start.54
  147.6 9.1 %collective-permute-start.55 = (bf16[192,256]{1,0:T(8,128)(2,1)S(1)}, bf16[192,256]{1,0:T(8,128)(2,1)S(1)}, u32[]{:S(2)}, u32[]{:S(2)}) collective-permute-start(bf16[192,256]{1,0:T(8,128)(2,1)S(1)} %get-tuple-element.200), channel_id=1, source_target_pairs={{0,8},{1,9},{2,10},{3,11},{4,12},{5,13},{6,14},{7,15},{8,0},{9,1},... | collective-permute-start | bytes 294920 | tf_op jit(solution)/shard_map/ppermute | solution.py:425
  156.9 1.3 collective-permute-start.58
  158.2 2.0 %collective-permute-start.59 = (bf16[192,256]{1,0:T(8,128)(2,1)S(1)}, bf16[192,256]{1,0:T(8,128)(2,1)S(1)}, u32[]{:S(2)}, u32[]{:S(2)}) collective-permute-start(bf16[192,256]{1,0:T(8,128)(2,1)S(1)} %get-tuple-element.208), channel_id=1, source_target_pairs={{0,8},{1,9},{2,10},{3,11},{4,12},{5,13},{6,14},{7,15},{8,0},{9,1},... | collective-permute-start | bytes 294920 | tf_op jit(solution)/shard_map/ppermute | solution.py:425
  160.3 1.7 collective-permute-start.60
  161.9 0.8 collective-permute-done.56.refs_3_
  162.7 1.0 collective-permute-done.58.refs_5_
  163.9 1.8 %collective-permute-done.60.refs_7_ = bf16[192,256]{1,0:T(8,128)(2,1)S(1)} collective-permute-done((bf16[192,256]{1,0:T(8,128)(2,1)S(1)}, bf16[192,256]{1,0:T(8,128)(2,1)S(1)}, u32[]{:S(2)}, u32[]{:S(2)}) %collective-permute-start.60) | collective-permute-done | bytes 98336 | tf_op jit(solution)/shard_map/ppermute | solution.py:425
  165.8 0.9 assemble.1
  (71 shorter events, 7.6 us)
Async XLA Ops:
  0.0 0.7 copy-start.2
  0.7 1.1 copy-start
  1.8 0.7 copy-start.1
  2.5 16.9 %copy-start.6 = (bf16[1,32,128,128]{3,2,1,0:T(8,128)(2,1)S(1)}, bf16[1,32,128,128]{3,2,1,0:T(8,128)(2,1)}, u32[]{:S(2)}) copy-start(bf16[1,32,128,128]{3,2,1,0:T(8,128)(2,1)} %refs_3_.3) | copy-start | bytes 3145732
  4.1 5.3 %collective-permute-start.42 = (bf16[512,128]{1,0:T(8,128)(2,1)S(1)}, bf16[512,128]{1,0:T(8,128)(2,1)S(1)}, u32[]{:S(2)}, u32[]{:S(2)}) collective-permute-start(bf16[512,128]{1,0:T(8,128)(2,1)S(1)} %get-tuple-element.176), channel_id=1, source_target_pairs={{0,1},{1,0},{2,3},{3,2},{4,5},{5,4},{6,7},{7,6},{8,9},{9,8},{10,11... | collective-permute-start | bytes 393224 | tf_op jit(solution)/shard_map/ppermute | solution.py:425
  4.6 6.9 %collective-permute-start.43 = (bf16[512,128]{1,0:T(8,128)(2,1)S(1)}, bf16[512,128]{1,0:T(8,128)(2,1)S(1)}, u32[]{:S(2)}, u32[]{:S(2)}) collective-permute-start(bf16[512,128]{1,0:T(8,128)(2,1)S(1)} %get-tuple-element.177), channel_id=1, source_target_pairs={{0,2},{1,3},{2,0},{3,1},{4,6},{5,7},{6,4},{7,5},{8,10},{9,11},{10,... | collective-permute-start | bytes 393224 | tf_op jit(solution)/shard_map/ppermute | solution.py:425
  7.2 6.7 %collective-permute-start.44 = (bf16[512,128]{1,0:T(8,128)(2,1)S(1)}, bf16[512,128]{1,0:T(8,128)(2,1)S(1)}, u32[]{:S(2)}, u32[]{:S(2)}) collective-permute-start(bf16[512,128]{1,0:T(8,128)(2,1)S(1)} %get-tuple-element.178), channel_id=1, source_target_pairs={{0,3},{1,2},{2,1},{3,0},{4,7},{5,6},{6,5},{7,4},{8,11},{9,10},{10,... | collective-permute-start | bytes 393224 | tf_op jit(solution)/shard_map/ppermute | solution.py:425
  7.2 10.7 %collective-permute-start.36 = (bf16[512,128]{1,0:T(8,128)(2,1)S(1)}, bf16[512,128]{1,0:T(8,128)(2,1)S(1)}, u32[]{:S(2)}, u32[]{:S(2)}) collective-permute-start(bf16[512,128]{1,0:T(8,128)(2,1)S(1)} %get-tuple-element.168), channel_id=1, source_target_pairs={{0,1},{1,0},{2,3},{3,2},{4,5},{5,4},{6,7},{7,6},{8,9},{9,8},{10,11... | collective-permute-start | bytes 393224 | tf_op jit(solution)/shard_map/ppermute | solution.py:425
  7.4 10.6 %collective-permute-start.37 = (bf16[512,128]{1,0:T(8,128)(2,1)S(1)}, bf16[512,128]{1,0:T(8,128)(2,1)S(1)}, u32[]{:S(2)}, u32[]{:S(2)}) collective-permute-start(bf16[512,128]{1,0:T(8,128)(2,1)S(1)} %get-tuple-element.169), channel_id=1, source_target_pairs={{0,2},{1,3},{2,0},{3,1},{4,6},{5,7},{6,4},{7,5},{8,10},{9,11},{10,... | collective-permute-start | bytes 393224 | tf_op jit(solution)/shard_map/ppermute | solution.py:425
  9.3 10.1 %collective-permute-start.38 = (bf16[512,128]{1,0:T(8,128)(2,1)S(1)}, bf16[512,128]{1,0:T(8,128)(2,1)S(1)}, u32[]{:S(2)}, u32[]{:S(2)}) collective-permute-start(bf16[512,128]{1,0:T(8,128)(2,1)S(1)} %get-tuple-element.170), channel_id=1, source_target_pairs={{0,3},{1,2},{2,1},{3,0},{4,7},{5,6},{6,5},{7,4},{8,11},{9,10},{10,... | collective-permute-start | bytes 393224 | tf_op jit(solution)/shard_map/ppermute | solution.py:425
  16.3 3.1 %copy-start.11 = (s32[1,32]{1,0:T(1,128)S(1)}, s32[1,32]{1,0:T(1,128)}, u32[]{:S(2)}) copy-start(s32[1,32]{1,0:T(1,128)} %refs_0_.3) | copy-start | bytes 388
  16.3 3.1 %copy-start.13 = (s32[1,32]{1,0:T(1,128)S(1)}, s32[1,32]{1,0:T(1,128)}, u32[]{:S(2)}) copy-start(s32[1,32]{1,0:T(1,128)} %refs_1_.5) | copy-start | bytes 388
  16.4 9.4 %collective-permute-start.45 = (bf16[192,128]{1,0:T(8,128)(2,1)S(1)}, bf16[192,128]{1,0:T(8,128)(2,1)S(1)}, u32[]{:S(2)}, u32[]{:S(2)}) collective-permute-start(bf16[192,128]{1,0:T(8,128)(2,1)S(1)} %get-tuple-element.180), channel_id=1, source_target_pairs={{0,4},{1,5},{2,6},{3,7},{4,0},{5,1},{6,2},{7,3},{8,12},{9,13},{10,... | collective-permute-start | bytes 147464 | tf_op jit(solution)/shard_map/ppermute | solution.py:425
  19.4 15.5 %copy-start.3 = (bf16[2,256,1024]{2,1,0:T(8,128)(2,1)S(1)}, bf16[2,256,1024]{2,1,0:T(8,128)(2,1)}, u32[]{:S(2)}) copy-start(bf16[2,256,1024]{2,1,0:T(8,128)(2,1)} %w_in.13) | copy-start | bytes 3145732
  19.5 15.5 %copy-start.4 = (bf16[2,256,1024]{2,1,0:T(8,128)(2,1)S(1)}, bf16[2,256,1024]{2,1,0:T(8,128)(2,1)}, u32[]{:S(2)}) copy-start(bf16[2,256,1024]{2,1,0:T(8,128)(2,1)} %w_rec.13) | copy-start | bytes 3145732
  20.6 12.1 %collective-permute-start.39 = (bf16[384,128]{1,0:T(8,128)(2,1)S(1)}, bf16[384,128]{1,0:T(8,128)(2,1)S(1)}, u32[]{:S(2)}, u32[]{:S(2)}) collective-permute-start(bf16[384,128]{1,0:T(8,128)(2,1)S(1)} %get-tuple-element.172), channel_id=1, source_target_pairs={{0,4},{1,5},{2,6},{3,7},{4,0},{5,1},{6,2},{7,3},{8,12},{9,13},{10,... | collective-permute-start | bytes 294920 | tf_op jit(solution)/shard_map/ppermute | solution.py:425
  22.2 12.0 %collective-permute-start.40 = (bf16[384,128]{1,0:T(8,128)(2,1)S(1)}, bf16[384,128]{1,0:T(8,128)(2,1)S(1)}, u32[]{:S(2)}, u32[]{:S(2)}) collective-permute-start(bf16[384,128]{1,0:T(8,128)(2,1)S(1)} %get-tuple-element.173), channel_id=1, source_target_pairs={{0,8},{1,9},{2,10},{3,11},{4,12},{5,13},{6,14},{7,15},{8,0},{9,1},... | collective-permute-start | bytes 294920 | tf_op jit(solution)/shard_map/ppermute | solution.py:425
  23.7 10.4 %collective-permute-start.41 = (bf16[384,128]{1,0:T(8,128)(2,1)S(1)}, bf16[384,128]{1,0:T(8,128)(2,1)S(1)}, u32[]{:S(2)}, u32[]{:S(2)}) collective-permute-start(bf16[384,128]{1,0:T(8,128)(2,1)S(1)} %get-tuple-element.174), channel_id=1, source_target_pairs={{0,12},{1,13},{2,14},{3,15},{4,8},{5,9},{6,10},{7,11},{8,4},{9,5},... | collective-permute-start | bytes 294920 | tf_op jit(solution)/shard_map/ppermute | solution.py:425
  24.2 6.5 %collective-permute-start.46 = (bf16[192,128]{1,0:T(8,128)(2,1)S(1)}, bf16[192,128]{1,0:T(8,128)(2,1)S(1)}, u32[]{:S(2)}, u32[]{:S(2)}) collective-permute-start(bf16[192,128]{1,0:T(8,128)(2,1)S(1)} %get-tuple-element.181), channel_id=1, source_target_pairs={{0,8},{1,9},{2,10},{3,11},{4,12},{5,13},{6,14},{7,15},{8,0},{9,1},... | collective-permute-start | bytes 147464 | tf_op jit(solution)/shard_map/ppermute | solution.py:425
  25.7 5.6 %collective-permute-start.47 = (bf16[192,128]{1,0:T(8,128)(2,1)S(1)}, bf16[192,128]{1,0:T(8,128)(2,1)S(1)}, u32[]{:S(2)}, u32[]{:S(2)}) collective-permute-start(bf16[192,128]{1,0:T(8,128)(2,1)S(1)} %get-tuple-element.182), channel_id=1, source_target_pairs={{0,12},{1,13},{2,14},{3,15},{4,8},{5,9},{6,10},{7,11},{8,4},{9,5},... | collective-permute-start | bytes 147464 | tf_op jit(solution)/shard_map/ppermute | solution.py:425
  30.6 7.2 %collective-permute-start.48 = (bf16[192,128]{1,0:T(8,128)(2,1)S(1)}, bf16[192,128]{1,0:T(8,128)(2,1)S(1)}, u32[]{:S(2)}, u32[]{:S(2)}) collective-permute-start(bf16[192,128]{1,0:T(8,128)(2,1)S(1)} %get-tuple-element.185), channel_id=1, source_target_pairs={{0,4},{1,5},{2,6},{3,7},{4,0},{5,1},{6,2},{7,3},{8,12},{9,13},{10,... | collective-permute-start | bytes 147464 | tf_op jit(solution)/shard_map/ppermute | solution.py:425
  31.3 6.5 %collective-permute-start.49 = (bf16[192,128]{1,0:T(8,128)(2,1)S(1)}, bf16[192,128]{1,0:T(8,128)(2,1)S(1)}, u32[]{:S(2)}, u32[]{:S(2)}) collective-permute-start(bf16[192,128]{1,0:T(8,128)(2,1)S(1)} %get-tuple-element.186), channel_id=1, source_target_pairs={{0,8},{1,9},{2,10},{3,11},{4,12},{5,13},{6,14},{7,15},{8,0},{9,1},... | collective-permute-start | bytes 147464 | tf_op jit(solution)/shard_map/ppermute | solution.py:425
  32.7 5.1 %collective-permute-start.50 = (bf16[192,128]{1,0:T(8,128)(2,1)S(1)}, bf16[192,128]{1,0:T(8,128)(2,1)S(1)}, u32[]{:S(2)}, u32[]{:S(2)}) collective-permute-start(bf16[192,128]{1,0:T(8,128)(2,1)S(1)} %get-tuple-element.187), channel_id=1, source_target_pairs={{0,12},{1,13},{2,14},{3,15},{4,8},{5,9},{6,10},{7,11},{8,4},{9,5},... | collective-permute-start | bytes 147464 | tf_op jit(solution)/shard_map/ppermute | solution.py:425
  37.9 1.8 %copy-start.9 = (bf16[4,192,256]{2,1,0:T(8,128)(2,1)}, bf16[4,192,256]{2,1,0:T(8,128)(2,1)S(1)}, u32[]{:S(2)}) copy-start(bf16[4,192,256]{2,1,0:T(8,128)(2,1)S(1)} %pack_chunk.3.refs_0_) | copy-start | bytes 1179652
  39.8 0.7 copy-start.12
  39.8 0.7 copy-start.14
  40.4 21.0 %copy-start.7 = (bf16[1,32,128,128]{3,2,1,0:T(8,128)(2,1)S(1)}, bf16[1,32,128,128]{3,2,1,0:T(8,128)(2,1)}, u32[]{:S(2)}) copy-start(bf16[1,32,128,128]{3,2,1,0:T(8,128)(2,1)} %get-tuple-element.56.refs_3_) | copy-start | bytes 3145732 | tf_op jit(solution)/shard_map/cond
  41.8 6.6 %collective-permute-start = (bf16[384,128]{1,0:T(8,128)(2,1)S(1)}, bf16[384,128]{1,0:T(8,128)(2,1)S(1)}, u32[]{:S(2)}, u32[]{:S(2)}) collective-permute-start(bf16[384,128]{1,0:T(8,128)(2,1)S(1)} %get-tuple-element.61), channel_id=1, source_target_pairs={{0,4},{1,5},{2,6},{3,7},{4,0},{5,1},{6,2},{7,3},{8,12},{9,13},{10,... | collective-permute-start | bytes 294920 | tf_op jit(solution)/shard_map/cond/branch_1_fun/ppermute | solution.py:425
  43.2 5.1 %collective-permute-start.1 = (bf16[384,128]{1,0:T(8,128)(2,1)S(1)}, bf16[384,128]{1,0:T(8,128)(2,1)S(1)}, u32[]{:S(2)}, u32[]{:S(2)}) collective-permute-start(bf16[384,128]{1,0:T(8,128)(2,1)S(1)} %get-tuple-element.62), channel_id=1, source_target_pairs={{0,8},{1,9},{2,10},{3,11},{4,12},{5,13},{6,14},{7,15},{8,0},{9,1},... | collective-permute-start | bytes 294920 | tf_op jit(solution)/shard_map/cond/branch_1_fun/ppermute | solution.py:425
  43.9 5.6 %collective-permute-start.2 = (bf16[384,128]{1,0:T(8,128)(2,1)S(1)}, bf16[384,128]{1,0:T(8,128)(2,1)S(1)}, u32[]{:S(2)}, u32[]{:S(2)}) collective-permute-start(bf16[384,128]{1,0:T(8,128)(2,1)S(1)} %get-tuple-element.63), channel_id=1, source_target_pairs={{0,12},{1,13},{2,14},{3,15},{4,8},{5,9},{6,10},{7,11},{8,4},{9,5},... | collective-permute-start | bytes 294920 | tf_op jit(solution)/shard_map/cond/branch_1_fun/ppermute | solution.py:425
  45.3 9.9 %collective-permute-start.9 = (bf16[384,128]{1,0:T(8,128)(2,1)S(1)}, bf16[384,128]{1,0:T(8,128)(2,1)S(1)}, u32[]{:S(2)}, u32[]{:S(2)}) collective-permute-start(bf16[384,128]{1,0:T(8,128)(2,1)S(1)} %get-tuple-element.73), channel_id=1, source_target_pairs={{0,4},{1,5},{2,6},{3,7},{4,0},{5,1},{6,2},{7,3},{8,12},{9,13},{10,... | collective-permute-start | bytes 294920 | tf_op jit(solution)/shard_map/cond/branch_1_fun/ppermute | solution.py:425
  50.3 11.1 %collective-permute-start.3 = (bf16[512,128]{1,0:T(8,128)(2,1)S(1)}, bf16[512,128]{1,0:T(8,128)(2,1)S(1)}, u32[]{:S(2)}, u32[]{:S(2)}) collective-permute-start(bf16[512,128]{1,0:T(8,128)(2,1)S(1)} %get-tuple-element.65), channel_id=1, source_target_pairs={{0,1},{1,0},{2,3},{3,2},{4,5},{5,4},{6,7},{7,6},{8,9},{9,8},{10,11... | collective-permute-start | bytes 393224 | tf_op jit(solution)/shard_map/cond/branch_1_fun/ppermute | solution.py:425
  50.4 5.7 %collective-permute-start.10 = (bf16[384,128]{1,0:T(8,128)(2,1)S(1)}, bf16[384,128]{1,0:T(8,128)(2,1)S(1)}, u32[]{:S(2)}, u32[]{:S(2)}) collective-permute-start(bf16[384,128]{1,0:T(8,128)(2,1)S(1)} %get-tuple-element.74), channel_id=1, source_target_pairs={{0,8},{1,9},{2,10},{3,11},{4,12},{5,13},{6,14},{7,15},{8,0},{9,1},... | collective-permute-start | bytes 294920 | tf_op jit(solution)/shard_map/cond/branch_1_fun/ppermute | solution.py:425
  51.8 6.9 %collective-permute-start.11 = (bf16[384,128]{1,0:T(8,128)(2,1)S(1)}, bf16[384,128]{1,0:T(8,128)(2,1)S(1)}, u32[]{:S(2)}, u32[]{:S(2)}) collective-permute-start(bf16[384,128]{1,0:T(8,128)(2,1)S(1)} %get-tuple-element.75), channel_id=1, source_target_pairs={{0,12},{1,13},{2,14},{3,15},{4,8},{5,9},{6,10},{7,11},{8,4},{9,5},... | collective-permute-start | bytes 294920 | tf_op jit(solution)/shard_map/cond/branch_1_fun/ppermute | solution.py:425
  53.5 8.0 %collective-permute-start.4 = (bf16[512,128]{1,0:T(8,128)(2,1)S(1)}, bf16[512,128]{1,0:T(8,128)(2,1)S(1)}, u32[]{:S(2)}, u32[]{:S(2)}) collective-permute-start(bf16[512,128]{1,0:T(8,128)(2,1)S(1)} %get-tuple-element.66), channel_id=1, source_target_pairs={{0,2},{1,3},{2,0},{3,1},{4,6},{5,7},{6,4},{7,5},{8,10},{9,11},{10,... | collective-permute-start | bytes 393224 | tf_op jit(solution)/shard_map/cond/branch_1_fun/ppermute | solution.py:425
  55.2 6.2 %collective-permute-start.5 = (bf16[512,128]{1,0:T(8,128)(2,1)S(1)}, bf16[512,128]{1,0:T(8,128)(2,1)S(1)}, u32[]{:S(2)}, u32[]{:S(2)}) collective-permute-start(bf16[512,128]{1,0:T(8,128)(2,1)S(1)} %get-tuple-element.67), channel_id=1, source_target_pairs={{0,3},{1,2},{2,1},{3,0},{4,7},{5,6},{6,5},{7,4},{8,11},{9,10},{10,... | collective-permute-start | bytes 393224 | tf_op jit(solution)/shard_map/cond/branch_1_fun/ppermute | solution.py:425
  59.5 5.3 %collective-permute-start.12 = (bf16[512,128]{1,0:T(8,128)(2,1)S(1)}, bf16[512,128]{1,0:T(8,128)(2,1)S(1)}, u32[]{:S(2)}, u32[]{:S(2)}) collective-permute-start(bf16[512,128]{1,0:T(8,128)(2,1)S(1)} %get-tuple-element.77), channel_id=1, source_target_pairs={{0,1},{1,0},{2,3},{3,2},{4,5},{5,4},{6,7},{7,6},{8,9},{9,8},{10,11... | collective-permute-start | bytes 393224 | tf_op jit(solution)/shard_map/cond/branch_1_fun/ppermute | solution.py:425
  59.6 6.7 %collective-permute-start.13 = (bf16[512,128]{1,0:T(8,128)(2,1)S(1)}, bf16[512,128]{1,0:T(8,128)(2,1)S(1)}, u32[]{:S(2)}, u32[]{:S(2)}) collective-permute-start(bf16[512,128]{1,0:T(8,128)(2,1)S(1)} %get-tuple-element.78), channel_id=1, source_target_pairs={{0,2},{1,3},{2,0},{3,1},{4,6},{5,7},{6,4},{7,5},{8,10},{9,11},{10,... | collective-permute-start | bytes 393224 | tf_op jit(solution)/shard_map/cond/branch_1_fun/ppermute | solution.py:425
  61.4 6.4 %collective-permute-start.14 = (bf16[512,128]{1,0:T(8,128)(2,1)S(1)}, bf16[512,128]{1,0:T(8,128)(2,1)S(1)}, u32[]{:S(2)}, u32[]{:S(2)}) collective-permute-start(bf16[512,128]{1,0:T(8,128)(2,1)S(1)} %get-tuple-element.79), channel_id=1, source_target_pairs={{0,3},{1,2},{2,1},{3,0},{4,7},{5,6},{6,5},{7,4},{8,11},{9,10},{10,... | collective-permute-start | bytes 393224 | tf_op jit(solution)/shard_map/cond/branch_1_fun/ppermute | solution.py:425
  62.7 8.7 %collective-permute-start.6 = (bf16[384,128]{1,0:T(8,128)(2,1)S(1)}, bf16[384,128]{1,0:T(8,128)(2,1)S(1)}, u32[]{:S(2)}, u32[]{:S(2)}) collective-permute-start(bf16[384,128]{1,0:T(8,128)(2,1)S(1)} %get-tuple-element.69), channel_id=1, source_target_pairs={{0,4},{1,5},{2,6},{3,7},{4,0},{5,1},{6,2},{7,3},{8,12},{9,13},{10,... | collective-permute-start | bytes 294920 | tf_op jit(solution)/shard_map/cond/branch_1_fun/ppermute | solution.py:425
  63.3 9.3 %collective-permute-start.7 = (bf16[384,128]{1,0:T(8,128)(2,1)S(1)}, bf16[384,128]{1,0:T(8,128)(2,1)S(1)}, u32[]{:S(2)}, u32[]{:S(2)}) collective-permute-start(bf16[384,128]{1,0:T(8,128)(2,1)S(1)} %get-tuple-element.70), channel_id=1, source_target_pairs={{0,8},{1,9},{2,10},{3,11},{4,12},{5,13},{6,14},{7,15},{8,0},{9,1},... | collective-permute-start | bytes 294920 | tf_op jit(solution)/shard_map/cond/branch_1_fun/ppermute | solution.py:425
  64.8 7.8 %collective-permute-start.8 = (bf16[384,128]{1,0:T(8,128)(2,1)S(1)}, bf16[384,128]{1,0:T(8,128)(2,1)S(1)}, u32[]{:S(2)}, u32[]{:S(2)}) collective-permute-start(bf16[384,128]{1,0:T(8,128)(2,1)S(1)} %get-tuple-element.71), channel_id=1, source_target_pairs={{0,12},{1,13},{2,14},{3,15},{4,8},{5,9},{6,10},{7,11},{8,4},{9,5},... | collective-permute-start | bytes 294920 | tf_op jit(solution)/shard_map/cond/branch_1_fun/ppermute | solution.py:425
  69.0 5.4 %collective-permute-start.15 = (bf16[384,128]{1,0:T(8,128)(2,1)S(1)}, bf16[384,128]{1,0:T(8,128)(2,1)S(1)}, u32[]{:S(2)}, u32[]{:S(2)}) collective-permute-start(bf16[384,128]{1,0:T(8,128)(2,1)S(1)} %get-tuple-element.81), channel_id=1, source_target_pairs={{0,4},{1,5},{2,6},{3,7},{4,0},{5,1},{6,2},{7,3},{8,12},{9,13},{10,... | collective-permute-start | bytes 294920 | tf_op jit(solution)/shard_map/cond/branch_1_fun/ppermute | solution.py:425
  69.7 5.7 %collective-permute-start.16 = (bf16[384,128]{1,0:T(8,128)(2,1)S(1)}, bf16[384,128]{1,0:T(8,128)(2,1)S(1)}, u32[]{:S(2)}, u32[]{:S(2)}) collective-permute-start(bf16[384,128]{1,0:T(8,128)(2,1)S(1)} %get-tuple-element.82), channel_id=1, source_target_pairs={{0,8},{1,9},{2,10},{3,11},{4,12},{5,13},{6,14},{7,15},{8,0},{9,1},... | collective-permute-start | bytes 294920 | tf_op jit(solution)/shard_map/cond/branch_1_fun/ppermute | solution.py:425
  71.4 6.3 %collective-permute-start.17 = (bf16[384,128]{1,0:T(8,128)(2,1)S(1)}, bf16[384,128]{1,0:T(8,128)(2,1)S(1)}, u32[]{:S(2)}, u32[]{:S(2)}) collective-permute-start(bf16[384,128]{1,0:T(8,128)(2,1)S(1)} %get-tuple-element.83), channel_id=1, source_target_pairs={{0,12},{1,13},{2,14},{3,15},{4,8},{5,9},{6,10},{7,11},{8,4},{9,5},... | collective-permute-start | bytes 294920 | tf_op jit(solution)/shard_map/cond/branch_1_fun/ppermute | solution.py:425
  78.7 6.6 %collective-permute-start.51 = (bf16[2,192,256]{2,1,0:T(8,128)(2,1)S(1)}, bf16[2,192,256]{2,1,0:T(8,128)(2,1)S(1)}, u32[]{:S(2)}, u32[]{:S(2)}) collective-permute-start(bf16[2,192,256]{2,1,0:T(8,128)(2,1)S(1)} %get-tuple-element.192), channel_id=1, source_target_pairs={{0,24},{1,25},{2,26},{3,27},{4,28},{5,29},{6,30},{7,31},{8,16},{9,... | collective-permute-start | bytes 589832 | tf_op jit(solution)/shard_map/ppermute | solution.py:425
  80.0 8.3 %collective-permute-start.52 = (bf16[2,192,256]{2,1,0:T(8,128)(2,1)S(1)}, bf16[2,192,256]{2,1,0:T(8,128)(2,1)S(1)}, u32[]{:S(2)}, u32[]{:S(2)}) collective-permute-start(bf16[2,192,256]{2,1,0:T(8,128)(2,1)S(1)} %get-tuple-element.193), channel_id=1, source_target_pairs={{0,24},{1,25},{2,26},{3,27},{4,28},{5,29},{6,30},{7,31},{8,16},{9,... | collective-permute-start | bytes 589832 | tf_op jit(solution)/shard_map/ppermute | solution.py:425
  81.4 4.0 %copy-start.5 = (bf16[2,256,1024]{2,1,0:T(8,128)(2,1)S(1)}, bf16[2,256,1024]{2,1,0:T(8,128)(2,1)}, u32[]{:S(2)}) copy-start(bf16[2,256,1024]{2,1,0:T(8,128)(2,1)} %w_rec.13) | copy-start | bytes 3145732
  88.4 56.9 %collective-permute-start.53 = (bf16[2,192,256]{2,1,0:T(8,128)(2,1)S(1)}, bf16[2,192,256]{2,1,0:T(8,128)(2,1)S(1)}, u32[]{:S(2)}, u32[]{:S(2)}) collective-permute-start(bf16[2,192,256]{2,1,0:T(8,128)(2,1)S(1)} %get-tuple-element.197), channel_id=1, source_target_pairs={{0,24},{1,25},{2,26},{3,27},{4,28},{5,29},{6,30},{7,31},{8,16},{9,... | collective-permute-start | bytes 589832 | tf_op jit(solution)/shard_map/ppermute | solution.py:425
  142.8 14.1 %collective-permute-start.57 = (bf16[2,192,256]{2,1,0:T(8,128)(2,1)S(1)}, bf16[2,192,256]{2,1,0:T(8,128)(2,1)S(1)}, u32[]{:S(2)}, u32[]{:S(2)}) collective-permute-start(bf16[2,192,256]{2,1,0:T(8,128)(2,1)S(1)} %get-tuple-element.205), channel_id=1, source_target_pairs={{0,24},{1,25},{2,26},{3,27},{4,28},{5,29},{6,30},{7,31},{8,16},{9,... | collective-permute-start | bytes 589832 | tf_op jit(solution)/shard_map/ppermute | solution.py:425
  145.2 11.7 %copy-start.10 = (bf16[4,192,256]{2,1,0:T(8,128)(2,1)S(1)}, bf16[4,192,256]{2,1,0:T(8,128)(2,1)}, u32[]{:S(2)}) copy-start(bf16[4,192,256]{2,1,0:T(8,128)(2,1)} %get-tuple-element.202.refs_0_) | copy-start | bytes 1179652
  146.3 14.0 %collective-permute-start.54 = (bf16[192,256]{1,0:T(8,128)(2,1)S(1)}, bf16[192,256]{1,0:T(8,128)(2,1)S(1)}, u32[]{:S(2)}, u32[]{:S(2)}) collective-permute-start(bf16[192,256]{1,0:T(8,128)(2,1)S(1)} %get-tuple-element.199), channel_id=1, source_target_pairs={{0,4},{1,5},{2,6},{3,7},{4,0},{5,1},{6,2},{7,3},{8,12},{9,13},{10,... | collective-permute-start | bytes 294920 | tf_op jit(solution)/shard_map/ppermute | solution.py:425
  147.6 14.3 %collective-permute-start.55 = (bf16[192,256]{1,0:T(8,128)(2,1)S(1)}, bf16[192,256]{1,0:T(8,128)(2,1)S(1)}, u32[]{:S(2)}, u32[]{:S(2)}) collective-permute-start(bf16[192,256]{1,0:T(8,128)(2,1)S(1)} %get-tuple-element.200), channel_id=1, source_target_pairs={{0,8},{1,9},{2,10},{3,11},{4,12},{5,13},{6,14},{7,15},{8,0},{9,1},... | collective-permute-start | bytes 294920 | tf_op jit(solution)/shard_map/ppermute | solution.py:425
  156.7 6.1 %collective-permute-start.56 = (bf16[192,256]{1,0:T(8,128)(2,1)S(1)}, bf16[192,256]{1,0:T(8,128)(2,1)S(1)}, u32[]{:S(2)}, u32[]{:S(2)}) collective-permute-start(bf16[192,256]{1,0:T(8,128)(2,1)S(1)} %get-tuple-element.201), channel_id=1, source_target_pairs={{0,12},{1,13},{2,14},{3,15},{4,8},{5,9},{6,10},{7,11},{8,4},{9,5},... | collective-permute-start | bytes 294920 | tf_op jit(solution)/shard_map/ppermute | solution.py:425
  156.9 6.8 %collective-permute-start.58 = (bf16[192,256]{1,0:T(8,128)(2,1)S(1)}, bf16[192,256]{1,0:T(8,128)(2,1)S(1)}, u32[]{:S(2)}, u32[]{:S(2)}) collective-permute-start(bf16[192,256]{1,0:T(8,128)(2,1)S(1)} %get-tuple-element.207), channel_id=1, source_target_pairs={{0,4},{1,5},{2,6},{3,7},{4,0},{5,1},{6,2},{7,3},{8,12},{9,13},{10,... | collective-permute-start | bytes 294920 | tf_op jit(solution)/shard_map/ppermute | solution.py:425
  158.2 5.7 %collective-permute-start.59 = (bf16[192,256]{1,0:T(8,128)(2,1)S(1)}, bf16[192,256]{1,0:T(8,128)(2,1)S(1)}, u32[]{:S(2)}, u32[]{:S(2)}) collective-permute-start(bf16[192,256]{1,0:T(8,128)(2,1)S(1)} %get-tuple-element.208), channel_id=1, source_target_pairs={{0,8},{1,9},{2,10},{3,11},{4,12},{5,13},{6,14},{7,15},{8,0},{9,1},... | collective-permute-start | bytes 294920 | tf_op jit(solution)/shard_map/ppermute | solution.py:425
  160.3 5.5 %collective-permute-start.60 = (bf16[192,256]{1,0:T(8,128)(2,1)S(1)}, bf16[192,256]{1,0:T(8,128)(2,1)S(1)}, u32[]{:S(2)}, u32[]{:S(2)}) collective-permute-start(bf16[192,256]{1,0:T(8,128)(2,1)S(1)} %get-tuple-element.209), channel_id=1, source_target_pairs={{0,12},{1,13},{2,14},{3,15},{4,8},{5,9},{6,10},{7,11},{8,4},{9,5},... | collective-permute-start | bytes 294920 | tf_op jit(solution)/shard_map/ppermute | solution.py:425
